TPU v7x, 32 devices: a whole 2x2x4 slice. The times are simulated.
32 devices in a mesh: member: 2 (over y), win: 4 (over z), seq: 4 (over x, core).
Axes of the slice: x: 2, y: 2, z: 4, core: 2. Of those that a mesh axis runs over, the one named last changes fastest.
Arguments:
- pixel_grid_input: bfloat16 [8, 8, 4, 64, 1536], P(('member', 'win'), None, 'seq'), parts along dimension 0, may hold values from -6 to 6
- mask_zone_labeling: int32 [8, 32, 64], P(('member', 'win')), parts along dimension 0, may hold values from 0 to 8, as said below
- standardize_multiplier: float32 [1536], replicated, may hold values from 0.25 to 1.75
- standardize_offset_vector: float32 [1536], replicated, may hold values from -3 to 3
- triple_projection_matrix: bfloat16 [3, 1536, 1536], P(None, None, 'seq'), may hold values from -0.15625 to 0.15625
- logit_scaling_per_part: float32 [16], P('seq'), may hold values from 1 to 45
- final_projection_matrix: bfloat16 [1536, 1536], P('seq'), may hold values from -0.15625 to 0.15625
Outputs:
- mixed: bfloat16 [8, 8, 4, 64, 1536], P(('member', 'win'), None, 'seq'), parts along dimension 0
There are 2 independent parts, one for each index of `member`. A program takes and returns all parts, laid end to end along the dimension named above; an argument that names none is the same for every part. Nothing has to cross between parts.
Inputs may be any that keep to these rules, and one draw needn't show every extreme that they name: `mask_zone_labeling`: region is 3 * (row band) + (column band) of the pixel on the rolled grid: the row band is 0 in the first 32 rows, 1 in the next rows and 2 in the last few rows, whose count is drawn once for each member from 4 to 27; the column bands are cut the same way within the last 32 columns of the grid, with a count drawn apart. Only windows in the last window row or the last window column of the grid hold more than one region.
All inputs are finite; a program needn't handle non-finite values.
Results may differ from a plain program's by a relative error of at most 0.0065.
The roundings to bfloat16 on the way count: a program that leaves them out, or rounds other values in their place, can miss the bound.
Values may be sent and summed in bfloat16 or wider, within the bound.
No kernel may reach another device: no remote copies, remote signals or barrier semaphores. Data moves between devices by JAX's collectives and lax.ppermute only.
A program may use at most 64 MiB of HBM per device.

v0:
```python
import functools
import math

import jax
import jax.numpy as jnp
from jax import lax
from jax.experimental import pallas as pl
from jax.experimental.pallas import tpu as pltpu
from jax.sharding import PartitionSpec as P


CHANNEL_PER_PART = 96
WS = 32
REGIONS = 32
LANE = 128
FAR = -1e30
F32 = jnp.float32
BF16 = jnp.bfloat16


def permute_by(value, axis, move):
    count = lax.axis_size(axis)
    pairs = [(source, move(source, count)) for source in range(count)]
    return lax.ppermute(value, axis, pairs)


def exchange(value, mask, axis="seq"):
    return permute_by(value, axis, lambda source, count: source ^ mask)


def masks_of(count):
    masks = []
    while count > 1:
        count //= 2
        masks.append(count)
    return masks


def gather_pieces(piece):
    pieces = {0: piece}
    for mask in masks_of(lax.axis_size("seq")):
        for offset in list(pieces):
            pieces[offset ^ mask] = exchange(pieces[offset], mask)
    return [pieces[offset] for offset in range(len(pieces))]


def padded(width):
    return (width + LANE - 1) // LANE * LANE


VMEM = pl.BlockSpec(memory_space=pltpu.VMEM)


def after(value, *earlier):
    return lax.optimization_barrier((value, *earlier))[0]


def normalized(held, gain, bias):
    values = held.astype(F32)
    average = jnp.mean(values, axis=-1, keepdims=True)
    centred = values - average
    variance = jnp.mean(centred * centred, axis=-1, keepdims=True)
    return (centred * lax.rsqrt(variance + 1e-05) * gain + bias).astype(BF16)


HELD = pl.BlockSpec(memory_space=pltpu.HBM)


def cut_kernel(boxes, pixel_ref, *refs):
    outs, semaphore = refs[:-1], refs[-1]
    copies = [
        pltpu.make_async_copy(
            pixel_ref.at[pl.ds(row, rows), pl.ds(left, size), :], out_ref, semaphore.at[index]
        )
        for index, ((row, rows, left, size), out_ref) in enumerate(zip(boxes, outs, strict=True))
    ]
    for copy in copies:
        copy.start()
    for copy in copies:
        copy.wait()


def cut(pixels, boxes):
    width = pixels.shape[2]
    return pl.pallas_call(
        functools.partial(cut_kernel, boxes),
        out_shape=[jax.ShapeDtypeStruct((rows, size, width), BF16) for _, rows, _, size in boxes],
        in_specs=[HELD],
        out_specs=[VMEM] * len(boxes),
        scratch_shapes=[pltpu.SemaphoreType.DMA((len(boxes),))],
        compiler_params=pltpu.CompilerParams(vmem_limit_bytes=8 << 20),
        cost_estimate=pl.CostEstimate(flops=0, bytes_accessed=2 * pixels.size, transcendentals=0),
        name="cut",
    )(pixels)


def norm_local_kernel(boxes, pixel_ref, gain_ref, bias_ref, *refs):
    outs, helds, semaphore = refs[: len(boxes)], refs[len(boxes) : -1], refs[-1]
    copies = [
        pltpu.make_async_copy(
            pixel_ref.at[pl.ds(row, rows), pl.ds(left, size), :], held, semaphore.at[index]
        )
        for index, ((row, rows, left, size), held) in enumerate(zip(boxes, helds, strict=True))
    ]
    for copy in copies:
        copy.start()
    gain, bias = gain_ref[...], bias_ref[...]
    for copy, held, out_ref in zip(copies, helds, outs, strict=True):
        copy.wait()
        size = held.shape[1]
        for row in range(held.shape[0]):
            out_ref[row * size : (row + 1) * size, :] = normalized(held[row], gain, bias)


def norm_local(pixels, gain, bias, boxes):
    width = pixels.shape[2]
    return pl.pallas_call(
        functools.partial(norm_local_kernel, boxes),
        out_shape=[jax.ShapeDtypeStruct((rows * size, width), BF16) for _, rows, _, size in boxes],
        in_specs=[HELD, VMEM, VMEM],
        out_specs=[VMEM] * len(boxes),
        scratch_shapes=[pltpu.VMEM((rows, size, width), BF16) for _, rows, _, size in boxes]
        + [pltpu.SemaphoreType.DMA((len(boxes),))],
        compiler_params=pltpu.CompilerParams(vmem_limit_bytes=8 << 20),
        cost_estimate=pl.CostEstimate(flops=5 * pixels.size, bytes_accessed=2 * pixels.size, transcendentals=0),
        name="norm_local",
    )(pixels, gain, bias)


def norm_kernel(spans, *refs):
    *sources, gain_ref, bias_ref, out_ref = refs
    into = 0
    gain, bias = gain_ref[...], bias_ref[...]
    for which, row, left, size in spans:
        held = sources[which][row, left : left + size, :]
        out_ref[into : into + size, :] = normalized(held, gain, bias)
        into += size


def norm(sources, gain, bias, spans):
    width = sources[0].shape[-1]
    total = sum(span[-1] for span in spans)
    return pl.pallas_call(
        functools.partial(norm_kernel, spans),
        out_shape=jax.ShapeDtypeStruct((total, width), BF16),
        in_specs=[VMEM] * (len(sources) + 2),
        out_specs=VMEM,
        compiler_params=pltpu.CompilerParams(vmem_limit_bytes=8 << 20),
        cost_estimate=pl.CostEstimate(
            flops=10 * total * width, bytes_accessed=4 * total * width, transcendentals=0
        ),
    )(*sources, gain, bias)


def tag_kernel(count, near, label_ref, *outs):
    query_0, key_0, query_1, key_1 = outs
    row_count, _ = label_ref.shape
    rows = row_count // (2 * count)
    device = lax.axis_index("seq")
    turned = jnp.transpose(label_ref[...].astype(F32)).astype(BF16)
    place = lax.broadcasted_iota(jnp.int32, (row_count, LANE), 0)
    lane = (lax.broadcasted_iota(jnp.int32, (1, LANE), 1) % REGIONS).astype(F32)
    group = count * rows
    for half in range(2):
        for offset in range(count):
            for row in range(rows):
                at = (half * rows + row) * count + jnp.bitwise_xor(device, offset)
                chosen = jnp.where(place == at, 1.0, 0.0).astype(BF16)
                region = jnp.dot(turned, chosen, preferred_element_type=F32)
                same = region == lane
                query = jnp.where(same, 1.0, 0.0).astype(BF16)
                key = jnp.where(same, 0.0, FAR).astype(BF16)
                slot = offset * rows + row
                apart, span = group * near, near + 2 * (WS - near)
                beside = apart + offset * rows * span
                spots = [
                    (query_0, key_0, (half * group + slot) * WS, 0, WS),
                    (query_1, key_1, beside + row * near if half else slot * near, WS, near),
                    (
                        query_1,
                        key_1,
                        beside + rows * near + (half * rows + row) * (WS - near),
                        WS + near,
                        WS - near,
                    ),
                ]
                for query_ref, key_ref, into, left, size in spots:
                    query_ref[into : into + size, :] = query[left : left + size]
                    key_ref[into : into + size, :] = key[left : left + size]


def region_tags(labels, count, near):
    pixels = labels.shape[0] * WS
    return pl.pallas_call(
        functools.partial(tag_kernel, count, near),
        out_shape=[jax.ShapeDtypeStruct((pixels, LANE), BF16)] * 4,
        in_specs=[VMEM],
        out_specs=[VMEM] * 4,
        compiler_params=pltpu.CompilerParams(vmem_limit_bytes=8 << 20),
        cost_estimate=pl.CostEstimate(
            flops=8 * pixels * LANE * labels.shape[0], bytes_accessed=8 * pixels * LANE, transcendentals=0
        ),
        name="tags",
    )(labels)


def project_kernel(counts, *refs):
    groups = []
    for count in counts:
        groups.append(refs[:count])
        refs = refs[count:]
    weight_ref, *outs = refs
    head_width = weight_ref.shape[2]
    slot = padded(head_width)
    block = jnp.concatenate([piece[...] for group in groups for piece in group], axis=0)
    if slot == head_width:
        weights = jnp.concatenate([weight_ref[t] for t in range(3)], axis=1)
        products = [(0, jnp.dot(block, weights, preferred_element_type=F32).astype(BF16))]
    else:
        products = [
            (t * slot, jnp.dot(block, weight_ref[t], preferred_element_type=F32).astype(BF16))
            for t in range(3)
        ]
    at = 0
    for out_ref in outs:
        for left, product in products:
            part = product[at : at + out_ref.shape[0]]
            out_ref[:, left : left + part.shape[1]] = part
        at += out_ref.shape[0]


def project(groups, weights):
    width = weights.shape[1]
    slot = padded(weights.shape[2])
    sizes = [sum(piece.shape[0] for piece in group) for group in groups]
    total = sum(sizes)
    return pl.pallas_call(
        functools.partial(project_kernel, [len(group) for group in groups]),
        out_shape=[jax.ShapeDtypeStruct((size, 3 * slot), BF16) for size in sizes],
        in_specs=[VMEM] * (sum(len(group) for group in groups) + 1),
        out_specs=[VMEM] * len(groups),
        compiler_params=pltpu.CompilerParams(vmem_limit_bytes=24 << 20),
        cost_estimate=pl.CostEstimate(
            flops=2 * total * width * 3 * slot,
            bytes_accessed=2 * (total * width + weights.size + total * 3 * slot),
            transcendentals=0,
        ),
    )(*[piece for group in groups for piece in group], weights)


def attend_kernel(count, parts, ranges, head_width, *refs):
    blocks = refs[:parts]
    query_tags, key_tags, scale_ref = refs[parts : parts + 3]
    outs = refs[parts + 3 :]
    slot = padded(head_width)
    sizes = [block.shape[0] // count for block in blocks]
    low, high = min(lo for lo, _ in ranges), max(hi for _, hi in ranges)
    heads = head_width // CHANNEL_PER_PART
    base = math.log2(math.e) / math.sqrt(CHANNEL_PER_PART)
    tiles = [None] * (slot // LANE)
    for head in range(heads):
        first = head * CHANNEL_PER_PART
        last = first + CHANNEL_PER_PART
        left, right = first // LANE * LANE, padded(last)
        reps = (right - left) // LANE
        lane = lax.broadcasted_iota(jnp.int32, (1, right - left), 1)
        inside = (lane >= first - left) & (lane < last - left)
        queries = jnp.concatenate(
            [b[low * z : high * z, left:right] for b, z in zip(blocks, sizes, strict=True)], axis=0
        )
        tags, at = [], 0
        for z in sizes:
            tags.append(query_tags[at + low * z : at + high * z, :])
            at += count * z
        tags = jnp.concatenate(tags, axis=0)
        queries = jnp.where(inside, queries, jnp.concatenate([tags] * reps, axis=1))
        keys = jnp.concatenate([b[:, slot + left : slot + right] for b in blocks], axis=0)
        tags = key_tags[...]
        keys = jnp.where(inside, keys, jnp.concatenate([tags] * reps, axis=1))
        values = jnp.concatenate([b[:, 2 * slot + left : 2 * slot + right] for b in blocks], axis=0)
        scores = lax.dot_general(
            queries, keys, (((1,), (1,)), ((), ())), preferred_element_type=F32
        )
        row_max = jnp.max(scores, axis=-1, keepdims=True)
        numerators = jnp.exp2((scores - row_max) * (scale_ref[head] * base))
        total = jnp.sum(numerators, axis=-1, keepdims=True)
        mixed = jnp.dot(numerators.astype(BF16), values, preferred_element_type=F32) / total
        for i in range(reps):
            tile = left // LANE + i
            own = mixed[:, i * LANE : (i + 1) * LANE]
            held = tiles[tile]
            tiles[tile] = own if held is None else jnp.where(inside[:, i * LANE : (i + 1) * LANE], own, held)
    result = jnp.concatenate(tiles, axis=1)[:, :head_width].astype(BF16)
    for out_ref, (lo, hi) in zip(outs, ranges, strict=True):
        for offset in range(lo, hi):
            start, into = 0, 0
            for z in sizes:
                at = start + (offset - low) * z
                out_ref[offset - lo, into : into + z, :] = result[at : at + z]
                start += (high - low) * z
                into += z


def attend(blocks, query_tags, key_tags, scales, count, ranges, head_width):
    parts = len(blocks)
    per_offset = sum(b.shape[0] for b in blocks) // count
    pixels = count * per_offset
    asked = sum(hi - lo for lo, hi in ranges) * per_offset
    vmem = pl.BlockSpec(memory_space=pltpu.VMEM)
    heads = head_width // CHANNEL_PER_PART
    return pl.pallas_call(
        functools.partial(attend_kernel, count, parts, ranges, head_width),
        out_shape=[
            jax.ShapeDtypeStruct((hi - lo, per_offset, head_width), BF16) for lo, hi in ranges
        ],
        in_specs=[vmem] * (parts + 2) + [pl.BlockSpec(memory_space=pltpu.SMEM)],
        out_specs=[vmem] * len(ranges),
        compiler_params=pltpu.CompilerParams(vmem_limit_bytes=28 << 20),
        cost_estimate=pl.CostEstimate(
            flops=4 * heads * asked * pixels * 2 * LANE,
            bytes_accessed=2 * pixels * 3 * padded(head_width),
            transcendentals=heads * asked * pixels,
        ),
    )(*blocks, query_tags, key_tags, scales)


def finish_kernel(count, spans, out_spans, *refs):
    refs = list(refs)
    attended = [refs.pop(0) for _ in range(count)]
    weights = [refs.pop(0) for _ in range(count)]
    *sources, out_ref = refs
    total = None
    for piece, weight in zip(attended, weights, strict=True):
        term = jnp.dot(piece[...], weight[...], preferred_element_type=F32)
        total = term if total is None else total + term
    at = 0
    for which, row, left, size, into, column in spans:
        held = sources[which][row, left : left + size, :].astype(F32)
        out_ref[into, column : column + size, :] = (held + total[at : at + size]).astype(BF16)
        at += size
    for which, row, left, size, into, column in out_spans:
        out_ref[into, column : column + size, :] = sources[which][row, left : left + size, :]


def finish(attended, weights, sources, spans, out_spans, shape):
    count = len(weights)
    width = shape[-1]
    pixels = attended[0].shape[0]
    return pl.pallas_call(
        functools.partial(finish_kernel, count, spans, out_spans),
        out_shape=jax.ShapeDtypeStruct(shape, BF16),
        in_specs=[VMEM] * (2 * count + len(sources)),
        out_specs=VMEM,
        compiler_params=pltpu.CompilerParams(vmem_limit_bytes=20 << 20),
        cost_estimate=pl.CostEstimate(
            flops=2 * pixels * width * width, bytes_accessed=2 * width * (width + 3 * pixels), transcendentals=0
        ),
    )(*attended, *weights, *sources)


def send_heads(outs):
    own = [outs[0]]
    for offset in range(1, len(outs)):
        own.append(exchange(outs[offset], offset))
    return [piece[0] for piece in own]


def pick_kernel(place, source_ref, out_ref, semaphore):
    size = out_ref.shape[0]
    start = pl.multiple_of(place() * size, 16)
    copy = pltpu.make_async_copy(source_ref.at[pl.ds(start, size), :], out_ref, semaphore)
    copy.start()
    copy.wait()


def join_kernel(place, own_ref, other_ref, out_ref):
    size = own_ref.shape[0]
    at = place()
    out_ref[pl.ds(pl.multiple_of(at * size, 16), size), :] = own_ref[...]
    out_ref[pl.ds(pl.multiple_of((1 - at) * size, 16), size), :] = other_ref[...]


def small_call(kernel, rows, *operands, spec=VMEM, scratch=()):
    width = operands[0].shape[1]
    return pl.pallas_call(
        kernel,
        out_shape=jax.ShapeDtypeStruct((rows, width), BF16),
        in_specs=[spec] * len(operands),
        out_specs=VMEM,
        scratch_shapes=scratch,
        compiler_params=pltpu.CompilerParams(vmem_limit_bytes=8 << 20),
        cost_estimate=pl.CostEstimate(flops=0, bytes_accessed=4 * rows * width, transcendentals=0),
    )(*operands)


def gather_weights(block):
    levels = []
    rows = block.shape[0]
    for axis in ("member", "win"):
        if lax.axis_size(axis) % 2 == 0 and rows % (32 << len(levels)) == 0:
            levels.append(axis)

    def bit(axis):
        return lax.axis_index(axis) & 1

    def part_index():
        index = 0
        for axis in levels:
            index = index * 2 + bit(axis)
        return index

    pieces = {0: block}
    for mask in masks_of(lax.axis_size("seq")):
        for offset in list(pieces):
            piece = pieces[offset]
            if mask > 1 and levels:
                size = rows >> len(levels)
                part = small_call(
                    functools.partial(pick_kernel, part_index),
                    size,
                    piece,
                    spec=HELD,
                    scratch=[pltpu.SemaphoreType.DMA],
                )
                part = exchange(part, mask)
                for axis in reversed(levels):
                    other = exchange(part, 1, axis)
                    size *= 2
                    part = small_call(functools.partial(join_kernel, functools.partial(bit, axis)), size, part, other)
                pieces[offset ^ mask] = part
            else:
                pieces[offset ^ mask] = exchange(piece, mask)
    return [pieces[offset] for offset in range(len(pieces))]


def on_device(
    pixel_grid_input,
    mask_zone_labeling,
    standardize_multiplier,
    standardize_offset_vector,
    triple_projection_matrix,
    logit_scaling_per_part,
    final_projection_matrix,
):
    count = lax.axis_size("seq")
    blocked = pixel_grid_input[0, :, 0]
    row_count, col_count, width = blocked.shape
    rows = row_count // 2
    half = WS // 2
    head_width = triple_projection_matrix.shape[2]

    def west(source, count):
        return (source - 2) % count

    def west_north(source, count):
        return ((source ^ 1) - 2) % count

    near = WS - half
    gain, bias = standardize_multiplier[None], standardize_offset_vector[None]
    weights = triple_projection_matrix
    scales = logit_scaling_per_part

    local_0, local_1 = norm_local(blocked, gain, bias, [(rows, rows, half, WS), (rows, rows, half + WS, near)])
    south_0, south_1, east, corner = cut(
        blocked, [(0, rows, half, WS), (0, rows, half + WS, near), (rows, rows, 0, half), (0, rows, 0, half)]
    )
    south_0 = exchange(south_0, 1, "win")
    south_1 = exchange(south_1, 1, "win")
    east = permute_by(east, "win", west)
    corner = permute_by(corner, "win", west_north)
    local_0_pieces = gather_pieces(local_0)
    local_1_pieces = gather_pieces(local_1)
    query_0, key_0, query_1, key_1 = region_tags(mask_zone_labeling[0], count, near)
    out_weights = gather_weights(final_projection_matrix)

    spans = [(0, row, 0, WS) for row in range(rows)]
    south_normed = norm([south_0], gain, bias, spans)
    south_pieces = gather_pieces(south_normed)
    local_0_pieces[0] = after(local_0, south_normed)
    local_0, local_1 = project([local_0_pieces, local_1_pieces], weights)
    spans = [(0, row, 0, near) for row in range(rows)]
    spans += [(which, row, 0, half) for which in (1, 2) for row in range(rows)]
    rest_normed = norm([after(south_1, local_0), east, corner], gain, bias, spans)
    rest_pieces = gather_pieces(rest_normed)
    south_pieces[0] = after(south_normed, local_0)
    (south_0_projected,) = project([south_pieces], weights)

    def attend_run(blocks, tags, earlier, lo, hi):
        blocks = [after(blocks[0], *earlier), *blocks[1:]]
        return list(attend(blocks, *tags, scales, count, [(i, i + 1) for i in range(lo, hi)], head_width))

    split = count // 2
    blocks, tags = [local_0, south_0_projected], (query_0, key_0)
    far = attend_run(blocks, tags, [], split, count)
    close = attend_run(blocks, tags, far, 0, split)
    outs_0 = close + far
    rest_pieces[0] = after(rest_normed, *outs_0)
    (rest_projected,) = project([rest_pieces], weights)
    blocks, tags = [local_1, rest_projected], (query_1, key_1)
    far = attend_run(blocks, tags, [], split, count)
    close = attend_run(blocks, tags, far, 0, split)
    outs_1 = close + far

    first = send_heads(outs_0)
    second = send_heads(outs_1)
    first[0] = after(first[0], *outs_1)
    spans = [(0, rows + row, half, WS, row, 0) for row in range(rows)]
    spans += [(1, row, 0, WS, rows + row, 0) for row in range(rows)]
    done = finish(first, out_weights, [blocked, south_0], spans, [], (row_count, WS, width))
    spans = [(0, rows + row, half + WS, near, row, WS) for row in range(rows)]
    spans += [(1, row, 0, near, rows + row, WS) for row in range(rows)]
    spans += [(2, row, 0, half, row, WS + near) for row in range(rows)]
    spans += [(3, row, 0, half, rows + row, WS + near) for row in range(rows)]
    kept = [(4, row, 0, WS, row, 0) for row in range(row_count)]
    mixed = finish(
        second, out_weights, [blocked, south_1, east, corner, done], spans, kept, (row_count, col_count, width)
    )
    return mixed[None, :, None]


def solution(mesh):
    in_specs = (
        P(("member", "win"), None, "seq", None, None),
        P(("member", "win"), None, None),
        P(),
        P(),
        P(None, None, "seq"),
        P("seq"),
        P("seq", None),
    )
    out_specs = P(("member", "win"), None, "seq", None, None)

    return jax.shard_map(on_device, mesh=mesh, in_specs=in_specs, out_specs=out_specs, check_vma=False)
```

profile of v0, /device:TPU:0, one launch (start us, length us, event | category | flops | bytes accessed | tf_op | source)
XLA Modules:
  0.0 104.4 jit_solution(3675810592118857726)
XLA Ops:
  0.0 0.7 broadcast_in_dim.10.bias_ref.refs_2_.refs_4_
  0.7 0.7 broadcast_in_dim.9.gain_ref.refs_1_.refs_3_
  1.4 1.4 %copy-done = bf16[1,8,1,64,1536]{4,3,2,1,0:T(8,128)(2,1)S(1)} copy-done((bf16[1,8,1,64,1536]{4,3,2,1,0:T(8,128)(2,1)S(1)}, bf16[1,8,1,64,1536]{4,3,2,1,0:T(8,128)(2,1)}, u32[]{:S(2)}) %copy-start) | copy-done | bytes 1572888
  2.8 0.7 norm_local.1
  3.5 3.0 %collective-permute-start.2 = (bf16[128,1536]{1,0:T(8,128)(2,1)S(1)}, bf16[128,1536]{1,0:T(8,128)(2,1)S(1)}, u32[]{:S(2)}, u32[]{:S(2)}) collective-permute-start(bf16[128,1536]{1,0:T(8,128)(2,1)S(1)} %get-tuple-element.34.refs_0_), channel_id=1, source_target_pairs={{0,2},{1,3},{2,0},{3,1},{4,6},{5,7},{6,4},{7,5},{8,10},{9,11},{10,... | collective-permute-start | bytes 1179656 | tf_op jit(solution)/shard_map/ppermute | solution.py:24
  6.5 1.3 %copy-done.2 = bf16[384,1536]{1,0:T(8,128)(2,1)S(1)} copy-done((bf16[384,1536]{1,0:T(8,128)(2,1)S(1)}, bf16[384,1536]{1,0:T(8,128)(2,1)}, u32[]{:S(2)}) %copy-start.2) | copy-done | bytes 1179672
  7.9 0.1 collective-permute-start.20
  8.0 0.3 cut.1
  8.3 2.1 %collective-permute-start = (bf16[4,32,1536]{2,1,0:T(8,128)(2,1)S(1)}, bf16[4,32,1536]{2,1,0:T(8,128)(2,1)S(1)}, u32[]{:S(2)}, u32[]{:S(2)}) collective-permute-start(bf16[4,32,1536]{2,1,0:T(8,128)(2,1)S(1)} %get-tuple-element.33), channel_id=1, source_target_pairs={{0,4},{4,0},{8,12},{12,8},{1,5},{5,1},{9,13},{13,9},{2,6},{6,2},{1... | collective-permute-start | bytes 1179656 | tf_op jit(solution)/shard_map/ppermute | solution.py:24
  10.4 1.5 %collective-permute-start.5 = (bf16[64,1536]{1,0:T(8,128)(2,1)S(1)}, bf16[64,1536]{1,0:T(8,128)(2,1)S(1)}, u32[]{:S(2)}, u32[]{:S(2)}) collective-permute-start(bf16[64,1536]{1,0:T(8,128)(2,1)S(1)} %get-tuple-element.35.refs_4_), channel_id=1, source_target_pairs={{0,2},{1,3},{2,0},{3,1},{4,6},{5,7},{6,4},{7,5},{8,10},{9,11},{10,... | collective-permute-start | bytes 589832 | tf_op jit(solution)/shard_map/ppermute | solution.py:24
  11.9 4.6 %collective-permute-done.2.refs_2_ = bf16[128,1536]{1,0:T(8,128)(2,1)S(1)} collective-permute-done((bf16[128,1536]{1,0:T(8,128)(2,1)S(1)}, bf16[128,1536]{1,0:T(8,128)(2,1)S(1)}, u32[]{:S(2)}, u32[]{:S(2)}) %collective-permute-start.2) | collective-permute-done | bytes 393248 | tf_op jit(solution)/shard_map/ppermute | solution.py:24
  16.5 9.7 %collective-permute-done.5.refs_6_ = bf16[64,1536]{1,0:T(8,128)(2,1)S(1)} collective-permute-done((bf16[64,1536]{1,0:T(8,128)(2,1)S(1)}, bf16[64,1536]{1,0:T(8,128)(2,1)S(1)}, u32[]{:S(2)}, u32[]{:S(2)}) %collective-permute-start.5) | collective-permute-done | bytes 196640 | tf_op jit(solution)/shard_map/ppermute | solution.py:24
  26.2 0.5 collective-permute-start.6
  26.7 1.8 %collective-permute-start.21 = (bf16[96,1536]{1,0:T(8,128)(2,1)S(1)}, bf16[96,1536]{1,0:T(8,128)(2,1)S(1)}, u32[]{:S(2)}, u32[]{:S(2)}) collective-permute-start(bf16[96,1536]{1,0:T(8,128)(2,1)S(1)} %collective-permute-done.20.own_ref), channel_id=1, source_target_pairs={{0,4},{4,0},{8,12},{12,8},{1,5},{5,1},{9,13},{13,9},{2,6},{6,2},{1... | collective-permute-start | bytes 884744 | tf_op jit(solution)/shard_map/ppermute | solution.py:24
  28.5 0.3 shard_map.73.refs_0_
  28.9 0.6 collective-permute-start.7
  29.5 2.6 %collective-permute-start.8 = (bf16[4,16,1536]{2,1,0:T(8,128)(2,1)S(1)}, bf16[4,16,1536]{2,1,0:T(8,128)(2,1)S(1)}, u32[]{:S(2)}, u32[]{:S(2)}) collective-permute-start(bf16[4,16,1536]{2,1,0:T(8,128)(2,1)S(1)} %get-tuple-element.40), channel_id=1, source_target_pairs={{0,8},{4,12},{8,0},{12,4},{1,9},{5,13},{9,1},{13,5},{2,10},{6,14},... | collective-permute-start | bytes 589832 | tf_op jit(solution)/shard_map/ppermute | solution.py:24
  32.1 1.3 %collective-permute-start.9 = (bf16[4,16,1536]{2,1,0:T(8,128)(2,1)S(1)}, bf16[4,16,1536]{2,1,0:T(8,128)(2,1)S(1)}, u32[]{:S(2)}, u32[]{:S(2)}) collective-permute-start(bf16[4,16,1536]{2,1,0:T(8,128)(2,1)S(1)} %get-tuple-element.41), channel_id=1, source_target_pairs={{0,12},{4,8},{8,4},{12,0},{1,13},{5,9},{9,5},{13,1},{2,14},{6,10},... | collective-permute-start | bytes 589832 | tf_op jit(solution)/shard_map/ppermute | solution.py:24
  33.3 1.5 %collective-permute-start.11 = (bf16[128,1536]{1,0:T(8,128)(2,1)S(1)}, bf16[128,1536]{1,0:T(8,128)(2,1)S(1)}, u32[]{:S(2)}, u32[]{:S(2)}) collective-permute-start(bf16[128,1536]{1,0:T(8,128)(2,1)S(1)} %shard_map.73.refs_0_), channel_id=1, source_target_pairs={{0,2},{1,3},{2,0},{3,1},{4,6},{5,7},{6,4},{7,5},{8,10},{9,11},{10,... | collective-permute-start | bytes 1179656 | tf_op jit(solution)/shard_map/ppermute | solution.py:24
  34.8 3.2 %shard_map.74 = (bf16[512,1152]{1,0:T(8,128)(2,1)S(1)}, bf16[256,1152]{1,0:T(8,128)(2,1)S(1)}) custom-call(bf16[128,1536]{1,0:T(8,128)(2,1)S(1)} %get-tuple-element.34.refs_0_, bf16[128,1536]{1,0:T(8,128)(2,1)S(1)} %collective-permute-done.1.refs_1_, bf16[128,1536]{1,0:T(8,128)(2,1)S(1)} %collective-permute-done.2.refs_2_, ...), custom_call_target="tpu_custom_call" | custom-call | flops 2717908992 | bytes 7667712 | tf_op jit(solution)/shard_map/pallas_call | solution.py:237
  38.0 6.2 %collective-permute-done.7.refs_0_.refs_9_ = bf16[4,16,1536]{2,1,0:T(8,128)(2,1)S(1)} collective-permute-done((bf16[4,16,1536]{2,1,0:T(8,128)(2,1)S(1)}, bf16[4,16,1536]{2,1,0:T(8,128)(2,1)S(1)}, u32[]{:S(2)}, u32[]{:S(2)}) %collective-permute-start.7) | collective-permute-done | bytes 196640 | tf_op jit(solution)/shard_map/ppermute | solution.py:24
  44.2 0.2 collective-permute-done.8.refs_1_.refs_10_
  44.4 6.2 %collective-permute-done.9.refs_2_.refs_11_ = bf16[4,16,1536]{2,1,0:T(8,128)(2,1)S(1)} collective-permute-done((bf16[4,16,1536]{2,1,0:T(8,128)(2,1)S(1)}, bf16[4,16,1536]{2,1,0:T(8,128)(2,1)S(1)}, u32[]{:S(2)}, u32[]{:S(2)}) %collective-permute-start.9) | collective-permute-done | bytes 196640 | tf_op jit(solution)/shard_map/ppermute | solution.py:24
  50.6 0.4 shard_map.75.refs_0_
  51.0 1.6 %collective-permute-start.14 = (bf16[192,1536]{1,0:T(8,128)(2,1)S(1)}, bf16[192,1536]{1,0:T(8,128)(2,1)S(1)}, u32[]{:S(2)}, u32[]{:S(2)}) collective-permute-start(bf16[192,1536]{1,0:T(8,128)(2,1)S(1)} %shard_map.75.refs_0_), channel_id=1, source_target_pairs={{0,2},{1,3},{2,0},{3,1},{4,6},{5,7},{6,4},{7,5},{8,10},{9,11},{10,... | collective-permute-start | bytes 1769480 | tf_op jit(solution)/shard_map/ppermute | solution.py:24
  52.6 1.6 %collective-permute-start.22 = (bf16[192,1536]{1,0:T(8,128)(2,1)S(1)}, bf16[192,1536]{1,0:T(8,128)(2,1)S(1)}, u32[]{:S(2)}, u32[]{:S(2)}) collective-permute-start(bf16[192,1536]{1,0:T(8,128)(2,1)S(1)} %shard_map.83.own_ref), channel_id=1, source_target_pairs={{0,16},{16,0},{1,17},{17,1},{2,18},{18,2},{3,19},{19,3},{4,20},{20... | collective-permute-start | bytes 1769480 | tf_op jit(solution)/shard_map/ppermute | solution.py:24
  54.2 0.5 collective-permute-start.12
  54.8 10.8 %collective-permute-done.14.refs_2_ = bf16[192,1536]{1,0:T(8,128)(2,1)S(1)} collective-permute-done((bf16[192,1536]{1,0:T(8,128)(2,1)S(1)}, bf16[192,1536]{1,0:T(8,128)(2,1)S(1)}, u32[]{:S(2)}, u32[]{:S(2)}) %collective-permute-start.14) | collective-permute-done | bytes 589856 | tf_op jit(solution)/shard_map/ppermute | solution.py:24
  65.5 0.4 tags.1
  65.9 1.0 collective-permute-done.22.other_ref
  66.9 0.1 shard_map.84.refs_6_
  67.0 0.6 collective-permute-start.23
  67.6 2.2 %shard_map.76.refs_1_ = bf16[512,1152]{1,0:T(8,128)(2,1)S(1)} custom-call(bf16[128,1536]{1,0:T(8,128)(2,1)S(1)} %shard_map.73.refs_0_, bf16[128,1536]{1,0:T(8,128)(2,1)S(1)} %collective-permute-done.10.refs_1_, bf16[128,1536]{1,0:T(8,128)(2,1)S(1)} %collective-permute-done.11.refs_2_, bf16[128,1536]{1,0:T(8,128)(2,1)S(1)} %collective-permute-done.12.refs_3_, ...), custom_call_target="tpu_custom_call" | custom-call | flops 1811939328 | bytes 6291456 | tf_op jit(solution)/shard_map/pallas_call | solution.py:237
  69.8 3.9 %shard_map.77 = (bf16[1,256,384]{2,1,0:T(8,128)(2,1)S(1)}, bf16[1,256,384]{2,1,0:T(8,128)(2,1)S(1)}) custom-call(bf16[512,1152]{1,0:T(8,128)(2,1)S(1)} %get-tuple-element.47.refs_0_, bf16[512,1152]{1,0:T(8,128)(2,1)S(1)} %shard_map.76.refs_1_, bf16[1024,128]{1,0:T(8,128)(2,1)S(1)} %get-tuple-element.43.refs_2_, ...), custom_call_target="tpu_custom_call" | custom-call | flops 2147483648 | bytes 2359296 | tf_op jit(solution)/shard_map/pallas_call | solution.py:311
  73.7 4.0 %shard_map.78 = (bf16[1,256,384]{2,1,0:T(8,128)(2,1)S(1)}, bf16[1,256,384]{2,1,0:T(8,128)(2,1)S(1)}) custom-call(bf16[512,1152]{1,0:T(8,128)(2,1)S(1)} %get-tuple-element.47.refs_0_, bf16[512,1152]{1,0:T(8,128)(2,1)S(1)} %shard_map.76.refs_1_, bf16[1024,128]{1,0:T(8,128)(2,1)S(1)} %get-tuple-element.43.refs_2_, ...), custom_call_target="tpu_custom_call" | custom-call | flops 2147483648 | bytes 2359296 | tf_op jit(solution)/shard_map/pallas_call | solution.py:311
  77.7 0.1 collective-permute-start.24
  77.8 1.1 %collective-permute-start.25 = (bf16[1,256,384]{2,1,0:T(8,128)(2,1)S(1)}, bf16[1,256,384]{2,1,0:T(8,128)(2,1)S(1)}, u32[]{:S(2)}, u32[]{:S(2)}) collective-permute-start(bf16[1,256,384]{2,1,0:T(8,128)(2,1)S(1)} %get-tuple-element.45), channel_id=1, source_target_pairs={{0,2},{1,3},{2,0},{3,1},{4,6},{5,7},{6,4},{7,5},{8,10},{9,11},{10,... | collective-permute-start | bytes 589832 | tf_op jit(solution)/shard_map/ppermute | solution.py:24
  78.9 0.8 collective-permute-start.26
  79.6 3.2 %shard_map.79.refs_1_ = bf16[768,1152]{1,0:T(8,128)(2,1)S(1)} custom-call(bf16[192,1536]{1,0:T(8,128)(2,1)S(1)} %shard_map.75.refs_0_, bf16[192,1536]{1,0:T(8,128)(2,1)S(1)} %collective-permute-done.13.refs_1_, bf16[192,1536]{1,0:T(8,128)(2,1)S(1)} %collective-permute-done.14.refs_2_, bf16[192,1536]{1,0:T(8,128)(2,1)S(1)} %collective-permute-done.15.refs_3_, ...), custom_call_target="tpu_custom_call" | custom-call | flops 2717908992 | bytes 7667712 | tf_op jit(solution)/shard_map/pallas_call | solution.py:237
  82.8 3.9 %shard_map.80 = (bf16[1,256,384]{2,1,0:T(8,128)(2,1)S(1)}, bf16[1,256,384]{2,1,0:T(8,128)(2,1)S(1)}) custom-call(bf16[256,1152]{1,0:T(8,128)(2,1)S(1)} %get-tuple-element.55.refs_0_, bf16[768,1152]{1,0:T(8,128)(2,1)S(1)} %shard_map.79.refs_1_, bf16[1024,128]{1,0:T(8,128)(2,1)S(1)} %get-tuple-element.51.refs_2_, ...), custom_call_target="tpu_custom_call" | custom-call | flops 2147483648 | bytes 2359296 | tf_op jit(solution)/shard_map/pallas_call | solution.py:311
  86.7 3.9 %shard_map.81 = (bf16[1,256,384]{2,1,0:T(8,128)(2,1)S(1)}, bf16[1,256,384]{2,1,0:T(8,128)(2,1)S(1)}) custom-call(bf16[256,1152]{1,0:T(8,128)(2,1)S(1)} %get-tuple-element.55.refs_0_, bf16[768,1152]{1,0:T(8,128)(2,1)S(1)} %shard_map.79.refs_1_, bf16[1024,128]{1,0:T(8,128)(2,1)S(1)} %get-tuple-element.51.refs_2_, ...), custom_call_target="tpu_custom_call" | custom-call | flops 2147483648 | bytes 2359296 | tf_op jit(solution)/shard_map/pallas_call | solution.py:311
  90.7 0.7 collective-permute-start.17
  91.4 0.4 collective-permute-start.16
  91.8 1.0 collective-permute-start.18
  92.9 1.8 %shard_map.85.refs_12_ = bf16[8,32,1536]{2,1,0:T(8,128)(2,1)S(1)} custom-call(bf16[256,384]{1,0:T(8,128)(2,1)S(1)} %bitcast.17, bf16[256,384]{1,0:T(8,128)(2,1)S(1)} %bitcast.18, bf16[256,384]{1,0:T(8,128)(2,1)S(1)} %bitcast.20, bf16[256,384]{1,0:T(8,128)(2,1)S(1)} %bitcast.21, bf16[384,1536]{1,0:T(8,128)(2,1)S(1)} %copy-done.3, ...), custom_call_target="tpu_custom_call" | custom-call | flops 1207959552 | bytes 7077888 | tf_op jit(solution)/shard_map/pallas_call | solution.py:349
  94.7 3.8 %collective-permute-done.17 = bf16[1,256,384]{2,1,0:T(8,128)(2,1)S(1)} collective-permute-done((bf16[1,256,384]{2,1,0:T(8,128)(2,1)S(1)}, bf16[1,256,384]{2,1,0:T(8,128)(2,1)S(1)}, u32[]{:S(2)}, u32[]{:S(2)}) %collective-permute-start.17) | collective-permute-done | bytes 196640 | tf_op jit(solution)/shard_map/ppermute | solution.py:24
  98.5 3.0 %collective-permute-done.18 = bf16[1,256,384]{2,1,0:T(8,128)(2,1)S(1)} collective-permute-done((bf16[1,256,384]{2,1,0:T(8,128)(2,1)S(1)}, bf16[1,256,384]{2,1,0:T(8,128)(2,1)S(1)}, u32[]{:S(2)}, u32[]{:S(2)}) %collective-permute-start.18) | collective-permute-done | bytes 196640 | tf_op jit(solution)/shard_map/ppermute | solution.py:24
  101.5 2.9 %shard_map.86 = bf16[8,64,1536]{2,1,0:T(8,128)(2,1)} custom-call(bf16[256,384]{1,0:T(8,128)(2,1)S(1)} %bitcast.19, bf16[256,384]{1,0:T(8,128)(2,1)S(1)} %bitcast.23, bf16[256,384]{1,0:T(8,128)(2,1)S(1)} %bitcast.22, bf16[256,384]{1,0:T(8,128)(2,1)S(1)} %bitcast.24, bf16[384,1536]{1,0:T(8,128)(2,1)S(1)} %copy-done.3, ...), custom_call_target="tpu_custom_call" | custom-call | flops 1207959552 | bytes 7077888 | tf_op jit(solution)/shard_map/pallas_call | solution.py:349
  (39 shorter events, 0.2 us)
Async XLA Ops:
  1.4 1.4 %copy-start = (bf16[1,8,1,64,1536]{4,3,2,1,0:T(8,128)(2,1)S(1)}, bf16[1,8,1,64,1536]{4,3,2,1,0:T(8,128)(2,1)}, u32[]{:S(2)}) copy-start(bf16[1,8,1,64,1536]{4,3,2,1,0:T(8,128)(2,1)} %param.7) | copy-start | bytes 4718596
  2.8 5.2 %copy-start.1 = (bf16[1,8,1,64,1536]{4,3,2,1,0:T(8,128)(2,1)S(1)}, bf16[1,8,1,64,1536]{4,3,2,1,0:T(8,128)(2,1)}, u32[]{:S(2)}) copy-start(bf16[1,8,1,64,1536]{4,3,2,1,0:T(8,128)(2,1)} %param.7) | copy-start | bytes 4718596
  3.5 13.0 %collective-permute-start.2 = (bf16[128,1536]{1,0:T(8,128)(2,1)S(1)}, bf16[128,1536]{1,0:T(8,128)(2,1)S(1)}, u32[]{:S(2)}, u32[]{:S(2)}) collective-permute-start(bf16[128,1536]{1,0:T(8,128)(2,1)S(1)} %get-tuple-element.34.refs_0_), channel_id=1, source_target_pairs={{0,2},{1,3},{2,0},{3,1},{4,6},{5,7},{6,4},{7,5},{8,10},{9,11},{10,... | collective-permute-start | bytes 1179656 | tf_op jit(solution)/shard_map/ppermute | solution.py:24
  6.5 1.3 %copy-start.2 = (bf16[384,1536]{1,0:T(8,128)(2,1)S(1)}, bf16[384,1536]{1,0:T(8,128)(2,1)}, u32[]{:S(2)}) copy-start(bf16[384,1536]{1,0:T(8,128)(2,1)} %refs_4_.15) | copy-start | bytes 3538948
  7.8 27.0 %copy-start.4 = (bf16[3,1536,384]{2,1,0:T(8,128)(2,1)S(1)}, bf16[3,1536,384]{2,1,0:T(8,128)(2,1)}, u32[]{:S(2)}) copy-start(bf16[3,1536,384]{2,1,0:T(8,128)(2,1)} %refs_4_.11) | copy-start | bytes 10616836
  7.9 18.3 %collective-permute-start.20 = (bf16[96,1536]{1,0:T(8,128)(2,1)S(1)}, bf16[96,1536]{1,0:T(8,128)(2,1)S(1)}, u32[]{:S(2)}, u32[]{:S(2)}) collective-permute-start(bf16[96,1536]{1,0:T(8,128)(2,1)S(1)} %shard_map.82), channel_id=1, source_target_pairs={{0,2},{1,3},{2,0},{3,1},{4,6},{5,7},{6,4},{7,5},{8,10},{9,11},{10,... | collective-permute-start | bytes 884744 | tf_op jit(solution)/shard_map/ppermute | solution.py:24
  8.3 18.4 %collective-permute-start = (bf16[4,32,1536]{2,1,0:T(8,128)(2,1)S(1)}, bf16[4,32,1536]{2,1,0:T(8,128)(2,1)S(1)}, u32[]{:S(2)}, u32[]{:S(2)}) collective-permute-start(bf16[4,32,1536]{2,1,0:T(8,128)(2,1)S(1)} %get-tuple-element.33), channel_id=1, source_target_pairs={{0,4},{4,0},{8,12},{12,8},{1,5},{5,1},{9,13},{13,9},{2,6},{6,2},{1... | collective-permute-start | bytes 1179656 | tf_op jit(solution)/shard_map/ppermute | solution.py:24
  10.4 15.8 %collective-permute-start.5 = (bf16[64,1536]{1,0:T(8,128)(2,1)S(1)}, bf16[64,1536]{1,0:T(8,128)(2,1)S(1)}, u32[]{:S(2)}, u32[]{:S(2)}) collective-permute-start(bf16[64,1536]{1,0:T(8,128)(2,1)S(1)} %get-tuple-element.35.refs_4_), channel_id=1, source_target_pairs={{0,2},{1,3},{2,0},{3,1},{4,6},{5,7},{6,4},{7,5},{8,10},{9,11},{10,... | collective-permute-start | bytes 589832 | tf_op jit(solution)/shard_map/ppermute | solution.py:24
  11.9 20.1 %collective-permute-start.1 = (bf16[128,1536]{1,0:T(8,128)(2,1)S(1)}, bf16[128,1536]{1,0:T(8,128)(2,1)S(1)}, u32[]{:S(2)}, u32[]{:S(2)}) collective-permute-start(bf16[128,1536]{1,0:T(8,128)(2,1)S(1)} %get-tuple-element.34.refs_0_), channel_id=1, source_target_pairs={{0,1},{1,0},{2,3},{3,2},{4,5},{5,4},{6,7},{7,6},{8,9},{9,8},{10,11... | collective-permute-start | bytes 1179656 | tf_op jit(solution)/shard_map/ppermute | solution.py:24
  16.5 16.8 %collective-permute-start.3 = (bf16[128,1536]{1,0:T(8,128)(2,1)S(1)}, bf16[128,1536]{1,0:T(8,128)(2,1)S(1)}, u32[]{:S(2)}, u32[]{:S(2)}) collective-permute-start(bf16[128,1536]{1,0:T(8,128)(2,1)S(1)} %collective-permute-done.2.refs_2_), channel_id=1, source_target_pairs={{0,1},{1,0},{2,3},{3,2},{4,5},{5,4},{6,7},{7,6},{8,9},{9,8},{10,11... | collective-permute-start | bytes 1179656 | tf_op jit(solution)/shard_map/ppermute | solution.py:24
  26.2 2.7 %collective-permute-start.4 = (bf16[64,1536]{1,0:T(8,128)(2,1)S(1)}, bf16[64,1536]{1,0:T(8,128)(2,1)S(1)}, u32[]{:S(2)}, u32[]{:S(2)}) collective-permute-start(bf16[64,1536]{1,0:T(8,128)(2,1)S(1)} %get-tuple-element.35.refs_4_), channel_id=1, source_target_pairs={{0,1},{1,0},{2,3},{3,2},{4,5},{5,4},{6,7},{7,6},{8,9},{9,8},{10,11... | collective-permute-start | bytes 589832 | tf_op jit(solution)/shard_map/ppermute | solution.py:24
  26.2 3.3 %collective-permute-start.6 = (bf16[64,1536]{1,0:T(8,128)(2,1)S(1)}, bf16[64,1536]{1,0:T(8,128)(2,1)S(1)}, u32[]{:S(2)}, u32[]{:S(2)}) collective-permute-start(bf16[64,1536]{1,0:T(8,128)(2,1)S(1)} %collective-permute-done.5.refs_6_), channel_id=1, source_target_pairs={{0,1},{1,0},{2,3},{3,2},{4,5},{5,4},{6,7},{7,6},{8,9},{9,8},{10,11... | collective-permute-start | bytes 589832 | tf_op jit(solution)/shard_map/ppermute | solution.py:24
  26.7 25.9 %collective-permute-start.21 = (bf16[96,1536]{1,0:T(8,128)(2,1)S(1)}, bf16[96,1536]{1,0:T(8,128)(2,1)S(1)}, u32[]{:S(2)}, u32[]{:S(2)}) collective-permute-start(bf16[96,1536]{1,0:T(8,128)(2,1)S(1)} %collective-permute-done.20.own_ref), channel_id=1, source_target_pairs={{0,4},{4,0},{8,12},{12,8},{1,5},{5,1},{9,13},{13,9},{2,6},{6,2},{1... | collective-permute-start | bytes 884744 | tf_op jit(solution)/shard_map/ppermute | solution.py:24
  28.9 15.3 %collective-permute-start.7 = (bf16[4,16,1536]{2,1,0:T(8,128)(2,1)S(1)}, bf16[4,16,1536]{2,1,0:T(8,128)(2,1)S(1)}, u32[]{:S(2)}, u32[]{:S(2)}) collective-permute-start(bf16[4,16,1536]{2,1,0:T(8,128)(2,1)S(1)} %get-tuple-element.37), channel_id=1, source_target_pairs={{0,4},{4,0},{8,12},{12,8},{1,5},{5,1},{9,13},{13,9},{2,6},{6,2},{1... | collective-permute-start | bytes 589832 | tf_op jit(solution)/shard_map/ppermute | solution.py:24
  29.5 14.9 %collective-permute-start.8 = (bf16[4,16,1536]{2,1,0:T(8,128)(2,1)S(1)}, bf16[4,16,1536]{2,1,0:T(8,128)(2,1)S(1)}, u32[]{:S(2)}, u32[]{:S(2)}) collective-permute-start(bf16[4,16,1536]{2,1,0:T(8,128)(2,1)S(1)} %get-tuple-element.40), channel_id=1, source_target_pairs={{0,8},{4,12},{8,0},{12,4},{1,9},{5,13},{9,1},{13,5},{2,10},{6,14},... | collective-permute-start | bytes 589832 | tf_op jit(solution)/shard_map/ppermute | solution.py:24
  32.1 18.6 %collective-permute-start.9 = (bf16[4,16,1536]{2,1,0:T(8,128)(2,1)S(1)}, bf16[4,16,1536]{2,1,0:T(8,128)(2,1)S(1)}, u32[]{:S(2)}, u32[]{:S(2)}) collective-permute-start(bf16[4,16,1536]{2,1,0:T(8,128)(2,1)S(1)} %get-tuple-element.41), channel_id=1, source_target_pairs={{0,12},{4,8},{8,4},{12,0},{1,13},{5,9},{9,5},{13,1},{2,14},{6,10},... | collective-permute-start | bytes 589832 | tf_op jit(solution)/shard_map/ppermute | solution.py:24
  33.3 20.9 %collective-permute-start.11 = (bf16[128,1536]{1,0:T(8,128)(2,1)S(1)}, bf16[128,1536]{1,0:T(8,128)(2,1)S(1)}, u32[]{:S(2)}, u32[]{:S(2)}) collective-permute-start(bf16[128,1536]{1,0:T(8,128)(2,1)S(1)} %shard_map.73.refs_0_), channel_id=1, source_target_pairs={{0,2},{1,3},{2,0},{3,1},{4,6},{5,7},{6,4},{7,5},{8,10},{9,11},{10,... | collective-permute-start | bytes 1179656 | tf_op jit(solution)/shard_map/ppermute | solution.py:24
  44.2 21.3 %copy-start.5 = (s32[1,32,64]{2,1,0:T(8,128)S(1)}, s32[1,32,64]{2,1,0:T(8,128)}, u32[]{:S(2)}) copy-start(s32[1,32,64]{2,1,0:T(8,128)} %param.8) | copy-start | bytes 24580
  44.2 22.7 %copy-start.3 = (bf16[384,1536]{1,0:T(8,128)(2,1)S(1)}, bf16[384,1536]{1,0:T(8,128)(2,1)}, u32[]{:S(2)}) copy-start(bf16[384,1536]{1,0:T(8,128)(2,1)} %refs_4_.15) | copy-start | bytes 3538948
  51.0 14.5 %collective-permute-start.14 = (bf16[192,1536]{1,0:T(8,128)(2,1)S(1)}, bf16[192,1536]{1,0:T(8,128)(2,1)S(1)}, u32[]{:S(2)}, u32[]{:S(2)}) collective-permute-start(bf16[192,1536]{1,0:T(8,128)(2,1)S(1)} %shard_map.75.refs_0_), channel_id=1, source_target_pairs={{0,2},{1,3},{2,0},{3,1},{4,6},{5,7},{6,4},{7,5},{8,10},{9,11},{10,... | collective-permute-start | bytes 1769480 | tf_op jit(solution)/shard_map/ppermute | solution.py:24
  52.6 14.2 %collective-permute-start.22 = (bf16[192,1536]{1,0:T(8,128)(2,1)S(1)}, bf16[192,1536]{1,0:T(8,128)(2,1)S(1)}, u32[]{:S(2)}, u32[]{:S(2)}) collective-permute-start(bf16[192,1536]{1,0:T(8,128)(2,1)S(1)} %shard_map.83.own_ref), channel_id=1, source_target_pairs={{0,16},{16,0},{1,17},{17,1},{2,18},{18,2},{3,19},{19,3},{4,20},{20... | collective-permute-start | bytes 1769480 | tf_op jit(solution)/shard_map/ppermute | solution.py:24
  54.2 12.8 %collective-permute-start.10 = (bf16[128,1536]{1,0:T(8,128)(2,1)S(1)}, bf16[128,1536]{1,0:T(8,128)(2,1)S(1)}, u32[]{:S(2)}, u32[]{:S(2)}) collective-permute-start(bf16[128,1536]{1,0:T(8,128)(2,1)S(1)} %shard_map.73.refs_0_), channel_id=1, source_target_pairs={{0,1},{1,0},{2,3},{3,2},{4,5},{5,4},{6,7},{7,6},{8,9},{9,8},{10,11... | collective-permute-start | bytes 1179656 | tf_op jit(solution)/shard_map/ppermute | solution.py:24
  54.2 13.3 %collective-permute-start.12 = (bf16[128,1536]{1,0:T(8,128)(2,1)S(1)}, bf16[128,1536]{1,0:T(8,128)(2,1)S(1)}, u32[]{:S(2)}, u32[]{:S(2)}) collective-permute-start(bf16[128,1536]{1,0:T(8,128)(2,1)S(1)} %collective-permute-done.11.refs_2_), channel_id=1, source_target_pairs={{0,1},{1,0},{2,3},{3,2},{4,5},{5,4},{6,7},{7,6},{8,9},{9,8},{10,11... | collective-permute-start | bytes 1179656 | tf_op jit(solution)/shard_map/ppermute | solution.py:24
  54.7 23.0 %collective-permute-start.13 = (bf16[192,1536]{1,0:T(8,128)(2,1)S(1)}, bf16[192,1536]{1,0:T(8,128)(2,1)S(1)}, u32[]{:S(2)}, u32[]{:S(2)}) collective-permute-start(bf16[192,1536]{1,0:T(8,128)(2,1)S(1)} %shard_map.75.refs_0_), channel_id=1, source_target_pairs={{0,1},{1,0},{2,3},{3,2},{4,5},{5,4},{6,7},{7,6},{8,9},{9,8},{10,11... | collective-permute-start | bytes 1769480 | tf_op jit(solution)/shard_map/ppermute | solution.py:24
  65.5 13.3 %collective-permute-start.15 = (bf16[192,1536]{1,0:T(8,128)(2,1)S(1)}, bf16[192,1536]{1,0:T(8,128)(2,1)S(1)}, u32[]{:S(2)}, u32[]{:S(2)}) collective-permute-start(bf16[192,1536]{1,0:T(8,128)(2,1)S(1)} %collective-permute-done.14.refs_2_), channel_id=1, source_target_pairs={{0,1},{1,0},{2,3},{3,2},{4,5},{5,4},{6,7},{7,6},{8,9},{9,8},{10,11... | collective-permute-start | bytes 1769480 | tf_op jit(solution)/shard_map/ppermute | solution.py:24
  66.9 23.8 %collective-permute-start.19 = (bf16[384,1536]{1,0:T(8,128)(2,1)S(1)}, bf16[384,1536]{1,0:T(8,128)(2,1)S(1)}, u32[]{:S(2)}, u32[]{:S(2)}) collective-permute-start(bf16[384,1536]{1,0:T(8,128)(2,1)S(1)} %copy-done.3), channel_id=1, source_target_pairs={{0,1},{1,0},{2,3},{3,2},{4,5},{5,4},{6,7},{7,6},{8,9},{9,8},{10,11... | collective-permute-start | bytes 3538952 | tf_op jit(solution)/shard_map/ppermute | solution.py:24
  67.0 2.8 %copy-start.6 = (f32[4]{0:T(128)S(1)}, f32[4]{0:T(128)}, u32[]{:S(2)}) copy-start(f32[4]{0:T(128)} %refs_4_.13) | copy-start | bytes 52
  67.0 25.9 %collective-permute-start.23 = (bf16[384,1536]{1,0:T(8,128)(2,1)S(1)}, bf16[384,1536]{1,0:T(8,128)(2,1)S(1)}, u32[]{:S(2)}, u32[]{:S(2)}) collective-permute-start(bf16[384,1536]{1,0:T(8,128)(2,1)S(1)} %shard_map.84.refs_6_), channel_id=1, source_target_pairs={{0,1},{1,0},{2,3},{3,2},{4,5},{5,4},{6,7},{7,6},{8,9},{9,8},{10,11... | collective-permute-start | bytes 3538952 | tf_op jit(solution)/shard_map/ppermute | solution.py:24
  77.7 13.7 %collective-permute-start.24 = (bf16[1,256,384]{2,1,0:T(8,128)(2,1)S(1)}, bf16[1,256,384]{2,1,0:T(8,128)(2,1)S(1)}, u32[]{:S(2)}, u32[]{:S(2)}) collective-permute-start(bf16[1,256,384]{2,1,0:T(8,128)(2,1)S(1)} %get-tuple-element.49), channel_id=1, source_target_pairs={{0,1},{1,0},{2,3},{3,2},{4,5},{5,4},{6,7},{7,6},{8,9},{9,8},{10,11... | collective-permute-start | bytes 589832 | tf_op jit(solution)/shard_map/ppermute | solution.py:24
  77.8 14.1 %collective-permute-start.25 = (bf16[1,256,384]{2,1,0:T(8,128)(2,1)S(1)}, bf16[1,256,384]{2,1,0:T(8,128)(2,1)S(1)}, u32[]{:S(2)}, u32[]{:S(2)}) collective-permute-start(bf16[1,256,384]{2,1,0:T(8,128)(2,1)S(1)} %get-tuple-element.45), channel_id=1, source_target_pairs={{0,2},{1,3},{2,0},{3,1},{4,6},{5,7},{6,4},{7,5},{8,10},{9,11},{10,... | collective-permute-start | bytes 589832 | tf_op jit(solution)/shard_map/ppermute | solution.py:24
  78.9 14.0 %collective-permute-start.26 = (bf16[1,256,384]{2,1,0:T(8,128)(2,1)S(1)}, bf16[1,256,384]{2,1,0:T(8,128)(2,1)S(1)}, u32[]{:S(2)}, u32[]{:S(2)}) collective-permute-start(bf16[1,256,384]{2,1,0:T(8,128)(2,1)S(1)} %get-tuple-element.46), channel_id=1, source_target_pairs={{0,3},{1,2},{2,1},{3,0},{4,7},{5,6},{6,5},{7,4},{8,11},{9,10},{10,... | collective-permute-start | bytes 589832 | tf_op jit(solution)/shard_map/ppermute | solution.py:24
  90.7 7.8 %collective-permute-start.17 = (bf16[1,256,384]{2,1,0:T(8,128)(2,1)S(1)}, bf16[1,256,384]{2,1,0:T(8,128)(2,1)S(1)}, u32[]{:S(2)}, u32[]{:S(2)}) collective-permute-start(bf16[1,256,384]{2,1,0:T(8,128)(2,1)S(1)} %get-tuple-element.53), channel_id=1, source_target_pairs={{0,2},{1,3},{2,0},{3,1},{4,6},{5,7},{6,4},{7,5},{8,10},{9,11},{10,... | collective-permute-start | bytes 589832 | tf_op jit(solution)/shard_map/ppermute | solution.py:24
  91.4 3.3 %collective-permute-start.16 = (bf16[1,256,384]{2,1,0:T(8,128)(2,1)S(1)}, bf16[1,256,384]{2,1,0:T(8,128)(2,1)S(1)}, u32[]{:S(2)}, u32[]{:S(2)}) collective-permute-start(bf16[1,256,384]{2,1,0:T(8,128)(2,1)S(1)} %get-tuple-element.57), channel_id=1, source_target_pairs={{0,1},{1,0},{2,3},{3,2},{4,5},{5,4},{6,7},{7,6},{8,9},{9,8},{10,11... | collective-permute-start | bytes 589832 | tf_op jit(solution)/shard_map/ppermute | solution.py:24
  91.8 9.7 %collective-permute-start.18 = (bf16[1,256,384]{2,1,0:T(8,128)(2,1)S(1)}, bf16[1,256,384]{2,1,0:T(8,128)(2,1)S(1)}, u32[]{:S(2)}, u32[]{:S(2)}) collective-permute-start(bf16[1,256,384]{2,1,0:T(8,128)(2,1)S(1)} %get-tuple-element.54), channel_id=1, source_target_pairs={{0,3},{1,2},{2,1},{3,0},{4,7},{5,6},{6,5},{7,4},{8,11},{9,10},{10,... | collective-permute-start | bytes 589832 | tf_op jit(solution)/shard_map/ppermute | solution.py:24
where the time goes:
time: 105 us; the launch traced here: 104 us
  waiting for transfers between devices  45.5 us (43%)
  Pallas kernels  31.3 us (30%)
  starting transfers between devices  23.4 us (22%)
  local copies, waits for them, and re-layouts  4.1 us (4%)
    ppermute x27, waiting for transfers between devices, permute_by(): return lax.ppermute(value, axis, pairs)  45.5 us
    ppermute x27, starting transfers between devices, permute_by(): return lax.ppermute(value, axis, pairs)  23.4 us
    pallas_call x4, Pallas kernels, attend(): pl.pallas_call(functools.partial(attend_kernel, count, parts, ranges, hea...  15.7 us
    pallas_call x3, Pallas kernels, project(): pl.pallas_call(functools.partial(project_kernel, [len(group) for group in...  8.6 us
    pallas_call x2, Pallas kernels, finish(): pl.pallas_call(functools.partial(finish_kernel, count, spans, out_spans),...  4.71 us
    unnamed x14, local copies, waits for them, and re-layouts  2.7 us
  transfers between devices with their start and end apart: 27, of which 9 were waited for; matrix products, arithmetic and copies ran while one was open for 0% of the time, Pallas kernels for 27%

commit v1 on v0

--- a/solution.py
+++ b/solution.py
@@ -104,7 +104,7 @@
     ]
     for copy in copies:
         copy.start()
-    gain, bias = gain_ref[...], bias_ref[...]
+    gain, bias = gain_ref[...][None], bias_ref[...][None]
     for copy, held, out_ref in zip(copies, helds, outs, strict=True):
         copy.wait()
         size = held.shape[1]
@@ -130,7 +130,7 @@
 def norm_kernel(spans, *refs):
     *sources, gain_ref, bias_ref, out_ref = refs
     into = 0
-    gain, bias = gain_ref[...], bias_ref[...]
+    gain, bias = gain_ref[...][None], bias_ref[...][None]
     for which, row, left, size in spans:
         held = sources[which][row, left : left + size, :]
         out_ref[into : into + size, :] = normalized(held, gain, bias)
@@ -456,7 +456,7 @@
         return ((source ^ 1) - 2) % count
 
     near = WS - half
-    gain, bias = standardize_multiplier[None], standardize_offset_vector[None]
+    gain, bias = standardize_multiplier, standardize_offset_vector
     weights = triple_projection_matrix
     scales = logit_scaling_per_part
 

time: 105 us -> 105 us (level)
    broadcast_in_dim x2 -> x0, local copies, waits for them, and re-layouts: 1.4 us -> none  [on_device(): gain, bias = (standardize_multiplier[None], standardize_offset_vector[None])]
    unnamed x14 -> x22, local copies, waits for them, and re-layouts: 2.7 us -> 4.1 us
where the time goes in v1:
time: 105 us; the launch traced here: 104 us
  waiting for transfers between devices  45.4 us (43%)
  Pallas kernels  31.3 us (30%)
  starting transfers between devices  23.4 us (22%)
  local copies, waits for them, and re-layouts  4.1 us (4%)
    ppermute x27, waiting for transfers between devices, permute_by(): return lax.ppermute(value, axis, pairs)  45.4 us
    ppermute x27, starting transfers between devices, permute_by(): return lax.ppermute(value, axis, pairs)  23.4 us
    pallas_call x4, Pallas kernels, attend(): pl.pallas_call(functools.partial(attend_kernel, count, parts, ranges, hea...  15.7 us
    pallas_call x3, Pallas kernels, project(): pl.pallas_call(functools.partial(project_kernel, [len(group) for group in...  8.6 us
    pallas_call x2, Pallas kernels, finish(): pl.pallas_call(functools.partial(finish_kernel, count, spans, out_spans),...  4.71 us
    unnamed x22, local copies, waits for them, and re-layouts  4.1 us
  transfers between devices with their start and end apart: 27, of which 9 were waited for; matrix products, arithmetic and copies ran while one was open for 0% of the time, Pallas kernels for 27%

profile of v1, /device:TPU:0, one launch (start us, length us, event | category | flops | bytes accessed | tf_op | source)
XLA Modules:
  0.0 104.4 jit_solution(14303985521936654214)
XLA Ops:
  0.0 1.4 %copy-done = bf16[1,8,1,64,1536]{4,3,2,1,0:T(8,128)(2,1)S(1)} copy-done((bf16[1,8,1,64,1536]{4,3,2,1,0:T(8,128)(2,1)S(1)}, bf16[1,8,1,64,1536]{4,3,2,1,0:T(8,128)(2,1)}, u32[]{:S(2)}) %copy-start) | copy-done | bytes 1572888
  1.4 0.7 copy-done.4
  2.1 0.7 copy-done.6
  2.8 0.7 norm_local.1
  3.5 3.0 %collective-permute-start.2 = (bf16[128,1536]{1,0:T(8,128)(2,1)S(1)}, bf16[128,1536]{1,0:T(8,128)(2,1)S(1)}, u32[]{:S(2)}, u32[]{:S(2)}) collective-permute-start(bf16[128,1536]{1,0:T(8,128)(2,1)S(1)} %get-tuple-element.34.refs_0_), channel_id=1, source_target_pairs={{0,2},{1,3},{2,0},{3,1},{4,6},{5,7},{6,4},{7,5},{8,10},{9,11},{10,... | collective-permute-start | bytes 1179656 | tf_op jit(solution)/shard_map/ppermute | solution.py:24
  6.5 1.3 %copy-done.2 = bf16[384,1536]{1,0:T(8,128)(2,1)S(1)} copy-done((bf16[384,1536]{1,0:T(8,128)(2,1)S(1)}, bf16[384,1536]{1,0:T(8,128)(2,1)}, u32[]{:S(2)}) %copy-start.2) | copy-done | bytes 1179672
  7.9 0.1 collective-permute-start.20
  8.0 0.3 cut.1
  8.3 2.1 %collective-permute-start = (bf16[4,32,1536]{2,1,0:T(8,128)(2,1)S(1)}, bf16[4,32,1536]{2,1,0:T(8,128)(2,1)S(1)}, u32[]{:S(2)}, u32[]{:S(2)}) collective-permute-start(bf16[4,32,1536]{2,1,0:T(8,128)(2,1)S(1)} %get-tuple-element.33), channel_id=1, source_target_pairs={{0,4},{4,0},{8,12},{12,8},{1,5},{5,1},{9,13},{13,9},{2,6},{6,2},{1... | collective-permute-start | bytes 1179656 | tf_op jit(solution)/shard_map/ppermute | solution.py:24
  10.4 1.5 %collective-permute-start.5 = (bf16[64,1536]{1,0:T(8,128)(2,1)S(1)}, bf16[64,1536]{1,0:T(8,128)(2,1)S(1)}, u32[]{:S(2)}, u32[]{:S(2)}) collective-permute-start(bf16[64,1536]{1,0:T(8,128)(2,1)S(1)} %get-tuple-element.35.refs_4_), channel_id=1, source_target_pairs={{0,2},{1,3},{2,0},{3,1},{4,6},{5,7},{6,4},{7,5},{8,10},{9,11},{10,... | collective-permute-start | bytes 589832 | tf_op jit(solution)/shard_map/ppermute | solution.py:24
  11.9 4.6 %collective-permute-done.2.refs_2_ = bf16[128,1536]{1,0:T(8,128)(2,1)S(1)} collective-permute-done((bf16[128,1536]{1,0:T(8,128)(2,1)S(1)}, bf16[128,1536]{1,0:T(8,128)(2,1)S(1)}, u32[]{:S(2)}, u32[]{:S(2)}) %collective-permute-start.2) | collective-permute-done | bytes 393248 | tf_op jit(solution)/shard_map/ppermute | solution.py:24
  16.5 9.7 %collective-permute-done.5.refs_6_ = bf16[64,1536]{1,0:T(8,128)(2,1)S(1)} collective-permute-done((bf16[64,1536]{1,0:T(8,128)(2,1)S(1)}, bf16[64,1536]{1,0:T(8,128)(2,1)S(1)}, u32[]{:S(2)}, u32[]{:S(2)}) %collective-permute-start.5) | collective-permute-done | bytes 196640 | tf_op jit(solution)/shard_map/ppermute | solution.py:24
  26.2 0.5 collective-permute-start.6
  26.7 1.8 %collective-permute-start.21 = (bf16[96,1536]{1,0:T(8,128)(2,1)S(1)}, bf16[96,1536]{1,0:T(8,128)(2,1)S(1)}, u32[]{:S(2)}, u32[]{:S(2)}) collective-permute-start(bf16[96,1536]{1,0:T(8,128)(2,1)S(1)} %collective-permute-done.20.own_ref), channel_id=1, source_target_pairs={{0,4},{4,0},{8,12},{12,8},{1,5},{5,1},{9,13},{13,9},{2,6},{6,2},{1... | collective-permute-start | bytes 884744 | tf_op jit(solution)/shard_map/ppermute | solution.py:24
  28.5 0.3 shard_map.73.refs_0_
  28.9 0.6 collective-permute-start.7
  29.4 2.6 %collective-permute-start.8 = (bf16[4,16,1536]{2,1,0:T(8,128)(2,1)S(1)}, bf16[4,16,1536]{2,1,0:T(8,128)(2,1)S(1)}, u32[]{:S(2)}, u32[]{:S(2)}) collective-permute-start(bf16[4,16,1536]{2,1,0:T(8,128)(2,1)S(1)} %get-tuple-element.40), channel_id=1, source_target_pairs={{0,8},{4,12},{8,0},{12,4},{1,9},{5,13},{9,1},{13,5},{2,10},{6,14},... | collective-permute-start | bytes 589832 | tf_op jit(solution)/shard_map/ppermute | solution.py:24
  32.0 1.3 %collective-permute-start.9 = (bf16[4,16,1536]{2,1,0:T(8,128)(2,1)S(1)}, bf16[4,16,1536]{2,1,0:T(8,128)(2,1)S(1)}, u32[]{:S(2)}, u32[]{:S(2)}) collective-permute-start(bf16[4,16,1536]{2,1,0:T(8,128)(2,1)S(1)} %get-tuple-element.41), channel_id=1, source_target_pairs={{0,12},{4,8},{8,4},{12,0},{1,13},{5,9},{9,5},{13,1},{2,14},{6,10},... | collective-permute-start | bytes 589832 | tf_op jit(solution)/shard_map/ppermute | solution.py:24
  33.3 1.5 %collective-permute-start.11 = (bf16[128,1536]{1,0:T(8,128)(2,1)S(1)}, bf16[128,1536]{1,0:T(8,128)(2,1)S(1)}, u32[]{:S(2)}, u32[]{:S(2)}) collective-permute-start(bf16[128,1536]{1,0:T(8,128)(2,1)S(1)} %shard_map.73.refs_0_), channel_id=1, source_target_pairs={{0,2},{1,3},{2,0},{3,1},{4,6},{5,7},{6,4},{7,5},{8,10},{9,11},{10,... | collective-permute-start | bytes 1179656 | tf_op jit(solution)/shard_map/ppermute | solution.py:24
  34.8 3.2 %shard_map.74 = (bf16[512,1152]{1,0:T(8,128)(2,1)S(1)}, bf16[256,1152]{1,0:T(8,128)(2,1)S(1)}) custom-call(bf16[128,1536]{1,0:T(8,128)(2,1)S(1)} %get-tuple-element.34.refs_0_, bf16[128,1536]{1,0:T(8,128)(2,1)S(1)} %collective-permute-done.1.refs_1_, bf16[128,1536]{1,0:T(8,128)(2,1)S(1)} %collective-permute-done.2.refs_2_, ...), custom_call_target="tpu_custom_call" | custom-call | flops 2717908992 | bytes 7667712 | tf_op jit(solution)/shard_map/pallas_call | solution.py:237
  38.0 6.2 %collective-permute-done.7.refs_0_.refs_9_ = bf16[4,16,1536]{2,1,0:T(8,128)(2,1)S(1)} collective-permute-done((bf16[4,16,1536]{2,1,0:T(8,128)(2,1)S(1)}, bf16[4,16,1536]{2,1,0:T(8,128)(2,1)S(1)}, u32[]{:S(2)}, u32[]{:S(2)}) %collective-permute-start.7) | collective-permute-done | bytes 196640 | tf_op jit(solution)/shard_map/ppermute | solution.py:24
  44.2 0.2 collective-permute-done.8.refs_1_.refs_10_
  44.4 6.2 %collective-permute-done.9.refs_2_.refs_11_ = bf16[4,16,1536]{2,1,0:T(8,128)(2,1)S(1)} collective-permute-done((bf16[4,16,1536]{2,1,0:T(8,128)(2,1)S(1)}, bf16[4,16,1536]{2,1,0:T(8,128)(2,1)S(1)}, u32[]{:S(2)}, u32[]{:S(2)}) %collective-permute-start.9) | collective-permute-done | bytes 196640 | tf_op jit(solution)/shard_map/ppermute | solution.py:24
  50.6 0.4 shard_map.75.refs_0_
  51.0 1.6 %collective-permute-start.14 = (bf16[192,1536]{1,0:T(8,128)(2,1)S(1)}, bf16[192,1536]{1,0:T(8,128)(2,1)S(1)}, u32[]{:S(2)}, u32[]{:S(2)}) collective-permute-start(bf16[192,1536]{1,0:T(8,128)(2,1)S(1)} %shard_map.75.refs_0_), channel_id=1, source_target_pairs={{0,2},{1,3},{2,0},{3,1},{4,6},{5,7},{6,4},{7,5},{8,10},{9,11},{10,... | collective-permute-start | bytes 1769480 | tf_op jit(solution)/shard_map/ppermute | solution.py:24
  52.6 1.6 %collective-permute-start.22 = (bf16[192,1536]{1,0:T(8,128)(2,1)S(1)}, bf16[192,1536]{1,0:T(8,128)(2,1)S(1)}, u32[]{:S(2)}, u32[]{:S(2)}) collective-permute-start(bf16[192,1536]{1,0:T(8,128)(2,1)S(1)} %shard_map.83.own_ref), channel_id=1, source_target_pairs={{0,16},{16,0},{1,17},{17,1},{2,18},{18,2},{3,19},{19,3},{4,20},{20... | collective-permute-start | bytes 1769480 | tf_op jit(solution)/shard_map/ppermute | solution.py:24
  54.2 0.5 collective-permute-start.12
  54.7 10.8 %collective-permute-done.14.refs_2_ = bf16[192,1536]{1,0:T(8,128)(2,1)S(1)} collective-permute-done((bf16[192,1536]{1,0:T(8,128)(2,1)S(1)}, bf16[192,1536]{1,0:T(8,128)(2,1)S(1)}, u32[]{:S(2)}, u32[]{:S(2)}) %collective-permute-start.14) | collective-permute-done | bytes 589856 | tf_op jit(solution)/shard_map/ppermute | solution.py:24
  65.5 0.4 tags.1
  65.9 1.0 collective-permute-done.22.other_ref
  66.9 0.1 shard_map.84.refs_6_
  67.0 0.6 collective-permute-start.23
  67.6 2.2 %shard_map.76.refs_1_ = bf16[512,1152]{1,0:T(8,128)(2,1)S(1)} custom-call(bf16[128,1536]{1,0:T(8,128)(2,1)S(1)} %shard_map.73.refs_0_, bf16[128,1536]{1,0:T(8,128)(2,1)S(1)} %collective-permute-done.10.refs_1_, bf16[128,1536]{1,0:T(8,128)(2,1)S(1)} %collective-permute-done.11.refs_2_, bf16[128,1536]{1,0:T(8,128)(2,1)S(1)} %collective-permute-done.12.refs_3_, ...), custom_call_target="tpu_custom_call" | custom-call | flops 1811939328 | bytes 6291456 | tf_op jit(solution)/shard_map/pallas_call | solution.py:237
  69.8 3.9 %shard_map.77 = (bf16[1,256,384]{2,1,0:T(8,128)(2,1)S(1)}, bf16[1,256,384]{2,1,0:T(8,128)(2,1)S(1)}) custom-call(bf16[512,1152]{1,0:T(8,128)(2,1)S(1)} %get-tuple-element.47.refs_0_, bf16[512,1152]{1,0:T(8,128)(2,1)S(1)} %shard_map.76.refs_1_, bf16[1024,128]{1,0:T(8,128)(2,1)S(1)} %get-tuple-element.43.refs_2_, ...), custom_call_target="tpu_custom_call" | custom-call | flops 2147483648 | bytes 2359296 | tf_op jit(solution)/shard_map/pallas_call | solution.py:311
  73.7 4.0 %shard_map.78 = (bf16[1,256,384]{2,1,0:T(8,128)(2,1)S(1)}, bf16[1,256,384]{2,1,0:T(8,128)(2,1)S(1)}) custom-call(bf16[512,1152]{1,0:T(8,128)(2,1)S(1)} %get-tuple-element.47.refs_0_, bf16[512,1152]{1,0:T(8,128)(2,1)S(1)} %shard_map.76.refs_1_, bf16[1024,128]{1,0:T(8,128)(2,1)S(1)} %get-tuple-element.43.refs_2_, ...), custom_call_target="tpu_custom_call" | custom-call | flops 2147483648 | bytes 2359296 | tf_op jit(solution)/shard_map/pallas_call | solution.py:311
  77.7 0.1 collective-permute-start.24
  77.8 1.1 %collective-permute-start.25 = (bf16[1,256,384]{2,1,0:T(8,128)(2,1)S(1)}, bf16[1,256,384]{2,1,0:T(8,128)(2,1)S(1)}, u32[]{:S(2)}, u32[]{:S(2)}) collective-permute-start(bf16[1,256,384]{2,1,0:T(8,128)(2,1)S(1)} %get-tuple-element.45), channel_id=1, source_target_pairs={{0,2},{1,3},{2,0},{3,1},{4,6},{5,7},{6,4},{7,5},{8,10},{9,11},{10,... | collective-permute-start | bytes 589832 | tf_op jit(solution)/shard_map/ppermute | solution.py:24
  78.9 0.8 collective-permute-start.26
  79.6 3.2 %shard_map.79.refs_1_ = bf16[768,1152]{1,0:T(8,128)(2,1)S(1)} custom-call(bf16[192,1536]{1,0:T(8,128)(2,1)S(1)} %shard_map.75.refs_0_, bf16[192,1536]{1,0:T(8,128)(2,1)S(1)} %collective-permute-done.13.refs_1_, bf16[192,1536]{1,0:T(8,128)(2,1)S(1)} %collective-permute-done.14.refs_2_, bf16[192,1536]{1,0:T(8,128)(2,1)S(1)} %collective-permute-done.15.refs_3_, ...), custom_call_target="tpu_custom_call" | custom-call | flops 2717908992 | bytes 7667712 | tf_op jit(solution)/shard_map/pallas_call | solution.py:237
  82.8 3.9 %shard_map.80 = (bf16[1,256,384]{2,1,0:T(8,128)(2,1)S(1)}, bf16[1,256,384]{2,1,0:T(8,128)(2,1)S(1)}) custom-call(bf16[256,1152]{1,0:T(8,128)(2,1)S(1)} %get-tuple-element.55.refs_0_, bf16[768,1152]{1,0:T(8,128)(2,1)S(1)} %shard_map.79.refs_1_, bf16[1024,128]{1,0:T(8,128)(2,1)S(1)} %get-tuple-element.51.refs_2_, ...), custom_call_target="tpu_custom_call" | custom-call | flops 2147483648 | bytes 2359296 | tf_op jit(solution)/shard_map/pallas_call | solution.py:311
  86.7 3.9 %shard_map.81 = (bf16[1,256,384]{2,1,0:T(8,128)(2,1)S(1)}, bf16[1,256,384]{2,1,0:T(8,128)(2,1)S(1)}) custom-call(bf16[256,1152]{1,0:T(8,128)(2,1)S(1)} %get-tuple-element.55.refs_0_, bf16[768,1152]{1,0:T(8,128)(2,1)S(1)} %shard_map.79.refs_1_, bf16[1024,128]{1,0:T(8,128)(2,1)S(1)} %get-tuple-element.51.refs_2_, ...), custom_call_target="tpu_custom_call" | custom-call | flops 2147483648 | bytes 2359296 | tf_op jit(solution)/shard_map/pallas_call | solution.py:311
  90.7 0.8 collective-permute-start.17
  91.4 0.4 collective-permute-start.16
  91.8 1.0 collective-permute-start.18
  92.9 1.8 %shard_map.85.refs_12_ = bf16[8,32,1536]{2,1,0:T(8,128)(2,1)S(1)} custom-call(bf16[256,384]{1,0:T(8,128)(2,1)S(1)} %bitcast.17, bf16[256,384]{1,0:T(8,128)(2,1)S(1)} %bitcast.18, bf16[256,384]{1,0:T(8,128)(2,1)S(1)} %bitcast.20, bf16[256,384]{1,0:T(8,128)(2,1)S(1)} %bitcast.21, bf16[384,1536]{1,0:T(8,128)(2,1)S(1)} %copy-done.3, ...), custom_call_target="tpu_custom_call" | custom-call | flops 1207959552 | bytes 7077888 | tf_op jit(solution)/shard_map/pallas_call | solution.py:349
  94.7 3.8 %collective-permute-done.17 = bf16[1,256,384]{2,1,0:T(8,128)(2,1)S(1)} collective-permute-done((bf16[1,256,384]{2,1,0:T(8,128)(2,1)S(1)}, bf16[1,256,384]{2,1,0:T(8,128)(2,1)S(1)}, u32[]{:S(2)}, u32[]{:S(2)}) %collective-permute-start.17) | collective-permute-done | bytes 196640 | tf_op jit(solution)/shard_map/ppermute | solution.py:24
  98.5 3.0 %collective-permute-done.18 = bf16[1,256,384]{2,1,0:T(8,128)(2,1)S(1)} collective-permute-done((bf16[1,256,384]{2,1,0:T(8,128)(2,1)S(1)}, bf16[1,256,384]{2,1,0:T(8,128)(2,1)S(1)}, u32[]{:S(2)}, u32[]{:S(2)}) %collective-permute-start.18) | collective-permute-done | bytes 196640 | tf_op jit(solution)/shard_map/ppermute | solution.py:24
  101.5 2.9 %shard_map.86 = bf16[8,64,1536]{2,1,0:T(8,128)(2,1)} custom-call(bf16[256,384]{1,0:T(8,128)(2,1)S(1)} %bitcast.19, bf16[256,384]{1,0:T(8,128)(2,1)S(1)} %bitcast.23, bf16[256,384]{1,0:T(8,128)(2,1)S(1)} %bitcast.22, bf16[256,384]{1,0:T(8,128)(2,1)S(1)} %bitcast.24, bf16[384,1536]{1,0:T(8,128)(2,1)S(1)} %copy-done.3, ...), custom_call_target="tpu_custom_call" | custom-call | flops 1207959552 | bytes 7077888 | tf_op jit(solution)/shard_map/pallas_call | solution.py:349
  (45 shorter events, 0.2 us)
Async XLA Ops:
  0.0 1.4 %copy-start = (bf16[1,8,1,64,1536]{4,3,2,1,0:T(8,128)(2,1)S(1)}, bf16[1,8,1,64,1536]{4,3,2,1,0:T(8,128)(2,1)}, u32[]{:S(2)}) copy-start(bf16[1,8,1,64,1536]{4,3,2,1,0:T(8,128)(2,1)} %param.7) | copy-start | bytes 4718596
  1.4 0.7 copy-start.4
  2.1 0.7 copy-start.6
  2.8 5.2 %copy-start.1 = (bf16[1,8,1,64,1536]{4,3,2,1,0:T(8,128)(2,1)S(1)}, bf16[1,8,1,64,1536]{4,3,2,1,0:T(8,128)(2,1)}, u32[]{:S(2)}) copy-start(bf16[1,8,1,64,1536]{4,3,2,1,0:T(8,128)(2,1)} %param.7) | copy-start | bytes 4718596
  3.5 13.0 %collective-permute-start.2 = (bf16[128,1536]{1,0:T(8,128)(2,1)S(1)}, bf16[128,1536]{1,0:T(8,128)(2,1)S(1)}, u32[]{:S(2)}, u32[]{:S(2)}) collective-permute-start(bf16[128,1536]{1,0:T(8,128)(2,1)S(1)} %get-tuple-element.34.refs_0_), channel_id=1, source_target_pairs={{0,2},{1,3},{2,0},{3,1},{4,6},{5,7},{6,4},{7,5},{8,10},{9,11},{10,... | collective-permute-start | bytes 1179656 | tf_op jit(solution)/shard_map/ppermute | solution.py:24
  6.5 1.3 %copy-start.2 = (bf16[384,1536]{1,0:T(8,128)(2,1)S(1)}, bf16[384,1536]{1,0:T(8,128)(2,1)}, u32[]{:S(2)}) copy-start(bf16[384,1536]{1,0:T(8,128)(2,1)} %refs_4_.17) | copy-start | bytes 3538948
  7.8 20.7 %copy-start.5 = (f32[1536]{0:T(1024)S(1)}, f32[1536]{0:T(1024)}, u32[]{:S(2)}) copy-start(f32[1536]{0:T(1024)} %refs_3_.1) | copy-start | bytes 18436
  7.8 20.7 %copy-start.7 = (f32[1536]{0:T(1024)S(1)}, f32[1536]{0:T(1024)}, u32[]{:S(2)}) copy-start(f32[1536]{0:T(1024)} %refs_4_.9) | copy-start | bytes 18436
  7.8 27.0 %copy-start.8 = (bf16[3,1536,384]{2,1,0:T(8,128)(2,1)S(1)}, bf16[3,1536,384]{2,1,0:T(8,128)(2,1)}, u32[]{:S(2)}) copy-start(bf16[3,1536,384]{2,1,0:T(8,128)(2,1)} %refs_4_.13) | copy-start | bytes 10616836
  7.9 18.3 %collective-permute-start.20 = (bf16[96,1536]{1,0:T(8,128)(2,1)S(1)}, bf16[96,1536]{1,0:T(8,128)(2,1)S(1)}, u32[]{:S(2)}, u32[]{:S(2)}) collective-permute-start(bf16[96,1536]{1,0:T(8,128)(2,1)S(1)} %shard_map.82), channel_id=1, source_target_pairs={{0,2},{1,3},{2,0},{3,1},{4,6},{5,7},{6,4},{7,5},{8,10},{9,11},{10,... | collective-permute-start | bytes 884744 | tf_op jit(solution)/shard_map/ppermute | solution.py:24
  8.3 18.4 %collective-permute-start = (bf16[4,32,1536]{2,1,0:T(8,128)(2,1)S(1)}, bf16[4,32,1536]{2,1,0:T(8,128)(2,1)S(1)}, u32[]{:S(2)}, u32[]{:S(2)}) collective-permute-start(bf16[4,32,1536]{2,1,0:T(8,128)(2,1)S(1)} %get-tuple-element.33), channel_id=1, source_target_pairs={{0,4},{4,0},{8,12},{12,8},{1,5},{5,1},{9,13},{13,9},{2,6},{6,2},{1... | collective-permute-start | bytes 1179656 | tf_op jit(solution)/shard_map/ppermute | solution.py:24
  10.4 15.8 %collective-permute-start.5 = (bf16[64,1536]{1,0:T(8,128)(2,1)S(1)}, bf16[64,1536]{1,0:T(8,128)(2,1)S(1)}, u32[]{:S(2)}, u32[]{:S(2)}) collective-permute-start(bf16[64,1536]{1,0:T(8,128)(2,1)S(1)} %get-tuple-element.35.refs_4_), channel_id=1, source_target_pairs={{0,2},{1,3},{2,0},{3,1},{4,6},{5,7},{6,4},{7,5},{8,10},{9,11},{10,... | collective-permute-start | bytes 589832 | tf_op jit(solution)/shard_map/ppermute | solution.py:24
  11.9 20.1 %collective-permute-start.1 = (bf16[128,1536]{1,0:T(8,128)(2,1)S(1)}, bf16[128,1536]{1,0:T(8,128)(2,1)S(1)}, u32[]{:S(2)}, u32[]{:S(2)}) collective-permute-start(bf16[128,1536]{1,0:T(8,128)(2,1)S(1)} %get-tuple-element.34.refs_0_), channel_id=1, source_target_pairs={{0,1},{1,0},{2,3},{3,2},{4,5},{5,4},{6,7},{7,6},{8,9},{9,8},{10,11... | collective-permute-start | bytes 1179656 | tf_op jit(solution)/shard_map/ppermute | solution.py:24
  16.5 16.8 %collective-permute-start.3 = (bf16[128,1536]{1,0:T(8,128)(2,1)S(1)}, bf16[128,1536]{1,0:T(8,128)(2,1)S(1)}, u32[]{:S(2)}, u32[]{:S(2)}) collective-permute-start(bf16[128,1536]{1,0:T(8,128)(2,1)S(1)} %collective-permute-done.2.refs_2_), channel_id=1, source_target_pairs={{0,1},{1,0},{2,3},{3,2},{4,5},{5,4},{6,7},{7,6},{8,9},{9,8},{10,11... | collective-permute-start | bytes 1179656 | tf_op jit(solution)/shard_map/ppermute | solution.py:24
  26.2 2.7 %collective-permute-start.4 = (bf16[64,1536]{1,0:T(8,128)(2,1)S(1)}, bf16[64,1536]{1,0:T(8,128)(2,1)S(1)}, u32[]{:S(2)}, u32[]{:S(2)}) collective-permute-start(bf16[64,1536]{1,0:T(8,128)(2,1)S(1)} %get-tuple-element.35.refs_4_), channel_id=1, source_target_pairs={{0,1},{1,0},{2,3},{3,2},{4,5},{5,4},{6,7},{7,6},{8,9},{9,8},{10,11... | collective-permute-start | bytes 589832 | tf_op jit(solution)/shard_map/ppermute | solution.py:24
  26.2 3.3 %collective-permute-start.6 = (bf16[64,1536]{1,0:T(8,128)(2,1)S(1)}, bf16[64,1536]{1,0:T(8,128)(2,1)S(1)}, u32[]{:S(2)}, u32[]{:S(2)}) collective-permute-start(bf16[64,1536]{1,0:T(8,128)(2,1)S(1)} %collective-permute-done.5.refs_6_), channel_id=1, source_target_pairs={{0,1},{1,0},{2,3},{3,2},{4,5},{5,4},{6,7},{7,6},{8,9},{9,8},{10,11... | collective-permute-start | bytes 589832 | tf_op jit(solution)/shard_map/ppermute | solution.py:24
  26.7 25.9 %collective-permute-start.21 = (bf16[96,1536]{1,0:T(8,128)(2,1)S(1)}, bf16[96,1536]{1,0:T(8,128)(2,1)S(1)}, u32[]{:S(2)}, u32[]{:S(2)}) collective-permute-start(bf16[96,1536]{1,0:T(8,128)(2,1)S(1)} %collective-permute-done.20.own_ref), channel_id=1, source_target_pairs={{0,4},{4,0},{8,12},{12,8},{1,5},{5,1},{9,13},{13,9},{2,6},{6,2},{1... | collective-permute-start | bytes 884744 | tf_op jit(solution)/shard_map/ppermute | solution.py:24
  28.9 15.3 %collective-permute-start.7 = (bf16[4,16,1536]{2,1,0:T(8,128)(2,1)S(1)}, bf16[4,16,1536]{2,1,0:T(8,128)(2,1)S(1)}, u32[]{:S(2)}, u32[]{:S(2)}) collective-permute-start(bf16[4,16,1536]{2,1,0:T(8,128)(2,1)S(1)} %get-tuple-element.37), channel_id=1, source_target_pairs={{0,4},{4,0},{8,12},{12,8},{1,5},{5,1},{9,13},{13,9},{2,6},{6,2},{1... | collective-permute-start | bytes 589832 | tf_op jit(solution)/shard_map/ppermute | solution.py:24
  29.4 14.9 %collective-permute-start.8 = (bf16[4,16,1536]{2,1,0:T(8,128)(2,1)S(1)}, bf16[4,16,1536]{2,1,0:T(8,128)(2,1)S(1)}, u32[]{:S(2)}, u32[]{:S(2)}) collective-permute-start(bf16[4,16,1536]{2,1,0:T(8,128)(2,1)S(1)} %get-tuple-element.40), channel_id=1, source_target_pairs={{0,8},{4,12},{8,0},{12,4},{1,9},{5,13},{9,1},{13,5},{2,10},{6,14},... | collective-permute-start | bytes 589832 | tf_op jit(solution)/shard_map/ppermute | solution.py:24
  32.0 18.6 %collective-permute-start.9 = (bf16[4,16,1536]{2,1,0:T(8,128)(2,1)S(1)}, bf16[4,16,1536]{2,1,0:T(8,128)(2,1)S(1)}, u32[]{:S(2)}, u32[]{:S(2)}) collective-permute-start(bf16[4,16,1536]{2,1,0:T(8,128)(2,1)S(1)} %get-tuple-element.41), channel_id=1, source_target_pairs={{0,12},{4,8},{8,4},{12,0},{1,13},{5,9},{9,5},{13,1},{2,14},{6,10},... | collective-permute-start | bytes 589832 | tf_op jit(solution)/shard_map/ppermute | solution.py:24
  33.3 20.9 %collective-permute-start.11 = (bf16[128,1536]{1,0:T(8,128)(2,1)S(1)}, bf16[128,1536]{1,0:T(8,128)(2,1)S(1)}, u32[]{:S(2)}, u32[]{:S(2)}) collective-permute-start(bf16[128,1536]{1,0:T(8,128)(2,1)S(1)} %shard_map.73.refs_0_), channel_id=1, source_target_pairs={{0,2},{1,3},{2,0},{3,1},{4,6},{5,7},{6,4},{7,5},{8,10},{9,11},{10,... | collective-permute-start | bytes 1179656 | tf_op jit(solution)/shard_map/ppermute | solution.py:24
  44.2 21.3 %copy-start.9 = (s32[1,32,64]{2,1,0:T(8,128)S(1)}, s32[1,32,64]{2,1,0:T(8,128)}, u32[]{:S(2)}) copy-start(s32[1,32,64]{2,1,0:T(8,128)} %param.8) | copy-start | bytes 24580
  44.2 22.7 %copy-start.3 = (bf16[384,1536]{1,0:T(8,128)(2,1)S(1)}, bf16[384,1536]{1,0:T(8,128)(2,1)}, u32[]{:S(2)}) copy-start(bf16[384,1536]{1,0:T(8,128)(2,1)} %refs_4_.17) | copy-start | bytes 3538948
  51.0 14.5 %collective-permute-start.14 = (bf16[192,1536]{1,0:T(8,128)(2,1)S(1)}, bf16[192,1536]{1,0:T(8,128)(2,1)S(1)}, u32[]{:S(2)}, u32[]{:S(2)}) collective-permute-start(bf16[192,1536]{1,0:T(8,128)(2,1)S(1)} %shard_map.75.refs_0_), channel_id=1, source_target_pairs={{0,2},{1,3},{2,0},{3,1},{4,6},{5,7},{6,4},{7,5},{8,10},{9,11},{10,... | collective-permute-start | bytes 1769480 | tf_op jit(solution)/shard_map/ppermute | solution.py:24
  52.6 14.2 %collective-permute-start.22 = (bf16[192,1536]{1,0:T(8,128)(2,1)S(1)}, bf16[192,1536]{1,0:T(8,128)(2,1)S(1)}, u32[]{:S(2)}, u32[]{:S(2)}) collective-permute-start(bf16[192,1536]{1,0:T(8,128)(2,1)S(1)} %shard_map.83.own_ref), channel_id=1, source_target_pairs={{0,16},{16,0},{1,17},{17,1},{2,18},{18,2},{3,19},{19,3},{4,20},{20... | collective-permute-start | bytes 1769480 | tf_op jit(solution)/shard_map/ppermute | solution.py:24
  54.2 12.8 %collective-permute-start.10 = (bf16[128,1536]{1,0:T(8,128)(2,1)S(1)}, bf16[128,1536]{1,0:T(8,128)(2,1)S(1)}, u32[]{:S(2)}, u32[]{:S(2)}) collective-permute-start(bf16[128,1536]{1,0:T(8,128)(2,1)S(1)} %shard_map.73.refs_0_), channel_id=1, source_target_pairs={{0,1},{1,0},{2,3},{3,2},{4,5},{5,4},{6,7},{7,6},{8,9},{9,8},{10,11... | collective-permute-start | bytes 1179656 | tf_op jit(solution)/shard_map/ppermute | solution.py:24
  54.2 13.3 %collective-permute-start.12 = (bf16[128,1536]{1,0:T(8,128)(2,1)S(1)}, bf16[128,1536]{1,0:T(8,128)(2,1)S(1)}, u32[]{:S(2)}, u32[]{:S(2)}) collective-permute-start(bf16[128,1536]{1,0:T(8,128)(2,1)S(1)} %collective-permute-done.11.refs_2_), channel_id=1, source_target_pairs={{0,1},{1,0},{2,3},{3,2},{4,5},{5,4},{6,7},{7,6},{8,9},{9,8},{10,11... | collective-permute-start | bytes 1179656 | tf_op jit(solution)/shard_map/ppermute | solution.py:24
  54.7 23.0 %collective-permute-start.13 = (bf16[192,1536]{1,0:T(8,128)(2,1)S(1)}, bf16[192,1536]{1,0:T(8,128)(2,1)S(1)}, u32[]{:S(2)}, u32[]{:S(2)}) collective-permute-start(bf16[192,1536]{1,0:T(8,128)(2,1)S(1)} %shard_map.75.refs_0_), channel_id=1, source_target_pairs={{0,1},{1,0},{2,3},{3,2},{4,5},{5,4},{6,7},{7,6},{8,9},{9,8},{10,11... | collective-permute-start | bytes 1769480 | tf_op jit(solution)/shard_map/ppermute | solution.py:24
  65.5 13.3 %collective-permute-start.15 = (bf16[192,1536]{1,0:T(8,128)(2,1)S(1)}, bf16[192,1536]{1,0:T(8,128)(2,1)S(1)}, u32[]{:S(2)}, u32[]{:S(2)}) collective-permute-start(bf16[192,1536]{1,0:T(8,128)(2,1)S(1)} %collective-permute-done.14.refs_2_), channel_id=1, source_target_pairs={{0,1},{1,0},{2,3},{3,2},{4,5},{5,4},{6,7},{7,6},{8,9},{9,8},{10,11... | collective-permute-start | bytes 1769480 | tf_op jit(solution)/shard_map/ppermute | solution.py:24
  66.9 23.8 %collective-permute-start.19 = (bf16[384,1536]{1,0:T(8,128)(2,1)S(1)}, bf16[384,1536]{1,0:T(8,128)(2,1)S(1)}, u32[]{:S(2)}, u32[]{:S(2)}) collective-permute-start(bf16[384,1536]{1,0:T(8,128)(2,1)S(1)} %copy-done.3), channel_id=1, source_target_pairs={{0,1},{1,0},{2,3},{3,2},{4,5},{5,4},{6,7},{7,6},{8,9},{9,8},{10,11... | collective-permute-start | bytes 3538952 | tf_op jit(solution)/shard_map/ppermute | solution.py:24
  67.0 2.8 %copy-start.10 = (f32[4]{0:T(128)S(1)}, f32[4]{0:T(128)}, u32[]{:S(2)}) copy-start(f32[4]{0:T(128)} %refs_4_.15) | copy-start | bytes 52
  67.0 25.9 %collective-permute-start.23 = (bf16[384,1536]{1,0:T(8,128)(2,1)S(1)}, bf16[384,1536]{1,0:T(8,128)(2,1)S(1)}, u32[]{:S(2)}, u32[]{:S(2)}) collective-permute-start(bf16[384,1536]{1,0:T(8,128)(2,1)S(1)} %shard_map.84.refs_6_), channel_id=1, source_target_pairs={{0,1},{1,0},{2,3},{3,2},{4,5},{5,4},{6,7},{7,6},{8,9},{9,8},{10,11... | collective-permute-start | bytes 3538952 | tf_op jit(solution)/shard_map/ppermute | solution.py:24
  77.7 13.7 %collective-permute-start.24 = (bf16[1,256,384]{2,1,0:T(8,128)(2,1)S(1)}, bf16[1,256,384]{2,1,0:T(8,128)(2,1)S(1)}, u32[]{:S(2)}, u32[]{:S(2)}) collective-permute-start(bf16[1,256,384]{2,1,0:T(8,128)(2,1)S(1)} %get-tuple-element.49), channel_id=1, source_target_pairs={{0,1},{1,0},{2,3},{3,2},{4,5},{5,4},{6,7},{7,6},{8,9},{9,8},{10,11... | collective-permute-start | bytes 589832 | tf_op jit(solution)/shard_map/ppermute | solution.py:24
  77.8 14.0 %collective-permute-start.25 = (bf16[1,256,384]{2,1,0:T(8,128)(2,1)S(1)}, bf16[1,256,384]{2,1,0:T(8,128)(2,1)S(1)}, u32[]{:S(2)}, u32[]{:S(2)}) collective-permute-start(bf16[1,256,384]{2,1,0:T(8,128)(2,1)S(1)} %get-tuple-element.45), channel_id=1, source_target_pairs={{0,2},{1,3},{2,0},{3,1},{4,6},{5,7},{6,4},{7,5},{8,10},{9,11},{10,... | collective-permute-start | bytes 589832 | tf_op jit(solution)/shard_map/ppermute | solution.py:24
  78.9 14.0 %collective-permute-start.26 = (bf16[1,256,384]{2,1,0:T(8,128)(2,1)S(1)}, bf16[1,256,384]{2,1,0:T(8,128)(2,1)S(1)}, u32[]{:S(2)}, u32[]{:S(2)}) collective-permute-start(bf16[1,256,384]{2,1,0:T(8,128)(2,1)S(1)} %get-tuple-element.46), channel_id=1, source_target_pairs={{0,3},{1,2},{2,1},{3,0},{4,7},{5,6},{6,5},{7,4},{8,11},{9,10},{10,... | collective-permute-start | bytes 589832 | tf_op jit(solution)/shard_map/ppermute | solution.py:24
  90.7 7.8 %collective-permute-start.17 = (bf16[1,256,384]{2,1,0:T(8,128)(2,1)S(1)}, bf16[1,256,384]{2,1,0:T(8,128)(2,1)S(1)}, u32[]{:S(2)}, u32[]{:S(2)}) collective-permute-start(bf16[1,256,384]{2,1,0:T(8,128)(2,1)S(1)} %get-tuple-element.53), channel_id=1, source_target_pairs={{0,2},{1,3},{2,0},{3,1},{4,6},{5,7},{6,4},{7,5},{8,10},{9,11},{10,... | collective-permute-start | bytes 589832 | tf_op jit(solution)/shard_map/ppermute | solution.py:24
  91.4 3.3 %collective-permute-start.16 = (bf16[1,256,384]{2,1,0:T(8,128)(2,1)S(1)}, bf16[1,256,384]{2,1,0:T(8,128)(2,1)S(1)}, u32[]{:S(2)}, u32[]{:S(2)}) collective-permute-start(bf16[1,256,384]{2,1,0:T(8,128)(2,1)S(1)} %get-tuple-element.57), channel_id=1, source_target_pairs={{0,1},{1,0},{2,3},{3,2},{4,5},{5,4},{6,7},{7,6},{8,9},{9,8},{10,11... | collective-permute-start | bytes 589832 | tf_op jit(solution)/shard_map/ppermute | solution.py:24
  91.8 9.7 %collective-permute-start.18 = (bf16[1,256,384]{2,1,0:T(8,128)(2,1)S(1)}, bf16[1,256,384]{2,1,0:T(8,128)(2,1)S(1)}, u32[]{:S(2)}, u32[]{:S(2)}) collective-permute-start(bf16[1,256,384]{2,1,0:T(8,128)(2,1)S(1)} %get-tuple-element.54), channel_id=1, source_target_pairs={{0,3},{1,2},{2,1},{3,0},{4,7},{5,6},{6,5},{7,4},{8,11},{9,10},{10,... | collective-permute-start | bytes 589832 | tf_op jit(solution)/shard_map/ppermute | solution.py:24

commit v2 on v1

--- a/solution.py
+++ b/solution.py
@@ -14,6 +14,7 @@
 REGIONS = 32
 LANE = 128
 FAR = -1e30
+ALL_VMEM = 67_043_328
 F32 = jnp.float32
 BF16 = jnp.bfloat16
 
@@ -88,7 +89,7 @@
         in_specs=[HELD],
         out_specs=[VMEM] * len(boxes),
         scratch_shapes=[pltpu.SemaphoreType.DMA((len(boxes),))],
-        compiler_params=pltpu.CompilerParams(vmem_limit_bytes=8 << 20),
+        compiler_params=pltpu.CompilerParams(vmem_limit_bytes=ALL_VMEM - (22 << 20) // 10),
         cost_estimate=pl.CostEstimate(flops=0, bytes_accessed=2 * pixels.size, transcendentals=0),
         name="cut",
     )(pixels)
@@ -121,7 +122,7 @@
         out_specs=[VMEM] * len(boxes),
         scratch_shapes=[pltpu.VMEM((rows, size, width), BF16) for _, rows, _, size in boxes]
         + [pltpu.SemaphoreType.DMA((len(boxes),))],
-        compiler_params=pltpu.CompilerParams(vmem_limit_bytes=8 << 20),
+        compiler_params=pltpu.CompilerParams(vmem_limit_bytes=ALL_VMEM - (12 << 20) // 10),
         cost_estimate=pl.CostEstimate(flops=5 * pixels.size, bytes_accessed=2 * pixels.size, transcendentals=0),
         name="norm_local",
     )(pixels, gain, bias)
@@ -152,7 +153,8 @@
     )(*sources, gain, bias)
 
 
-def tag_kernel(count, near, label_ref, *outs):
+def tag_kernel(count, near, label_ref, weight_ref, *outs):
+    del weight_ref
     query_0, key_0, query_1, key_1 = outs
     row_count, _ = label_ref.shape
     rows = row_count // (2 * count)
@@ -189,19 +191,19 @@
                     key_ref[into : into + size, :] = key[left : left + size]
 
 
-def region_tags(labels, count, near):
+def region_tags(labels, weights, count, near):
     pixels = labels.shape[0] * WS
     return pl.pallas_call(
         functools.partial(tag_kernel, count, near),
         out_shape=[jax.ShapeDtypeStruct((pixels, LANE), BF16)] * 4,
-        in_specs=[VMEM],
+        in_specs=[VMEM] * 2,
         out_specs=[VMEM] * 4,
         compiler_params=pltpu.CompilerParams(vmem_limit_bytes=8 << 20),
         cost_estimate=pl.CostEstimate(
             flops=8 * pixels * LANE * labels.shape[0], bytes_accessed=8 * pixels * LANE, transcendentals=0
         ),
         name="tags",
-    )(labels)
+    )(labels, weights)
 
 
 def project_kernel(counts, *refs):
@@ -210,9 +212,9 @@
         groups.append(refs[:count])
         refs = refs[count:]
     weight_ref, *outs = refs
+    block = jnp.concatenate([piece[...] for group in groups for piece in group], axis=0)
     head_width = weight_ref.shape[2]
     slot = padded(head_width)
-    block = jnp.concatenate([piece[...] for group in groups for piece in group], axis=0)
     if slot == head_width:
         weights = jnp.concatenate([weight_ref[t] for t in range(3)], axis=1)
         products = [(0, jnp.dot(block, weights, preferred_element_type=F32).astype(BF16))]
@@ -230,7 +232,7 @@
 
 
 def project(groups, weights):
-    width = weights.shape[1]
+    width = groups[0][0].shape[1]
     slot = padded(weights.shape[2])
     sizes = [sum(piece.shape[0] for piece in group) for group in groups]
     total = sum(sizes)
@@ -258,34 +260,43 @@
     heads = head_width // CHANNEL_PER_PART
     base = math.log2(math.e) / math.sqrt(CHANNEL_PER_PART)
     tiles = [None] * (slot // LANE)
-    for head in range(heads):
+    key_rows = key_tags[...]
+    query_rows, at = [], 0
+    for z in sizes:
+        query_rows.append(query_tags[at + low * z : at + high * z, :])
+        at += count * z
+    query_rows = jnp.concatenate(query_rows, axis=0)
+
+    def span(head):
         first = head * CHANNEL_PER_PART
         last = first + CHANNEL_PER_PART
         left, right = first // LANE * LANE, padded(last)
+        lane = lax.broadcasted_iota(jnp.int32, (1, right - left), 1)
+        return left, right, (lane >= first - left) & (lane < last - left)
+
+    def scores_of(head):
+        left, right, inside = span(head)
         reps = (right - left) // LANE
-        lane = lax.broadcasted_iota(jnp.int32, (1, right - left), 1)
-        inside = (lane >= first - left) & (lane < last - left)
         queries = jnp.concatenate(
             [b[low * z : high * z, left:right] for b, z in zip(blocks, sizes, strict=True)], axis=0
         )
-        tags, at = [], 0
-        for z in sizes:
-            tags.append(query_tags[at + low * z : at + high * z, :])
-            at += count * z
-        tags = jnp.concatenate(tags, axis=0)
-        queries = jnp.where(inside, queries, jnp.concatenate([tags] * reps, axis=1))
+        queries = jnp.where(inside, queries, jnp.concatenate([query_rows] * reps, axis=1))
         keys = jnp.concatenate([b[:, slot + left : slot + right] for b in blocks], axis=0)
-        tags = key_tags[...]
-        keys = jnp.where(inside, keys, jnp.concatenate([tags] * reps, axis=1))
-        values = jnp.concatenate([b[:, 2 * slot + left : 2 * slot + right] for b in blocks], axis=0)
-        scores = lax.dot_general(
-            queries, keys, (((1,), (1,)), ((), ())), preferred_element_type=F32
-        )
+        keys = jnp.where(inside, keys, jnp.concatenate([key_rows] * reps, axis=1))
+        return lax.dot_general(queries, keys, (((1,), (1,)), ((), ())), preferred_element_type=F32)
+
+    following = scores_of(0)
+    for head in range(heads):
+        scores = following
+        if head + 1 < heads:
+            following = scores_of(head + 1)
+        left, right, inside = span(head)
         row_max = jnp.max(scores, axis=-1, keepdims=True)
         numerators = jnp.exp2((scores - row_max) * (scale_ref[head] * base))
         total = jnp.sum(numerators, axis=-1, keepdims=True)
+        values = jnp.concatenate([b[:, 2 * slot + left : 2 * slot + right] for b in blocks], axis=0)
         mixed = jnp.dot(numerators.astype(BF16), values, preferred_element_type=F32) / total
-        for i in range(reps):
+        for i in range((right - left) // LANE):
             tile = left // LANE + i
             own = mixed[:, i * LANE : (i + 1) * LANE]
             held = tiles[tile]
@@ -324,38 +335,91 @@
     )(*blocks, query_tags, key_tags, scales)
 
 
-def finish_kernel(count, spans, out_spans, *refs):
+def product(attended, weights, columns=slice(None)):
+    total = None
+    for piece, weight in zip(attended, weights, strict=True):
+        term = jnp.dot(piece[...], weight[:, columns], preferred_element_type=F32)
+        total = term if total is None else total + term
+    return total
+
+
+def partial_kernel(count, *refs):
+    *refs, out_ref = refs
+    out_ref[...] = product(refs[:count], refs[count:])
+
+
+def partial(attended, weights):
+    pixels, depth = attended[0].shape
+    width = weights[0].shape[1]
+    return pl.pallas_call(
+        functools.partial(partial_kernel, len(weights)),
+        out_shape=jax.ShapeDtypeStruct((pixels, width), F32),
+        in_specs=[VMEM] * (2 * len(weights)),
+        out_specs=VMEM,
+        compiler_params=pltpu.CompilerParams(vmem_limit_bytes=20 << 20),
+        cost_estimate=pl.CostEstimate(
+            flops=2 * pixels * width * depth * len(weights), bytes_accessed=2 * width * (depth + 2 * pixels), transcendentals=0
+        ),
+    )(*attended, *weights)
+
+
+def finish_kernel(count, chunks, spans, box, with_base, with_held, *refs):
     refs = list(refs)
     attended = [refs.pop(0) for _ in range(count)]
     weights = [refs.pop(0) for _ in range(count)]
-    *sources, out_ref = refs
-    total = None
-    for piece, weight in zip(attended, weights, strict=True):
-        term = jnp.dot(piece[...], weight[...], preferred_element_type=F32)
-        total = term if total is None else total + term
-    at = 0
-    for which, row, left, size, into, column in spans:
-        held = sources[which][row, left : left + size, :].astype(F32)
-        out_ref[into, column : column + size, :] = (held + total[at : at + size]).astype(BF16)
-        at += size
-    for which, row, left, size, into, column in out_spans:
-        out_ref[into, column : column + size, :] = sources[which][row, left : left + size, :]
-
-
-def finish(attended, weights, sources, spans, out_spans, shape):
+    base_ref = refs.pop(0) if with_base else None
+    if with_held:
+        refs.pop(0)
+    *sources, out_ref, ready, semaphore = refs
+    left, size = box
+    wide = out_ref.shape[2] // chunks
+    copies = []
+    for chunk in range(chunks):
+        columns = slice(chunk * wide, (chunk + 1) * wide)
+        total = product(attended, weights, columns)
+        if base_ref is not None:
+            total = total + base_ref[:, columns]
+        at = 0
+        for which, row, start, pixels, into, column in spans:
+            held = sources[which][row, start : start + pixels, columns].astype(F32)
+            ready[into, column - left : column - left + pixels, columns] = (
+                held + total[at : at + pixels]
+            ).astype(BF16)
+            at += pixels
+        place = pl.ds(chunk * wide, wide)
+        copy = pltpu.make_async_copy(
+            ready.at[:, :, place], out_ref.at[:, pl.ds(left, size), place], semaphore.at[chunk]
+        )
+        copy.start()
+        copies.append(copy)
+    for copy in copies:
+        copy.wait()
+
+
+def finish(attended, weights, base, held, sources, spans, box, shape):
     count = len(weights)
-    width = shape[-1]
+    row_count, _, width = shape
     pixels = attended[0].shape[0]
-    return pl.pallas_call(
-        functools.partial(finish_kernel, count, spans, out_spans),
+    chunks = 3 if width % (3 * 2 * LANE) == 0 else 1
+    operands = [*attended, *weights, *([] if base is None else [base])]
+    specs = [VMEM] * len(operands)
+    aliases = {}
+    if held is not None:
+        aliases = {len(operands): 0}
+        operands.append(held)
+        specs.append(HELD)
+    return pl.pallas_call(
+        functools.partial(finish_kernel, count, chunks, spans, box, base is not None, held is not None),
         out_shape=jax.ShapeDtypeStruct(shape, BF16),
-        in_specs=[VMEM] * (2 * count + len(sources)),
-        out_specs=VMEM,
+        in_specs=specs + [VMEM] * len(sources),
+        out_specs=HELD,
+        scratch_shapes=[pltpu.VMEM((row_count, box[1], width), BF16), pltpu.SemaphoreType.DMA((chunks,))],
+        input_output_aliases=aliases,
         compiler_params=pltpu.CompilerParams(vmem_limit_bytes=20 << 20),
         cost_estimate=pl.CostEstimate(
             flops=2 * pixels * width * width, bytes_accessed=2 * width * (width + 3 * pixels), transcendentals=0
         ),
-    )(*attended, *weights, *sources)
+    )(*operands, *sources)
 
 
 def send_heads(outs):
@@ -470,7 +534,7 @@
     corner = permute_by(corner, "win", west_north)
     local_0_pieces = gather_pieces(local_0)
     local_1_pieces = gather_pieces(local_1)
-    query_0, key_0, query_1, key_1 = region_tags(mask_zone_labeling[0], count, near)
+    query_0, key_0, query_1, key_1 = region_tags(mask_zone_labeling[0], weights, count, near)
     out_weights = gather_weights(final_projection_matrix)
 
     spans = [(0, row, 0, WS) for row in range(rows)]
@@ -506,14 +570,16 @@
     first[0] = after(first[0], *outs_1)
     spans = [(0, rows + row, half, WS, row, 0) for row in range(rows)]
     spans += [(1, row, 0, WS, rows + row, 0) for row in range(rows)]
-    done = finish(first, out_weights, [blocked, south_0], spans, [], (row_count, WS, width))
+    shape = (row_count, col_count, width)
+    done = finish(first, out_weights, None, None, [blocked, south_0], spans, (0, WS), shape)
+    second[0] = after(second[0], done)
+    base = partial(second[:split], out_weights[:split])
     spans = [(0, rows + row, half + WS, near, row, WS) for row in range(rows)]
     spans += [(1, row, 0, near, rows + row, WS) for row in range(rows)]
     spans += [(2, row, 0, half, row, WS + near) for row in range(rows)]
     spans += [(3, row, 0, half, rows + row, WS + near) for row in range(rows)]
-    kept = [(4, row, 0, WS, row, 0) for row in range(row_count)]
     mixed = finish(
-        second, out_weights, [blocked, south_1, east, corner, done], spans, kept, (row_count, col_count, width)
+        second[split:], out_weights[split:], base, done, [blocked, south_1, east, corner], spans, (WS, WS), shape
     )
     return mixed[None, :, None]
 

time: 105 us -> 103 us (0.981)
  waiting for transfers between devices: 45.4 us -> 39 us
  Pallas kernels: 31.3 us -> 36.2 us
  local copies, waits for them, and re-layouts: 4.1 us -> 2.97 us
    ppermute x27, waiting for transfers between devices: 45.4 us -> 39 us  [permute_by(): return lax.ppermute(value, axis, pairs)]
    pallas_call x1, Pallas kernels: 0.68 us -> 3.04 us  [norm_local(): pl.pallas_call(functools.partial(norm_local_kernel, boxes), out_shape=[ja...]
    pallas_call x1, Pallas kernels: 0.29 us -> 2.25 us  [cut(): pl.pallas_call(functools.partial(cut_kernel, boxes), out_shape=[jax.Shape...]
    pallas_call x4, Pallas kernels: 15.7 us -> 14.1 us  [attend(): pl.pallas_call(functools.partial(attend_kernel, count, parts, ranges, hea...]
    pallas_call x2 -> x3, Pallas kernels: 4.71 us -> 5.85 us  [the longest x2 4.89 us: finish(): pl.pallas_call(functools.partial(finish_kernel, count, chunks, spans, box...]
    unnamed x22 -> x20, local copies, waits for them, and re-layouts: 4.1 us -> 2.97 us
  transfers between devices with their start and end apart: 27 -> 27, of which waited for: 9 -> 9; matrix products, arithmetic and copies ran while one was open for 0% -> 0% of each run, Pallas kernels for 27% -> 30%
where the time goes in v2:
time: 103 us; the launch traced here: 102 us
  waiting for transfers between devices  39 us (38%)
  Pallas kernels  36.2 us (35%)
  starting transfers between devices  23.5 us (23%)
  local copies, waits for them, and re-layouts  2.97 us (3%)
    ppermute x27, waiting for transfers between devices, permute_by(): return lax.ppermute(value, axis, pairs)  39 us
    ppermute x27, starting transfers between devices, permute_by(): return lax.ppermute(value, axis, pairs)  23.5 us
    pallas_call x4, Pallas kernels, attend(): pl.pallas_call(functools.partial(attend_kernel, count, parts, ranges, hea...  14.1 us
    pallas_call x3, Pallas kernels, project(): pl.pallas_call(functools.partial(project_kernel, [len(group) for group in...  9.65 us
    pallas_call x2, Pallas kernels, finish(): pl.pallas_call(functools.partial(finish_kernel, count, chunks, spans, box...  4.89 us
    pallas_call x1, Pallas kernels, norm_local(): pl.pallas_call(functools.partial(norm_local_kernel, boxes), out_shape=[ja...  3.04 us
    unnamed x20, local copies, waits for them, and re-layouts  2.97 us
    pallas_call x1, Pallas kernels, cut(): pl.pallas_call(functools.partial(cut_kernel, boxes), out_shape=[jax.Shape...  2.25 us
  transfers between devices with their start and end apart: 27, of which 9 were waited for; matrix products, arithmetic and copies ran while one was open for 0% of the time, Pallas kernels for 30%

profile of v2, /device:TPU:0, one launch (start us, length us, event | category | flops | bytes accessed | tf_op | source)
XLA Modules:
  0.0 102.1 jit_solution(9454411734489248930)
XLA Ops:
  0.0 3.0 %norm_local.1 = (bf16[128,1536]{1,0:T(8,128)(2,1)}, bf16[64,1536]{1,0:T(8,128)(2,1)}) custom-call(bf16[8,64,1536]{2,1,0:T(8,128)(2,1)} %bitcast.13, f32[1536]{0:T(1024)} %refs_3_.1, f32[1536]{0:T(1024)} %refs_4_.8), custom_call_target="tpu_custom_call" | custom-call | flops 3932160 | bytes 1572864 | tf_op jit(solution)/shard_map/norm_local/pallas_call | solution.py:118
  3.1 0.0 copy-start.5
  3.1 3.0 %collective-permute-start.2 = (bf16[128,1536]{1,0:T(8,128)(2,1)}, bf16[128,1536]{1,0:T(8,128)(2,1)}, u32[]{:S(2)}, u32[]{:S(2)}) collective-permute-start(bf16[128,1536]{1,0:T(8,128)(2,1)} %get-tuple-element.35.refs_0_), channel_id=1, source_target_pairs={{0,2},{1,3},{2,0},{3,1},{4,6},{5,7},{6,4},{7,5},{8,10},{9,11},{10,... | collective-permute-start | bytes 1179656 | tf_op jit(solution)/shard_map/ppermute | solution.py:25
  6.1 0.1 shard_map.81
  6.2 0.1 collective-permute-start.18
  6.3 2.3 %cut.1 = (bf16[4,32,1536]{2,1,0:T(8,128)(2,1)}, bf16[4,16,1536]{2,1,0:T(8,128)(2,1)}, bf16[4,16,1536]{2,1,0:T(8,128)(2,1)}, bf16[4,16,1536]{2,1,0:T(8,128)(2,1)}) custom-call(bf16[8,64,1536]{2,1,0:T(8,128)(2,1)} %bitcast.14), custom_call_target="tpu_custom_call" | custom-call | bytes 1572864 | tf_op jit(solution)/shard_map/cut/pallas_call | solution.py:86
  8.6 2.1 %collective-permute-start = (bf16[4,32,1536]{2,1,0:T(8,128)(2,1)}, bf16[4,32,1536]{2,1,0:T(8,128)(2,1)S(1)}, u32[]{:S(2)}, u32[]{:S(2)}) collective-permute-start(bf16[4,32,1536]{2,1,0:T(8,128)(2,1)} %get-tuple-element.34), channel_id=1, source_target_pairs={{0,4},{4,0},{8,12},{12,8},{1,5},{5,1},{9,13},{13,9},{2,6},{6,2},{1... | collective-permute-start | bytes 1179656 | tf_op jit(solution)/shard_map/ppermute | solution.py:25
  10.7 1.5 %collective-permute-start.5 = (bf16[64,1536]{1,0:T(8,128)(2,1)}, bf16[64,1536]{1,0:T(8,128)(2,1)S(1)}, u32[]{:S(2)}, u32[]{:S(2)}) collective-permute-start(bf16[64,1536]{1,0:T(8,128)(2,1)} %get-tuple-element.36.refs_4_), channel_id=1, source_target_pairs={{0,2},{1,3},{2,0},{3,1},{4,6},{5,7},{6,4},{7,5},{8,10},{9,11},{10,... | collective-permute-start | bytes 589832 | tf_op jit(solution)/shard_map/ppermute | solution.py:25
  12.2 4.2 %collective-permute-done.2.refs_2_ = bf16[128,1536]{1,0:T(8,128)(2,1)} collective-permute-done((bf16[128,1536]{1,0:T(8,128)(2,1)}, bf16[128,1536]{1,0:T(8,128)(2,1)}, u32[]{:S(2)}, u32[]{:S(2)}) %collective-permute-start.2) | collective-permute-done | bytes 393248 | tf_op jit(solution)/shard_map/ppermute | solution.py:25
  16.4 9.6 %collective-permute-done.5.refs_6_ = bf16[64,1536]{1,0:T(8,128)(2,1)S(1)} collective-permute-done((bf16[64,1536]{1,0:T(8,128)(2,1)}, bf16[64,1536]{1,0:T(8,128)(2,1)S(1)}, u32[]{:S(2)}, u32[]{:S(2)}) %collective-permute-start.5) | collective-permute-done | bytes 196640 | tf_op jit(solution)/shard_map/ppermute | solution.py:25
  26.0 0.5 collective-permute-start.6
  26.5 1.8 %collective-permute-start.19 = (bf16[96,1536]{1,0:T(8,128)(2,1)S(1)}, bf16[96,1536]{1,0:T(8,128)(2,1)S(1)}, u32[]{:S(2)}, u32[]{:S(2)}) collective-permute-start(bf16[96,1536]{1,0:T(8,128)(2,1)S(1)} %collective-permute-done.18.own_ref), channel_id=1, source_target_pairs={{0,4},{4,0},{8,12},{12,8},{1,5},{5,1},{9,13},{13,9},{2,6},{6,2},{1... | collective-permute-start | bytes 884744 | tf_op jit(solution)/shard_map/ppermute | solution.py:25
  28.3 0.3 shard_map.73.refs_0_
  28.7 0.8 collective-permute-start.7
  29.5 2.6 %collective-permute-start.8 = (bf16[4,16,1536]{2,1,0:T(8,128)(2,1)}, bf16[4,16,1536]{2,1,0:T(8,128)(2,1)S(1)}, u32[]{:S(2)}, u32[]{:S(2)}) collective-permute-start(bf16[4,16,1536]{2,1,0:T(8,128)(2,1)} %get-tuple-element.41), channel_id=1, source_target_pairs={{0,8},{4,12},{8,0},{12,4},{1,9},{5,13},{9,1},{13,5},{2,10},{6,14},... | collective-permute-start | bytes 589832 | tf_op jit(solution)/shard_map/ppermute | solution.py:25
  32.0 1.1 %collective-permute-start.9 = (bf16[4,16,1536]{2,1,0:T(8,128)(2,1)}, bf16[4,16,1536]{2,1,0:T(8,128)(2,1)S(1)}, u32[]{:S(2)}, u32[]{:S(2)}) collective-permute-start(bf16[4,16,1536]{2,1,0:T(8,128)(2,1)} %get-tuple-element.42), channel_id=1, source_target_pairs={{0,12},{4,8},{8,4},{12,0},{1,13},{5,9},{9,5},{13,1},{2,14},{6,10},... | collective-permute-start | bytes 589832 | tf_op jit(solution)/shard_map/ppermute | solution.py:25
  33.1 1.5 %collective-permute-start.11 = (bf16[128,1536]{1,0:T(8,128)(2,1)S(1)}, bf16[128,1536]{1,0:T(8,128)(2,1)S(1)}, u32[]{:S(2)}, u32[]{:S(2)}) collective-permute-start(bf16[128,1536]{1,0:T(8,128)(2,1)S(1)} %shard_map.73.refs_0_), channel_id=1, source_target_pairs={{0,2},{1,3},{2,0},{3,1},{4,6},{5,7},{6,4},{7,5},{8,10},{9,11},{10,... | collective-permute-start | bytes 1179656 | tf_op jit(solution)/shard_map/ppermute | solution.py:25
  34.6 2.0 %copy-done.2 = bf16[3,1536,384]{2,1,0:T(8,128)(2,1)S(1)} copy-done((bf16[3,1536,384]{2,1,0:T(8,128)(2,1)S(1)}, bf16[3,1536,384]{2,1,0:T(8,128)(2,1)}, u32[]{:S(2)}) %copy-start.2) | copy-done | bytes 3538968
  36.6 0.9 copy-done.8
  37.5 4.2 %shard_map.74 = (bf16[512,1152]{1,0:T(8,128)(2,1)S(1)}, bf16[256,1152]{1,0:T(8,128)(2,1)S(1)}) custom-call(bf16[128,1536]{1,0:T(8,128)(2,1)S(1)} %copy-done.7, bf16[128,1536]{1,0:T(8,128)(2,1)S(1)} %collective-permute-done.1.refs_1_, bf16[128,1536]{1,0:T(8,128)(2,1)} %collective-permute-done.2.refs_2_, bf16[128,1536]{1,0:T(8,128)(2,1)S(1)} %collective-permute-done.3.refs_3_, ...), custom_call_target="tpu_custom_call" | custom-call | flops 2717908992 | bytes 7667712 | tf_op jit(solution)/shard_map/pallas_call | solution.py:239
  41.8 2.2 %collective-permute-done.7.refs_0_.refs_7_ = bf16[4,16,1536]{2,1,0:T(8,128)(2,1)S(1)} collective-permute-done((bf16[4,16,1536]{2,1,0:T(8,128)(2,1)}, bf16[4,16,1536]{2,1,0:T(8,128)(2,1)S(1)}, u32[]{:S(2)}, u32[]{:S(2)}) %collective-permute-start.7) | collective-permute-done | bytes 196640 | tf_op jit(solution)/shard_map/ppermute | solution.py:25
  44.0 0.3 collective-permute-done.8.refs_1_.refs_8_
  44.3 6.1 %collective-permute-done.9.refs_2_.refs_9_ = bf16[4,16,1536]{2,1,0:T(8,128)(2,1)S(1)} collective-permute-done((bf16[4,16,1536]{2,1,0:T(8,128)(2,1)}, bf16[4,16,1536]{2,1,0:T(8,128)(2,1)S(1)}, u32[]{:S(2)}, u32[]{:S(2)}) %collective-permute-start.9) | collective-permute-done | bytes 196640 | tf_op jit(solution)/shard_map/ppermute | solution.py:25
  50.4 0.4 shard_map.75.refs_0_
  50.8 1.6 %collective-permute-start.14 = (bf16[192,1536]{1,0:T(8,128)(2,1)S(1)}, bf16[192,1536]{1,0:T(8,128)(2,1)S(1)}, u32[]{:S(2)}, u32[]{:S(2)}) collective-permute-start(bf16[192,1536]{1,0:T(8,128)(2,1)S(1)} %shard_map.75.refs_0_), channel_id=1, source_target_pairs={{0,2},{1,3},{2,0},{3,1},{4,6},{5,7},{6,4},{7,5},{8,10},{9,11},{10,... | collective-permute-start | bytes 1769480 | tf_op jit(solution)/shard_map/ppermute | solution.py:25
  52.4 0.1 shard_map.82.own_ref
  52.4 1.6 %collective-permute-start.20 = (bf16[192,1536]{1,0:T(8,128)(2,1)S(1)}, bf16[192,1536]{1,0:T(8,128)(2,1)S(1)}, u32[]{:S(2)}, u32[]{:S(2)}) collective-permute-start(bf16[192,1536]{1,0:T(8,128)(2,1)S(1)} %shard_map.82.own_ref), channel_id=1, source_target_pairs={{0,16},{16,0},{1,17},{17,1},{2,18},{18,2},{3,19},{19,3},{4,20},{20... | collective-permute-start | bytes 1769480 | tf_op jit(solution)/shard_map/ppermute | solution.py:25
  54.0 0.5 collective-permute-start.12
  54.5 10.8 %collective-permute-done.14.refs_2_ = bf16[192,1536]{1,0:T(8,128)(2,1)S(1)} collective-permute-done((bf16[192,1536]{1,0:T(8,128)(2,1)S(1)}, bf16[192,1536]{1,0:T(8,128)(2,1)S(1)}, u32[]{:S(2)}, u32[]{:S(2)}) %collective-permute-start.14) | collective-permute-done | bytes 589856 | tf_op jit(solution)/shard_map/ppermute | solution.py:25
  65.3 0.4 tags.1
  65.7 0.9 collective-permute-done.20.other_ref
  66.7 0.1 shard_map.83.refs_6_.refs_2_
  66.8 0.6 collective-permute-start.21
  67.4 2.2 %shard_map.76.refs_1_ = bf16[512,1152]{1,0:T(8,128)(2,1)S(1)} custom-call(bf16[128,1536]{1,0:T(8,128)(2,1)S(1)} %shard_map.73.refs_0_, bf16[128,1536]{1,0:T(8,128)(2,1)S(1)} %collective-permute-done.10.refs_1_, bf16[128,1536]{1,0:T(8,128)(2,1)S(1)} %collective-permute-done.11.refs_2_, bf16[128,1536]{1,0:T(8,128)(2,1)S(1)} %collective-permute-done.12.refs_3_, ...), custom_call_target="tpu_custom_call" | custom-call | flops 1811939328 | bytes 6291456 | tf_op jit(solution)/shard_map/pallas_call | solution.py:239
  69.6 3.5 %shard_map.77 = (bf16[1,256,384]{2,1,0:T(8,128)(2,1)S(1)}, bf16[1,256,384]{2,1,0:T(8,128)(2,1)S(1)}) custom-call(bf16[512,1152]{1,0:T(8,128)(2,1)S(1)} %get-tuple-element.48.refs_0_, bf16[512,1152]{1,0:T(8,128)(2,1)S(1)} %shard_map.76.refs_1_, bf16[1024,128]{1,0:T(8,128)(2,1)S(1)} %get-tuple-element.44.refs_2_, ...), custom_call_target="tpu_custom_call" | custom-call | flops 2147483648 | bytes 2359296 | tf_op jit(solution)/shard_map/pallas_call | solution.py:322
  73.1 3.5 %shard_map.78 = (bf16[1,256,384]{2,1,0:T(8,128)(2,1)S(1)}, bf16[1,256,384]{2,1,0:T(8,128)(2,1)S(1)}) custom-call(bf16[512,1152]{1,0:T(8,128)(2,1)S(1)} %get-tuple-element.48.refs_0_, bf16[512,1152]{1,0:T(8,128)(2,1)S(1)} %shard_map.76.refs_1_, bf16[1024,128]{1,0:T(8,128)(2,1)S(1)} %get-tuple-element.44.refs_2_, ...), custom_call_target="tpu_custom_call" | custom-call | flops 2147483648 | bytes 2359296 | tf_op jit(solution)/shard_map/pallas_call | solution.py:322
  76.6 0.5 collective-permute-start.22
  77.2 1.5 %collective-permute-start.23 = (bf16[1,256,384]{2,1,0:T(8,128)(2,1)S(1)}, bf16[1,256,384]{2,1,0:T(8,128)(2,1)S(1)}, u32[]{:S(2)}, u32[]{:S(2)}) collective-permute-start(bf16[1,256,384]{2,1,0:T(8,128)(2,1)S(1)} %get-tuple-element.46), channel_id=1, source_target_pairs={{0,2},{1,3},{2,0},{3,1},{4,6},{5,7},{6,4},{7,5},{8,10},{9,11},{10,... | collective-permute-start | bytes 589832 | tf_op jit(solution)/shard_map/ppermute | solution.py:25
  78.7 3.2 %shard_map.79.refs_1_ = bf16[768,1152]{1,0:T(8,128)(2,1)S(1)} custom-call(bf16[192,1536]{1,0:T(8,128)(2,1)S(1)} %shard_map.75.refs_0_, bf16[192,1536]{1,0:T(8,128)(2,1)S(1)} %collective-permute-done.13.refs_1_, bf16[192,1536]{1,0:T(8,128)(2,1)S(1)} %collective-permute-done.14.refs_2_, bf16[192,1536]{1,0:T(8,128)(2,1)S(1)} %collective-permute-done.15.refs_3_, ...), custom_call_target="tpu_custom_call" | custom-call | flops 2717908992 | bytes 7667712 | tf_op jit(solution)/shard_map/pallas_call | solution.py:239
  81.9 3.5 %shard_map.80 = (bf16[1,256,384]{2,1,0:T(8,128)(2,1)S(1)}, bf16[1,256,384]{2,1,0:T(8,128)(2,1)S(1)}) custom-call(bf16[256,1152]{1,0:T(8,128)(2,1)S(1)} %get-tuple-element.56.refs_0_, bf16[768,1152]{1,0:T(8,128)(2,1)S(1)} %shard_map.79.refs_1_, bf16[1024,128]{1,0:T(8,128)(2,1)S(1)} %get-tuple-element.52.refs_2_, ...), custom_call_target="tpu_custom_call" | custom-call | flops 2147483648 | bytes 2359296 | tf_op jit(solution)/shard_map/pallas_call | solution.py:322
  85.5 3.5 %shard_map.84 = (bf16[1,256,384]{2,1,0:T(8,128)(2,1)S(1)}, bf16[1,256,384]{2,1,0:T(8,128)(2,1)S(1)}) custom-call(bf16[256,1152]{1,0:T(8,128)(2,1)S(1)} %get-tuple-element.56.refs_0_, bf16[768,1152]{1,0:T(8,128)(2,1)S(1)} %shard_map.79.refs_1_, bf16[1024,128]{1,0:T(8,128)(2,1)S(1)} %get-tuple-element.52.refs_2_, ...), custom_call_target="tpu_custom_call" | custom-call | flops 2147483648 | bytes 2359296 | tf_op jit(solution)/shard_map/pallas_call | solution.py:322
  89.0 0.7 collective-permute-start.26
  89.7 1.5 %collective-permute-start.16 = (bf16[1,256,384]{2,1,0:T(8,128)(2,1)S(1)}, bf16[1,256,384]{2,1,0:T(8,128)(2,1)S(1)}, u32[]{:S(2)}, u32[]{:S(2)}) collective-permute-start(bf16[1,256,384]{2,1,0:T(8,128)(2,1)S(1)} %get-tuple-element.54), channel_id=1, source_target_pairs={{0,2},{1,3},{2,0},{3,1},{4,6},{5,7},{6,4},{7,5},{8,10},{9,11},{10,... | collective-permute-start | bytes 589832 | tf_op jit(solution)/shard_map/ppermute | solution.py:25
  91.2 2.8 %shard_map.85.refs_5_ = bf16[8,64,1536]{2,1,0:T(8,128)(2,1)} custom-call(bf16[256,384]{1,0:T(8,128)(2,1)S(1)} %bitcast.19, bf16[256,384]{1,0:T(8,128)(2,1)S(1)} %bitcast.20, bf16[256,384]{1,0:T(8,128)(2,1)S(1)} %bitcast.21, bf16[256,384]{1,0:T(8,128)(2,1)S(1)} %bitcast.22, bf16[384,1536]{1,0:T(8,128)(2,1)S(1)} %copy-done.1, ...), custom_call_target="tpu_custom_call" | custom-call | flops 1207959552 | bytes 7077888 | tf_op jit(solution)/shard_map/pallas_call | solution.py:411
  94.1 1.0 shard_map.86.refs_4_
  95.1 2.4 %collective-permute-done.16 = bf16[1,256,384]{2,1,0:T(8,128)(2,1)S(1)} collective-permute-done((bf16[1,256,384]{2,1,0:T(8,128)(2,1)S(1)}, bf16[1,256,384]{2,1,0:T(8,128)(2,1)S(1)}, u32[]{:S(2)}, u32[]{:S(2)}) %collective-permute-start.16) | collective-permute-done | bytes 196640 | tf_op jit(solution)/shard_map/ppermute | solution.py:25
  97.5 2.4 %collective-permute-done.17 = bf16[1,256,384]{2,1,0:T(8,128)(2,1)S(1)} collective-permute-done((bf16[1,256,384]{2,1,0:T(8,128)(2,1)S(1)}, bf16[1,256,384]{2,1,0:T(8,128)(2,1)S(1)}, u32[]{:S(2)}, u32[]{:S(2)}) %collective-permute-start.17) | collective-permute-done | bytes 196640 | tf_op jit(solution)/shard_map/ppermute | solution.py:25
  99.9 2.0 %shard_map.87 = bf16[8,64,1536]{2,1,0:T(8,128)(2,1)} custom-call(bf16[256,384]{1,0:T(8,128)(2,1)S(1)} %bitcast.23, bf16[256,384]{1,0:T(8,128)(2,1)S(1)} %bitcast.24, bf16[384,1536]{1,0:T(8,128)(2,1)S(1)} %shard_map.83.refs_6_.refs_2_, bf16[384,1536]{1,0:T(8,128)(2,1)S(1)} %collective-permute-done.21.refs_7_.refs_3_, ...), custom_call_target="tpu_custom_call", output_to_operand_aliasing={{}: (5, {})} | custom-call | flops 1207959552 | bytes 7077888 | tf_op jit(solution)/shard_map/pallas_call | solution.py:411
  (44 shorter events, 0.1 us)
Async XLA Ops:
  0.0 6.1 %copy-start.1 = (bf16[384,1536]{1,0:T(8,128)(2,1)S(1)}, bf16[384,1536]{1,0:T(8,128)(2,1)}, u32[]{:S(2)}) copy-start(bf16[384,1536]{1,0:T(8,128)(2,1)} %refs_2_.3) | copy-start | bytes 3538948
  3.0 9.1 %copy-start.7 = (bf16[128,1536]{1,0:T(8,128)(2,1)S(1)}, bf16[128,1536]{1,0:T(8,128)(2,1)}, u32[]{:S(2)}) copy-start(bf16[128,1536]{1,0:T(8,128)(2,1)} %get-tuple-element.35.refs_0_) | copy-start | bytes 1179652
  3.1 25.3 %copy-start.4 = (f32[1536]{0:T(1024)S(1)}, f32[1536]{0:T(1024)}, u32[]{:S(2)}) copy-start(f32[1536]{0:T(1024)} %refs_3_.1) | copy-start | bytes 18436
  3.1 25.3 %copy-start.5 = (f32[1536]{0:T(1024)S(1)}, f32[1536]{0:T(1024)}, u32[]{:S(2)}) copy-start(f32[1536]{0:T(1024)} %refs_4_.8) | copy-start | bytes 18436
  3.1 13.3 %collective-permute-start.2 = (bf16[128,1536]{1,0:T(8,128)(2,1)}, bf16[128,1536]{1,0:T(8,128)(2,1)}, u32[]{:S(2)}, u32[]{:S(2)}) collective-permute-start(bf16[128,1536]{1,0:T(8,128)(2,1)} %get-tuple-element.35.refs_0_), channel_id=1, source_target_pairs={{0,2},{1,3},{2,0},{3,1},{4,6},{5,7},{6,4},{7,5},{8,10},{9,11},{10,... | collective-permute-start | bytes 1179656 | tf_op jit(solution)/shard_map/ppermute | solution.py:25
  6.2 19.8 %collective-permute-start.18 = (bf16[96,1536]{1,0:T(8,128)(2,1)S(1)}, bf16[96,1536]{1,0:T(8,128)(2,1)S(1)}, u32[]{:S(2)}, u32[]{:S(2)}) collective-permute-start(bf16[96,1536]{1,0:T(8,128)(2,1)S(1)} %shard_map.81), channel_id=1, source_target_pairs={{0,2},{1,3},{2,0},{3,1},{4,6},{5,7},{6,4},{7,5},{8,10},{9,11},{10,... | collective-permute-start | bytes 884744 | tf_op jit(solution)/shard_map/ppermute | solution.py:25
  8.6 17.9 %collective-permute-start = (bf16[4,32,1536]{2,1,0:T(8,128)(2,1)}, bf16[4,32,1536]{2,1,0:T(8,128)(2,1)S(1)}, u32[]{:S(2)}, u32[]{:S(2)}) collective-permute-start(bf16[4,32,1536]{2,1,0:T(8,128)(2,1)} %get-tuple-element.34), channel_id=1, source_target_pairs={{0,4},{4,0},{8,12},{12,8},{1,5},{5,1},{9,13},{13,9},{2,6},{6,2},{1... | collective-permute-start | bytes 1179656 | tf_op jit(solution)/shard_map/ppermute | solution.py:25
  10.7 15.3 %collective-permute-start.5 = (bf16[64,1536]{1,0:T(8,128)(2,1)}, bf16[64,1536]{1,0:T(8,128)(2,1)S(1)}, u32[]{:S(2)}, u32[]{:S(2)}) collective-permute-start(bf16[64,1536]{1,0:T(8,128)(2,1)} %get-tuple-element.36.refs_4_), channel_id=1, source_target_pairs={{0,2},{1,3},{2,0},{3,1},{4,6},{5,7},{6,4},{7,5},{8,10},{9,11},{10,... | collective-permute-start | bytes 589832 | tf_op jit(solution)/shard_map/ppermute | solution.py:25
  12.2 19.9 %collective-permute-start.1 = (bf16[128,1536]{1,0:T(8,128)(2,1)S(1)}, bf16[128,1536]{1,0:T(8,128)(2,1)S(1)}, u32[]{:S(2)}, u32[]{:S(2)}) collective-permute-start(bf16[128,1536]{1,0:T(8,128)(2,1)S(1)} %copy-done.7), channel_id=1, source_target_pairs={{0,1},{1,0},{2,3},{3,2},{4,5},{5,4},{6,7},{7,6},{8,9},{9,8},{10,11... | collective-permute-start | bytes 1179656 | tf_op jit(solution)/shard_map/ppermute | solution.py:25
  16.4 16.7 %collective-permute-start.3 = (bf16[128,1536]{1,0:T(8,128)(2,1)}, bf16[128,1536]{1,0:T(8,128)(2,1)S(1)}, u32[]{:S(2)}, u32[]{:S(2)}) collective-permute-start(bf16[128,1536]{1,0:T(8,128)(2,1)} %collective-permute-done.2.refs_2_), channel_id=1, source_target_pairs={{0,1},{1,0},{2,3},{3,2},{4,5},{5,4},{6,7},{7,6},{8,9},{9,8},{10,11... | collective-permute-start | bytes 1179656 | tf_op jit(solution)/shard_map/ppermute | solution.py:25
  26.0 2.7 %collective-permute-start.4 = (bf16[64,1536]{1,0:T(8,128)(2,1)}, bf16[64,1536]{1,0:T(8,128)(2,1)S(1)}, u32[]{:S(2)}, u32[]{:S(2)}) collective-permute-start(bf16[64,1536]{1,0:T(8,128)(2,1)} %get-tuple-element.36.refs_4_), channel_id=1, source_target_pairs={{0,1},{1,0},{2,3},{3,2},{4,5},{5,4},{6,7},{7,6},{8,9},{9,8},{10,11... | collective-permute-start | bytes 589832 | tf_op jit(solution)/shard_map/ppermute | solution.py:25
  26.0 3.5 %collective-permute-start.6 = (bf16[64,1536]{1,0:T(8,128)(2,1)S(1)}, bf16[64,1536]{1,0:T(8,128)(2,1)S(1)}, u32[]{:S(2)}, u32[]{:S(2)}) collective-permute-start(bf16[64,1536]{1,0:T(8,128)(2,1)S(1)} %collective-permute-done.5.refs_6_), channel_id=1, source_target_pairs={{0,1},{1,0},{2,3},{3,2},{4,5},{5,4},{6,7},{7,6},{8,9},{9,8},{10,11... | collective-permute-start | bytes 589832 | tf_op jit(solution)/shard_map/ppermute | solution.py:25
  26.5 25.9 %collective-permute-start.19 = (bf16[96,1536]{1,0:T(8,128)(2,1)S(1)}, bf16[96,1536]{1,0:T(8,128)(2,1)S(1)}, u32[]{:S(2)}, u32[]{:S(2)}) collective-permute-start(bf16[96,1536]{1,0:T(8,128)(2,1)S(1)} %collective-permute-done.18.own_ref), channel_id=1, source_target_pairs={{0,4},{4,0},{8,12},{12,8},{1,5},{5,1},{9,13},{13,9},{2,6},{6,2},{1... | collective-permute-start | bytes 884744 | tf_op jit(solution)/shard_map/ppermute | solution.py:25
  28.7 15.3 %collective-permute-start.7 = (bf16[4,16,1536]{2,1,0:T(8,128)(2,1)}, bf16[4,16,1536]{2,1,0:T(8,128)(2,1)S(1)}, u32[]{:S(2)}, u32[]{:S(2)}) collective-permute-start(bf16[4,16,1536]{2,1,0:T(8,128)(2,1)} %get-tuple-element.38), channel_id=1, source_target_pairs={{0,4},{4,0},{8,12},{12,8},{1,5},{5,1},{9,13},{13,9},{2,6},{6,2},{1... | collective-permute-start | bytes 589832 | tf_op jit(solution)/shard_map/ppermute | solution.py:25
  29.5 14.8 %collective-permute-start.8 = (bf16[4,16,1536]{2,1,0:T(8,128)(2,1)}, bf16[4,16,1536]{2,1,0:T(8,128)(2,1)S(1)}, u32[]{:S(2)}, u32[]{:S(2)}) collective-permute-start(bf16[4,16,1536]{2,1,0:T(8,128)(2,1)} %get-tuple-element.41), channel_id=1, source_target_pairs={{0,8},{4,12},{8,0},{12,4},{1,9},{5,13},{9,1},{13,5},{2,10},{6,14},... | collective-permute-start | bytes 589832 | tf_op jit(solution)/shard_map/ppermute | solution.py:25
  32.0 18.3 %collective-permute-start.9 = (bf16[4,16,1536]{2,1,0:T(8,128)(2,1)}, bf16[4,16,1536]{2,1,0:T(8,128)(2,1)S(1)}, u32[]{:S(2)}, u32[]{:S(2)}) collective-permute-start(bf16[4,16,1536]{2,1,0:T(8,128)(2,1)} %get-tuple-element.42), channel_id=1, source_target_pairs={{0,12},{4,8},{8,4},{12,0},{1,13},{5,9},{9,5},{13,1},{2,14},{6,10},... | collective-permute-start | bytes 589832 | tf_op jit(solution)/shard_map/ppermute | solution.py:25
  33.1 20.9 %collective-permute-start.11 = (bf16[128,1536]{1,0:T(8,128)(2,1)S(1)}, bf16[128,1536]{1,0:T(8,128)(2,1)S(1)}, u32[]{:S(2)}, u32[]{:S(2)}) collective-permute-start(bf16[128,1536]{1,0:T(8,128)(2,1)S(1)} %shard_map.73.refs_0_), channel_id=1, source_target_pairs={{0,2},{1,3},{2,0},{3,1},{4,6},{5,7},{6,4},{7,5},{8,10},{9,11},{10,... | collective-permute-start | bytes 1179656 | tf_op jit(solution)/shard_map/ppermute | solution.py:25
  34.6 2.0 %copy-start.2 = (bf16[3,1536,384]{2,1,0:T(8,128)(2,1)S(1)}, bf16[3,1536,384]{2,1,0:T(8,128)(2,1)}, u32[]{:S(2)}) copy-start(bf16[3,1536,384]{2,1,0:T(8,128)(2,1)} %refs_4_.12) | copy-start | bytes 10616836
  36.6 0.9 copy-start.8
  41.8 23.6 %copy-start.6 = (s32[1,32,64]{2,1,0:T(8,128)S(1)}, s32[1,32,64]{2,1,0:T(8,128)}, u32[]{:S(2)}) copy-start(s32[1,32,64]{2,1,0:T(8,128)} %param.8) | copy-start | bytes 24580
  50.8 14.5 %collective-permute-start.14 = (bf16[192,1536]{1,0:T(8,128)(2,1)S(1)}, bf16[192,1536]{1,0:T(8,128)(2,1)S(1)}, u32[]{:S(2)}, u32[]{:S(2)}) collective-permute-start(bf16[192,1536]{1,0:T(8,128)(2,1)S(1)} %shard_map.75.refs_0_), channel_id=1, source_target_pairs={{0,2},{1,3},{2,0},{3,1},{4,6},{5,7},{6,4},{7,5},{8,10},{9,11},{10,... | collective-permute-start | bytes 1769480 | tf_op jit(solution)/shard_map/ppermute | solution.py:25
  52.4 14.2 %collective-permute-start.20 = (bf16[192,1536]{1,0:T(8,128)(2,1)S(1)}, bf16[192,1536]{1,0:T(8,128)(2,1)S(1)}, u32[]{:S(2)}, u32[]{:S(2)}) collective-permute-start(bf16[192,1536]{1,0:T(8,128)(2,1)S(1)} %shard_map.82.own_ref), channel_id=1, source_target_pairs={{0,16},{16,0},{1,17},{17,1},{2,18},{18,2},{3,19},{19,3},{4,20},{20... | collective-permute-start | bytes 1769480 | tf_op jit(solution)/shard_map/ppermute | solution.py:25
  54.0 12.8 %collective-permute-start.10 = (bf16[128,1536]{1,0:T(8,128)(2,1)S(1)}, bf16[128,1536]{1,0:T(8,128)(2,1)S(1)}, u32[]{:S(2)}, u32[]{:S(2)}) collective-permute-start(bf16[128,1536]{1,0:T(8,128)(2,1)S(1)} %shard_map.73.refs_0_), channel_id=1, source_target_pairs={{0,1},{1,0},{2,3},{3,2},{4,5},{5,4},{6,7},{7,6},{8,9},{9,8},{10,11... | collective-permute-start | bytes 1179656 | tf_op jit(solution)/shard_map/ppermute | solution.py:25
  54.0 13.3 %collective-permute-start.12 = (bf16[128,1536]{1,0:T(8,128)(2,1)S(1)}, bf16[128,1536]{1,0:T(8,128)(2,1)S(1)}, u32[]{:S(2)}, u32[]{:S(2)}) collective-permute-start(bf16[128,1536]{1,0:T(8,128)(2,1)S(1)} %collective-permute-done.11.refs_2_), channel_id=1, source_target_pairs={{0,1},{1,0},{2,3},{3,2},{4,5},{5,4},{6,7},{7,6},{8,9},{9,8},{10,11... | collective-permute-start | bytes 1179656 | tf_op jit(solution)/shard_map/ppermute | solution.py:25
  54.5 22.6 %collective-permute-start.13 = (bf16[192,1536]{1,0:T(8,128)(2,1)S(1)}, bf16[192,1536]{1,0:T(8,128)(2,1)S(1)}, u32[]{:S(2)}, u32[]{:S(2)}) collective-permute-start(bf16[192,1536]{1,0:T(8,128)(2,1)S(1)} %shard_map.75.refs_0_), channel_id=1, source_target_pairs={{0,1},{1,0},{2,3},{3,2},{4,5},{5,4},{6,7},{7,6},{8,9},{9,8},{10,11... | collective-permute-start | bytes 1769480 | tf_op jit(solution)/shard_map/ppermute | solution.py:25
  65.3 13.3 %collective-permute-start.15 = (bf16[192,1536]{1,0:T(8,128)(2,1)S(1)}, bf16[192,1536]{1,0:T(8,128)(2,1)S(1)}, u32[]{:S(2)}, u32[]{:S(2)}) collective-permute-start(bf16[192,1536]{1,0:T(8,128)(2,1)S(1)} %collective-permute-done.14.refs_2_), channel_id=1, source_target_pairs={{0,1},{1,0},{2,3},{3,2},{4,5},{5,4},{6,7},{7,6},{8,9},{9,8},{10,11... | collective-permute-start | bytes 1769480 | tf_op jit(solution)/shard_map/ppermute | solution.py:25
  65.3 2.0 %copy-start.3 = (bf16[3,1536,384]{2,1,0:T(8,128)(2,1)S(1)}, bf16[3,1536,384]{2,1,0:T(8,128)(2,1)}, u32[]{:S(2)}) copy-start(bf16[3,1536,384]{2,1,0:T(8,128)(2,1)} %refs_4_.12) | copy-start | bytes 10616836
  66.7 22.3 %collective-permute-start.25 = (bf16[384,1536]{1,0:T(8,128)(2,1)S(1)}, bf16[384,1536]{1,0:T(8,128)(2,1)S(1)}, u32[]{:S(2)}, u32[]{:S(2)}) collective-permute-start(bf16[384,1536]{1,0:T(8,128)(2,1)S(1)} %copy-done.1), channel_id=1, source_target_pairs={{0,1},{1,0},{2,3},{3,2},{4,5},{5,4},{6,7},{7,6},{8,9},{9,8},{10,11... | collective-permute-start | bytes 3538952 | tf_op jit(solution)/shard_map/ppermute | solution.py:25
  66.8 2.8 %copy-start.9 = (f32[4]{0:T(128)S(1)}, f32[4]{0:T(128)}, u32[]{:S(2)}) copy-start(f32[4]{0:T(128)} %refs_4_.14) | copy-start | bytes 52
  66.8 24.4 %collective-permute-start.21 = (bf16[384,1536]{1,0:T(8,128)(2,1)S(1)}, bf16[384,1536]{1,0:T(8,128)(2,1)S(1)}, u32[]{:S(2)}, u32[]{:S(2)}) collective-permute-start(bf16[384,1536]{1,0:T(8,128)(2,1)S(1)} %shard_map.83.refs_6_.refs_2_), channel_id=1, source_target_pairs={{0,1},{1,0},{2,3},{3,2},{4,5},{5,4},{6,7},{7,6},{8,9},{9,8},{10,11... | collective-permute-start | bytes 3538952 | tf_op jit(solution)/shard_map/ppermute | solution.py:25
  76.6 13.1 %collective-permute-start.22 = (bf16[1,256,384]{2,1,0:T(8,128)(2,1)S(1)}, bf16[1,256,384]{2,1,0:T(8,128)(2,1)S(1)}, u32[]{:S(2)}, u32[]{:S(2)}) collective-permute-start(bf16[1,256,384]{2,1,0:T(8,128)(2,1)S(1)} %get-tuple-element.50), channel_id=1, source_target_pairs={{0,1},{1,0},{2,3},{3,2},{4,5},{5,4},{6,7},{7,6},{8,9},{9,8},{10,11... | collective-permute-start | bytes 589832 | tf_op jit(solution)/shard_map/ppermute | solution.py:25
  77.2 14.0 %collective-permute-start.23 = (bf16[1,256,384]{2,1,0:T(8,128)(2,1)S(1)}, bf16[1,256,384]{2,1,0:T(8,128)(2,1)S(1)}, u32[]{:S(2)}, u32[]{:S(2)}) collective-permute-start(bf16[1,256,384]{2,1,0:T(8,128)(2,1)S(1)} %get-tuple-element.46), channel_id=1, source_target_pairs={{0,2},{1,3},{2,0},{3,1},{4,6},{5,7},{6,4},{7,5},{8,10},{9,11},{10,... | collective-permute-start | bytes 589832 | tf_op jit(solution)/shard_map/ppermute | solution.py:25
  78.7 12.6 %collective-permute-start.24 = (bf16[1,256,384]{2,1,0:T(8,128)(2,1)S(1)}, bf16[1,256,384]{2,1,0:T(8,128)(2,1)S(1)}, u32[]{:S(2)}, u32[]{:S(2)}) collective-permute-start(bf16[1,256,384]{2,1,0:T(8,128)(2,1)S(1)} %get-tuple-element.47), channel_id=1, source_target_pairs={{0,3},{1,2},{2,1},{3,0},{4,7},{5,6},{6,5},{7,4},{8,11},{9,10},{10,... | collective-permute-start | bytes 589832 | tf_op jit(solution)/shard_map/ppermute | solution.py:25
  85.4 5.8 %copy-start = (bf16[1,8,1,64,1536]{4,3,2,1,0:T(8,128)(2,1)S(1)}, bf16[1,8,1,64,1536]{4,3,2,1,0:T(8,128)(2,1)}, u32[]{:S(2)}) copy-start(bf16[1,8,1,64,1536]{4,3,2,1,0:T(8,128)(2,1)} %param.7) | copy-start | bytes 4718596
  89.0 5.1 %collective-permute-start.26 = (bf16[1,256,384]{2,1,0:T(8,128)(2,1)S(1)}, bf16[1,256,384]{2,1,0:T(8,128)(2,1)S(1)}, u32[]{:S(2)}, u32[]{:S(2)}) collective-permute-start(bf16[1,256,384]{2,1,0:T(8,128)(2,1)S(1)} %get-tuple-element.58), channel_id=1, source_target_pairs={{0,1},{1,0},{2,3},{3,2},{4,5},{5,4},{6,7},{7,6},{8,9},{9,8},{10,11... | collective-permute-start | bytes 589832 | tf_op jit(solution)/shard_map/ppermute | solution.py:25
  89.7 7.8 %collective-permute-start.16 = (bf16[1,256,384]{2,1,0:T(8,128)(2,1)S(1)}, bf16[1,256,384]{2,1,0:T(8,128)(2,1)S(1)}, u32[]{:S(2)}, u32[]{:S(2)}) collective-permute-start(bf16[1,256,384]{2,1,0:T(8,128)(2,1)S(1)} %get-tuple-element.54), channel_id=1, source_target_pairs={{0,2},{1,3},{2,0},{3,1},{4,6},{5,7},{6,4},{7,5},{8,10},{9,11},{10,... | collective-permute-start | bytes 589832 | tf_op jit(solution)/shard_map/ppermute | solution.py:25
  91.2 8.7 %collective-permute-start.17 = (bf16[1,256,384]{2,1,0:T(8,128)(2,1)S(1)}, bf16[1,256,384]{2,1,0:T(8,128)(2,1)S(1)}, u32[]{:S(2)}, u32[]{:S(2)}) collective-permute-start(bf16[1,256,384]{2,1,0:T(8,128)(2,1)S(1)} %get-tuple-element.55), channel_id=1, source_target_pairs={{0,3},{1,2},{2,1},{3,0},{4,7},{5,6},{6,5},{7,4},{8,11},{9,10},{10,... | collective-permute-start | bytes 589832 | tf_op jit(solution)/shard_map/ppermute | solution.py:25

commit v3 on v2

--- a/solution.py
+++ b/solution.py
@@ -14,7 +14,6 @@
 REGIONS = 32
 LANE = 128
 FAR = -1e30
-ALL_VMEM = 67_043_328
 F32 = jnp.float32
 BF16 = jnp.bfloat16
 
@@ -67,88 +66,47 @@
 HELD = pl.BlockSpec(memory_space=pltpu.HBM)
 
 
-def cut_kernel(boxes, pixel_ref, *refs):
-    outs, semaphore = refs[:-1], refs[-1]
-    copies = [
-        pltpu.make_async_copy(
-            pixel_ref.at[pl.ds(row, rows), pl.ds(left, size), :], out_ref, semaphore.at[index]
-        )
-        for index, ((row, rows, left, size), out_ref) in enumerate(zip(boxes, outs, strict=True))
-    ]
-    for copy in copies:
-        copy.start()
-    for copy in copies:
-        copy.wait()
-
-
-def cut(pixels, boxes):
+def cut_kernel(boxes, pixel_ref, *outs):
+    for (row, left, size), out_ref in zip(boxes, outs, strict=True):
+        out_ref[...] = pixel_ref[row : row + out_ref.shape[0], left : left + size, :]
+
+
+def cut(pixels, rows, boxes):
     width = pixels.shape[2]
     return pl.pallas_call(
         functools.partial(cut_kernel, boxes),
-        out_shape=[jax.ShapeDtypeStruct((rows, size, width), BF16) for _, rows, _, size in boxes],
-        in_specs=[HELD],
+        out_shape=[jax.ShapeDtypeStruct((rows, size, width), BF16) for _, _, size in boxes],
+        in_specs=[VMEM],
         out_specs=[VMEM] * len(boxes),
-        scratch_shapes=[pltpu.SemaphoreType.DMA((len(boxes),))],
-        compiler_params=pltpu.CompilerParams(vmem_limit_bytes=ALL_VMEM - (22 << 20) // 10),
+        compiler_params=pltpu.CompilerParams(vmem_limit_bytes=8 << 20),
         cost_estimate=pl.CostEstimate(flops=0, bytes_accessed=2 * pixels.size, transcendentals=0),
         name="cut",
     )(pixels)
 
 
-def norm_local_kernel(boxes, pixel_ref, gain_ref, bias_ref, *refs):
-    outs, helds, semaphore = refs[: len(boxes)], refs[len(boxes) : -1], refs[-1]
-    copies = [
-        pltpu.make_async_copy(
-            pixel_ref.at[pl.ds(row, rows), pl.ds(left, size), :], held, semaphore.at[index]
-        )
-        for index, ((row, rows, left, size), held) in enumerate(zip(boxes, helds, strict=True))
-    ]
-    for copy in copies:
-        copy.start()
+def norm_kernel(groups, *refs):
+    refs, outs = refs[: -len(groups)], refs[-len(groups) :]
+    *sources, gain_ref, bias_ref = refs
     gain, bias = gain_ref[...][None], bias_ref[...][None]
-    for copy, held, out_ref in zip(copies, helds, outs, strict=True):
-        copy.wait()
-        size = held.shape[1]
-        for row in range(held.shape[0]):
-            out_ref[row * size : (row + 1) * size, :] = normalized(held[row], gain, bias)
-
-
-def norm_local(pixels, gain, bias, boxes):
-    width = pixels.shape[2]
-    return pl.pallas_call(
-        functools.partial(norm_local_kernel, boxes),
-        out_shape=[jax.ShapeDtypeStruct((rows * size, width), BF16) for _, rows, _, size in boxes],
-        in_specs=[HELD, VMEM, VMEM],
-        out_specs=[VMEM] * len(boxes),
-        scratch_shapes=[pltpu.VMEM((rows, size, width), BF16) for _, rows, _, size in boxes]
-        + [pltpu.SemaphoreType.DMA((len(boxes),))],
-        compiler_params=pltpu.CompilerParams(vmem_limit_bytes=ALL_VMEM - (12 << 20) // 10),
-        cost_estimate=pl.CostEstimate(flops=5 * pixels.size, bytes_accessed=2 * pixels.size, transcendentals=0),
-        name="norm_local",
-    )(pixels, gain, bias)
-
-
-def norm_kernel(spans, *refs):
-    *sources, gain_ref, bias_ref, out_ref = refs
-    into = 0
-    gain, bias = gain_ref[...][None], bias_ref[...][None]
-    for which, row, left, size in spans:
-        held = sources[which][row, left : left + size, :]
-        out_ref[into : into + size, :] = normalized(held, gain, bias)
-        into += size
-
-
-def norm(sources, gain, bias, spans):
+    for spans, out_ref in zip(groups, outs, strict=True):
+        into = 0
+        for which, row, left, size in spans:
+            held = sources[which][row, left : left + size, :]
+            out_ref[into : into + size, :] = normalized(held, gain, bias)
+            into += size
+
+
+def norm(sources, gain, bias, groups):
     width = sources[0].shape[-1]
-    total = sum(span[-1] for span in spans)
-    return pl.pallas_call(
-        functools.partial(norm_kernel, spans),
-        out_shape=jax.ShapeDtypeStruct((total, width), BF16),
+    totals = [sum(span[-1] for span in spans) for spans in groups]
+    return pl.pallas_call(
+        functools.partial(norm_kernel, groups),
+        out_shape=[jax.ShapeDtypeStruct((total, width), BF16) for total in totals],
         in_specs=[VMEM] * (len(sources) + 2),
-        out_specs=VMEM,
+        out_specs=[VMEM] * len(groups),
         compiler_params=pltpu.CompilerParams(vmem_limit_bytes=8 << 20),
         cost_estimate=pl.CostEstimate(
-            flops=10 * total * width, bytes_accessed=4 * total * width, transcendentals=0
+            flops=10 * sum(totals) * width, bytes_accessed=4 * sum(totals) * width, transcendentals=0
         ),
     )(*sources, gain, bias)
 
@@ -363,22 +321,43 @@
     )(*attended, *weights)
 
 
-def finish_kernel(count, chunks, spans, box, with_base, with_held, *refs):
-    refs = list(refs)
-    attended = [refs.pop(0) for _ in range(count)]
-    weights = [refs.pop(0) for _ in range(count)]
-    base_ref = refs.pop(0) if with_base else None
-    if with_held:
-        refs.pop(0)
-    *sources, out_ref, ready, semaphore = refs
-    left, size = box
-    wide = out_ref.shape[2] // chunks
-    copies = []
+def finish_kernel(count, spans, *refs):
+    attended, weights, sources, out_ref = refs[:count], refs[count : 2 * count], refs[2 * count : -1], refs[-1]
+    total = product(attended, weights)
+    at = 0
+    for which, row, start, pixels, into, column in spans:
+        held = sources[which][row, start : start + pixels, :].astype(F32)
+        out_ref[into, column : column + pixels, :] = (held + total[at : at + pixels]).astype(BF16)
+        at += pixels
+
+
+def finish(attended, weights, sources, spans, shape):
+    count = len(weights)
+    pixels, width = attended[0].shape[0], shape[-1]
+    return pl.pallas_call(
+        functools.partial(finish_kernel, count, spans),
+        out_shape=jax.ShapeDtypeStruct(shape, BF16),
+        in_specs=[VMEM] * (2 * count + len(sources)),
+        out_specs=VMEM,
+        compiler_params=pltpu.CompilerParams(vmem_limit_bytes=20 << 20),
+        cost_estimate=pl.CostEstimate(
+            flops=2 * pixels * width * width, bytes_accessed=2 * width * (width + 3 * pixels), transcendentals=0
+        ),
+    )(*attended, *weights, *sources)
+
+
+def last_kernel(count, chunks, spans, *refs):
+    attended, weights = refs[:count], refs[count : 2 * count]
+    base_ref, done_ref, *sources, out_ref, ready, semaphore = refs[2 * count :]
+    left, size, width = done_ref.shape[1], ready.shape[1], ready.shape[2]
+    wide = width // chunks
+    copies = [
+        pltpu.make_async_copy(done_ref, out_ref.at[:, pl.ds(0, left), :], semaphore.at[chunks])
+    ]
+    copies[0].start()
     for chunk in range(chunks):
         columns = slice(chunk * wide, (chunk + 1) * wide)
-        total = product(attended, weights, columns)
-        if base_ref is not None:
-            total = total + base_ref[:, columns]
+        total = product(attended, weights, columns) + base_ref[:, columns]
         at = 0
         for which, row, start, pixels, into, column in spans:
             held = sources[which][row, start : start + pixels, columns].astype(F32)
@@ -396,30 +375,25 @@
         copy.wait()
 
 
-def finish(attended, weights, base, held, sources, spans, box, shape):
+def finish_last(attended, weights, base, done, sources, spans, shape):
     count = len(weights)
-    row_count, _, width = shape
-    pixels = attended[0].shape[0]
+    row_count, col_count, width = shape
+    pixels, depth = attended[0].shape
     chunks = 3 if width % (3 * 2 * LANE) == 0 else 1
-    operands = [*attended, *weights, *([] if base is None else [base])]
-    specs = [VMEM] * len(operands)
-    aliases = {}
-    if held is not None:
-        aliases = {len(operands): 0}
-        operands.append(held)
-        specs.append(HELD)
-    return pl.pallas_call(
-        functools.partial(finish_kernel, count, chunks, spans, box, base is not None, held is not None),
+    return pl.pallas_call(
+        functools.partial(last_kernel, count, chunks, spans),
         out_shape=jax.ShapeDtypeStruct(shape, BF16),
-        in_specs=specs + [VMEM] * len(sources),
+        in_specs=[VMEM] * (2 * count + 2 + len(sources)),
         out_specs=HELD,
-        scratch_shapes=[pltpu.VMEM((row_count, box[1], width), BF16), pltpu.SemaphoreType.DMA((chunks,))],
-        input_output_aliases=aliases,
+        scratch_shapes=[
+            pltpu.VMEM((row_count, col_count - done.shape[1], width), BF16),
+            pltpu.SemaphoreType.DMA((chunks + 1,)),
+        ],
         compiler_params=pltpu.CompilerParams(vmem_limit_bytes=20 << 20),
         cost_estimate=pl.CostEstimate(
-            flops=2 * pixels * width * width, bytes_accessed=2 * width * (width + 3 * pixels), transcendentals=0
-        ),
-    )(*operands, *sources)
+            flops=2 * pixels * width * depth * count, bytes_accessed=2 * width * (width + 3 * pixels), transcendentals=0
+        ),
+    )(*attended, *weights, base, done, *sources)
 
 
 def send_heads(outs):
@@ -524,10 +498,10 @@
     weights = triple_projection_matrix
     scales = logit_scaling_per_part
 
-    local_0, local_1 = norm_local(blocked, gain, bias, [(rows, rows, half, WS), (rows, rows, half + WS, near)])
-    south_0, south_1, east, corner = cut(
-        blocked, [(0, rows, half, WS), (0, rows, half + WS, near), (rows, rows, 0, half), (0, rows, 0, half)]
-    )
+    groups = [[(0, rows + row, left, size) for row in range(rows)] for left, size in ((half, WS), (half + WS, near))]
+    local_0, local_1 = norm([blocked], gain, bias, groups)
+    boxes = [(0, half, WS), (0, half + WS, near), (rows, 0, half), (0, 0, half)]
+    south_0, south_1, east, corner = cut(blocked, rows, boxes)
     south_0 = exchange(south_0, 1, "win")
     south_1 = exchange(south_1, 1, "win")
     east = permute_by(east, "win", west)
@@ -538,13 +512,13 @@
     out_weights = gather_weights(final_projection_matrix)
 
     spans = [(0, row, 0, WS) for row in range(rows)]
-    south_normed = norm([south_0], gain, bias, spans)
+    (south_normed,) = norm([south_0], gain, bias, [spans])
     south_pieces = gather_pieces(south_normed)
     local_0_pieces[0] = after(local_0, south_normed)
     local_0, local_1 = project([local_0_pieces, local_1_pieces], weights)
     spans = [(0, row, 0, near) for row in range(rows)]
     spans += [(which, row, 0, half) for which in (1, 2) for row in range(rows)]
-    rest_normed = norm([after(south_1, local_0), east, corner], gain, bias, spans)
+    (rest_normed,) = norm([after(south_1, local_0), east, corner], gain, bias, [spans])
     rest_pieces = gather_pieces(rest_normed)
     south_pieces[0] = after(south_normed, local_0)
     (south_0_projected,) = project([south_pieces], weights)
@@ -555,9 +529,7 @@
 
     split = count // 2
     blocks, tags = [local_0, south_0_projected], (query_0, key_0)
-    far = attend_run(blocks, tags, [], split, count)
-    close = attend_run(blocks, tags, far, 0, split)
-    outs_0 = close + far
+    outs_0 = attend_run(blocks, tags, [], 0, count)
     rest_pieces[0] = after(rest_normed, *outs_0)
     (rest_projected,) = project([rest_pieces], weights)
     blocks, tags = [local_1, rest_projected], (query_1, key_1)
@@ -571,16 +543,14 @@
     spans = [(0, rows + row, half, WS, row, 0) for row in range(rows)]
     spans += [(1, row, 0, WS, rows + row, 0) for row in range(rows)]
     shape = (row_count, col_count, width)
-    done = finish(first, out_weights, None, None, [blocked, south_0], spans, (0, WS), shape)
+    done = finish(first, out_weights, [blocked, south_0], spans, (row_count, WS, width))
     second[0] = after(second[0], done)
     base = partial(second[:split], out_weights[:split])
     spans = [(0, rows + row, half + WS, near, row, WS) for row in range(rows)]
     spans += [(1, row, 0, near, rows + row, WS) for row in range(rows)]
     spans += [(2, row, 0, half, row, WS + near) for row in range(rows)]
     spans += [(3, row, 0, half, rows + row, WS + near) for row in range(rows)]
-    mixed = finish(
-        second[split:], out_weights[split:], base, done, [blocked, south_1, east, corner], spans, (WS, WS), shape
-    )
+    mixed = finish_last(second[split:], out_weights[split:], base, done, [blocked, south_1, east, corner], spans, shape)
     return mixed[None, :, None]
 
 

time: 103 us -> 102 us (level)
  Pallas kernels: 36.2 us -> 28.8 us
  waiting for transfers between devices: 39 us -> 44.7 us
  local copies, waits for them, and re-layouts: 2.97 us -> 4.1 us
    ppermute x27, waiting for transfers between devices: 39 us -> 44.7 us  [permute_by(): return lax.ppermute(value, axis, pairs)]
    pallas_call x5, Pallas kernels: 8.67 us -> 5 us  [the longest x1 2.05 us: finish_last(): pl.pallas_call(functools.partial(last_kernel, count, chunks, spans), out_...]
    pallas_call x1, Pallas kernels: 2.25 us -> 0.07 us  [cut(): pl.pallas_call(functools.partial(cut_kernel, boxes), out_shape=[jax.Shape...]
    unnamed x20 -> x22, local copies, waits for them, and re-layouts: 2.97 us -> 4.1 us
    pallas_call x4 -> x3, Pallas kernels: 14.1 us -> 13.3 us  [attend(): pl.pallas_call(functools.partial(attend_kernel, count, parts, ranges, hea...]
  transfers between devices with their start and end apart: 27 -> 27, of which waited for: 9 -> 9; matrix products, arithmetic and copies ran while one was open for 0% -> 0% of each run, Pallas kernels for 30% -> 26%
where the time goes in v3:
time: 102 us; the launch traced here: 101 us
  waiting for transfers between devices  44.7 us (44%)
  Pallas kernels  28.8 us (28%)
  starting transfers between devices  23.5 us (23%)
  local copies, waits for them, and re-layouts  4.1 us (4%)
    ppermute x27, waiting for transfers between devices, permute_by(): return lax.ppermute(value, axis, pairs)  44.7 us
    ppermute x27, starting transfers between devices, permute_by(): return lax.ppermute(value, axis, pairs)  23.5 us
    pallas_call x3, Pallas kernels, attend(): pl.pallas_call(functools.partial(attend_kernel, count, parts, ranges, hea...  13.3 us
    pallas_call x3, Pallas kernels, project(): pl.pallas_call(functools.partial(project_kernel, [len(group) for group in...  8.84 us
    unnamed x22, local copies, waits for them, and re-layouts  4.1 us
    pallas_call x1, Pallas kernels, finish_last(): pl.pallas_call(functools.partial(last_kernel, count, chunks, spans), out_...  2.05 us
  transfers between devices with their start and end apart: 27, of which 9 were waited for; matrix products, arithmetic and copies ran while one was open for 0% of the time, Pallas kernels for 26%

profile of v3, /device:TPU:0, one launch (start us, length us, event | category | flops | bytes accessed | tf_op | source)
XLA Modules:
  0.0 101.4 jit_solution(7368887823306741485)
XLA Ops:
  0.0 1.4 %copy-done = bf16[1,8,1,64,1536]{4,3,2,1,0:T(8,128)(2,1)S(1)} copy-done((bf16[1,8,1,64,1536]{4,3,2,1,0:T(8,128)(2,1)S(1)}, bf16[1,8,1,64,1536]{4,3,2,1,0:T(8,128)(2,1)}, u32[]{:S(2)}) %copy-start) | copy-done | bytes 1572888
  1.4 0.7 copy-done.5
  2.1 0.7 copy-done.7
  2.8 0.4 shard_map.73
  3.2 3.0 %collective-permute-start.2 = (bf16[128,1536]{1,0:T(8,128)(2,1)S(1)}, bf16[128,1536]{1,0:T(8,128)(2,1)S(1)}, u32[]{:S(2)}, u32[]{:S(2)}) collective-permute-start(bf16[128,1536]{1,0:T(8,128)(2,1)S(1)} %get-tuple-element.34.refs_0_), channel_id=1, source_target_pairs={{0,2},{1,3},{2,0},{3,1},{4,6},{5,7},{6,4},{7,5},{8,10},{9,11},{10,... | collective-permute-start | bytes 1179656 | tf_op jit(solution)/shard_map/ppermute | solution.py:24
  6.3 1.3 %copy-done.2 = bf16[384,1536]{1,0:T(8,128)(2,1)S(1)} copy-done((bf16[384,1536]{1,0:T(8,128)(2,1)S(1)}, bf16[384,1536]{1,0:T(8,128)(2,1)}, u32[]{:S(2)}) %copy-start.2) | copy-done | bytes 1179672
  7.5 0.1 shard_map.81
  7.6 0.1 collective-permute-start.18
  7.7 0.1 cut.1
  7.8 2.1 %collective-permute-start = (bf16[4,32,1536]{2,1,0:T(8,128)(2,1)S(1)}, bf16[4,32,1536]{2,1,0:T(8,128)(2,1)S(1)}, u32[]{:S(2)}, u32[]{:S(2)}) collective-permute-start(bf16[4,32,1536]{2,1,0:T(8,128)(2,1)S(1)} %get-tuple-element.33), channel_id=1, source_target_pairs={{0,4},{4,0},{8,12},{12,8},{1,5},{5,1},{9,13},{13,9},{2,6},{6,2},{1... | collective-permute-start | bytes 1179656 | tf_op jit(solution)/shard_map/ppermute | solution.py:24
  9.9 1.5 %collective-permute-start.5 = (bf16[64,1536]{1,0:T(8,128)(2,1)S(1)}, bf16[64,1536]{1,0:T(8,128)(2,1)S(1)}, u32[]{:S(2)}, u32[]{:S(2)}) collective-permute-start(bf16[64,1536]{1,0:T(8,128)(2,1)S(1)} %get-tuple-element.35.refs_4_), channel_id=1, source_target_pairs={{0,2},{1,3},{2,0},{3,1},{4,6},{5,7},{6,4},{7,5},{8,10},{9,11},{10,... | collective-permute-start | bytes 589832 | tf_op jit(solution)/shard_map/ppermute | solution.py:24
  11.4 4.8 %collective-permute-done.2.refs_2_ = bf16[128,1536]{1,0:T(8,128)(2,1)S(1)} collective-permute-done((bf16[128,1536]{1,0:T(8,128)(2,1)S(1)}, bf16[128,1536]{1,0:T(8,128)(2,1)S(1)}, u32[]{:S(2)}, u32[]{:S(2)}) %collective-permute-start.2) | collective-permute-done | bytes 393248 | tf_op jit(solution)/shard_map/ppermute | solution.py:24
  16.2 9.7 %collective-permute-done.5.refs_6_ = bf16[64,1536]{1,0:T(8,128)(2,1)S(1)} collective-permute-done((bf16[64,1536]{1,0:T(8,128)(2,1)S(1)}, bf16[64,1536]{1,0:T(8,128)(2,1)S(1)}, u32[]{:S(2)}, u32[]{:S(2)}) %collective-permute-start.5) | collective-permute-done | bytes 196640 | tf_op jit(solution)/shard_map/ppermute | solution.py:24
  25.9 0.5 collective-permute-start.6
  26.4 1.8 %collective-permute-start.19 = (bf16[96,1536]{1,0:T(8,128)(2,1)S(1)}, bf16[96,1536]{1,0:T(8,128)(2,1)S(1)}, u32[]{:S(2)}, u32[]{:S(2)}) collective-permute-start(bf16[96,1536]{1,0:T(8,128)(2,1)S(1)} %collective-permute-done.18.own_ref), channel_id=1, source_target_pairs={{0,4},{4,0},{8,12},{12,8},{1,5},{5,1},{9,13},{13,9},{2,6},{6,2},{1... | collective-permute-start | bytes 884744 | tf_op jit(solution)/shard_map/ppermute | solution.py:24
  28.3 0.3 shard_map.74.refs_0_
  28.6 0.6 collective-permute-start.7
  29.2 2.6 %collective-permute-start.8 = (bf16[4,16,1536]{2,1,0:T(8,128)(2,1)S(1)}, bf16[4,16,1536]{2,1,0:T(8,128)(2,1)S(1)}, u32[]{:S(2)}, u32[]{:S(2)}) collective-permute-start(bf16[4,16,1536]{2,1,0:T(8,128)(2,1)S(1)} %get-tuple-element.40), channel_id=1, source_target_pairs={{0,8},{4,12},{8,0},{12,4},{1,9},{5,13},{9,1},{13,5},{2,10},{6,14},... | collective-permute-start | bytes 589832 | tf_op jit(solution)/shard_map/ppermute | solution.py:24
  31.8 1.3 %collective-permute-start.9 = (bf16[4,16,1536]{2,1,0:T(8,128)(2,1)S(1)}, bf16[4,16,1536]{2,1,0:T(8,128)(2,1)S(1)}, u32[]{:S(2)}, u32[]{:S(2)}) collective-permute-start(bf16[4,16,1536]{2,1,0:T(8,128)(2,1)S(1)} %get-tuple-element.41), channel_id=1, source_target_pairs={{0,12},{4,8},{8,4},{12,0},{1,13},{5,9},{9,5},{13,1},{2,14},{6,10},... | collective-permute-start | bytes 589832 | tf_op jit(solution)/shard_map/ppermute | solution.py:24
  33.1 1.5 %collective-permute-start.11 = (bf16[128,1536]{1,0:T(8,128)(2,1)S(1)}, bf16[128,1536]{1,0:T(8,128)(2,1)S(1)}, u32[]{:S(2)}, u32[]{:S(2)}) collective-permute-start(bf16[128,1536]{1,0:T(8,128)(2,1)S(1)} %shard_map.74.refs_0_), channel_id=1, source_target_pairs={{0,2},{1,3},{2,0},{3,1},{4,6},{5,7},{6,4},{7,5},{8,10},{9,11},{10,... | collective-permute-start | bytes 1179656 | tf_op jit(solution)/shard_map/ppermute | solution.py:24
  34.6 3.2 %shard_map.75 = (bf16[512,1152]{1,0:T(8,128)(2,1)S(1)}, bf16[256,1152]{1,0:T(8,128)(2,1)S(1)}) custom-call(bf16[128,1536]{1,0:T(8,128)(2,1)S(1)} %get-tuple-element.34.refs_0_, bf16[128,1536]{1,0:T(8,128)(2,1)S(1)} %collective-permute-done.1.refs_1_, bf16[128,1536]{1,0:T(8,128)(2,1)S(1)} %collective-permute-done.2.refs_2_, ...), custom_call_target="tpu_custom_call" | custom-call | flops 2717908992 | bytes 7667712 | tf_op jit(solution)/shard_map/pallas_call | solution.py:197
  37.8 6.1 %collective-permute-done.7.refs_0_.refs_7_ = bf16[4,16,1536]{2,1,0:T(8,128)(2,1)S(1)} collective-permute-done((bf16[4,16,1536]{2,1,0:T(8,128)(2,1)S(1)}, bf16[4,16,1536]{2,1,0:T(8,128)(2,1)S(1)}, u32[]{:S(2)}, u32[]{:S(2)}) %collective-permute-start.7) | collective-permute-done | bytes 196640 | tf_op jit(solution)/shard_map/ppermute | solution.py:24
  43.9 0.2 collective-permute-done.8.refs_1_.refs_8_
  44.1 6.2 %collective-permute-done.9.refs_2_.refs_9_ = bf16[4,16,1536]{2,1,0:T(8,128)(2,1)S(1)} collective-permute-done((bf16[4,16,1536]{2,1,0:T(8,128)(2,1)S(1)}, bf16[4,16,1536]{2,1,0:T(8,128)(2,1)S(1)}, u32[]{:S(2)}, u32[]{:S(2)}) %collective-permute-start.9) | collective-permute-done | bytes 196640 | tf_op jit(solution)/shard_map/ppermute | solution.py:24
  50.3 0.4 shard_map.76.refs_0_
  50.8 1.6 %collective-permute-start.14 = (bf16[192,1536]{1,0:T(8,128)(2,1)S(1)}, bf16[192,1536]{1,0:T(8,128)(2,1)S(1)}, u32[]{:S(2)}, u32[]{:S(2)}) collective-permute-start(bf16[192,1536]{1,0:T(8,128)(2,1)S(1)} %shard_map.76.refs_0_), channel_id=1, source_target_pairs={{0,2},{1,3},{2,0},{3,1},{4,6},{5,7},{6,4},{7,5},{8,10},{9,11},{10,... | collective-permute-start | bytes 1769480 | tf_op jit(solution)/shard_map/ppermute | solution.py:24
  52.4 1.6 %collective-permute-start.20 = (bf16[192,1536]{1,0:T(8,128)(2,1)S(1)}, bf16[192,1536]{1,0:T(8,128)(2,1)S(1)}, u32[]{:S(2)}, u32[]{:S(2)}) collective-permute-start(bf16[192,1536]{1,0:T(8,128)(2,1)S(1)} %shard_map.82.own_ref), channel_id=1, source_target_pairs={{0,16},{16,0},{1,17},{17,1},{2,18},{18,2},{3,19},{19,3},{4,20},{20... | collective-permute-start | bytes 1769480 | tf_op jit(solution)/shard_map/ppermute | solution.py:24
  54.0 0.5 collective-permute-start.12
  54.5 10.8 %collective-permute-done.14.refs_2_ = bf16[192,1536]{1,0:T(8,128)(2,1)S(1)} collective-permute-done((bf16[192,1536]{1,0:T(8,128)(2,1)S(1)}, bf16[192,1536]{1,0:T(8,128)(2,1)S(1)}, u32[]{:S(2)}, u32[]{:S(2)}) %collective-permute-start.14) | collective-permute-done | bytes 589856 | tf_op jit(solution)/shard_map/ppermute | solution.py:24
  65.3 0.4 tags.1
  65.7 1.0 collective-permute-done.20.other_ref
  66.6 0.4 collective-permute-start.25
  67.1 0.1 shard_map.83.refs_6_.refs_2_
  67.2 0.1 collective-permute-start.21
  67.3 2.2 %shard_map.77.refs_1_ = bf16[512,1152]{1,0:T(8,128)(2,1)S(1)} custom-call(bf16[128,1536]{1,0:T(8,128)(2,1)S(1)} %shard_map.74.refs_0_, bf16[128,1536]{1,0:T(8,128)(2,1)S(1)} %collective-permute-done.10.refs_1_, bf16[128,1536]{1,0:T(8,128)(2,1)S(1)} %collective-permute-done.11.refs_2_, bf16[128,1536]{1,0:T(8,128)(2,1)S(1)} %collective-permute-done.12.refs_3_, ...), custom_call_target="tpu_custom_call" | custom-call | flops 1811939328 | bytes 6291456 | tf_op jit(solution)/shard_map/pallas_call | solution.py:197
  69.5 6.3 %shard_map.78 = (bf16[1,256,384]{2,1,0:T(8,128)(2,1)S(1)}, bf16[1,256,384]{2,1,0:T(8,128)(2,1)S(1)}, bf16[1,256,384]{2,1,0:T(8,128)(2,1)S(1)}, bf16[1,256,384]{2,1,0:T(8,128)(2,1)S(1)}) custom-call(bf16[512,1152]{1,0:T(8,128)(2,1)S(1)} %get-tuple-element.38.refs_0_, bf16[512,1152]{1,0:T(8,128)(2,1)S(1)} %shard_map.77.refs_1_, ...), custom_call_target="tpu_custom_call" | custom-call | flops 4294967296 | bytes 2359296 | tf_op jit(solution)/shard_map/pallas_call | solution.py:280
  75.8 0.5 collective-permute-start.22
  76.3 1.5 %collective-permute-start.23 = (bf16[1,256,384]{2,1,0:T(8,128)(2,1)S(1)}, bf16[1,256,384]{2,1,0:T(8,128)(2,1)S(1)}, u32[]{:S(2)}, u32[]{:S(2)}) collective-permute-start(bf16[1,256,384]{2,1,0:T(8,128)(2,1)S(1)} %get-tuple-element.47), channel_id=1, source_target_pairs={{0,2},{1,3},{2,0},{3,1},{4,6},{5,7},{6,4},{7,5},{8,10},{9,11},{10,... | collective-permute-start | bytes 589832 | tf_op jit(solution)/shard_map/ppermute | solution.py:24
  77.8 3.4 %shard_map.79.refs_1_ = bf16[768,1152]{1,0:T(8,128)(2,1)S(1)} custom-call(bf16[192,1536]{1,0:T(8,128)(2,1)S(1)} %shard_map.76.refs_0_, bf16[192,1536]{1,0:T(8,128)(2,1)S(1)} %collective-permute-done.13.refs_1_, bf16[192,1536]{1,0:T(8,128)(2,1)S(1)} %collective-permute-done.14.refs_2_, bf16[192,1536]{1,0:T(8,128)(2,1)S(1)} %collective-permute-done.15.refs_3_, ...), custom_call_target="tpu_custom_call" | custom-call | flops 2717908992 | bytes 7667712 | tf_op jit(solution)/shard_map/pallas_call | solution.py:197
  81.2 3.5 %shard_map.80 = (bf16[1,256,384]{2,1,0:T(8,128)(2,1)S(1)}, bf16[1,256,384]{2,1,0:T(8,128)(2,1)S(1)}) custom-call(bf16[256,1152]{1,0:T(8,128)(2,1)S(1)} %get-tuple-element.54.refs_0_, bf16[768,1152]{1,0:T(8,128)(2,1)S(1)} %shard_map.79.refs_1_, bf16[1024,128]{1,0:T(8,128)(2,1)S(1)} %get-tuple-element.50.refs_2_, ...), custom_call_target="tpu_custom_call" | custom-call | flops 2147483648 | bytes 2359296 | tf_op jit(solution)/shard_map/pallas_call | solution.py:280
  84.7 3.5 %shard_map.84 = (bf16[1,256,384]{2,1,0:T(8,128)(2,1)S(1)}, bf16[1,256,384]{2,1,0:T(8,128)(2,1)S(1)}) custom-call(bf16[256,1152]{1,0:T(8,128)(2,1)S(1)} %get-tuple-element.54.refs_0_, bf16[768,1152]{1,0:T(8,128)(2,1)S(1)} %shard_map.79.refs_1_, bf16[1024,128]{1,0:T(8,128)(2,1)S(1)} %get-tuple-element.50.refs_2_, ...), custom_call_target="tpu_custom_call" | custom-call | flops 2147483648 | bytes 2359296 | tf_op jit(solution)/shard_map/pallas_call | solution.py:280
  88.3 0.7 collective-permute-start.26
  89.0 1.5 %collective-permute-start.16 = (bf16[1,256,384]{2,1,0:T(8,128)(2,1)S(1)}, bf16[1,256,384]{2,1,0:T(8,128)(2,1)S(1)}, u32[]{:S(2)}, u32[]{:S(2)}) collective-permute-start(bf16[1,256,384]{2,1,0:T(8,128)(2,1)S(1)} %get-tuple-element.52), channel_id=1, source_target_pairs={{0,2},{1,3},{2,0},{3,1},{4,6},{5,7},{6,4},{7,5},{8,10},{9,11},{10,... | collective-permute-start | bytes 589832 | tf_op jit(solution)/shard_map/ppermute | solution.py:24
  90.5 1.8 %shard_map.85.refs_5_ = bf16[8,32,1536]{2,1,0:T(8,128)(2,1)S(1)} custom-call(bf16[256,384]{1,0:T(8,128)(2,1)S(1)} %bitcast.19, bf16[256,384]{1,0:T(8,128)(2,1)S(1)} %bitcast.20, bf16[256,384]{1,0:T(8,128)(2,1)S(1)} %bitcast.21, bf16[256,384]{1,0:T(8,128)(2,1)S(1)} %bitcast.22, bf16[384,1536]{1,0:T(8,128)(2,1)S(1)} %copy-done.3, ...), custom_call_target="tpu_custom_call" | custom-call | flops 1207959552 | bytes 7077888 | tf_op jit(solution)/shard_map/pallas_call | solution.py:337
  92.3 1.0 shard_map.86.refs_4_
  93.3 3.5 %collective-permute-done.16 = bf16[1,256,384]{2,1,0:T(8,128)(2,1)S(1)} collective-permute-done((bf16[1,256,384]{2,1,0:T(8,128)(2,1)S(1)}, bf16[1,256,384]{2,1,0:T(8,128)(2,1)S(1)}, u32[]{:S(2)}, u32[]{:S(2)}) %collective-permute-start.16) | collective-permute-done | bytes 196640 | tf_op jit(solution)/shard_map/ppermute | solution.py:24
  96.8 2.4 %collective-permute-done.17 = bf16[1,256,384]{2,1,0:T(8,128)(2,1)S(1)} collective-permute-done((bf16[1,256,384]{2,1,0:T(8,128)(2,1)S(1)}, bf16[1,256,384]{2,1,0:T(8,128)(2,1)S(1)}, u32[]{:S(2)}, u32[]{:S(2)}) %collective-permute-start.17) | collective-permute-done | bytes 196640 | tf_op jit(solution)/shard_map/ppermute | solution.py:24
  99.2 2.0 %shard_map.87 = bf16[8,64,1536]{2,1,0:T(8,128)(2,1)} custom-call(bf16[256,384]{1,0:T(8,128)(2,1)S(1)} %bitcast.23, bf16[256,384]{1,0:T(8,128)(2,1)S(1)} %bitcast.24, bf16[384,1536]{1,0:T(8,128)(2,1)S(1)} %shard_map.83.refs_6_.refs_2_, bf16[384,1536]{1,0:T(8,128)(2,1)S(1)} %collective-permute-done.21.refs_7_.refs_3_, f32[256,1536]{1,0:T(8,128)S(1)} %shard_map.86.refs_4_, ...), custom_call_target="tpu_custom_call" | custom-call | flops 603979776 | bytes 7077888 | tf_op jit(solution)/shard_map/pallas_call | solution.py:383
  (45 shorter events, 0.2 us)
Async XLA Ops:
  0.0 1.4 %copy-start = (bf16[1,8,1,64,1536]{4,3,2,1,0:T(8,128)(2,1)S(1)}, bf16[1,8,1,64,1536]{4,3,2,1,0:T(8,128)(2,1)}, u32[]{:S(2)}) copy-start(bf16[1,8,1,64,1536]{4,3,2,1,0:T(8,128)(2,1)} %param.7) | copy-start | bytes 4718596
  1.4 0.7 copy-start.5
  2.1 0.7 copy-start.7
  2.8 4.9 %copy-start.1 = (bf16[1,8,1,64,1536]{4,3,2,1,0:T(8,128)(2,1)S(1)}, bf16[1,8,1,64,1536]{4,3,2,1,0:T(8,128)(2,1)}, u32[]{:S(2)}) copy-start(bf16[1,8,1,64,1536]{4,3,2,1,0:T(8,128)(2,1)} %param.7) | copy-start | bytes 4718596
  2.8 25.5 %copy-start.6 = (f32[1536]{0:T(1024)S(1)}, f32[1536]{0:T(1024)}, u32[]{:S(2)}) copy-start(f32[1536]{0:T(1024)} %refs_3_.1) | copy-start | bytes 18436
  2.8 25.5 %copy-start.8 = (f32[1536]{0:T(1024)S(1)}, f32[1536]{0:T(1024)}, u32[]{:S(2)}) copy-start(f32[1536]{0:T(1024)} %refs_4_.7) | copy-start | bytes 18436
  3.2 13.0 %collective-permute-start.2 = (bf16[128,1536]{1,0:T(8,128)(2,1)S(1)}, bf16[128,1536]{1,0:T(8,128)(2,1)S(1)}, u32[]{:S(2)}, u32[]{:S(2)}) collective-permute-start(bf16[128,1536]{1,0:T(8,128)(2,1)S(1)} %get-tuple-element.34.refs_0_), channel_id=1, source_target_pairs={{0,2},{1,3},{2,0},{3,1},{4,6},{5,7},{6,4},{7,5},{8,10},{9,11},{10,... | collective-permute-start | bytes 1179656 | tf_op jit(solution)/shard_map/ppermute | solution.py:24
  6.3 1.3 %copy-start.2 = (bf16[384,1536]{1,0:T(8,128)(2,1)S(1)}, bf16[384,1536]{1,0:T(8,128)(2,1)}, u32[]{:S(2)}) copy-start(bf16[384,1536]{1,0:T(8,128)(2,1)} %refs_2_.5) | copy-start | bytes 3538948
  7.5 27.0 %copy-start.4 = (bf16[3,1536,384]{2,1,0:T(8,128)(2,1)S(1)}, bf16[3,1536,384]{2,1,0:T(8,128)(2,1)}, u32[]{:S(2)}) copy-start(bf16[3,1536,384]{2,1,0:T(8,128)(2,1)} %refs_4_.10) | copy-start | bytes 10616836
  7.6 18.3 %collective-permute-start.18 = (bf16[96,1536]{1,0:T(8,128)(2,1)S(1)}, bf16[96,1536]{1,0:T(8,128)(2,1)S(1)}, u32[]{:S(2)}, u32[]{:S(2)}) collective-permute-start(bf16[96,1536]{1,0:T(8,128)(2,1)S(1)} %shard_map.81), channel_id=1, source_target_pairs={{0,2},{1,3},{2,0},{3,1},{4,6},{5,7},{6,4},{7,5},{8,10},{9,11},{10,... | collective-permute-start | bytes 884744 | tf_op jit(solution)/shard_map/ppermute | solution.py:24
  7.8 18.7 %collective-permute-start = (bf16[4,32,1536]{2,1,0:T(8,128)(2,1)S(1)}, bf16[4,32,1536]{2,1,0:T(8,128)(2,1)S(1)}, u32[]{:S(2)}, u32[]{:S(2)}) collective-permute-start(bf16[4,32,1536]{2,1,0:T(8,128)(2,1)S(1)} %get-tuple-element.33), channel_id=1, source_target_pairs={{0,4},{4,0},{8,12},{12,8},{1,5},{5,1},{9,13},{13,9},{2,6},{6,2},{1... | collective-permute-start | bytes 1179656 | tf_op jit(solution)/shard_map/ppermute | solution.py:24
  9.9 16.0 %collective-permute-start.5 = (bf16[64,1536]{1,0:T(8,128)(2,1)S(1)}, bf16[64,1536]{1,0:T(8,128)(2,1)S(1)}, u32[]{:S(2)}, u32[]{:S(2)}) collective-permute-start(bf16[64,1536]{1,0:T(8,128)(2,1)S(1)} %get-tuple-element.35.refs_4_), channel_id=1, source_target_pairs={{0,2},{1,3},{2,0},{3,1},{4,6},{5,7},{6,4},{7,5},{8,10},{9,11},{10,... | collective-permute-start | bytes 589832 | tf_op jit(solution)/shard_map/ppermute | solution.py:24
  11.4 20.4 %collective-permute-start.1 = (bf16[128,1536]{1,0:T(8,128)(2,1)S(1)}, bf16[128,1536]{1,0:T(8,128)(2,1)S(1)}, u32[]{:S(2)}, u32[]{:S(2)}) collective-permute-start(bf16[128,1536]{1,0:T(8,128)(2,1)S(1)} %get-tuple-element.34.refs_0_), channel_id=1, source_target_pairs={{0,1},{1,0},{2,3},{3,2},{4,5},{5,4},{6,7},{7,6},{8,9},{9,8},{10,11... | collective-permute-start | bytes 1179656 | tf_op jit(solution)/shard_map/ppermute | solution.py:24
  16.2 16.8 %collective-permute-start.3 = (bf16[128,1536]{1,0:T(8,128)(2,1)S(1)}, bf16[128,1536]{1,0:T(8,128)(2,1)S(1)}, u32[]{:S(2)}, u32[]{:S(2)}) collective-permute-start(bf16[128,1536]{1,0:T(8,128)(2,1)S(1)} %collective-permute-done.2.refs_2_), channel_id=1, source_target_pairs={{0,1},{1,0},{2,3},{3,2},{4,5},{5,4},{6,7},{7,6},{8,9},{9,8},{10,11... | collective-permute-start | bytes 1179656 | tf_op jit(solution)/shard_map/ppermute | solution.py:24
  25.9 2.7 %collective-permute-start.4 = (bf16[64,1536]{1,0:T(8,128)(2,1)S(1)}, bf16[64,1536]{1,0:T(8,128)(2,1)S(1)}, u32[]{:S(2)}, u32[]{:S(2)}) collective-permute-start(bf16[64,1536]{1,0:T(8,128)(2,1)S(1)} %get-tuple-element.35.refs_4_), channel_id=1, source_target_pairs={{0,1},{1,0},{2,3},{3,2},{4,5},{5,4},{6,7},{7,6},{8,9},{9,8},{10,11... | collective-permute-start | bytes 589832 | tf_op jit(solution)/shard_map/ppermute | solution.py:24
  25.9 3.3 %collective-permute-start.6 = (bf16[64,1536]{1,0:T(8,128)(2,1)S(1)}, bf16[64,1536]{1,0:T(8,128)(2,1)S(1)}, u32[]{:S(2)}, u32[]{:S(2)}) collective-permute-start(bf16[64,1536]{1,0:T(8,128)(2,1)S(1)} %collective-permute-done.5.refs_6_), channel_id=1, source_target_pairs={{0,1},{1,0},{2,3},{3,2},{4,5},{5,4},{6,7},{7,6},{8,9},{9,8},{10,11... | collective-permute-start | bytes 589832 | tf_op jit(solution)/shard_map/ppermute | solution.py:24
  26.4 25.9 %collective-permute-start.19 = (bf16[96,1536]{1,0:T(8,128)(2,1)S(1)}, bf16[96,1536]{1,0:T(8,128)(2,1)S(1)}, u32[]{:S(2)}, u32[]{:S(2)}) collective-permute-start(bf16[96,1536]{1,0:T(8,128)(2,1)S(1)} %collective-permute-done.18.own_ref), channel_id=1, source_target_pairs={{0,4},{4,0},{8,12},{12,8},{1,5},{5,1},{9,13},{13,9},{2,6},{6,2},{1... | collective-permute-start | bytes 884744 | tf_op jit(solution)/shard_map/ppermute | solution.py:24
  28.6 15.3 %collective-permute-start.7 = (bf16[4,16,1536]{2,1,0:T(8,128)(2,1)S(1)}, bf16[4,16,1536]{2,1,0:T(8,128)(2,1)S(1)}, u32[]{:S(2)}, u32[]{:S(2)}) collective-permute-start(bf16[4,16,1536]{2,1,0:T(8,128)(2,1)S(1)} %get-tuple-element.37), channel_id=1, source_target_pairs={{0,4},{4,0},{8,12},{12,8},{1,5},{5,1},{9,13},{13,9},{2,6},{6,2},{1... | collective-permute-start | bytes 589832 | tf_op jit(solution)/shard_map/ppermute | solution.py:24
  29.2 14.9 %collective-permute-start.8 = (bf16[4,16,1536]{2,1,0:T(8,128)(2,1)S(1)}, bf16[4,16,1536]{2,1,0:T(8,128)(2,1)S(1)}, u32[]{:S(2)}, u32[]{:S(2)}) collective-permute-start(bf16[4,16,1536]{2,1,0:T(8,128)(2,1)S(1)} %get-tuple-element.40), channel_id=1, source_target_pairs={{0,8},{4,12},{8,0},{12,4},{1,9},{5,13},{9,1},{13,5},{2,10},{6,14},... | collective-permute-start | bytes 589832 | tf_op jit(solution)/shard_map/ppermute | solution.py:24
  31.8 18.6 %collective-permute-start.9 = (bf16[4,16,1536]{2,1,0:T(8,128)(2,1)S(1)}, bf16[4,16,1536]{2,1,0:T(8,128)(2,1)S(1)}, u32[]{:S(2)}, u32[]{:S(2)}) collective-permute-start(bf16[4,16,1536]{2,1,0:T(8,128)(2,1)S(1)} %get-tuple-element.41), channel_id=1, source_target_pairs={{0,12},{4,8},{8,4},{12,0},{1,13},{5,9},{9,5},{13,1},{2,14},{6,10},... | collective-permute-start | bytes 589832 | tf_op jit(solution)/shard_map/ppermute | solution.py:24
  33.1 20.9 %collective-permute-start.11 = (bf16[128,1536]{1,0:T(8,128)(2,1)S(1)}, bf16[128,1536]{1,0:T(8,128)(2,1)S(1)}, u32[]{:S(2)}, u32[]{:S(2)}) collective-permute-start(bf16[128,1536]{1,0:T(8,128)(2,1)S(1)} %shard_map.74.refs_0_), channel_id=1, source_target_pairs={{0,2},{1,3},{2,0},{3,1},{4,6},{5,7},{6,4},{7,5},{8,10},{9,11},{10,... | collective-permute-start | bytes 1179656 | tf_op jit(solution)/shard_map/ppermute | solution.py:24
  43.9 21.3 %copy-start.9 = (s32[1,32,64]{2,1,0:T(8,128)S(1)}, s32[1,32,64]{2,1,0:T(8,128)}, u32[]{:S(2)}) copy-start(s32[1,32,64]{2,1,0:T(8,128)} %param.8) | copy-start | bytes 24580
  50.8 14.5 %collective-permute-start.14 = (bf16[192,1536]{1,0:T(8,128)(2,1)S(1)}, bf16[192,1536]{1,0:T(8,128)(2,1)S(1)}, u32[]{:S(2)}, u32[]{:S(2)}) collective-permute-start(bf16[192,1536]{1,0:T(8,128)(2,1)S(1)} %shard_map.76.refs_0_), channel_id=1, source_target_pairs={{0,2},{1,3},{2,0},{3,1},{4,6},{5,7},{6,4},{7,5},{8,10},{9,11},{10,... | collective-permute-start | bytes 1769480 | tf_op jit(solution)/shard_map/ppermute | solution.py:24
  52.4 14.2 %collective-permute-start.20 = (bf16[192,1536]{1,0:T(8,128)(2,1)S(1)}, bf16[192,1536]{1,0:T(8,128)(2,1)S(1)}, u32[]{:S(2)}, u32[]{:S(2)}) collective-permute-start(bf16[192,1536]{1,0:T(8,128)(2,1)S(1)} %shard_map.82.own_ref), channel_id=1, source_target_pairs={{0,16},{16,0},{1,17},{17,1},{2,18},{18,2},{3,19},{19,3},{4,20},{20... | collective-permute-start | bytes 1769480 | tf_op jit(solution)/shard_map/ppermute | solution.py:24
  54.0 13.2 %collective-permute-start.10 = (bf16[128,1536]{1,0:T(8,128)(2,1)S(1)}, bf16[128,1536]{1,0:T(8,128)(2,1)S(1)}, u32[]{:S(2)}, u32[]{:S(2)}) collective-permute-start(bf16[128,1536]{1,0:T(8,128)(2,1)S(1)} %shard_map.74.refs_0_), channel_id=1, source_target_pairs={{0,1},{1,0},{2,3},{3,2},{4,5},{5,4},{6,7},{7,6},{8,9},{9,8},{10,11... | collective-permute-start | bytes 1179656 | tf_op jit(solution)/shard_map/ppermute | solution.py:24
  54.0 13.3 %collective-permute-start.12 = (bf16[128,1536]{1,0:T(8,128)(2,1)S(1)}, bf16[128,1536]{1,0:T(8,128)(2,1)S(1)}, u32[]{:S(2)}, u32[]{:S(2)}) collective-permute-start(bf16[128,1536]{1,0:T(8,128)(2,1)S(1)} %collective-permute-done.11.refs_2_), channel_id=1, source_target_pairs={{0,1},{1,0},{2,3},{3,2},{4,5},{5,4},{6,7},{7,6},{8,9},{9,8},{10,11... | collective-permute-start | bytes 1179656 | tf_op jit(solution)/shard_map/ppermute | solution.py:24
  54.5 21.8 %collective-permute-start.13 = (bf16[192,1536]{1,0:T(8,128)(2,1)S(1)}, bf16[192,1536]{1,0:T(8,128)(2,1)S(1)}, u32[]{:S(2)}, u32[]{:S(2)}) collective-permute-start(bf16[192,1536]{1,0:T(8,128)(2,1)S(1)} %shard_map.76.refs_0_), channel_id=1, source_target_pairs={{0,1},{1,0},{2,3},{3,2},{4,5},{5,4},{6,7},{7,6},{8,9},{9,8},{10,11... | collective-permute-start | bytes 1769480 | tf_op jit(solution)/shard_map/ppermute | solution.py:24
  65.3 12.6 %collective-permute-start.15 = (bf16[192,1536]{1,0:T(8,128)(2,1)S(1)}, bf16[192,1536]{1,0:T(8,128)(2,1)S(1)}, u32[]{:S(2)}, u32[]{:S(2)}) collective-permute-start(bf16[192,1536]{1,0:T(8,128)(2,1)S(1)} %collective-permute-done.14.refs_2_), channel_id=1, source_target_pairs={{0,1},{1,0},{2,3},{3,2},{4,5},{5,4},{6,7},{7,6},{8,9},{9,8},{10,11... | collective-permute-start | bytes 1769480 | tf_op jit(solution)/shard_map/ppermute | solution.py:24
  65.3 1.3 %copy-start.3 = (bf16[384,1536]{1,0:T(8,128)(2,1)S(1)}, bf16[384,1536]{1,0:T(8,128)(2,1)}, u32[]{:S(2)}) copy-start(bf16[384,1536]{1,0:T(8,128)(2,1)} %refs_2_.5) | copy-start | bytes 3538948
  66.6 21.7 %collective-permute-start.25 = (bf16[384,1536]{1,0:T(8,128)(2,1)S(1)}, bf16[384,1536]{1,0:T(8,128)(2,1)S(1)}, u32[]{:S(2)}, u32[]{:S(2)}) collective-permute-start(bf16[384,1536]{1,0:T(8,128)(2,1)S(1)} %copy-done.3), channel_id=1, source_target_pairs={{0,1},{1,0},{2,3},{3,2},{4,5},{5,4},{6,7},{7,6},{8,9},{9,8},{10,11... | collective-permute-start | bytes 3538952 | tf_op jit(solution)/shard_map/ppermute | solution.py:24
  67.1 2.4 %copy-start.10 = (f32[4]{0:T(128)S(1)}, f32[4]{0:T(128)}, u32[]{:S(2)}) copy-start(f32[4]{0:T(128)} %refs_4_.12) | copy-start | bytes 52
  67.2 23.3 %collective-permute-start.21 = (bf16[384,1536]{1,0:T(8,128)(2,1)S(1)}, bf16[384,1536]{1,0:T(8,128)(2,1)S(1)}, u32[]{:S(2)}, u32[]{:S(2)}) collective-permute-start(bf16[384,1536]{1,0:T(8,128)(2,1)S(1)} %shard_map.83.refs_6_.refs_2_), channel_id=1, source_target_pairs={{0,1},{1,0},{2,3},{3,2},{4,5},{5,4},{6,7},{7,6},{8,9},{9,8},{10,11... | collective-permute-start | bytes 3538952 | tf_op jit(solution)/shard_map/ppermute | solution.py:24
  75.8 13.2 %collective-permute-start.22 = (bf16[1,256,384]{2,1,0:T(8,128)(2,1)S(1)}, bf16[1,256,384]{2,1,0:T(8,128)(2,1)S(1)}, u32[]{:S(2)}, u32[]{:S(2)}) collective-permute-start(bf16[1,256,384]{2,1,0:T(8,128)(2,1)S(1)} %get-tuple-element.46), channel_id=1, source_target_pairs={{0,1},{1,0},{2,3},{3,2},{4,5},{5,4},{6,7},{7,6},{8,9},{9,8},{10,11... | collective-permute-start | bytes 589832 | tf_op jit(solution)/shard_map/ppermute | solution.py:24
  76.3 14.2 %collective-permute-start.23 = (bf16[1,256,384]{2,1,0:T(8,128)(2,1)S(1)}, bf16[1,256,384]{2,1,0:T(8,128)(2,1)S(1)}, u32[]{:S(2)}, u32[]{:S(2)}) collective-permute-start(bf16[1,256,384]{2,1,0:T(8,128)(2,1)S(1)} %get-tuple-element.47), channel_id=1, source_target_pairs={{0,2},{1,3},{2,0},{3,1},{4,6},{5,7},{6,4},{7,5},{8,10},{9,11},{10,... | collective-permute-start | bytes 589832 | tf_op jit(solution)/shard_map/ppermute | solution.py:24
  77.8 12.7 %collective-permute-start.24 = (bf16[1,256,384]{2,1,0:T(8,128)(2,1)S(1)}, bf16[1,256,384]{2,1,0:T(8,128)(2,1)S(1)}, u32[]{:S(2)}, u32[]{:S(2)}) collective-permute-start(bf16[1,256,384]{2,1,0:T(8,128)(2,1)S(1)} %get-tuple-element.48), channel_id=1, source_target_pairs={{0,3},{1,2},{2,1},{3,0},{4,7},{5,6},{6,5},{7,4},{8,11},{9,10},{10,... | collective-permute-start | bytes 589832 | tf_op jit(solution)/shard_map/ppermute | solution.py:24
  88.3 4.0 %collective-permute-start.26 = (bf16[1,256,384]{2,1,0:T(8,128)(2,1)S(1)}, bf16[1,256,384]{2,1,0:T(8,128)(2,1)S(1)}, u32[]{:S(2)}, u32[]{:S(2)}) collective-permute-start(bf16[1,256,384]{2,1,0:T(8,128)(2,1)S(1)} %get-tuple-element.56), channel_id=1, source_target_pairs={{0,1},{1,0},{2,3},{3,2},{4,5},{5,4},{6,7},{7,6},{8,9},{9,8},{10,11... | collective-permute-start | bytes 589832 | tf_op jit(solution)/shard_map/ppermute | solution.py:24
  89.0 7.8 %collective-permute-start.16 = (bf16[1,256,384]{2,1,0:T(8,128)(2,1)S(1)}, bf16[1,256,384]{2,1,0:T(8,128)(2,1)S(1)}, u32[]{:S(2)}, u32[]{:S(2)}) collective-permute-start(bf16[1,256,384]{2,1,0:T(8,128)(2,1)S(1)} %get-tuple-element.52), channel_id=1, source_target_pairs={{0,2},{1,3},{2,0},{3,1},{4,6},{5,7},{6,4},{7,5},{8,10},{9,11},{10,... | collective-permute-start | bytes 589832 | tf_op jit(solution)/shard_map/ppermute | solution.py:24
  90.5 8.7 %collective-permute-start.17 = (bf16[1,256,384]{2,1,0:T(8,128)(2,1)S(1)}, bf16[1,256,384]{2,1,0:T(8,128)(2,1)S(1)}, u32[]{:S(2)}, u32[]{:S(2)}) collective-permute-start(bf16[1,256,384]{2,1,0:T(8,128)(2,1)S(1)} %get-tuple-element.53), channel_id=1, source_target_pairs={{0,3},{1,2},{2,1},{3,0},{4,7},{5,6},{6,5},{7,4},{8,11},{9,10},{10,... | collective-permute-start | bytes 589832 | tf_op jit(solution)/shard_map/ppermute | solution.py:24

commit v4 on v3

--- a/solution.py
+++ b/solution.py
@@ -498,10 +498,10 @@
     weights = triple_projection_matrix
     scales = logit_scaling_per_part
 
-    groups = [[(0, rows + row, left, size) for row in range(rows)] for left, size in ((half, WS), (half + WS, near))]
-    local_0, local_1 = norm([blocked], gain, bias, groups)
-    boxes = [(0, half, WS), (0, half + WS, near), (rows, 0, half), (0, 0, half)]
-    south_0, south_1, east, corner = cut(blocked, rows, boxes)
+    boxes = [(rows, half, WS), (0, half, WS), (0, half + WS, near), (rows, 0, half), (0, 0, half)]
+    local_0, south_0, south_1, east, corner = cut(blocked, rows, boxes)
+    spans = [(0, rows + row, half + WS, near) for row in range(rows)]
+    (local_1,) = norm([blocked], gain, bias, [spans])
     south_0 = exchange(south_0, 1, "win")
     south_1 = exchange(south_1, 1, "win")
     east = permute_by(east, "win", west)
@@ -514,8 +514,10 @@
     spans = [(0, row, 0, WS) for row in range(rows)]
     (south_normed,) = norm([south_0], gain, bias, [spans])
     south_pieces = gather_pieces(south_normed)
-    local_0_pieces[0] = after(local_0, south_normed)
-    local_0, local_1 = project([local_0_pieces, local_1_pieces], weights)
+    spans = [(piece, row, 0, WS) for piece in range(count) for row in range(rows)]
+    (local_0_normed,) = norm(local_0_pieces, gain, bias, [spans])
+    local_1_pieces[0] = after(local_1, south_normed)
+    local_0, local_1 = project([[local_0_normed], local_1_pieces], weights)
     spans = [(0, row, 0, near) for row in range(rows)]
     spans += [(which, row, 0, half) for which in (1, 2) for row in range(rows)]
     (rest_normed,) = norm([after(south_1, local_0), east, corner], gain, bias, [spans])

time: 102 us -> 100 us (0.980)
  waiting for transfers between devices: 44.7 us -> 41.4 us
    ppermute x27, waiting for transfers between devices: 44.7 us -> 41.4 us  [permute_by(): return lax.ppermute(value, axis, pairs)]
    pallas_call x3 -> x4, Pallas kernels: 1.17 us -> 2.11 us  [norm(): pl.pallas_call(functools.partial(norm_kernel, groups), out_shape=[jax.Sha...]
  transfers between devices with their start and end apart: 27 -> 27, of which waited for: 9 -> 9; matrix products, arithmetic and copies ran while one was open for 0% -> 0% of each run, Pallas kernels for 26% -> 28%
where the time goes in v4:
time: 100 us; the launch traced here: 99.7 us
  waiting for transfers between devices  41.4 us (41%)
  Pallas kernels  29.7 us (30%)
  starting transfers between devices  24.1 us (24%)
  local copies, waits for them, and re-layouts  4.11 us (4%)
    ppermute x27, waiting for transfers between devices, permute_by(): return lax.ppermute(value, axis, pairs)  41.4 us
    ppermute x27, starting transfers between devices, permute_by(): return lax.ppermute(value, axis, pairs)  24.1 us
    pallas_call x3, Pallas kernels, attend(): pl.pallas_call(functools.partial(attend_kernel, count, parts, ranges, hea...  13.5 us
    pallas_call x3, Pallas kernels, project(): pl.pallas_call(functools.partial(project_kernel, [len(group) for group in...  8.68 us
    unnamed x22, local copies, waits for them, and re-layouts  4.11 us
    pallas_call x4, Pallas kernels, norm(): pl.pallas_call(functools.partial(norm_kernel, groups), out_shape=[jax.Sha...  2.11 us
    pallas_call x1, Pallas kernels, finish_last(): pl.pallas_call(functools.partial(last_kernel, count, chunks, spans), out_...  2.05 us
  transfers between devices with their start and end apart: 27, of which 9 were waited for; matrix products, arithmetic and copies ran while one was open for 0% of the time, Pallas kernels for 28%

profile of v4, /device:TPU:0, one launch (start us, length us, event | category | flops | bytes accessed | tf_op | source)
XLA Modules:
  0.0 99.7 jit_solution(17168473872440640020)
XLA Ops:
  0.0 1.4 %copy-done = bf16[1,8,1,64,1536]{4,3,2,1,0:T(8,128)(2,1)S(1)} copy-done((bf16[1,8,1,64,1536]{4,3,2,1,0:T(8,128)(2,1)S(1)}, bf16[1,8,1,64,1536]{4,3,2,1,0:T(8,128)(2,1)}, u32[]{:S(2)}) %copy-start) | copy-done | bytes 1572888
  1.4 0.1 cut.1
  1.5 3.0 %collective-permute-start.1 = (bf16[4,32,1536]{2,1,0:T(8,128)(2,1)S(1)}, bf16[4,32,1536]{2,1,0:T(8,128)(2,1)S(1)}, u32[]{:S(2)}, u32[]{:S(2)}) collective-permute-start(bf16[4,32,1536]{2,1,0:T(8,128)(2,1)S(1)} %get-tuple-element.31.refs_0_), channel_id=1, source_target_pairs={{0,2},{1,3},{2,0},{3,1},{4,6},{5,7},{6,4},{7,5},{8,10},{9,11},{10,... | collective-permute-start | bytes 1179656 | tf_op jit(solution)/shard_map/ppermute | solution.py:24
  4.5 1.3 %copy-done.2 = bf16[384,1536]{1,0:T(8,128)(2,1)S(1)} copy-done((bf16[384,1536]{1,0:T(8,128)(2,1)S(1)}, bf16[384,1536]{1,0:T(8,128)(2,1)}, u32[]{:S(2)}) %copy-start.2) | copy-done | bytes 1179672
  5.9 0.2 collective-permute-start.18
  6.0 2.0 %collective-permute-start.3 = (bf16[4,32,1536]{2,1,0:T(8,128)(2,1)S(1)}, bf16[4,32,1536]{2,1,0:T(8,128)(2,1)S(1)}, u32[]{:S(2)}, u32[]{:S(2)}) collective-permute-start(bf16[4,32,1536]{2,1,0:T(8,128)(2,1)S(1)} %get-tuple-element.32), channel_id=1, source_target_pairs={{0,4},{4,0},{8,12},{12,8},{1,5},{5,1},{9,13},{13,9},{2,6},{6,2},{1... | collective-permute-start | bytes 1179656 | tf_op jit(solution)/shard_map/ppermute | solution.py:24
  8.1 6.4 %collective-permute-done.1.refs_2_ = bf16[4,32,1536]{2,1,0:T(8,128)(2,1)S(1)} collective-permute-done((bf16[4,32,1536]{2,1,0:T(8,128)(2,1)S(1)}, bf16[4,32,1536]{2,1,0:T(8,128)(2,1)S(1)}, u32[]{:S(2)}, u32[]{:S(2)}) %collective-permute-start.1) | collective-permute-done | bytes 393248 | tf_op jit(solution)/shard_map/ppermute | solution.py:24
  14.5 0.7 copy-done.5
  15.2 0.7 copy-done.7
  15.9 0.2 shard_map.74.refs_1_
  16.2 2.1 %collective-permute-start.5 = (bf16[64,1536]{1,0:T(8,128)(2,1)S(1)}, bf16[64,1536]{1,0:T(8,128)(2,1)S(1)}, u32[]{:S(2)}, u32[]{:S(2)}) collective-permute-start(bf16[64,1536]{1,0:T(8,128)(2,1)S(1)} %shard_map.74.refs_1_), channel_id=1, source_target_pairs={{0,2},{1,3},{2,0},{3,1},{4,6},{5,7},{6,4},{7,5},{8,10},{9,11},{10,... | collective-permute-start | bytes 589832 | tf_op jit(solution)/shard_map/ppermute | solution.py:24
  18.2 5.9 %collective-permute-done.5.refs_3_ = bf16[64,1536]{1,0:T(8,128)(2,1)S(1)} collective-permute-done((bf16[64,1536]{1,0:T(8,128)(2,1)S(1)}, bf16[64,1536]{1,0:T(8,128)(2,1)S(1)}, u32[]{:S(2)}, u32[]{:S(2)}) %collective-permute-start.5) | collective-permute-done | bytes 196640 | tf_op jit(solution)/shard_map/ppermute | solution.py:24
  24.2 0.5 collective-permute-start.6
  24.7 1.8 %collective-permute-start.19 = (bf16[96,1536]{1,0:T(8,128)(2,1)S(1)}, bf16[96,1536]{1,0:T(8,128)(2,1)S(1)}, u32[]{:S(2)}, u32[]{:S(2)}) collective-permute-start(bf16[96,1536]{1,0:T(8,128)(2,1)S(1)} %collective-permute-done.18.own_ref), channel_id=1, source_target_pairs={{0,4},{4,0},{8,12},{12,8},{1,5},{5,1},{9,13},{13,9},{2,6},{6,2},{1... | collective-permute-start | bytes 884744 | tf_op jit(solution)/shard_map/ppermute | solution.py:24
  26.5 0.3 shard_map.75.refs_0_
  26.9 0.3 collective-permute-start.7
  27.1 2.8 %collective-permute-start.8 = (bf16[4,16,1536]{2,1,0:T(8,128)(2,1)S(1)}, bf16[4,16,1536]{2,1,0:T(8,128)(2,1)S(1)}, u32[]{:S(2)}, u32[]{:S(2)}) collective-permute-start(bf16[4,16,1536]{2,1,0:T(8,128)(2,1)S(1)} %get-tuple-element.38), channel_id=1, source_target_pairs={{0,8},{4,12},{8,0},{12,4},{1,9},{5,13},{9,1},{13,5},{2,10},{6,14},... | collective-permute-start | bytes 589832 | tf_op jit(solution)/shard_map/ppermute | solution.py:24
  30.0 1.1 %shard_map.73.refs_0_ = bf16[512,1536]{1,0:T(8,128)(2,1)S(1)} custom-call(bf16[4,32,1536]{2,1,0:T(8,128)(2,1)S(1)} %get-tuple-element.31.refs_0_, bf16[4,32,1536]{2,1,0:T(8,128)(2,1)S(1)} %collective-permute-done.refs_1_, bf16[4,32,1536]{2,1,0:T(8,128)(2,1)S(1)} %collective-permute-done.1.refs_2_, bf16[4,32,1536]{2,1,0:T(8,128)(2,1)S(1)} %collective-permute-done.2.refs_3_, ...), custom_call_target="tpu_custom_call" | custom-call | flops 7864320 | bytes 3145728 | tf_op jit(solution)/shard_map/pallas_call | solution.py:102
  31.1 1.4 %collective-permute-start.9 = (bf16[4,16,1536]{2,1,0:T(8,128)(2,1)S(1)}, bf16[4,16,1536]{2,1,0:T(8,128)(2,1)S(1)}, u32[]{:S(2)}, u32[]{:S(2)}) collective-permute-start(bf16[4,16,1536]{2,1,0:T(8,128)(2,1)S(1)} %get-tuple-element.39), channel_id=1, source_target_pairs={{0,12},{4,8},{8,4},{12,0},{1,13},{5,9},{9,5},{13,1},{2,14},{6,10},... | collective-permute-start | bytes 589832 | tf_op jit(solution)/shard_map/ppermute | solution.py:24
  32.6 1.5 %collective-permute-start.11 = (bf16[128,1536]{1,0:T(8,128)(2,1)S(1)}, bf16[128,1536]{1,0:T(8,128)(2,1)S(1)}, u32[]{:S(2)}, u32[]{:S(2)}) collective-permute-start(bf16[128,1536]{1,0:T(8,128)(2,1)S(1)} %shard_map.75.refs_0_), channel_id=1, source_target_pairs={{0,2},{1,3},{2,0},{3,1},{4,6},{5,7},{6,4},{7,5},{8,10},{9,11},{10,... | collective-permute-start | bytes 1179656 | tf_op jit(solution)/shard_map/ppermute | solution.py:24
  34.0 3.2 %shard_map.76 = (bf16[512,1152]{1,0:T(8,128)(2,1)S(1)}, bf16[256,1152]{1,0:T(8,128)(2,1)S(1)}) custom-call(bf16[512,1536]{1,0:T(8,128)(2,1)S(1)} %shard_map.73.refs_0_, bf16[64,1536]{1,0:T(8,128)(2,1)S(1)} %shard_map.74.refs_1_, bf16[64,1536]{1,0:T(8,128)(2,1)S(1)} %collective-permute-done.4.refs_2_, bf16[64,1536]{1,0:T(8,128)(2,1)S(1)} %collective-permute-done.5.refs_3_, ...), custom_call_target="tpu_custom_call" | custom-call | flops 2717908992 | bytes 7667712 | tf_op jit(solution)/shard_map/pallas_call | solution.py:197
  37.3 4.9 %collective-permute-done.7.refs_0_.refs_7_ = bf16[4,16,1536]{2,1,0:T(8,128)(2,1)S(1)} collective-permute-done((bf16[4,16,1536]{2,1,0:T(8,128)(2,1)S(1)}, bf16[4,16,1536]{2,1,0:T(8,128)(2,1)S(1)}, u32[]{:S(2)}, u32[]{:S(2)}) %collective-permute-start.7) | collective-permute-done | bytes 196640 | tf_op jit(solution)/shard_map/ppermute | solution.py:24
  42.2 0.2 collective-permute-done.8.refs_1_.refs_8_
  42.4 6.2 %collective-permute-done.9.refs_2_.refs_9_ = bf16[4,16,1536]{2,1,0:T(8,128)(2,1)S(1)} collective-permute-done((bf16[4,16,1536]{2,1,0:T(8,128)(2,1)S(1)}, bf16[4,16,1536]{2,1,0:T(8,128)(2,1)S(1)}, u32[]{:S(2)}, u32[]{:S(2)}) %collective-permute-start.9) | collective-permute-done | bytes 196640 | tf_op jit(solution)/shard_map/ppermute | solution.py:24
  48.6 0.4 shard_map.77.refs_0_
  49.0 1.6 %collective-permute-start.14 = (bf16[192,1536]{1,0:T(8,128)(2,1)S(1)}, bf16[192,1536]{1,0:T(8,128)(2,1)S(1)}, u32[]{:S(2)}, u32[]{:S(2)}) collective-permute-start(bf16[192,1536]{1,0:T(8,128)(2,1)S(1)} %shard_map.77.refs_0_), channel_id=1, source_target_pairs={{0,2},{1,3},{2,0},{3,1},{4,6},{5,7},{6,4},{7,5},{8,10},{9,11},{10,... | collective-permute-start | bytes 1769480 | tf_op jit(solution)/shard_map/ppermute | solution.py:24
  50.7 1.6 %collective-permute-start.20 = (bf16[192,1536]{1,0:T(8,128)(2,1)S(1)}, bf16[192,1536]{1,0:T(8,128)(2,1)S(1)}, u32[]{:S(2)}, u32[]{:S(2)}) collective-permute-start(bf16[192,1536]{1,0:T(8,128)(2,1)S(1)} %shard_map.83.own_ref), channel_id=1, source_target_pairs={{0,16},{16,0},{1,17},{17,1},{2,18},{18,2},{3,19},{19,3},{4,20},{20... | collective-permute-start | bytes 1769480 | tf_op jit(solution)/shard_map/ppermute | solution.py:24
  52.2 0.5 collective-permute-start.12
  52.8 10.8 %collective-permute-done.14.refs_2_ = bf16[192,1536]{1,0:T(8,128)(2,1)S(1)} collective-permute-done((bf16[192,1536]{1,0:T(8,128)(2,1)S(1)}, bf16[192,1536]{1,0:T(8,128)(2,1)S(1)}, u32[]{:S(2)}, u32[]{:S(2)}) %collective-permute-start.14) | collective-permute-done | bytes 589856 | tf_op jit(solution)/shard_map/ppermute | solution.py:24
  63.6 0.4 tags.1
  63.9 1.0 collective-permute-done.20.other_ref
  64.9 0.4 collective-permute-start.25
  65.3 0.1 shard_map.84.refs_6_.refs_2_
  65.4 0.1 collective-permute-start.21
  65.6 2.2 %shard_map.78.refs_1_ = bf16[512,1152]{1,0:T(8,128)(2,1)S(1)} custom-call(bf16[128,1536]{1,0:T(8,128)(2,1)S(1)} %shard_map.75.refs_0_, bf16[128,1536]{1,0:T(8,128)(2,1)S(1)} %collective-permute-done.10.refs_1_, bf16[128,1536]{1,0:T(8,128)(2,1)S(1)} %collective-permute-done.11.refs_2_, bf16[128,1536]{1,0:T(8,128)(2,1)S(1)} %collective-permute-done.12.refs_3_, ...), custom_call_target="tpu_custom_call" | custom-call | flops 1811939328 | bytes 6291456 | tf_op jit(solution)/shard_map/pallas_call | solution.py:197
  67.8 6.4 %shard_map.79 = (bf16[1,256,384]{2,1,0:T(8,128)(2,1)S(1)}, bf16[1,256,384]{2,1,0:T(8,128)(2,1)S(1)}, bf16[1,256,384]{2,1,0:T(8,128)(2,1)S(1)}, bf16[1,256,384]{2,1,0:T(8,128)(2,1)S(1)}) custom-call(bf16[512,1152]{1,0:T(8,128)(2,1)S(1)} %get-tuple-element.36.refs_0_, bf16[512,1152]{1,0:T(8,128)(2,1)S(1)} %shard_map.78.refs_1_, ...), custom_call_target="tpu_custom_call" | custom-call | flops 4294967296 | bytes 2359296 | tf_op jit(solution)/shard_map/pallas_call | solution.py:280
  74.3 0.5 collective-permute-start.22
  74.8 1.5 %collective-permute-start.23 = (bf16[1,256,384]{2,1,0:T(8,128)(2,1)S(1)}, bf16[1,256,384]{2,1,0:T(8,128)(2,1)S(1)}, u32[]{:S(2)}, u32[]{:S(2)}) collective-permute-start(bf16[1,256,384]{2,1,0:T(8,128)(2,1)S(1)} %get-tuple-element.45), channel_id=1, source_target_pairs={{0,2},{1,3},{2,0},{3,1},{4,6},{5,7},{6,4},{7,5},{8,10},{9,11},{10,... | collective-permute-start | bytes 589832 | tf_op jit(solution)/shard_map/ppermute | solution.py:24
  76.3 3.2 %shard_map.80.refs_1_ = bf16[768,1152]{1,0:T(8,128)(2,1)S(1)} custom-call(bf16[192,1536]{1,0:T(8,128)(2,1)S(1)} %shard_map.77.refs_0_, bf16[192,1536]{1,0:T(8,128)(2,1)S(1)} %collective-permute-done.13.refs_1_, bf16[192,1536]{1,0:T(8,128)(2,1)S(1)} %collective-permute-done.14.refs_2_, bf16[192,1536]{1,0:T(8,128)(2,1)S(1)} %collective-permute-done.15.refs_3_, ...), custom_call_target="tpu_custom_call" | custom-call | flops 2717908992 | bytes 7667712 | tf_op jit(solution)/shard_map/pallas_call | solution.py:197
  79.5 3.5 %shard_map.81 = (bf16[1,256,384]{2,1,0:T(8,128)(2,1)S(1)}, bf16[1,256,384]{2,1,0:T(8,128)(2,1)S(1)}) custom-call(bf16[256,1152]{1,0:T(8,128)(2,1)S(1)} %get-tuple-element.52.refs_0_, bf16[768,1152]{1,0:T(8,128)(2,1)S(1)} %shard_map.80.refs_1_, bf16[1024,128]{1,0:T(8,128)(2,1)S(1)} %get-tuple-element.48.refs_2_, ...), custom_call_target="tpu_custom_call" | custom-call | flops 2147483648 | bytes 2359296 | tf_op jit(solution)/shard_map/pallas_call | solution.py:280
  83.0 3.5 %shard_map.85 = (bf16[1,256,384]{2,1,0:T(8,128)(2,1)S(1)}, bf16[1,256,384]{2,1,0:T(8,128)(2,1)S(1)}) custom-call(bf16[256,1152]{1,0:T(8,128)(2,1)S(1)} %get-tuple-element.52.refs_0_, bf16[768,1152]{1,0:T(8,128)(2,1)S(1)} %shard_map.80.refs_1_, bf16[1024,128]{1,0:T(8,128)(2,1)S(1)} %get-tuple-element.48.refs_2_, ...), custom_call_target="tpu_custom_call" | custom-call | flops 2147483648 | bytes 2359296 | tf_op jit(solution)/shard_map/pallas_call | solution.py:280
  86.6 0.7 collective-permute-start.26
  87.3 1.5 %collective-permute-start.16 = (bf16[1,256,384]{2,1,0:T(8,128)(2,1)S(1)}, bf16[1,256,384]{2,1,0:T(8,128)(2,1)S(1)}, u32[]{:S(2)}, u32[]{:S(2)}) collective-permute-start(bf16[1,256,384]{2,1,0:T(8,128)(2,1)S(1)} %get-tuple-element.50), channel_id=1, source_target_pairs={{0,2},{1,3},{2,0},{3,1},{4,6},{5,7},{6,4},{7,5},{8,10},{9,11},{10,... | collective-permute-start | bytes 589832 | tf_op jit(solution)/shard_map/ppermute | solution.py:24
  88.8 1.8 %shard_map.86.refs_5_ = bf16[8,32,1536]{2,1,0:T(8,128)(2,1)S(1)} custom-call(bf16[256,384]{1,0:T(8,128)(2,1)S(1)} %bitcast.19, bf16[256,384]{1,0:T(8,128)(2,1)S(1)} %bitcast.20, bf16[256,384]{1,0:T(8,128)(2,1)S(1)} %bitcast.21, bf16[256,384]{1,0:T(8,128)(2,1)S(1)} %bitcast.22, bf16[384,1536]{1,0:T(8,128)(2,1)S(1)} %copy-done.3, ...), custom_call_target="tpu_custom_call" | custom-call | flops 1207959552 | bytes 7077888 | tf_op jit(solution)/shard_map/pallas_call | solution.py:337
  90.6 1.0 shard_map.87.refs_4_
  91.6 3.5 %collective-permute-done.16 = bf16[1,256,384]{2,1,0:T(8,128)(2,1)S(1)} collective-permute-done((bf16[1,256,384]{2,1,0:T(8,128)(2,1)S(1)}, bf16[1,256,384]{2,1,0:T(8,128)(2,1)S(1)}, u32[]{:S(2)}, u32[]{:S(2)}) %collective-permute-start.16) | collective-permute-done | bytes 196640 | tf_op jit(solution)/shard_map/ppermute | solution.py:24
  95.0 2.4 %collective-permute-done.17 = bf16[1,256,384]{2,1,0:T(8,128)(2,1)S(1)} collective-permute-done((bf16[1,256,384]{2,1,0:T(8,128)(2,1)S(1)}, bf16[1,256,384]{2,1,0:T(8,128)(2,1)S(1)}, u32[]{:S(2)}, u32[]{:S(2)}) %collective-permute-start.17) | collective-permute-done | bytes 196640 | tf_op jit(solution)/shard_map/ppermute | solution.py:24
  97.5 2.0 %shard_map.88 = bf16[8,64,1536]{2,1,0:T(8,128)(2,1)} custom-call(bf16[256,384]{1,0:T(8,128)(2,1)S(1)} %bitcast.23, bf16[256,384]{1,0:T(8,128)(2,1)S(1)} %bitcast.24, bf16[384,1536]{1,0:T(8,128)(2,1)S(1)} %shard_map.84.refs_6_.refs_2_, bf16[384,1536]{1,0:T(8,128)(2,1)S(1)} %collective-permute-done.21.refs_7_.refs_3_, f32[256,1536]{1,0:T(8,128)S(1)} %shard_map.87.refs_4_, ...), custom_call_target="tpu_custom_call" | custom-call | flops 603979776 | bytes 7077888 | tf_op jit(solution)/shard_map/pallas_call | solution.py:383
  (46 shorter events, 0.2 us)
Async XLA Ops:
  0.0 1.4 %copy-start = (bf16[1,8,1,64,1536]{4,3,2,1,0:T(8,128)(2,1)S(1)}, bf16[1,8,1,64,1536]{4,3,2,1,0:T(8,128)(2,1)}, u32[]{:S(2)}) copy-start(bf16[1,8,1,64,1536]{4,3,2,1,0:T(8,128)(2,1)} %param.7) | copy-start | bytes 4718596
  1.4 13.1 %copy-start.1 = (bf16[1,8,1,64,1536]{4,3,2,1,0:T(8,128)(2,1)S(1)}, bf16[1,8,1,64,1536]{4,3,2,1,0:T(8,128)(2,1)}, u32[]{:S(2)}) copy-start(bf16[1,8,1,64,1536]{4,3,2,1,0:T(8,128)(2,1)} %param.7) | copy-start | bytes 4718596
  1.5 13.0 %collective-permute-start.1 = (bf16[4,32,1536]{2,1,0:T(8,128)(2,1)S(1)}, bf16[4,32,1536]{2,1,0:T(8,128)(2,1)S(1)}, u32[]{:S(2)}, u32[]{:S(2)}) collective-permute-start(bf16[4,32,1536]{2,1,0:T(8,128)(2,1)S(1)} %get-tuple-element.31.refs_0_), channel_id=1, source_target_pairs={{0,2},{1,3},{2,0},{3,1},{4,6},{5,7},{6,4},{7,5},{8,10},{9,11},{10,... | collective-permute-start | bytes 1179656 | tf_op jit(solution)/shard_map/ppermute | solution.py:24
  4.5 1.3 %copy-start.2 = (bf16[384,1536]{1,0:T(8,128)(2,1)S(1)}, bf16[384,1536]{1,0:T(8,128)(2,1)}, u32[]{:S(2)}) copy-start(bf16[384,1536]{1,0:T(8,128)(2,1)} %refs_2_.5) | copy-start | bytes 3538948
  5.9 18.3 %collective-permute-start.18 = (bf16[96,1536]{1,0:T(8,128)(2,1)S(1)}, bf16[96,1536]{1,0:T(8,128)(2,1)S(1)}, u32[]{:S(2)}, u32[]{:S(2)}) collective-permute-start(bf16[96,1536]{1,0:T(8,128)(2,1)S(1)} %shard_map.82), channel_id=1, source_target_pairs={{0,2},{1,3},{2,0},{3,1},{4,6},{5,7},{6,4},{7,5},{8,10},{9,11},{10,... | collective-permute-start | bytes 884744 | tf_op jit(solution)/shard_map/ppermute | solution.py:24
  6.0 18.7 %collective-permute-start.3 = (bf16[4,32,1536]{2,1,0:T(8,128)(2,1)S(1)}, bf16[4,32,1536]{2,1,0:T(8,128)(2,1)S(1)}, u32[]{:S(2)}, u32[]{:S(2)}) collective-permute-start(bf16[4,32,1536]{2,1,0:T(8,128)(2,1)S(1)} %get-tuple-element.32), channel_id=1, source_target_pairs={{0,4},{4,0},{8,12},{12,8},{1,5},{5,1},{9,13},{13,9},{2,6},{6,2},{1... | collective-permute-start | bytes 1179656 | tf_op jit(solution)/shard_map/ppermute | solution.py:24
  8.1 18.8 %collective-permute-start = (bf16[4,32,1536]{2,1,0:T(8,128)(2,1)S(1)}, bf16[4,32,1536]{2,1,0:T(8,128)(2,1)S(1)}, u32[]{:S(2)}, u32[]{:S(2)}) collective-permute-start(bf16[4,32,1536]{2,1,0:T(8,128)(2,1)S(1)} %get-tuple-element.31.refs_0_), channel_id=1, source_target_pairs={{0,1},{1,0},{2,3},{3,2},{4,5},{5,4},{6,7},{7,6},{8,9},{9,8},{10,11... | collective-permute-start | bytes 1179656 | tf_op jit(solution)/shard_map/ppermute | solution.py:24
  14.5 12.6 %collective-permute-start.2 = (bf16[4,32,1536]{2,1,0:T(8,128)(2,1)S(1)}, bf16[4,32,1536]{2,1,0:T(8,128)(2,1)S(1)}, u32[]{:S(2)}, u32[]{:S(2)}) collective-permute-start(bf16[4,32,1536]{2,1,0:T(8,128)(2,1)S(1)} %collective-permute-done.1.refs_2_), channel_id=1, source_target_pairs={{0,1},{1,0},{2,3},{3,2},{4,5},{5,4},{6,7},{7,6},{8,9},{9,8},{10,11... | collective-permute-start | bytes 1179656 | tf_op jit(solution)/shard_map/ppermute | solution.py:24
  14.5 0.7 copy-start.5
  15.2 0.7 copy-start.7
  16.2 8.0 %collective-permute-start.5 = (bf16[64,1536]{1,0:T(8,128)(2,1)S(1)}, bf16[64,1536]{1,0:T(8,128)(2,1)S(1)}, u32[]{:S(2)}, u32[]{:S(2)}) collective-permute-start(bf16[64,1536]{1,0:T(8,128)(2,1)S(1)} %shard_map.74.refs_1_), channel_id=1, source_target_pairs={{0,2},{1,3},{2,0},{3,1},{4,6},{5,7},{6,4},{7,5},{8,10},{9,11},{10,... | collective-permute-start | bytes 589832 | tf_op jit(solution)/shard_map/ppermute | solution.py:24
  24.2 6.9 %collective-permute-start.4 = (bf16[64,1536]{1,0:T(8,128)(2,1)S(1)}, bf16[64,1536]{1,0:T(8,128)(2,1)S(1)}, u32[]{:S(2)}, u32[]{:S(2)}) collective-permute-start(bf16[64,1536]{1,0:T(8,128)(2,1)S(1)} %shard_map.74.refs_1_), channel_id=1, source_target_pairs={{0,1},{1,0},{2,3},{3,2},{4,5},{5,4},{6,7},{7,6},{8,9},{9,8},{10,11... | collective-permute-start | bytes 589832 | tf_op jit(solution)/shard_map/ppermute | solution.py:24
  24.2 8.4 %collective-permute-start.6 = (bf16[64,1536]{1,0:T(8,128)(2,1)S(1)}, bf16[64,1536]{1,0:T(8,128)(2,1)S(1)}, u32[]{:S(2)}, u32[]{:S(2)}) collective-permute-start(bf16[64,1536]{1,0:T(8,128)(2,1)S(1)} %collective-permute-done.5.refs_3_), channel_id=1, source_target_pairs={{0,1},{1,0},{2,3},{3,2},{4,5},{5,4},{6,7},{7,6},{8,9},{9,8},{10,11... | collective-permute-start | bytes 589832 | tf_op jit(solution)/shard_map/ppermute | solution.py:24
  24.7 25.9 %collective-permute-start.19 = (bf16[96,1536]{1,0:T(8,128)(2,1)S(1)}, bf16[96,1536]{1,0:T(8,128)(2,1)S(1)}, u32[]{:S(2)}, u32[]{:S(2)}) collective-permute-start(bf16[96,1536]{1,0:T(8,128)(2,1)S(1)} %collective-permute-done.18.own_ref), channel_id=1, source_target_pairs={{0,4},{4,0},{8,12},{12,8},{1,5},{5,1},{9,13},{13,9},{2,6},{6,2},{1... | collective-permute-start | bytes 884744 | tf_op jit(solution)/shard_map/ppermute | solution.py:24
  26.5 7.5 %copy-start.4 = (bf16[3,1536,384]{2,1,0:T(8,128)(2,1)S(1)}, bf16[3,1536,384]{2,1,0:T(8,128)(2,1)}, u32[]{:S(2)}) copy-start(bf16[3,1536,384]{2,1,0:T(8,128)(2,1)} %refs_4_.12) | copy-start | bytes 10616836
  26.9 15.3 %collective-permute-start.7 = (bf16[4,16,1536]{2,1,0:T(8,128)(2,1)S(1)}, bf16[4,16,1536]{2,1,0:T(8,128)(2,1)S(1)}, u32[]{:S(2)}, u32[]{:S(2)}) collective-permute-start(bf16[4,16,1536]{2,1,0:T(8,128)(2,1)S(1)} %get-tuple-element.35), channel_id=1, source_target_pairs={{0,4},{4,0},{8,12},{12,8},{1,5},{5,1},{9,13},{13,9},{2,6},{6,2},{1... | collective-permute-start | bytes 589832 | tf_op jit(solution)/shard_map/ppermute | solution.py:24
  27.1 15.3 %collective-permute-start.8 = (bf16[4,16,1536]{2,1,0:T(8,128)(2,1)S(1)}, bf16[4,16,1536]{2,1,0:T(8,128)(2,1)S(1)}, u32[]{:S(2)}, u32[]{:S(2)}) collective-permute-start(bf16[4,16,1536]{2,1,0:T(8,128)(2,1)S(1)} %get-tuple-element.38), channel_id=1, source_target_pairs={{0,8},{4,12},{8,0},{12,4},{1,9},{5,13},{9,1},{13,5},{2,10},{6,14},... | collective-permute-start | bytes 589832 | tf_op jit(solution)/shard_map/ppermute | solution.py:24
  31.1 17.5 %copy-start.6 = (f32[1536]{0:T(1024)S(1)}, f32[1536]{0:T(1024)}, u32[]{:S(2)}) copy-start(f32[1536]{0:T(1024)} %refs_3_.1) | copy-start | bytes 18436
  31.1 17.5 %copy-start.8 = (f32[1536]{0:T(1024)S(1)}, f32[1536]{0:T(1024)}, u32[]{:S(2)}) copy-start(f32[1536]{0:T(1024)} %refs_4_.9) | copy-start | bytes 18436
  31.1 17.5 %collective-permute-start.9 = (bf16[4,16,1536]{2,1,0:T(8,128)(2,1)S(1)}, bf16[4,16,1536]{2,1,0:T(8,128)(2,1)S(1)}, u32[]{:S(2)}, u32[]{:S(2)}) collective-permute-start(bf16[4,16,1536]{2,1,0:T(8,128)(2,1)S(1)} %get-tuple-element.39), channel_id=1, source_target_pairs={{0,12},{4,8},{8,4},{12,0},{1,13},{5,9},{9,5},{13,1},{2,14},{6,10},... | collective-permute-start | bytes 589832 | tf_op jit(solution)/shard_map/ppermute | solution.py:24
  32.6 19.7 %collective-permute-start.11 = (bf16[128,1536]{1,0:T(8,128)(2,1)S(1)}, bf16[128,1536]{1,0:T(8,128)(2,1)S(1)}, u32[]{:S(2)}, u32[]{:S(2)}) collective-permute-start(bf16[128,1536]{1,0:T(8,128)(2,1)S(1)} %shard_map.75.refs_0_), channel_id=1, source_target_pairs={{0,2},{1,3},{2,0},{3,1},{4,6},{5,7},{6,4},{7,5},{8,10},{9,11},{10,... | collective-permute-start | bytes 1179656 | tf_op jit(solution)/shard_map/ppermute | solution.py:24
  37.3 26.2 %copy-start.9 = (s32[1,32,64]{2,1,0:T(8,128)S(1)}, s32[1,32,64]{2,1,0:T(8,128)}, u32[]{:S(2)}) copy-start(s32[1,32,64]{2,1,0:T(8,128)} %param.8) | copy-start | bytes 24580
  49.0 14.5 %collective-permute-start.14 = (bf16[192,1536]{1,0:T(8,128)(2,1)S(1)}, bf16[192,1536]{1,0:T(8,128)(2,1)S(1)}, u32[]{:S(2)}, u32[]{:S(2)}) collective-permute-start(bf16[192,1536]{1,0:T(8,128)(2,1)S(1)} %shard_map.77.refs_0_), channel_id=1, source_target_pairs={{0,2},{1,3},{2,0},{3,1},{4,6},{5,7},{6,4},{7,5},{8,10},{9,11},{10,... | collective-permute-start | bytes 1769480 | tf_op jit(solution)/shard_map/ppermute | solution.py:24
  50.7 14.2 %collective-permute-start.20 = (bf16[192,1536]{1,0:T(8,128)(2,1)S(1)}, bf16[192,1536]{1,0:T(8,128)(2,1)S(1)}, u32[]{:S(2)}, u32[]{:S(2)}) collective-permute-start(bf16[192,1536]{1,0:T(8,128)(2,1)S(1)} %shard_map.83.own_ref), channel_id=1, source_target_pairs={{0,16},{16,0},{1,17},{17,1},{2,18},{18,2},{3,19},{19,3},{4,20},{20... | collective-permute-start | bytes 1769480 | tf_op jit(solution)/shard_map/ppermute | solution.py:24
  52.2 13.2 %collective-permute-start.10 = (bf16[128,1536]{1,0:T(8,128)(2,1)S(1)}, bf16[128,1536]{1,0:T(8,128)(2,1)S(1)}, u32[]{:S(2)}, u32[]{:S(2)}) collective-permute-start(bf16[128,1536]{1,0:T(8,128)(2,1)S(1)} %shard_map.75.refs_0_), channel_id=1, source_target_pairs={{0,1},{1,0},{2,3},{3,2},{4,5},{5,4},{6,7},{7,6},{8,9},{9,8},{10,11... | collective-permute-start | bytes 1179656 | tf_op jit(solution)/shard_map/ppermute | solution.py:24
  52.2 13.3 %collective-permute-start.12 = (bf16[128,1536]{1,0:T(8,128)(2,1)S(1)}, bf16[128,1536]{1,0:T(8,128)(2,1)S(1)}, u32[]{:S(2)}, u32[]{:S(2)}) collective-permute-start(bf16[128,1536]{1,0:T(8,128)(2,1)S(1)} %collective-permute-done.11.refs_2_), channel_id=1, source_target_pairs={{0,1},{1,0},{2,3},{3,2},{4,5},{5,4},{6,7},{7,6},{8,9},{9,8},{10,11... | collective-permute-start | bytes 1179656 | tf_op jit(solution)/shard_map/ppermute | solution.py:24
  52.8 22.0 %collective-permute-start.13 = (bf16[192,1536]{1,0:T(8,128)(2,1)S(1)}, bf16[192,1536]{1,0:T(8,128)(2,1)S(1)}, u32[]{:S(2)}, u32[]{:S(2)}) collective-permute-start(bf16[192,1536]{1,0:T(8,128)(2,1)S(1)} %shard_map.77.refs_0_), channel_id=1, source_target_pairs={{0,1},{1,0},{2,3},{3,2},{4,5},{5,4},{6,7},{7,6},{8,9},{9,8},{10,11... | collective-permute-start | bytes 1769480 | tf_op jit(solution)/shard_map/ppermute | solution.py:24
  63.5 12.7 %collective-permute-start.15 = (bf16[192,1536]{1,0:T(8,128)(2,1)S(1)}, bf16[192,1536]{1,0:T(8,128)(2,1)S(1)}, u32[]{:S(2)}, u32[]{:S(2)}) collective-permute-start(bf16[192,1536]{1,0:T(8,128)(2,1)S(1)} %collective-permute-done.14.refs_2_), channel_id=1, source_target_pairs={{0,1},{1,0},{2,3},{3,2},{4,5},{5,4},{6,7},{7,6},{8,9},{9,8},{10,11... | collective-permute-start | bytes 1769480 | tf_op jit(solution)/shard_map/ppermute | solution.py:24
  63.5 1.3 %copy-start.3 = (bf16[384,1536]{1,0:T(8,128)(2,1)S(1)}, bf16[384,1536]{1,0:T(8,128)(2,1)}, u32[]{:S(2)}) copy-start(bf16[384,1536]{1,0:T(8,128)(2,1)} %refs_2_.5) | copy-start | bytes 3538948
  64.9 21.7 %collective-permute-start.25 = (bf16[384,1536]{1,0:T(8,128)(2,1)S(1)}, bf16[384,1536]{1,0:T(8,128)(2,1)S(1)}, u32[]{:S(2)}, u32[]{:S(2)}) collective-permute-start(bf16[384,1536]{1,0:T(8,128)(2,1)S(1)} %copy-done.3), channel_id=1, source_target_pairs={{0,1},{1,0},{2,3},{3,2},{4,5},{5,4},{6,7},{7,6},{8,9},{9,8},{10,11... | collective-permute-start | bytes 3538952 | tf_op jit(solution)/shard_map/ppermute | solution.py:24
  65.4 2.4 %copy-start.10 = (f32[4]{0:T(128)S(1)}, f32[4]{0:T(128)}, u32[]{:S(2)}) copy-start(f32[4]{0:T(128)} %refs_4_.14) | copy-start | bytes 52
  65.4 23.3 %collective-permute-start.21 = (bf16[384,1536]{1,0:T(8,128)(2,1)S(1)}, bf16[384,1536]{1,0:T(8,128)(2,1)S(1)}, u32[]{:S(2)}, u32[]{:S(2)}) collective-permute-start(bf16[384,1536]{1,0:T(8,128)(2,1)S(1)} %shard_map.84.refs_6_.refs_2_), channel_id=1, source_target_pairs={{0,1},{1,0},{2,3},{3,2},{4,5},{5,4},{6,7},{7,6},{8,9},{9,8},{10,11... | collective-permute-start | bytes 3538952 | tf_op jit(solution)/shard_map/ppermute | solution.py:24
  74.3 13.0 %collective-permute-start.22 = (bf16[1,256,384]{2,1,0:T(8,128)(2,1)S(1)}, bf16[1,256,384]{2,1,0:T(8,128)(2,1)S(1)}, u32[]{:S(2)}, u32[]{:S(2)}) collective-permute-start(bf16[1,256,384]{2,1,0:T(8,128)(2,1)S(1)} %get-tuple-element.44), channel_id=1, source_target_pairs={{0,1},{1,0},{2,3},{3,2},{4,5},{5,4},{6,7},{7,6},{8,9},{9,8},{10,11... | collective-permute-start | bytes 589832 | tf_op jit(solution)/shard_map/ppermute | solution.py:24
  74.8 14.0 %collective-permute-start.23 = (bf16[1,256,384]{2,1,0:T(8,128)(2,1)S(1)}, bf16[1,256,384]{2,1,0:T(8,128)(2,1)S(1)}, u32[]{:S(2)}, u32[]{:S(2)}) collective-permute-start(bf16[1,256,384]{2,1,0:T(8,128)(2,1)S(1)} %get-tuple-element.45), channel_id=1, source_target_pairs={{0,2},{1,3},{2,0},{3,1},{4,6},{5,7},{6,4},{7,5},{8,10},{9,11},{10,... | collective-permute-start | bytes 589832 | tf_op jit(solution)/shard_map/ppermute | solution.py:24
  76.3 12.5 %collective-permute-start.24 = (bf16[1,256,384]{2,1,0:T(8,128)(2,1)S(1)}, bf16[1,256,384]{2,1,0:T(8,128)(2,1)S(1)}, u32[]{:S(2)}, u32[]{:S(2)}) collective-permute-start(bf16[1,256,384]{2,1,0:T(8,128)(2,1)S(1)} %get-tuple-element.46), channel_id=1, source_target_pairs={{0,3},{1,2},{2,1},{3,0},{4,7},{5,6},{6,5},{7,4},{8,11},{9,10},{10,... | collective-permute-start | bytes 589832 | tf_op jit(solution)/shard_map/ppermute | solution.py:24
  86.6 4.0 %collective-permute-start.26 = (bf16[1,256,384]{2,1,0:T(8,128)(2,1)S(1)}, bf16[1,256,384]{2,1,0:T(8,128)(2,1)S(1)}, u32[]{:S(2)}, u32[]{:S(2)}) collective-permute-start(bf16[1,256,384]{2,1,0:T(8,128)(2,1)S(1)} %get-tuple-element.54), channel_id=1, source_target_pairs={{0,1},{1,0},{2,3},{3,2},{4,5},{5,4},{6,7},{7,6},{8,9},{9,8},{10,11... | collective-permute-start | bytes 589832 | tf_op jit(solution)/shard_map/ppermute | solution.py:24
  87.3 7.8 %collective-permute-start.16 = (bf16[1,256,384]{2,1,0:T(8,128)(2,1)S(1)}, bf16[1,256,384]{2,1,0:T(8,128)(2,1)S(1)}, u32[]{:S(2)}, u32[]{:S(2)}) collective-permute-start(bf16[1,256,384]{2,1,0:T(8,128)(2,1)S(1)} %get-tuple-element.50), channel_id=1, source_target_pairs={{0,2},{1,3},{2,0},{3,1},{4,6},{5,7},{6,4},{7,5},{8,10},{9,11},{10,... | collective-permute-start | bytes 589832 | tf_op jit(solution)/shard_map/ppermute | solution.py:24
  88.8 8.7 %collective-permute-start.17 = (bf16[1,256,384]{2,1,0:T(8,128)(2,1)S(1)}, bf16[1,256,384]{2,1,0:T(8,128)(2,1)S(1)}, u32[]{:S(2)}, u32[]{:S(2)}) collective-permute-start(bf16[1,256,384]{2,1,0:T(8,128)(2,1)S(1)} %get-tuple-element.51), channel_id=1, source_target_pairs={{0,3},{1,2},{2,1},{3,0},{4,7},{5,6},{6,5},{7,4},{8,11},{9,10},{10,... | collective-permute-start | bytes 589832 | tf_op jit(solution)/shard_map/ppermute | solution.py:24

commit v5 on v4

--- a/solution.py
+++ b/solution.py
@@ -208,21 +208,25 @@
     )(*[piece for group in groups for piece in group], weights)
 
 
-def attend_kernel(count, parts, ranges, head_width, *refs):
+def attend_kernel(layout, ranges, head_width, *refs):
+    parts = len(layout)
     blocks = refs[:parts]
     query_tags, key_tags, scale_ref = refs[parts : parts + 3]
     outs = refs[parts + 3 :]
     slot = padded(head_width)
-    sizes = [block.shape[0] // count for block in blocks]
     low, high = min(lo for lo, _ in ranges), max(hi for _, hi in ranges)
     heads = head_width // CHANNEL_PER_PART
     base = math.log2(math.e) / math.sqrt(CHANNEL_PER_PART)
     tiles = [None] * (slot // LANE)
     key_rows = key_tags[...]
-    query_rows, at = [], 0
-    for z in sizes:
-        query_rows.append(query_tags[at + low * z : at + high * z, :])
-        at += count * z
+    runs, query_rows, at = [], [], 0
+    for block, (lo, hi) in zip(blocks, layout, strict=True):
+        z = block.shape[0] // (hi - lo)
+        first, last = max(low, lo), min(high, hi)
+        if first < last:
+            runs.append((block, (first - lo) * z, (last - lo) * z, z, first, last))
+            query_rows.append(query_tags[at + (first - lo) * z : at + (last - lo) * z, :])
+        at += block.shape[0]
     query_rows = jnp.concatenate(query_rows, axis=0)
 
     def span(head):
@@ -235,9 +239,7 @@
     def scores_of(head):
         left, right, inside = span(head)
         reps = (right - left) // LANE
-        queries = jnp.concatenate(
-            [b[low * z : high * z, left:right] for b, z in zip(blocks, sizes, strict=True)], axis=0
-        )
+        queries = jnp.concatenate([run[0][run[1] : run[2], left:right] for run in runs], axis=0)
         queries = jnp.where(inside, queries, jnp.concatenate([query_rows] * reps, axis=1))
         keys = jnp.concatenate([b[:, slot + left : slot + right] for b in blocks], axis=0)
         keys = jnp.where(inside, keys, jnp.concatenate([key_rows] * reps, axis=1))
@@ -260,30 +262,33 @@
             held = tiles[tile]
             tiles[tile] = own if held is None else jnp.where(inside[:, i * LANE : (i + 1) * LANE], own, held)
     result = jnp.concatenate(tiles, axis=1)[:, :head_width].astype(BF16)
-    for out_ref, (lo, hi) in zip(outs, ranges, strict=True):
-        for offset in range(lo, hi):
-            start, into = 0, 0
-            for z in sizes:
-                at = start + (offset - low) * z
-                out_ref[offset - lo, into : into + z, :] = result[at : at + z]
-                start += (high - low) * z
-                into += z
-
-
-def attend(blocks, query_tags, key_tags, scales, count, ranges, head_width):
-    parts = len(blocks)
-    per_offset = sum(b.shape[0] for b in blocks) // count
-    pixels = count * per_offset
+    places = {
+        offset: (out_ref, offset - lo)
+        for out_ref, (lo, hi) in zip(outs, ranges, strict=True)
+        for offset in range(lo, hi)
+    }
+    into = dict.fromkeys(places, 0)
+    at = 0
+    for _, _, _, z, first, last in runs:
+        for offset in range(first, last):
+            out_ref, index = places[offset]
+            out_ref[index, into[offset] : into[offset] + z, :] = result[at : at + z]
+            into[offset] += z
+            at += z
+
+
+def attend(blocks, layout, query_tags, key_tags, scales, count, ranges, head_width):
+    pixels = sum(block.shape[0] for block in blocks)
+    per_offset = pixels // count
     asked = sum(hi - lo for lo, hi in ranges) * per_offset
-    vmem = pl.BlockSpec(memory_space=pltpu.VMEM)
     heads = head_width // CHANNEL_PER_PART
     return pl.pallas_call(
-        functools.partial(attend_kernel, count, parts, ranges, head_width),
+        functools.partial(attend_kernel, layout, ranges, head_width),
         out_shape=[
             jax.ShapeDtypeStruct((hi - lo, per_offset, head_width), BF16) for lo, hi in ranges
         ],
-        in_specs=[vmem] * (parts + 2) + [pl.BlockSpec(memory_space=pltpu.SMEM)],
-        out_specs=[vmem] * len(ranges),
+        in_specs=[VMEM] * (len(blocks) + 2) + [pl.BlockSpec(memory_space=pltpu.SMEM)],
+        out_specs=[VMEM] * len(ranges),
         compiler_params=pltpu.CompilerParams(vmem_limit_bytes=28 << 20),
         cost_estimate=pl.CostEstimate(
             flops=4 * heads * asked * pixels * 2 * LANE,
@@ -498,8 +503,9 @@
     weights = triple_projection_matrix
     scales = logit_scaling_per_part
 
-    boxes = [(rows, half, WS), (0, half, WS), (0, half + WS, near), (rows, 0, half), (0, 0, half)]
-    local_0, south_0, south_1, east, corner = cut(blocked, rows, boxes)
+    local_0 = blocked[rows:, half : half + WS]
+    boxes = [(0, half, WS), (0, half + WS, near), (rows, 0, half), (0, 0, half)]
+    south_0, south_1, east, corner = cut(blocked, rows, boxes)
     spans = [(0, rows + row, half + WS, near) for row in range(rows)]
     (local_1,) = norm([blocked], gain, bias, [spans])
     south_0 = exchange(south_0, 1, "win")
@@ -522,21 +528,25 @@
     spans += [(which, row, 0, half) for which in (1, 2) for row in range(rows)]
     (rest_normed,) = norm([after(south_1, local_0), east, corner], gain, bias, [spans])
     rest_pieces = gather_pieces(rest_normed)
-    south_pieces[0] = after(south_normed, local_0)
-    (south_0_projected,) = project([south_pieces], weights)
-
-    def attend_run(blocks, tags, earlier, lo, hi):
+    split = count // 2
+    near_lanes, far_lanes, all_lanes = (0, split), (split, count), (0, count)
+    (south_near,) = project([south_pieces[:split]], weights)
+    south_pieces[split] = after(south_pieces[split], south_near)
+    (south_far,) = project([south_pieces[split:]], weights)
+    (rest_near,) = project([rest_pieces[:split]], weights)
+
+    def attend_run(blocks, layout, tags, earlier, lo, hi):
         blocks = [after(blocks[0], *earlier), *blocks[1:]]
-        return list(attend(blocks, *tags, scales, count, [(i, i + 1) for i in range(lo, hi)], head_width))
-
-    split = count // 2
-    blocks, tags = [local_0, south_0_projected], (query_0, key_0)
-    outs_0 = attend_run(blocks, tags, [], 0, count)
-    rest_pieces[0] = after(rest_normed, *outs_0)
-    (rest_projected,) = project([rest_pieces], weights)
-    blocks, tags = [local_1, rest_projected], (query_1, key_1)
-    far = attend_run(blocks, tags, [], split, count)
-    close = attend_run(blocks, tags, far, 0, split)
+        singles = [(i, i + 1) for i in range(lo, hi)]
+        return list(attend(blocks, layout, *tags, scales, count, singles, head_width))
+
+    blocks, layout, tags = [local_0, south_near, south_far], [all_lanes, near_lanes, far_lanes], (query_0, key_0)
+    outs_0 = attend_run(blocks, layout, tags, [], 0, count)
+    rest_pieces[split] = after(rest_pieces[split], *outs_0)
+    (rest_far,) = project([rest_pieces[split:]], weights)
+    blocks, layout, tags = [local_1, rest_near, rest_far], [all_lanes, near_lanes, far_lanes], (query_1, key_1)
+    far = attend_run(blocks, layout, tags, [], split, count)
+    close = attend_run(blocks, layout, tags, far, 0, split)
     outs_1 = close + far
 
     first = send_heads(outs_0)

time: 100 us -> 92.8 us (0.928)
  the two profiles are of different devices: /device:TPU:0 before, /device:TPU:17 now
where the time goes in v5:
time: 92.8 us; the launch traced here: 92.6 us
  waiting for transfers between devices  30.3 us (33%)
  Pallas kernels  30 us (32%)
  starting transfers between devices  29 us (31%)
  local copies, waits for them, and re-layouts  2.88 us (3%)
    ppermute x27, waiting for transfers between devices, permute_by(): return lax.ppermute(value, axis, pairs)  30.3 us
    ppermute x27, starting transfers between devices, permute_by(): return lax.ppermute(value, axis, pairs)  29 us
    pallas_call x3, Pallas kernels, attend(): pl.pallas_call(functools.partial(attend_kernel, layout, ranges, head_widt...  13.5 us
    pallas_call x5, Pallas kernels, project(): pl.pallas_call(functools.partial(project_kernel, [len(group) for group in...  8.99 us
    pallas_call x4, Pallas kernels, norm(): pl.pallas_call(functools.partial(norm_kernel, groups), out_shape=[jax.Sha...  2.11 us
    pallas_call x1, Pallas kernels, finish_last(): pl.pallas_call(functools.partial(last_kernel, count, chunks, spans), out_...  2.06 us
  transfers between devices with their start and end apart: 27, of which 8 were waited for; matrix products, arithmetic and copies ran while one was open for 0% of the time, Pallas kernels for 30%

profile of v5, /device:TPU:17, one launch (start us, length us, event | category | flops | bytes accessed | tf_op | source)
XLA Modules:
  0.0 92.6 jit_solution(172421734197399187)
XLA Ops:
  0.0 1.1 %slice.4.refs_0_ = bf16[4,32,1536]{2,1,0:T(8,128)(2,1)S(1)} slice(bf16[8,64,1536]{2,1,0:T(8,128)(2,1)} %bitcast.13), slice={[4:8], [16:48], [0:1536]} | slice | bytes 786432 | tf_op jit(solution)/shard_map/slice | solution.py:506
  1.1 1.3 %collective-permute-start.1 = (bf16[4,32,1536]{2,1,0:T(8,128)(2,1)S(1)}, bf16[4,32,1536]{2,1,0:T(8,128)(2,1)S(1)}, u32[]{:S(2)}, u32[]{:S(2)}) collective-permute-start(bf16[4,32,1536]{2,1,0:T(8,128)(2,1)S(1)} %slice.4.refs_0_), channel_id=1, source_target_pairs={{0,2},{1,3},{2,0},{3,1},{4,6},{5,7},{6,4},{7,5},{8,10},{9,11},{10,... | collective-permute-start | bytes 1179656 | tf_op jit(solution)/shard_map/ppermute | solution.py:24
  2.4 1.3 %copy-done.2 = bf16[384,1536]{1,0:T(8,128)(2,1)S(1)} copy-done((bf16[384,1536]{1,0:T(8,128)(2,1)S(1)}, bf16[384,1536]{1,0:T(8,128)(2,1)}, u32[]{:S(2)}) %copy-start.2) | copy-done | bytes 1179672
  3.8 0.3 collective-permute-start.18
  4.2 1.4 %collective-permute-start.3 = (bf16[4,32,1536]{2,1,0:T(8,128)(2,1)S(1)}, bf16[4,32,1536]{2,1,0:T(8,128)(2,1)S(1)}, u32[]{:S(2)}, u32[]{:S(2)}) collective-permute-start(bf16[4,32,1536]{2,1,0:T(8,128)(2,1)S(1)} %get-tuple-element.30), channel_id=1, source_target_pairs={{0,4},{4,0},{8,12},{12,8},{1,5},{5,1},{9,13},{13,9},{2,6},{6,2},{1... | collective-permute-start | bytes 1179656 | tf_op jit(solution)/shard_map/ppermute | solution.py:24
  5.5 1.5 %collective-permute-start = (bf16[4,32,1536]{2,1,0:T(8,128)(2,1)S(1)}, bf16[4,32,1536]{2,1,0:T(8,128)(2,1)S(1)}, u32[]{:S(2)}, u32[]{:S(2)}) collective-permute-start(bf16[4,32,1536]{2,1,0:T(8,128)(2,1)S(1)} %slice.4.refs_0_), channel_id=1, source_target_pairs={{0,1},{1,0},{2,3},{3,2},{4,5},{5,4},{6,7},{7,6},{8,9},{9,8},{10,11... | collective-permute-start | bytes 1179656 | tf_op jit(solution)/shard_map/ppermute | solution.py:24
  7.0 4.2 %collective-permute-done.1.refs_2_ = bf16[4,32,1536]{2,1,0:T(8,128)(2,1)S(1)} collective-permute-done((bf16[4,32,1536]{2,1,0:T(8,128)(2,1)S(1)}, bf16[4,32,1536]{2,1,0:T(8,128)(2,1)S(1)}, u32[]{:S(2)}, u32[]{:S(2)}) %collective-permute-start.1) | collective-permute-done | bytes 393248 | tf_op jit(solution)/shard_map/ppermute | solution.py:24
  11.2 2.7 %collective-permute-start.2 = (bf16[4,32,1536]{2,1,0:T(8,128)(2,1)S(1)}, bf16[4,32,1536]{2,1,0:T(8,128)(2,1)S(1)}, u32[]{:S(2)}, u32[]{:S(2)}) collective-permute-start(bf16[4,32,1536]{2,1,0:T(8,128)(2,1)S(1)} %collective-permute-done.1.refs_2_), channel_id=1, source_target_pairs={{0,1},{1,0},{2,3},{3,2},{4,5},{5,4},{6,7},{7,6},{8,9},{9,8},{10,11... | collective-permute-start | bytes 1179656 | tf_op jit(solution)/shard_map/ppermute | solution.py:24
  13.9 0.2 shard_map.74.refs_1_
  14.1 1.3 %collective-permute-start.5 = (bf16[64,1536]{1,0:T(8,128)(2,1)S(1)}, bf16[64,1536]{1,0:T(8,128)(2,1)S(1)}, u32[]{:S(2)}, u32[]{:S(2)}) collective-permute-start(bf16[64,1536]{1,0:T(8,128)(2,1)S(1)} %shard_map.74.refs_1_), channel_id=1, source_target_pairs={{0,2},{1,3},{2,0},{3,1},{4,6},{5,7},{6,4},{7,5},{8,10},{9,11},{10,... | collective-permute-start | bytes 589832 | tf_op jit(solution)/shard_map/ppermute | solution.py:24
  15.4 2.1 %collective-permute-done.18.own_ref = bf16[96,1536]{1,0:T(8,128)(2,1)S(1)} collective-permute-done((bf16[96,1536]{1,0:T(8,128)(2,1)S(1)}, bf16[96,1536]{1,0:T(8,128)(2,1)S(1)}, u32[]{:S(2)}, u32[]{:S(2)}) %collective-permute-start.18) | collective-permute-done | bytes 294944 | tf_op jit(solution)/shard_map/ppermute | solution.py:24
  17.5 1.3 %collective-permute-start.19 = (bf16[96,1536]{1,0:T(8,128)(2,1)S(1)}, bf16[96,1536]{1,0:T(8,128)(2,1)S(1)}, u32[]{:S(2)}, u32[]{:S(2)}) collective-permute-start(bf16[96,1536]{1,0:T(8,128)(2,1)S(1)} %collective-permute-done.18.own_ref), channel_id=1, source_target_pairs={{0,4},{4,0},{8,12},{12,8},{1,5},{5,1},{9,13},{13,9},{2,6},{6,2},{1... | collective-permute-start | bytes 884744 | tf_op jit(solution)/shard_map/ppermute | solution.py:24
  18.8 2.9 %collective-permute-done.5.refs_3_ = bf16[64,1536]{1,0:T(8,128)(2,1)S(1)} collective-permute-done((bf16[64,1536]{1,0:T(8,128)(2,1)S(1)}, bf16[64,1536]{1,0:T(8,128)(2,1)S(1)}, u32[]{:S(2)}, u32[]{:S(2)}) %collective-permute-start.5) | collective-permute-done | bytes 196640 | tf_op jit(solution)/shard_map/ppermute | solution.py:24
  21.7 1.5 %collective-permute-start.4 = (bf16[64,1536]{1,0:T(8,128)(2,1)S(1)}, bf16[64,1536]{1,0:T(8,128)(2,1)S(1)}, u32[]{:S(2)}, u32[]{:S(2)}) collective-permute-start(bf16[64,1536]{1,0:T(8,128)(2,1)S(1)} %shard_map.74.refs_1_), channel_id=1, source_target_pairs={{0,1},{1,0},{2,3},{3,2},{4,5},{5,4},{6,7},{7,6},{8,9},{9,8},{10,11... | collective-permute-start | bytes 589832 | tf_op jit(solution)/shard_map/ppermute | solution.py:24
  23.3 0.3 shard_map.75.refs_0_
  23.6 1.4 %collective-permute-start.7 = (bf16[4,16,1536]{2,1,0:T(8,128)(2,1)S(1)}, bf16[4,16,1536]{2,1,0:T(8,128)(2,1)S(1)}, u32[]{:S(2)}, u32[]{:S(2)}) collective-permute-start(bf16[4,16,1536]{2,1,0:T(8,128)(2,1)S(1)} %get-tuple-element.33), channel_id=1, source_target_pairs={{0,4},{4,0},{8,12},{12,8},{1,5},{5,1},{9,13},{13,9},{2,6},{6,2},{1... | collective-permute-start | bytes 589832 | tf_op jit(solution)/shard_map/ppermute | solution.py:24
  25.2 1.3 %collective-permute-start.9 = (bf16[4,16,1536]{2,1,0:T(8,128)(2,1)S(1)}, bf16[4,16,1536]{2,1,0:T(8,128)(2,1)S(1)}, u32[]{:S(2)}, u32[]{:S(2)}) collective-permute-start(bf16[4,16,1536]{2,1,0:T(8,128)(2,1)S(1)} %get-tuple-element.37), channel_id=1, source_target_pairs={{0,12},{4,8},{8,4},{12,0},{1,13},{5,9},{9,5},{13,1},{2,14},{6,10},... | collective-permute-start | bytes 589832 | tf_op jit(solution)/shard_map/ppermute | solution.py:24
  26.5 1.1 %shard_map.73.refs_0_ = bf16[512,1536]{1,0:T(8,128)(2,1)S(1)} custom-call(bf16[4,32,1536]{2,1,0:T(8,128)(2,1)S(1)} %slice.4.refs_0_, bf16[4,32,1536]{2,1,0:T(8,128)(2,1)S(1)} %collective-permute-done.refs_1_, bf16[4,32,1536]{2,1,0:T(8,128)(2,1)S(1)} %collective-permute-done.1.refs_2_, bf16[4,32,1536]{2,1,0:T(8,128)(2,1)S(1)} %collective-permute-done.2.refs_3_, ...), custom_call_target="tpu_custom_call" | custom-call | flops 7864320 | bytes 3145728 | tf_op jit(solution)/shard_map/pallas_call | solution.py:102
  27.6 1.3 %collective-permute-start.13 = (bf16[128,1536]{1,0:T(8,128)(2,1)S(1)}, bf16[128,1536]{1,0:T(8,128)(2,1)S(1)}, u32[]{:S(2)}, u32[]{:S(2)}) collective-permute-start(bf16[128,1536]{1,0:T(8,128)(2,1)S(1)} %shard_map.75.refs_0_), channel_id=1, source_target_pairs={{0,2},{1,3},{2,0},{3,1},{4,6},{5,7},{6,4},{7,5},{8,10},{9,11},{10,... | collective-permute-start | bytes 1179656 | tf_op jit(solution)/shard_map/ppermute | solution.py:24
  28.9 1.2 %collective-permute-start.20 = (bf16[192,1536]{1,0:T(8,128)(2,1)S(1)}, bf16[192,1536]{1,0:T(8,128)(2,1)S(1)}, u32[]{:S(2)}, u32[]{:S(2)}) collective-permute-start(bf16[192,1536]{1,0:T(8,128)(2,1)S(1)} %shard_map.85.own_ref), channel_id=1, source_target_pairs={{0,16},{16,0},{1,17},{17,1},{2,18},{18,2},{3,19},{19,3},{4,20},{20... | collective-permute-start | bytes 1769480 | tf_op jit(solution)/shard_map/ppermute | solution.py:24
  30.1 3.2 %shard_map.76 = (bf16[512,1152]{1,0:T(8,128)(2,1)S(1)}, bf16[256,1152]{1,0:T(8,128)(2,1)S(1)}) custom-call(bf16[512,1536]{1,0:T(8,128)(2,1)S(1)} %shard_map.73.refs_0_, bf16[64,1536]{1,0:T(8,128)(2,1)S(1)} %shard_map.74.refs_1_, bf16[64,1536]{1,0:T(8,128)(2,1)S(1)} %collective-permute-done.4.refs_2_, bf16[64,1536]{1,0:T(8,128)(2,1)S(1)} %collective-permute-done.5.refs_3_, ...), custom_call_target="tpu_custom_call" | custom-call | flops 2717908992 | bytes 7667712 | tf_op jit(solution)/shard_map/pallas_call | solution.py:197
  33.4 9.4 %collective-permute-done.9.refs_2_.refs_9_ = bf16[4,16,1536]{2,1,0:T(8,128)(2,1)S(1)} collective-permute-done((bf16[4,16,1536]{2,1,0:T(8,128)(2,1)S(1)}, bf16[4,16,1536]{2,1,0:T(8,128)(2,1)S(1)}, u32[]{:S(2)}, u32[]{:S(2)}) %collective-permute-start.9) | collective-permute-done | bytes 196640 | tf_op jit(solution)/shard_map/ppermute | solution.py:24
  42.8 0.4 shard_map.77.refs_0_
  43.2 1.3 %collective-permute-start.11 = (bf16[192,1536]{1,0:T(8,128)(2,1)S(1)}, bf16[192,1536]{1,0:T(8,128)(2,1)S(1)}, u32[]{:S(2)}, u32[]{:S(2)}) collective-permute-start(bf16[192,1536]{1,0:T(8,128)(2,1)S(1)} %shard_map.77.refs_0_), channel_id=1, source_target_pairs={{0,2},{1,3},{2,0},{3,1},{4,6},{5,7},{6,4},{7,5},{8,10},{9,11},{10,... | collective-permute-start | bytes 1769480 | tf_op jit(solution)/shard_map/ppermute | solution.py:24
  44.5 2.5 %collective-permute-start.12 = (bf16[128,1536]{1,0:T(8,128)(2,1)S(1)}, bf16[128,1536]{1,0:T(8,128)(2,1)S(1)}, u32[]{:S(2)}, u32[]{:S(2)}) collective-permute-start(bf16[128,1536]{1,0:T(8,128)(2,1)S(1)} %shard_map.75.refs_0_), channel_id=1, source_target_pairs={{0,1},{1,0},{2,3},{3,2},{4,5},{5,4},{6,7},{7,6},{8,9},{9,8},{10,11... | collective-permute-start | bytes 1179656 | tf_op jit(solution)/shard_map/ppermute | solution.py:24
  47.0 0.5 collective-permute-start.10
  47.6 0.4 tags.1
  47.9 0.5 collective-permute-done.12.refs_1_
  48.4 0.4 copy-done.3
  48.8 1.2 %shard_map.79.refs_1_ = bf16[256,1152]{1,0:T(8,128)(2,1)S(1)} custom-call(bf16[128,1536]{1,0:T(8,128)(2,1)S(1)} %shard_map.75.refs_0_, bf16[128,1536]{1,0:T(8,128)(2,1)S(1)} %collective-permute-done.12.refs_1_, bf16[3,1536,384]{2,1,0:T(8,128)(2,1)S(1)} %copy-done), custom_call_target="tpu_custom_call" | custom-call | flops 905969664 | bytes 4915200 | tf_op jit(solution)/shard_map/pallas_call | solution.py:197
  50.2 0.6 collective-permute-start.21
  50.7 5.2 %collective-permute-done.11.refs_0_ = bf16[192,1536]{1,0:T(8,128)(2,1)S(1)} collective-permute-done((bf16[192,1536]{1,0:T(8,128)(2,1)S(1)}, bf16[192,1536]{1,0:T(8,128)(2,1)S(1)}, u32[]{:S(2)}, u32[]{:S(2)}) %collective-permute-start.11) | collective-permute-done | bytes 589856 | tf_op jit(solution)/shard_map/ppermute | solution.py:24
  55.9 3.1 %collective-permute-start.15 = (bf16[192,1536]{1,0:T(8,128)(2,1)S(1)}, bf16[192,1536]{1,0:T(8,128)(2,1)S(1)}, u32[]{:S(2)}, u32[]{:S(2)}) collective-permute-start(bf16[192,1536]{1,0:T(8,128)(2,1)S(1)} %collective-permute-done.11.refs_0_), channel_id=1, source_target_pairs={{0,1},{1,0},{2,3},{3,2},{4,5},{5,4},{6,7},{7,6},{8,9},{9,8},{10,11... | collective-permute-start | bytes 1769480 | tf_op jit(solution)/shard_map/ppermute | solution.py:24
  59.0 1.2 %shard_map.80.refs_2_ = bf16[256,1152]{1,0:T(8,128)(2,1)S(1)} custom-call(bf16[128,1536]{1,0:T(8,128)(2,1)S(1)} %collective-permute-done.13.refs_0_, bf16[128,1536]{1,0:T(8,128)(2,1)S(1)} %collective-permute-done.14.refs_1_, bf16[3,1536,384]{2,1,0:T(8,128)(2,1)S(1)} %copy-done), custom_call_target="tpu_custom_call" | custom-call | flops 905969664 | bytes 4915200 | tf_op jit(solution)/shard_map/pallas_call | solution.py:197
  60.2 6.5 %shard_map.81 = (bf16[1,256,384]{2,1,0:T(8,128)(2,1)S(1)}, bf16[1,256,384]{2,1,0:T(8,128)(2,1)S(1)}, bf16[1,256,384]{2,1,0:T(8,128)(2,1)S(1)}, bf16[1,256,384]{2,1,0:T(8,128)(2,1)S(1)}) custom-call(bf16[512,1152]{1,0:T(8,128)(2,1)S(1)} %get-tuple-element.34.refs_0_, bf16[256,1152]{1,0:T(8,128)(2,1)S(1)} %shard_map.79.refs_1_, ...), custom_call_target="tpu_custom_call" | custom-call | flops 4294967296 | bytes 2359296 | tf_op jit(solution)/shard_map/pallas_call | solution.py:285
  66.8 1.3 %collective-permute-start.23 = (bf16[1,256,384]{2,1,0:T(8,128)(2,1)S(1)}, bf16[1,256,384]{2,1,0:T(8,128)(2,1)S(1)}, u32[]{:S(2)}, u32[]{:S(2)}) collective-permute-start(bf16[1,256,384]{2,1,0:T(8,128)(2,1)S(1)} %get-tuple-element.43), channel_id=1, source_target_pairs={{0,2},{1,3},{2,0},{3,1},{4,6},{5,7},{6,4},{7,5},{8,10},{9,11},{10,... | collective-permute-start | bytes 589832 | tf_op jit(solution)/shard_map/ppermute | solution.py:24
  68.1 1.7 %shard_map.78.refs_1_ = bf16[384,1152]{1,0:T(8,128)(2,1)S(1)} custom-call(bf16[192,1536]{1,0:T(8,128)(2,1)S(1)} %shard_map.77.refs_0_, bf16[192,1536]{1,0:T(8,128)(2,1)S(1)} %collective-permute-done.10.refs_1_, bf16[3,1536,384]{2,1,0:T(8,128)(2,1)S(1)} %copy-done), custom_call_target="tpu_custom_call" | custom-call | flops 1358954496 | bytes 5603328 | tf_op jit(solution)/shard_map/pallas_call | solution.py:197
  69.8 0.9 collective-permute-start.24
  70.7 1.7 %shard_map.82.refs_2_ = bf16[384,1152]{1,0:T(8,128)(2,1)S(1)} custom-call(bf16[192,1536]{1,0:T(8,128)(2,1)S(1)} %collective-permute-done.11.refs_0_, bf16[192,1536]{1,0:T(8,128)(2,1)S(1)} %collective-permute-done.15.refs_1_, bf16[3,1536,384]{2,1,0:T(8,128)(2,1)S(1)} %copy-done), custom_call_target="tpu_custom_call" | custom-call | flops 1358954496 | bytes 5603328 | tf_op jit(solution)/shard_map/pallas_call | solution.py:197
  72.4 3.5 %shard_map.83 = (bf16[1,256,384]{2,1,0:T(8,128)(2,1)S(1)}, bf16[1,256,384]{2,1,0:T(8,128)(2,1)S(1)}) custom-call(bf16[256,1152]{1,0:T(8,128)(2,1)S(1)} %get-tuple-element.50.refs_0_, bf16[384,1152]{1,0:T(8,128)(2,1)S(1)} %shard_map.78.refs_1_, bf16[384,1152]{1,0:T(8,128)(2,1)S(1)} %shard_map.82.refs_2_, bf16[1024,128]{1,0:T(8,128)(2,1)S(1)} %get-tuple-element.46.refs_3_, ...), custom_call_target="tpu_custom_call" | custom-call | flops 2147483648 | bytes 2359296 | tf_op jit(solution)/shard_map/pallas_call | solution.py:285
  75.9 3.5 %shard_map.87 = (bf16[1,256,384]{2,1,0:T(8,128)(2,1)S(1)}, bf16[1,256,384]{2,1,0:T(8,128)(2,1)S(1)}) custom-call(bf16[256,1152]{1,0:T(8,128)(2,1)S(1)} %get-tuple-element.50.refs_0_, bf16[384,1152]{1,0:T(8,128)(2,1)S(1)} %shard_map.78.refs_1_, bf16[384,1152]{1,0:T(8,128)(2,1)S(1)} %shard_map.82.refs_2_, bf16[1024,128]{1,0:T(8,128)(2,1)S(1)} %get-tuple-element.46.refs_3_, ...), custom_call_target="tpu_custom_call" | custom-call | flops 2147483648 | bytes 2359296 | tf_op jit(solution)/shard_map/pallas_call | solution.py:285
  79.5 1.3 %collective-permute-start.16 = (bf16[1,256,384]{2,1,0:T(8,128)(2,1)S(1)}, bf16[1,256,384]{2,1,0:T(8,128)(2,1)S(1)}, u32[]{:S(2)}, u32[]{:S(2)}) collective-permute-start(bf16[1,256,384]{2,1,0:T(8,128)(2,1)S(1)} %get-tuple-element.48), channel_id=1, source_target_pairs={{0,2},{1,3},{2,0},{3,1},{4,6},{5,7},{6,4},{7,5},{8,10},{9,11},{10,... | collective-permute-start | bytes 589832 | tf_op jit(solution)/shard_map/ppermute | solution.py:24
  80.8 0.8 collective-permute-start.17
  81.6 1.8 %shard_map.88.refs_5_ = bf16[8,32,1536]{2,1,0:T(8,128)(2,1)S(1)} custom-call(bf16[256,384]{1,0:T(8,128)(2,1)S(1)} %bitcast.20, bf16[256,384]{1,0:T(8,128)(2,1)S(1)} %bitcast.21, bf16[256,384]{1,0:T(8,128)(2,1)S(1)} %bitcast.22, bf16[256,384]{1,0:T(8,128)(2,1)S(1)} %bitcast.23, bf16[384,1536]{1,0:T(8,128)(2,1)S(1)} %copy-done.3, ...), custom_call_target="tpu_custom_call" | custom-call | flops 1207959552 | bytes 7077888 | tf_op jit(solution)/shard_map/pallas_call | solution.py:342
  83.4 1.0 %shard_map.89.refs_4_ = f32[256,1536]{1,0:T(8,128)S(1)} custom-call(bf16[256,384]{1,0:T(8,128)(2,1)S(1)} %bitcast.18, bf16[256,384]{1,0:T(8,128)(2,1)S(1)} %bitcast.19, bf16[384,1536]{1,0:T(8,128)(2,1)S(1)} %copy-done.3, bf16[384,1536]{1,0:T(8,128)(2,1)S(1)} %collective-permute-done.25.refs_5_.refs_3_), custom_call_target="tpu_custom_call" | custom-call | flops 603979776 | bytes 2752512 | tf_op jit(solution)/shard_map/pallas_call | solution.py:317
  84.4 1.2 %collective-permute-done.16 = bf16[1,256,384]{2,1,0:T(8,128)(2,1)S(1)} collective-permute-done((bf16[1,256,384]{2,1,0:T(8,128)(2,1)S(1)}, bf16[1,256,384]{2,1,0:T(8,128)(2,1)S(1)}, u32[]{:S(2)}, u32[]{:S(2)}) %collective-permute-start.16) | collective-permute-done | bytes 196640 | tf_op jit(solution)/shard_map/ppermute | solution.py:24
  85.6 4.8 %collective-permute-done.17 = bf16[1,256,384]{2,1,0:T(8,128)(2,1)S(1)} collective-permute-done((bf16[1,256,384]{2,1,0:T(8,128)(2,1)S(1)}, bf16[1,256,384]{2,1,0:T(8,128)(2,1)S(1)}, u32[]{:S(2)}, u32[]{:S(2)}) %collective-permute-start.17) | collective-permute-done | bytes 196640 | tf_op jit(solution)/shard_map/ppermute | solution.py:24
  90.4 2.1 %shard_map.90 = bf16[8,64,1536]{2,1,0:T(8,128)(2,1)} custom-call(bf16[256,384]{1,0:T(8,128)(2,1)S(1)} %bitcast.24, bf16[256,384]{1,0:T(8,128)(2,1)S(1)} %bitcast.25, bf16[384,1536]{1,0:T(8,128)(2,1)S(1)} %shard_map.86.refs_6_.refs_2_, bf16[384,1536]{1,0:T(8,128)(2,1)S(1)} %collective-permute-done.21.refs_7_.refs_3_, f32[256,1536]{1,0:T(8,128)S(1)} %shard_map.89.refs_4_, ...), custom_call_target="tpu_custom_call" | custom-call | flops 603979776 | bytes 7077888 | tf_op jit(solution)/shard_map/pallas_call | solution.py:388
  (43 shorter events, 0.6 us)
Async XLA Ops:
  0.0 4.1 %copy-start.1 = (bf16[1,8,1,64,1536]{4,3,2,1,0:T(8,128)(2,1)S(1)}, bf16[1,8,1,64,1536]{4,3,2,1,0:T(8,128)(2,1)}, u32[]{:S(2)}) copy-start(bf16[1,8,1,64,1536]{4,3,2,1,0:T(8,128)(2,1)} %param.7) | copy-start | bytes 4718596
  1.1 10.1 %collective-permute-start.1 = (bf16[4,32,1536]{2,1,0:T(8,128)(2,1)S(1)}, bf16[4,32,1536]{2,1,0:T(8,128)(2,1)S(1)}, u32[]{:S(2)}, u32[]{:S(2)}) collective-permute-start(bf16[4,32,1536]{2,1,0:T(8,128)(2,1)S(1)} %slice.4.refs_0_), channel_id=1, source_target_pairs={{0,2},{1,3},{2,0},{3,1},{4,6},{5,7},{6,4},{7,5},{8,10},{9,11},{10,... | collective-permute-start | bytes 1179656 | tf_op jit(solution)/shard_map/ppermute | solution.py:24
  2.4 1.3 %copy-start.2 = (bf16[384,1536]{1,0:T(8,128)(2,1)S(1)}, bf16[384,1536]{1,0:T(8,128)(2,1)}, u32[]{:S(2)}) copy-start(bf16[384,1536]{1,0:T(8,128)(2,1)} %refs_2_.13) | copy-start | bytes 3538948
  3.7 10.2 %copy-start.4 = (f32[1536]{0:T(1024)S(1)}, f32[1536]{0:T(1024)}, u32[]{:S(2)}) copy-start(f32[1536]{0:T(1024)} %refs_3_.1) | copy-start | bytes 18436
  3.7 10.2 %copy-start.5 = (f32[1536]{0:T(1024)S(1)}, f32[1536]{0:T(1024)}, u32[]{:S(2)}) copy-start(f32[1536]{0:T(1024)} %refs_4_.4) | copy-start | bytes 18436
  3.8 13.8 %collective-permute-start.18 = (bf16[96,1536]{1,0:T(8,128)(2,1)S(1)}, bf16[96,1536]{1,0:T(8,128)(2,1)S(1)}, u32[]{:S(2)}, u32[]{:S(2)}) collective-permute-start(bf16[96,1536]{1,0:T(8,128)(2,1)S(1)} %shard_map.84), channel_id=1, source_target_pairs={{0,2},{1,3},{2,0},{3,1},{4,6},{5,7},{6,4},{7,5},{8,10},{9,11},{10,... | collective-permute-start | bytes 884744 | tf_op jit(solution)/shard_map/ppermute | solution.py:24
  4.2 19.1 %collective-permute-start.3 = (bf16[4,32,1536]{2,1,0:T(8,128)(2,1)S(1)}, bf16[4,32,1536]{2,1,0:T(8,128)(2,1)S(1)}, u32[]{:S(2)}, u32[]{:S(2)}) collective-permute-start(bf16[4,32,1536]{2,1,0:T(8,128)(2,1)S(1)} %get-tuple-element.30), channel_id=1, source_target_pairs={{0,4},{4,0},{8,12},{12,8},{1,5},{5,1},{9,13},{13,9},{2,6},{6,2},{1... | collective-permute-start | bytes 1179656 | tf_op jit(solution)/shard_map/ppermute | solution.py:24
  5.5 19.5 %collective-permute-start = (bf16[4,32,1536]{2,1,0:T(8,128)(2,1)S(1)}, bf16[4,32,1536]{2,1,0:T(8,128)(2,1)S(1)}, u32[]{:S(2)}, u32[]{:S(2)}) collective-permute-start(bf16[4,32,1536]{2,1,0:T(8,128)(2,1)S(1)} %slice.4.refs_0_), channel_id=1, source_target_pairs={{0,1},{1,0},{2,3},{3,2},{4,5},{5,4},{6,7},{7,6},{8,9},{9,8},{10,11... | collective-permute-start | bytes 1179656 | tf_op jit(solution)/shard_map/ppermute | solution.py:24
  11.2 14.0 %collective-permute-start.2 = (bf16[4,32,1536]{2,1,0:T(8,128)(2,1)S(1)}, bf16[4,32,1536]{2,1,0:T(8,128)(2,1)S(1)}, u32[]{:S(2)}, u32[]{:S(2)}) collective-permute-start(bf16[4,32,1536]{2,1,0:T(8,128)(2,1)S(1)} %collective-permute-done.1.refs_2_), channel_id=1, source_target_pairs={{0,1},{1,0},{2,3},{3,2},{4,5},{5,4},{6,7},{7,6},{8,9},{9,8},{10,11... | collective-permute-start | bytes 1179656 | tf_op jit(solution)/shard_map/ppermute | solution.py:24
  14.1 7.6 %collective-permute-start.5 = (bf16[64,1536]{1,0:T(8,128)(2,1)S(1)}, bf16[64,1536]{1,0:T(8,128)(2,1)S(1)}, u32[]{:S(2)}, u32[]{:S(2)}) collective-permute-start(bf16[64,1536]{1,0:T(8,128)(2,1)S(1)} %shard_map.74.refs_1_), channel_id=1, source_target_pairs={{0,2},{1,3},{2,0},{3,1},{4,6},{5,7},{6,4},{7,5},{8,10},{9,11},{10,... | collective-permute-start | bytes 589832 | tf_op jit(solution)/shard_map/ppermute | solution.py:24
  17.5 6.1 %collective-permute-start.19 = (bf16[96,1536]{1,0:T(8,128)(2,1)S(1)}, bf16[96,1536]{1,0:T(8,128)(2,1)S(1)}, u32[]{:S(2)}, u32[]{:S(2)}) collective-permute-start(bf16[96,1536]{1,0:T(8,128)(2,1)S(1)} %collective-permute-done.18.own_ref), channel_id=1, source_target_pairs={{0,4},{4,0},{8,12},{12,8},{1,5},{5,1},{9,13},{13,9},{2,6},{6,2},{1... | collective-permute-start | bytes 884744 | tf_op jit(solution)/shard_map/ppermute | solution.py:24
  21.7 5.9 %collective-permute-start.4 = (bf16[64,1536]{1,0:T(8,128)(2,1)S(1)}, bf16[64,1536]{1,0:T(8,128)(2,1)S(1)}, u32[]{:S(2)}, u32[]{:S(2)}) collective-permute-start(bf16[64,1536]{1,0:T(8,128)(2,1)S(1)} %shard_map.74.refs_1_), channel_id=1, source_target_pairs={{0,1},{1,0},{2,3},{3,2},{4,5},{5,4},{6,7},{7,6},{8,9},{9,8},{10,11... | collective-permute-start | bytes 589832 | tf_op jit(solution)/shard_map/ppermute | solution.py:24
  23.3 5.6 %collective-permute-start.6 = (bf16[64,1536]{1,0:T(8,128)(2,1)S(1)}, bf16[64,1536]{1,0:T(8,128)(2,1)S(1)}, u32[]{:S(2)}, u32[]{:S(2)}) collective-permute-start(bf16[64,1536]{1,0:T(8,128)(2,1)S(1)} %collective-permute-done.5.refs_3_), channel_id=1, source_target_pairs={{0,1},{1,0},{2,3},{3,2},{4,5},{5,4},{6,7},{7,6},{8,9},{9,8},{10,11... | collective-permute-start | bytes 589832 | tf_op jit(solution)/shard_map/ppermute | solution.py:24
  23.6 9.8 %collective-permute-start.7 = (bf16[4,16,1536]{2,1,0:T(8,128)(2,1)S(1)}, bf16[4,16,1536]{2,1,0:T(8,128)(2,1)S(1)}, u32[]{:S(2)}, u32[]{:S(2)}) collective-permute-start(bf16[4,16,1536]{2,1,0:T(8,128)(2,1)S(1)} %get-tuple-element.33), channel_id=1, source_target_pairs={{0,4},{4,0},{8,12},{12,8},{1,5},{5,1},{9,13},{13,9},{2,6},{6,2},{1... | collective-permute-start | bytes 589832 | tf_op jit(solution)/shard_map/ppermute | solution.py:24
  25.0 5.2 %copy-start = (bf16[3,1536,384]{2,1,0:T(8,128)(2,1)S(1)}, bf16[3,1536,384]{2,1,0:T(8,128)(2,1)}, u32[]{:S(2)}) copy-start(bf16[3,1536,384]{2,1,0:T(8,128)(2,1)} %refs_2_.12) | copy-start | bytes 10616836
  25.1 8.4 %collective-permute-start.8 = (bf16[4,16,1536]{2,1,0:T(8,128)(2,1)S(1)}, bf16[4,16,1536]{2,1,0:T(8,128)(2,1)S(1)}, u32[]{:S(2)}, u32[]{:S(2)}) collective-permute-start(bf16[4,16,1536]{2,1,0:T(8,128)(2,1)S(1)} %get-tuple-element.36), channel_id=1, source_target_pairs={{0,8},{4,12},{8,0},{12,4},{1,9},{5,13},{9,1},{13,5},{2,10},{6,14},... | collective-permute-start | bytes 589832 | tf_op jit(solution)/shard_map/ppermute | solution.py:24
  25.2 17.6 %collective-permute-start.9 = (bf16[4,16,1536]{2,1,0:T(8,128)(2,1)S(1)}, bf16[4,16,1536]{2,1,0:T(8,128)(2,1)S(1)}, u32[]{:S(2)}, u32[]{:S(2)}) collective-permute-start(bf16[4,16,1536]{2,1,0:T(8,128)(2,1)S(1)} %get-tuple-element.37), channel_id=1, source_target_pairs={{0,12},{4,8},{8,4},{12,0},{1,13},{5,9},{9,5},{13,1},{2,14},{6,10},... | collective-permute-start | bytes 589832 | tf_op jit(solution)/shard_map/ppermute | solution.py:24
  27.6 20.0 %copy-start.6 = (s32[1,32,64]{2,1,0:T(8,128)S(1)}, s32[1,32,64]{2,1,0:T(8,128)}, u32[]{:S(2)}) copy-start(s32[1,32,64]{2,1,0:T(8,128)} %param.8) | copy-start | bytes 24580
  27.6 19.4 %collective-permute-start.13 = (bf16[128,1536]{1,0:T(8,128)(2,1)S(1)}, bf16[128,1536]{1,0:T(8,128)(2,1)S(1)}, u32[]{:S(2)}, u32[]{:S(2)}) collective-permute-start(bf16[128,1536]{1,0:T(8,128)(2,1)S(1)} %shard_map.75.refs_0_), channel_id=1, source_target_pairs={{0,2},{1,3},{2,0},{3,1},{4,6},{5,7},{6,4},{7,5},{8,10},{9,11},{10,... | collective-permute-start | bytes 1179656 | tf_op jit(solution)/shard_map/ppermute | solution.py:24
  28.9 21.1 %collective-permute-start.20 = (bf16[192,1536]{1,0:T(8,128)(2,1)S(1)}, bf16[192,1536]{1,0:T(8,128)(2,1)S(1)}, u32[]{:S(2)}, u32[]{:S(2)}) collective-permute-start(bf16[192,1536]{1,0:T(8,128)(2,1)S(1)} %shard_map.85.own_ref), channel_id=1, source_target_pairs={{0,16},{16,0},{1,17},{17,1},{2,18},{18,2},{3,19},{19,3},{4,20},{20... | collective-permute-start | bytes 1769480 | tf_op jit(solution)/shard_map/ppermute | solution.py:24
  43.2 12.7 %collective-permute-start.11 = (bf16[192,1536]{1,0:T(8,128)(2,1)S(1)}, bf16[192,1536]{1,0:T(8,128)(2,1)S(1)}, u32[]{:S(2)}, u32[]{:S(2)}) collective-permute-start(bf16[192,1536]{1,0:T(8,128)(2,1)S(1)} %shard_map.77.refs_0_), channel_id=1, source_target_pairs={{0,2},{1,3},{2,0},{3,1},{4,6},{5,7},{6,4},{7,5},{8,10},{9,11},{10,... | collective-permute-start | bytes 1769480 | tf_op jit(solution)/shard_map/ppermute | solution.py:24
  44.5 3.9 %collective-permute-start.12 = (bf16[128,1536]{1,0:T(8,128)(2,1)S(1)}, bf16[128,1536]{1,0:T(8,128)(2,1)S(1)}, u32[]{:S(2)}, u32[]{:S(2)}) collective-permute-start(bf16[128,1536]{1,0:T(8,128)(2,1)S(1)} %shard_map.75.refs_0_), channel_id=1, source_target_pairs={{0,1},{1,0},{2,3},{3,2},{4,5},{5,4},{6,7},{7,6},{8,9},{9,8},{10,11... | collective-permute-start | bytes 1179656 | tf_op jit(solution)/shard_map/ppermute | solution.py:24
  47.0 12.0 %collective-permute-start.14 = (bf16[128,1536]{1,0:T(8,128)(2,1)S(1)}, bf16[128,1536]{1,0:T(8,128)(2,1)S(1)}, u32[]{:S(2)}, u32[]{:S(2)}) collective-permute-start(bf16[128,1536]{1,0:T(8,128)(2,1)S(1)} %collective-permute-done.13.refs_0_), channel_id=1, source_target_pairs={{0,1},{1,0},{2,3},{3,2},{4,5},{5,4},{6,7},{7,6},{8,9},{9,8},{10,11... | collective-permute-start | bytes 1179656 | tf_op jit(solution)/shard_map/ppermute | solution.py:24
  47.0 19.7 %collective-permute-start.10 = (bf16[192,1536]{1,0:T(8,128)(2,1)S(1)}, bf16[192,1536]{1,0:T(8,128)(2,1)S(1)}, u32[]{:S(2)}, u32[]{:S(2)}) collective-permute-start(bf16[192,1536]{1,0:T(8,128)(2,1)S(1)} %shard_map.77.refs_0_), channel_id=1, source_target_pairs={{0,1},{1,0},{2,3},{3,2},{4,5},{5,4},{6,7},{7,6},{8,9},{9,8},{10,11... | collective-permute-start | bytes 1769480 | tf_op jit(solution)/shard_map/ppermute | solution.py:24
  47.6 1.3 %copy-start.3 = (bf16[384,1536]{1,0:T(8,128)(2,1)S(1)}, bf16[384,1536]{1,0:T(8,128)(2,1)}, u32[]{:S(2)}) copy-start(bf16[384,1536]{1,0:T(8,128)(2,1)} %refs_2_.13) | copy-start | bytes 3538948
  48.8 30.6 %collective-permute-start.25 = (bf16[384,1536]{1,0:T(8,128)(2,1)S(1)}, bf16[384,1536]{1,0:T(8,128)(2,1)S(1)}, u32[]{:S(2)}, u32[]{:S(2)}) collective-permute-start(bf16[384,1536]{1,0:T(8,128)(2,1)S(1)} %copy-done.3), channel_id=1, source_target_pairs={{0,1},{1,0},{2,3},{3,2},{4,5},{5,4},{6,7},{7,6},{8,9},{9,8},{10,11... | collective-permute-start | bytes 3538952 | tf_op jit(solution)/shard_map/ppermute | solution.py:24
  50.2 10.1 %copy-start.7 = (f32[4]{0:T(128)S(1)}, f32[4]{0:T(128)}, u32[]{:S(2)}) copy-start(f32[4]{0:T(128)} %refs_5_.9) | copy-start | bytes 52
  50.2 31.5 %collective-permute-start.21 = (bf16[384,1536]{1,0:T(8,128)(2,1)S(1)}, bf16[384,1536]{1,0:T(8,128)(2,1)S(1)}, u32[]{:S(2)}, u32[]{:S(2)}) collective-permute-start(bf16[384,1536]{1,0:T(8,128)(2,1)S(1)} %shard_map.86.refs_6_.refs_2_), channel_id=1, source_target_pairs={{0,1},{1,0},{2,3},{3,2},{4,5},{5,4},{6,7},{7,6},{8,9},{9,8},{10,11... | collective-permute-start | bytes 3538952 | tf_op jit(solution)/shard_map/ppermute | solution.py:24
  55.9 13.9 %collective-permute-start.15 = (bf16[192,1536]{1,0:T(8,128)(2,1)S(1)}, bf16[192,1536]{1,0:T(8,128)(2,1)S(1)}, u32[]{:S(2)}, u32[]{:S(2)}) collective-permute-start(bf16[192,1536]{1,0:T(8,128)(2,1)S(1)} %collective-permute-done.11.refs_0_), channel_id=1, source_target_pairs={{0,1},{1,0},{2,3},{3,2},{4,5},{5,4},{6,7},{7,6},{8,9},{9,8},{10,11... | collective-permute-start | bytes 1769480 | tf_op jit(solution)/shard_map/ppermute | solution.py:24
  66.7 12.8 %collective-permute-start.22 = (bf16[1,256,384]{2,1,0:T(8,128)(2,1)S(1)}, bf16[1,256,384]{2,1,0:T(8,128)(2,1)S(1)}, u32[]{:S(2)}, u32[]{:S(2)}) collective-permute-start(bf16[1,256,384]{2,1,0:T(8,128)(2,1)S(1)} %get-tuple-element.42), channel_id=1, source_target_pairs={{0,1},{1,0},{2,3},{3,2},{4,5},{5,4},{6,7},{7,6},{8,9},{9,8},{10,11... | collective-permute-start | bytes 589832 | tf_op jit(solution)/shard_map/ppermute | solution.py:24
  66.8 14.0 %collective-permute-start.23 = (bf16[1,256,384]{2,1,0:T(8,128)(2,1)S(1)}, bf16[1,256,384]{2,1,0:T(8,128)(2,1)S(1)}, u32[]{:S(2)}, u32[]{:S(2)}) collective-permute-start(bf16[1,256,384]{2,1,0:T(8,128)(2,1)S(1)} %get-tuple-element.43), channel_id=1, source_target_pairs={{0,2},{1,3},{2,0},{3,1},{4,6},{5,7},{6,4},{7,5},{8,10},{9,11},{10,... | collective-permute-start | bytes 589832 | tf_op jit(solution)/shard_map/ppermute | solution.py:24
  69.8 11.9 %collective-permute-start.24 = (bf16[1,256,384]{2,1,0:T(8,128)(2,1)S(1)}, bf16[1,256,384]{2,1,0:T(8,128)(2,1)S(1)}, u32[]{:S(2)}, u32[]{:S(2)}) collective-permute-start(bf16[1,256,384]{2,1,0:T(8,128)(2,1)S(1)} %get-tuple-element.44), channel_id=1, source_target_pairs={{0,3},{1,2},{2,1},{3,0},{4,7},{5,6},{6,5},{7,4},{8,11},{9,10},{10,... | collective-permute-start | bytes 589832 | tf_op jit(solution)/shard_map/ppermute | solution.py:24
  79.4 4.0 %collective-permute-start.26 = (bf16[1,256,384]{2,1,0:T(8,128)(2,1)S(1)}, bf16[1,256,384]{2,1,0:T(8,128)(2,1)S(1)}, u32[]{:S(2)}, u32[]{:S(2)}) collective-permute-start(bf16[1,256,384]{2,1,0:T(8,128)(2,1)S(1)} %get-tuple-element.52), channel_id=1, source_target_pairs={{0,1},{1,0},{2,3},{3,2},{4,5},{5,4},{6,7},{7,6},{8,9},{9,8},{10,11... | collective-permute-start | bytes 589832 | tf_op jit(solution)/shard_map/ppermute | solution.py:24
  79.5 6.1 %collective-permute-start.16 = (bf16[1,256,384]{2,1,0:T(8,128)(2,1)S(1)}, bf16[1,256,384]{2,1,0:T(8,128)(2,1)S(1)}, u32[]{:S(2)}, u32[]{:S(2)}) collective-permute-start(bf16[1,256,384]{2,1,0:T(8,128)(2,1)S(1)} %get-tuple-element.48), channel_id=1, source_target_pairs={{0,2},{1,3},{2,0},{3,1},{4,6},{5,7},{6,4},{7,5},{8,10},{9,11},{10,... | collective-permute-start | bytes 589832 | tf_op jit(solution)/shard_map/ppermute | solution.py:24
  80.8 9.6 %collective-permute-start.17 = (bf16[1,256,384]{2,1,0:T(8,128)(2,1)S(1)}, bf16[1,256,384]{2,1,0:T(8,128)(2,1)S(1)}, u32[]{:S(2)}, u32[]{:S(2)}) collective-permute-start(bf16[1,256,384]{2,1,0:T(8,128)(2,1)S(1)} %get-tuple-element.49), channel_id=1, source_target_pairs={{0,3},{1,2},{2,1},{3,0},{4,7},{5,6},{6,5},{7,4},{8,11},{9,10},{10,... | collective-permute-start | bytes 589832 | tf_op jit(solution)/shard_map/ppermute | solution.py:24

commit v6 on v5

--- a/solution.py
+++ b/solution.py
@@ -439,7 +439,7 @@
 def gather_weights(block):
     levels = []
     rows = block.shape[0]
-    for axis in ("member", "win"):
+    for axis in ("win", "member"):
         if lax.axis_size(axis) % 2 == 0 and rows % (32 << len(levels)) == 0:
             levels.append(axis)
 
@@ -503,9 +503,8 @@
     weights = triple_projection_matrix
     scales = logit_scaling_per_part
 
-    local_0 = blocked[rows:, half : half + WS]
-    boxes = [(0, half, WS), (0, half + WS, near), (rows, 0, half), (0, 0, half)]
-    south_0, south_1, east, corner = cut(blocked, rows, boxes)
+    boxes = [(rows, half, WS), (0, half, WS), (0, half + WS, near), (rows, 0, half), (0, 0, half)]
+    local_0, south_0, south_1, east, corner = cut(blocked, rows, boxes)
     spans = [(0, rows + row, half + WS, near) for row in range(rows)]
     (local_1,) = norm([blocked], gain, bias, [spans])
     south_0 = exchange(south_0, 1, "win")

time: 92.8 us -> 93.8 us (1.011)
  the two profiles are of different devices: /device:TPU:17 before, /device:TPU:19 now
where the time goes in v6:
time: 93.8 us; the launch traced here: 93.5 us
  waiting for transfers between devices  30.5 us (33%)
  Pallas kernels  30 us (32%)
  starting transfers between devices  27.9 us (30%)
  local copies, waits for them, and re-layouts  4.6 us (5%)
    ppermute x27, waiting for transfers between devices, permute_by(): return lax.ppermute(value, axis, pairs)  30.5 us
    ppermute x27, starting transfers between devices, permute_by(): return lax.ppermute(value, axis, pairs)  27.9 us
    pallas_call x3, Pallas kernels, attend(): pl.pallas_call(functools.partial(attend_kernel, layout, ranges, head_widt...  13.5 us
    pallas_call x5, Pallas kernels, project(): pl.pallas_call(functools.partial(project_kernel, [len(group) for group in...  8.99 us
    unnamed x22, local copies, waits for them, and re-layouts  4.6 us
    pallas_call x4, Pallas kernels, norm(): pl.pallas_call(functools.partial(norm_kernel, groups), out_shape=[jax.Sha...  2.11 us
    pallas_call x1, Pallas kernels, finish_last(): pl.pallas_call(functools.partial(last_kernel, count, chunks, spans), out_...  2.06 us
  transfers between devices with their start and end apart: 27, of which 10 were waited for; matrix products, arithmetic and copies ran while one was open for 0% of the time, Pallas kernels for 30%

profile of v6, /device:TPU:19, one launch (start us, length us, event | category | flops | bytes accessed | tf_op | source)
XLA Modules:
  0.0 93.5 jit_solution(4133600061041878895)
XLA Ops:
  0.0 1.4 %copy-done.1 = bf16[1,8,1,64,1536]{4,3,2,1,0:T(8,128)(2,1)S(1)} copy-done((bf16[1,8,1,64,1536]{4,3,2,1,0:T(8,128)(2,1)S(1)}, bf16[1,8,1,64,1536]{4,3,2,1,0:T(8,128)(2,1)}, u32[]{:S(2)}) %copy-start.1) | copy-done | bytes 1572888
  1.5 0.3 collective-permute-start.1
  1.8 1.3 %copy-done.3 = bf16[384,1536]{1,0:T(8,128)(2,1)S(1)} copy-done((bf16[384,1536]{1,0:T(8,128)(2,1)S(1)}, bf16[384,1536]{1,0:T(8,128)(2,1)}, u32[]{:S(2)}) %copy-start.3) | copy-done | bytes 1179672
  3.2 1.2 %collective-permute-start.18 = (bf16[96,1536]{1,0:T(8,128)(2,1)S(1)}, bf16[96,1536]{1,0:T(8,128)(2,1)S(1)}, u32[]{:S(2)}, u32[]{:S(2)}) collective-permute-start(bf16[96,1536]{1,0:T(8,128)(2,1)S(1)} %shard_map.84), channel_id=1, source_target_pairs={{0,2},{1,3},{2,0},{3,1},{4,6},{5,7},{6,4},{7,5},{8,10},{9,11},{10,... | collective-permute-start | bytes 884744 | tf_op jit(solution)/shard_map/ppermute | solution.py:24
  4.4 1.3 %collective-permute-start.3 = (bf16[4,32,1536]{2,1,0:T(8,128)(2,1)S(1)}, bf16[4,32,1536]{2,1,0:T(8,128)(2,1)S(1)}, u32[]{:S(2)}, u32[]{:S(2)}) collective-permute-start(bf16[4,32,1536]{2,1,0:T(8,128)(2,1)S(1)} %get-tuple-element.32), channel_id=1, source_target_pairs={{0,4},{4,0},{8,12},{12,8},{1,5},{5,1},{9,13},{13,9},{2,6},{6,2},{1... | collective-permute-start | bytes 1179656 | tf_op jit(solution)/shard_map/ppermute | solution.py:24
  5.7 1.5 %collective-permute-start = (bf16[4,32,1536]{2,1,0:T(8,128)(2,1)S(1)}, bf16[4,32,1536]{2,1,0:T(8,128)(2,1)S(1)}, u32[]{:S(2)}, u32[]{:S(2)}) collective-permute-start(bf16[4,32,1536]{2,1,0:T(8,128)(2,1)S(1)} %get-tuple-element.31.refs_0_), channel_id=1, source_target_pairs={{0,1},{1,0},{2,3},{3,2},{4,5},{5,4},{6,7},{7,6},{8,9},{9,8},{10,11... | collective-permute-start | bytes 1179656 | tf_op jit(solution)/shard_map/ppermute | solution.py:24
  7.3 4.3 %collective-permute-done.1.refs_2_ = bf16[4,32,1536]{2,1,0:T(8,128)(2,1)S(1)} collective-permute-done((bf16[4,32,1536]{2,1,0:T(8,128)(2,1)S(1)}, bf16[4,32,1536]{2,1,0:T(8,128)(2,1)S(1)}, u32[]{:S(2)}, u32[]{:S(2)}) %collective-permute-start.1) | collective-permute-done | bytes 393248 | tf_op jit(solution)/shard_map/ppermute | solution.py:24
  11.6 2.7 %collective-permute-start.2 = (bf16[4,32,1536]{2,1,0:T(8,128)(2,1)S(1)}, bf16[4,32,1536]{2,1,0:T(8,128)(2,1)S(1)}, u32[]{:S(2)}, u32[]{:S(2)}) collective-permute-start(bf16[4,32,1536]{2,1,0:T(8,128)(2,1)S(1)} %collective-permute-done.1.refs_2_), channel_id=1, source_target_pairs={{0,1},{1,0},{2,3},{3,2},{4,5},{5,4},{6,7},{7,6},{8,9},{9,8},{10,11... | collective-permute-start | bytes 1179656 | tf_op jit(solution)/shard_map/ppermute | solution.py:24
  14.2 0.7 copy-done.5
  14.9 0.7 copy-done.7
  15.9 0.3 collective-permute-start.5
  16.2 1.7 %collective-permute-done.18.own_ref = bf16[96,1536]{1,0:T(8,128)(2,1)S(1)} collective-permute-done((bf16[96,1536]{1,0:T(8,128)(2,1)S(1)}, bf16[96,1536]{1,0:T(8,128)(2,1)S(1)}, u32[]{:S(2)}, u32[]{:S(2)}) %collective-permute-start.18) | collective-permute-done | bytes 294944 | tf_op jit(solution)/shard_map/ppermute | solution.py:24
  17.9 1.2 %collective-permute-start.19 = (bf16[96,1536]{1,0:T(8,128)(2,1)S(1)}, bf16[96,1536]{1,0:T(8,128)(2,1)S(1)}, u32[]{:S(2)}, u32[]{:S(2)}) collective-permute-start(bf16[96,1536]{1,0:T(8,128)(2,1)S(1)} %collective-permute-done.18.own_ref), channel_id=1, source_target_pairs={{0,16},{16,0},{1,17},{17,1},{2,18},{18,2},{3,19},{19,3},{4,20},{20... | collective-permute-start | bytes 884744 | tf_op jit(solution)/shard_map/ppermute | solution.py:24
  19.1 3.7 %collective-permute-done.5.refs_3_ = bf16[64,1536]{1,0:T(8,128)(2,1)S(1)} collective-permute-done((bf16[64,1536]{1,0:T(8,128)(2,1)S(1)}, bf16[64,1536]{1,0:T(8,128)(2,1)S(1)}, u32[]{:S(2)}, u32[]{:S(2)}) %collective-permute-start.5) | collective-permute-done | bytes 196640 | tf_op jit(solution)/shard_map/ppermute | solution.py:24
  22.9 0.8 collective-permute-start.4
  23.6 0.3 shard_map.75.refs_0_
  24.0 0.6 collective-permute-done.19.other_ref
  24.6 1.3 %collective-permute-start.7 = (bf16[4,16,1536]{2,1,0:T(8,128)(2,1)S(1)}, bf16[4,16,1536]{2,1,0:T(8,128)(2,1)S(1)}, u32[]{:S(2)}, u32[]{:S(2)}) collective-permute-start(bf16[4,16,1536]{2,1,0:T(8,128)(2,1)S(1)} %get-tuple-element.35), channel_id=1, source_target_pairs={{0,4},{4,0},{8,12},{12,8},{1,5},{5,1},{9,13},{13,9},{2,6},{6,2},{1... | collective-permute-start | bytes 589832 | tf_op jit(solution)/shard_map/ppermute | solution.py:24
  26.1 1.3 %collective-permute-start.9 = (bf16[4,16,1536]{2,1,0:T(8,128)(2,1)S(1)}, bf16[4,16,1536]{2,1,0:T(8,128)(2,1)S(1)}, u32[]{:S(2)}, u32[]{:S(2)}) collective-permute-start(bf16[4,16,1536]{2,1,0:T(8,128)(2,1)S(1)} %get-tuple-element.39), channel_id=1, source_target_pairs={{0,12},{4,8},{8,4},{12,0},{1,13},{5,9},{9,5},{13,1},{2,14},{6,10},... | collective-permute-start | bytes 589832 | tf_op jit(solution)/shard_map/ppermute | solution.py:24
  27.3 1.1 %shard_map.73.refs_0_ = bf16[512,1536]{1,0:T(8,128)(2,1)S(1)} custom-call(bf16[4,32,1536]{2,1,0:T(8,128)(2,1)S(1)} %get-tuple-element.31.refs_0_, bf16[4,32,1536]{2,1,0:T(8,128)(2,1)S(1)} %collective-permute-done.refs_1_, bf16[4,32,1536]{2,1,0:T(8,128)(2,1)S(1)} %collective-permute-done.1.refs_2_, bf16[4,32,1536]{2,1,0:T(8,128)(2,1)S(1)} %collective-permute-done.2.refs_3_, ...), custom_call_target="tpu_custom_call" | custom-call | flops 7864320 | bytes 3145728 | tf_op jit(solution)/shard_map/pallas_call | solution.py:102
  28.8 2.2 %collective-permute-start.20 = (bf16[192,1536]{1,0:T(8,128)(2,1)S(1)}, bf16[192,1536]{1,0:T(8,128)(2,1)S(1)}, u32[]{:S(2)}, u32[]{:S(2)}) collective-permute-start(bf16[192,1536]{1,0:T(8,128)(2,1)S(1)} %shard_map.85.own_ref), channel_id=1, source_target_pairs={{0,4},{4,0},{8,12},{12,8},{1,5},{5,1},{9,13},{13,9},{2,6},{6,2},{1... | collective-permute-start | bytes 1769480 | tf_op jit(solution)/shard_map/ppermute | solution.py:24
  31.0 3.2 %shard_map.76 = (bf16[512,1152]{1,0:T(8,128)(2,1)S(1)}, bf16[256,1152]{1,0:T(8,128)(2,1)S(1)}) custom-call(bf16[512,1536]{1,0:T(8,128)(2,1)S(1)} %shard_map.73.refs_0_, bf16[64,1536]{1,0:T(8,128)(2,1)S(1)} %shard_map.74.refs_1_, bf16[64,1536]{1,0:T(8,128)(2,1)S(1)} %collective-permute-done.4.refs_2_, bf16[64,1536]{1,0:T(8,128)(2,1)S(1)} %collective-permute-done.5.refs_3_, ...), custom_call_target="tpu_custom_call" | custom-call | flops 2717908992 | bytes 7667712 | tf_op jit(solution)/shard_map/pallas_call | solution.py:197
  34.3 9.3 %collective-permute-done.9.refs_2_.refs_9_ = bf16[4,16,1536]{2,1,0:T(8,128)(2,1)S(1)} collective-permute-done((bf16[4,16,1536]{2,1,0:T(8,128)(2,1)S(1)}, bf16[4,16,1536]{2,1,0:T(8,128)(2,1)S(1)}, u32[]{:S(2)}, u32[]{:S(2)}) %collective-permute-start.9) | collective-permute-done | bytes 196640 | tf_op jit(solution)/shard_map/ppermute | solution.py:24
  43.7 0.4 shard_map.77.refs_0_
  44.4 2.5 %collective-permute-start.12 = (bf16[128,1536]{1,0:T(8,128)(2,1)S(1)}, bf16[128,1536]{1,0:T(8,128)(2,1)S(1)}, u32[]{:S(2)}, u32[]{:S(2)}) collective-permute-start(bf16[128,1536]{1,0:T(8,128)(2,1)S(1)} %shard_map.75.refs_0_), channel_id=1, source_target_pairs={{0,1},{1,0},{2,3},{3,2},{4,5},{5,4},{6,7},{7,6},{8,9},{9,8},{10,11... | collective-permute-start | bytes 1179656 | tf_op jit(solution)/shard_map/ppermute | solution.py:24
  46.9 0.5 collective-permute-start.10
  47.4 0.4 tags.1
  47.8 0.5 collective-permute-done.12.refs_1_
  48.3 0.4 copy-done.4
  48.7 1.2 %shard_map.79.refs_1_ = bf16[256,1152]{1,0:T(8,128)(2,1)S(1)} custom-call(bf16[128,1536]{1,0:T(8,128)(2,1)S(1)} %shard_map.75.refs_0_, bf16[128,1536]{1,0:T(8,128)(2,1)S(1)} %collective-permute-done.12.refs_1_, bf16[3,1536,384]{2,1,0:T(8,128)(2,1)S(1)} %copy-done), custom_call_target="tpu_custom_call" | custom-call | flops 905969664 | bytes 4915200 | tf_op jit(solution)/shard_map/pallas_call | solution.py:197
  49.9 0.6 collective-permute-done.20.other_ref
  50.7 2.5 %collective-permute-start.21 = (bf16[384,1536]{1,0:T(8,128)(2,1)S(1)}, bf16[384,1536]{1,0:T(8,128)(2,1)S(1)}, u32[]{:S(2)}, u32[]{:S(2)}) collective-permute-start(bf16[384,1536]{1,0:T(8,128)(2,1)S(1)} %shard_map.86.refs_6_.refs_2_), channel_id=1, source_target_pairs={{0,1},{1,0},{2,3},{3,2},{4,5},{5,4},{6,7},{7,6},{8,9},{9,8},{10,11... | collective-permute-start | bytes 3538952 | tf_op jit(solution)/shard_map/ppermute | solution.py:24
  53.2 3.7 %collective-permute-done.11.refs_0_ = bf16[192,1536]{1,0:T(8,128)(2,1)S(1)} collective-permute-done((bf16[192,1536]{1,0:T(8,128)(2,1)S(1)}, bf16[192,1536]{1,0:T(8,128)(2,1)S(1)}, u32[]{:S(2)}, u32[]{:S(2)}) %collective-permute-start.11) | collective-permute-done | bytes 589856 | tf_op jit(solution)/shard_map/ppermute | solution.py:24
  56.8 3.1 %collective-permute-start.15 = (bf16[192,1536]{1,0:T(8,128)(2,1)S(1)}, bf16[192,1536]{1,0:T(8,128)(2,1)S(1)}, u32[]{:S(2)}, u32[]{:S(2)}) collective-permute-start(bf16[192,1536]{1,0:T(8,128)(2,1)S(1)} %collective-permute-done.11.refs_0_), channel_id=1, source_target_pairs={{0,1},{1,0},{2,3},{3,2},{4,5},{5,4},{6,7},{7,6},{8,9},{9,8},{10,11... | collective-permute-start | bytes 1769480 | tf_op jit(solution)/shard_map/ppermute | solution.py:24
  59.9 1.2 %shard_map.80.refs_2_ = bf16[256,1152]{1,0:T(8,128)(2,1)S(1)} custom-call(bf16[128,1536]{1,0:T(8,128)(2,1)S(1)} %collective-permute-done.13.refs_0_, bf16[128,1536]{1,0:T(8,128)(2,1)S(1)} %collective-permute-done.14.refs_1_, bf16[3,1536,384]{2,1,0:T(8,128)(2,1)S(1)} %copy-done), custom_call_target="tpu_custom_call" | custom-call | flops 905969664 | bytes 4915200 | tf_op jit(solution)/shard_map/pallas_call | solution.py:197
  61.1 6.5 %shard_map.81 = (bf16[1,256,384]{2,1,0:T(8,128)(2,1)S(1)}, bf16[1,256,384]{2,1,0:T(8,128)(2,1)S(1)}, bf16[1,256,384]{2,1,0:T(8,128)(2,1)S(1)}, bf16[1,256,384]{2,1,0:T(8,128)(2,1)S(1)}) custom-call(bf16[512,1152]{1,0:T(8,128)(2,1)S(1)} %get-tuple-element.36.refs_0_, bf16[256,1152]{1,0:T(8,128)(2,1)S(1)} %shard_map.79.refs_1_, ...), custom_call_target="tpu_custom_call" | custom-call | flops 4294967296 | bytes 2359296 | tf_op jit(solution)/shard_map/pallas_call | solution.py:285
  67.7 0.3 collective-permute-start.23
  68.0 1.7 %shard_map.78.refs_1_ = bf16[384,1152]{1,0:T(8,128)(2,1)S(1)} custom-call(bf16[192,1536]{1,0:T(8,128)(2,1)S(1)} %shard_map.77.refs_0_, bf16[192,1536]{1,0:T(8,128)(2,1)S(1)} %collective-permute-done.10.refs_1_, bf16[3,1536,384]{2,1,0:T(8,128)(2,1)S(1)} %copy-done), custom_call_target="tpu_custom_call" | custom-call | flops 1358954496 | bytes 5603328 | tf_op jit(solution)/shard_map/pallas_call | solution.py:197
  69.7 1.9 %collective-permute-start.24 = (bf16[1,256,384]{2,1,0:T(8,128)(2,1)S(1)}, bf16[1,256,384]{2,1,0:T(8,128)(2,1)S(1)}, u32[]{:S(2)}, u32[]{:S(2)}) collective-permute-start(bf16[1,256,384]{2,1,0:T(8,128)(2,1)S(1)} %get-tuple-element.46), channel_id=1, source_target_pairs={{0,3},{1,2},{2,1},{3,0},{4,7},{5,6},{6,5},{7,4},{8,11},{9,10},{10,... | collective-permute-start | bytes 589832 | tf_op jit(solution)/shard_map/ppermute | solution.py:24
  71.6 1.7 %shard_map.82.refs_2_ = bf16[384,1152]{1,0:T(8,128)(2,1)S(1)} custom-call(bf16[192,1536]{1,0:T(8,128)(2,1)S(1)} %collective-permute-done.11.refs_0_, bf16[192,1536]{1,0:T(8,128)(2,1)S(1)} %collective-permute-done.15.refs_1_, bf16[3,1536,384]{2,1,0:T(8,128)(2,1)S(1)} %copy-done), custom_call_target="tpu_custom_call" | custom-call | flops 1358954496 | bytes 5603328 | tf_op jit(solution)/shard_map/pallas_call | solution.py:197
  73.2 3.5 %shard_map.83 = (bf16[1,256,384]{2,1,0:T(8,128)(2,1)S(1)}, bf16[1,256,384]{2,1,0:T(8,128)(2,1)S(1)}) custom-call(bf16[256,1152]{1,0:T(8,128)(2,1)S(1)} %get-tuple-element.52.refs_0_, bf16[384,1152]{1,0:T(8,128)(2,1)S(1)} %shard_map.78.refs_1_, bf16[384,1152]{1,0:T(8,128)(2,1)S(1)} %shard_map.82.refs_2_, bf16[1024,128]{1,0:T(8,128)(2,1)S(1)} %get-tuple-element.48.refs_3_, ...), custom_call_target="tpu_custom_call" | custom-call | flops 2147483648 | bytes 2359296 | tf_op jit(solution)/shard_map/pallas_call | solution.py:285
  76.8 3.5 %shard_map.87 = (bf16[1,256,384]{2,1,0:T(8,128)(2,1)S(1)}, bf16[1,256,384]{2,1,0:T(8,128)(2,1)S(1)}) custom-call(bf16[256,1152]{1,0:T(8,128)(2,1)S(1)} %get-tuple-element.52.refs_0_, bf16[384,1152]{1,0:T(8,128)(2,1)S(1)} %shard_map.78.refs_1_, bf16[384,1152]{1,0:T(8,128)(2,1)S(1)} %shard_map.82.refs_2_, bf16[1024,128]{1,0:T(8,128)(2,1)S(1)} %get-tuple-element.48.refs_3_, ...), custom_call_target="tpu_custom_call" | custom-call | flops 2147483648 | bytes 2359296 | tf_op jit(solution)/shard_map/pallas_call | solution.py:285
  80.7 1.8 %collective-permute-start.17 = (bf16[1,256,384]{2,1,0:T(8,128)(2,1)S(1)}, bf16[1,256,384]{2,1,0:T(8,128)(2,1)S(1)}, u32[]{:S(2)}, u32[]{:S(2)}) collective-permute-start(bf16[1,256,384]{2,1,0:T(8,128)(2,1)S(1)} %get-tuple-element.51), channel_id=1, source_target_pairs={{0,3},{1,2},{2,1},{3,0},{4,7},{5,6},{6,5},{7,4},{8,11},{9,10},{10,... | collective-permute-start | bytes 589832 | tf_op jit(solution)/shard_map/ppermute | solution.py:24
  82.5 1.8 %shard_map.88.refs_5_ = bf16[8,32,1536]{2,1,0:T(8,128)(2,1)S(1)} custom-call(bf16[256,384]{1,0:T(8,128)(2,1)S(1)} %bitcast.19, bf16[256,384]{1,0:T(8,128)(2,1)S(1)} %bitcast.20, bf16[256,384]{1,0:T(8,128)(2,1)S(1)} %bitcast.21, bf16[256,384]{1,0:T(8,128)(2,1)S(1)} %bitcast.22, bf16[384,1536]{1,0:T(8,128)(2,1)S(1)} %copy-done.4, ...), custom_call_target="tpu_custom_call" | custom-call | flops 1207959552 | bytes 7077888 | tf_op jit(solution)/shard_map/pallas_call | solution.py:342
  84.3 1.0 %shard_map.89.refs_4_ = f32[256,1536]{1,0:T(8,128)S(1)} custom-call(bf16[256,384]{1,0:T(8,128)(2,1)S(1)} %bitcast.17, bf16[256,384]{1,0:T(8,128)(2,1)S(1)} %bitcast.18, bf16[384,1536]{1,0:T(8,128)(2,1)S(1)} %copy-done.4, bf16[384,1536]{1,0:T(8,128)(2,1)S(1)} %collective-permute-done.25.refs_5_.refs_3_), custom_call_target="tpu_custom_call" | custom-call | flops 603979776 | bytes 2752512 | tf_op jit(solution)/shard_map/pallas_call | solution.py:317
  85.3 1.2 %collective-permute-done.16 = bf16[1,256,384]{2,1,0:T(8,128)(2,1)S(1)} collective-permute-done((bf16[1,256,384]{2,1,0:T(8,128)(2,1)S(1)}, bf16[1,256,384]{2,1,0:T(8,128)(2,1)S(1)}, u32[]{:S(2)}, u32[]{:S(2)}) %collective-permute-start.16) | collective-permute-done | bytes 196640 | tf_op jit(solution)/shard_map/ppermute | solution.py:24
  86.5 4.8 %collective-permute-done.17 = bf16[1,256,384]{2,1,0:T(8,128)(2,1)S(1)} collective-permute-done((bf16[1,256,384]{2,1,0:T(8,128)(2,1)S(1)}, bf16[1,256,384]{2,1,0:T(8,128)(2,1)S(1)}, u32[]{:S(2)}, u32[]{:S(2)}) %collective-permute-start.17) | collective-permute-done | bytes 196640 | tf_op jit(solution)/shard_map/ppermute | solution.py:24
  91.3 2.1 %shard_map.90 = bf16[8,64,1536]{2,1,0:T(8,128)(2,1)} custom-call(bf16[256,384]{1,0:T(8,128)(2,1)S(1)} %bitcast.23, bf16[256,384]{1,0:T(8,128)(2,1)S(1)} %bitcast.24, bf16[384,1536]{1,0:T(8,128)(2,1)S(1)} %shard_map.86.refs_6_.refs_2_, bf16[384,1536]{1,0:T(8,128)(2,1)S(1)} %collective-permute-done.21.refs_7_.refs_3_, f32[256,1536]{1,0:T(8,128)S(1)} %shard_map.89.refs_4_, ...), custom_call_target="tpu_custom_call" | custom-call | flops 603979776 | bytes 7077888 | tf_op jit(solution)/shard_map/pallas_call | solution.py:388
  (48 shorter events, 1.9 us)
Async XLA Ops:
  0.0 1.4 %copy-start.1 = (bf16[1,8,1,64,1536]{4,3,2,1,0:T(8,128)(2,1)S(1)}, bf16[1,8,1,64,1536]{4,3,2,1,0:T(8,128)(2,1)}, u32[]{:S(2)}) copy-start(bf16[1,8,1,64,1536]{4,3,2,1,0:T(8,128)(2,1)} %param.7) | copy-start | bytes 4718596
  1.4 12.8 %copy-start.2 = (bf16[1,8,1,64,1536]{4,3,2,1,0:T(8,128)(2,1)S(1)}, bf16[1,8,1,64,1536]{4,3,2,1,0:T(8,128)(2,1)}, u32[]{:S(2)}) copy-start(bf16[1,8,1,64,1536]{4,3,2,1,0:T(8,128)(2,1)} %param.7) | copy-start | bytes 4718596
  1.5 10.1 %collective-permute-start.1 = (bf16[4,32,1536]{2,1,0:T(8,128)(2,1)S(1)}, bf16[4,32,1536]{2,1,0:T(8,128)(2,1)S(1)}, u32[]{:S(2)}, u32[]{:S(2)}) collective-permute-start(bf16[4,32,1536]{2,1,0:T(8,128)(2,1)S(1)} %get-tuple-element.31.refs_0_), channel_id=1, source_target_pairs={{0,2},{1,3},{2,0},{3,1},{4,6},{5,7},{6,4},{7,5},{8,10},{9,11},{10,... | collective-permute-start | bytes 1179656 | tf_op jit(solution)/shard_map/ppermute | solution.py:24
  1.8 1.3 %copy-start.3 = (bf16[384,1536]{1,0:T(8,128)(2,1)S(1)}, bf16[384,1536]{1,0:T(8,128)(2,1)}, u32[]{:S(2)}) copy-start(bf16[384,1536]{1,0:T(8,128)(2,1)} %refs_2_.13) | copy-start | bytes 3538948
  3.2 14.7 %collective-permute-start.18 = (bf16[96,1536]{1,0:T(8,128)(2,1)S(1)}, bf16[96,1536]{1,0:T(8,128)(2,1)S(1)}, u32[]{:S(2)}, u32[]{:S(2)}) collective-permute-start(bf16[96,1536]{1,0:T(8,128)(2,1)S(1)} %shard_map.84), channel_id=1, source_target_pairs={{0,2},{1,3},{2,0},{3,1},{4,6},{5,7},{6,4},{7,5},{8,10},{9,11},{10,... | collective-permute-start | bytes 884744 | tf_op jit(solution)/shard_map/ppermute | solution.py:24
  4.4 19.2 %collective-permute-start.3 = (bf16[4,32,1536]{2,1,0:T(8,128)(2,1)S(1)}, bf16[4,32,1536]{2,1,0:T(8,128)(2,1)S(1)}, u32[]{:S(2)}, u32[]{:S(2)}) collective-permute-start(bf16[4,32,1536]{2,1,0:T(8,128)(2,1)S(1)} %get-tuple-element.32), channel_id=1, source_target_pairs={{0,4},{4,0},{8,12},{12,8},{1,5},{5,1},{9,13},{13,9},{2,6},{6,2},{1... | collective-permute-start | bytes 1179656 | tf_op jit(solution)/shard_map/ppermute | solution.py:24
  5.7 20.2 %collective-permute-start = (bf16[4,32,1536]{2,1,0:T(8,128)(2,1)S(1)}, bf16[4,32,1536]{2,1,0:T(8,128)(2,1)S(1)}, u32[]{:S(2)}, u32[]{:S(2)}) collective-permute-start(bf16[4,32,1536]{2,1,0:T(8,128)(2,1)S(1)} %get-tuple-element.31.refs_0_), channel_id=1, source_target_pairs={{0,1},{1,0},{2,3},{3,2},{4,5},{5,4},{6,7},{7,6},{8,9},{9,8},{10,11... | collective-permute-start | bytes 1179656 | tf_op jit(solution)/shard_map/ppermute | solution.py:24
  11.6 14.5 %collective-permute-start.2 = (bf16[4,32,1536]{2,1,0:T(8,128)(2,1)S(1)}, bf16[4,32,1536]{2,1,0:T(8,128)(2,1)S(1)}, u32[]{:S(2)}, u32[]{:S(2)}) collective-permute-start(bf16[4,32,1536]{2,1,0:T(8,128)(2,1)S(1)} %collective-permute-done.1.refs_2_), channel_id=1, source_target_pairs={{0,1},{1,0},{2,3},{3,2},{4,5},{5,4},{6,7},{7,6},{8,9},{9,8},{10,11... | collective-permute-start | bytes 1179656 | tf_op jit(solution)/shard_map/ppermute | solution.py:24
  14.2 0.7 copy-start.5
  14.9 0.7 copy-start.7
  15.9 7.0 %collective-permute-start.5 = (bf16[64,1536]{1,0:T(8,128)(2,1)S(1)}, bf16[64,1536]{1,0:T(8,128)(2,1)S(1)}, u32[]{:S(2)}, u32[]{:S(2)}) collective-permute-start(bf16[64,1536]{1,0:T(8,128)(2,1)S(1)} %shard_map.74.refs_1_), channel_id=1, source_target_pairs={{0,2},{1,3},{2,0},{3,1},{4,6},{5,7},{6,4},{7,5},{8,10},{9,11},{10,... | collective-permute-start | bytes 589832 | tf_op jit(solution)/shard_map/ppermute | solution.py:24
  17.9 6.7 %collective-permute-start.19 = (bf16[96,1536]{1,0:T(8,128)(2,1)S(1)}, bf16[96,1536]{1,0:T(8,128)(2,1)S(1)}, u32[]{:S(2)}, u32[]{:S(2)}) collective-permute-start(bf16[96,1536]{1,0:T(8,128)(2,1)S(1)} %collective-permute-done.18.own_ref), channel_id=1, source_target_pairs={{0,16},{16,0},{1,17},{17,1},{2,18},{18,2},{3,19},{19,3},{4,20},{20... | collective-permute-start | bytes 884744 | tf_op jit(solution)/shard_map/ppermute | solution.py:24
  22.9 5.6 %collective-permute-start.4 = (bf16[64,1536]{1,0:T(8,128)(2,1)S(1)}, bf16[64,1536]{1,0:T(8,128)(2,1)S(1)}, u32[]{:S(2)}, u32[]{:S(2)}) collective-permute-start(bf16[64,1536]{1,0:T(8,128)(2,1)S(1)} %shard_map.74.refs_1_), channel_id=1, source_target_pairs={{0,1},{1,0},{2,3},{3,2},{4,5},{5,4},{6,7},{7,6},{8,9},{9,8},{10,11... | collective-permute-start | bytes 589832 | tf_op jit(solution)/shard_map/ppermute | solution.py:24
  23.6 5.2 %collective-permute-start.6 = (bf16[64,1536]{1,0:T(8,128)(2,1)S(1)}, bf16[64,1536]{1,0:T(8,128)(2,1)S(1)}, u32[]{:S(2)}, u32[]{:S(2)}) collective-permute-start(bf16[64,1536]{1,0:T(8,128)(2,1)S(1)} %collective-permute-done.5.refs_3_), channel_id=1, source_target_pairs={{0,1},{1,0},{2,3},{3,2},{4,5},{5,4},{6,7},{7,6},{8,9},{9,8},{10,11... | collective-permute-start | bytes 589832 | tf_op jit(solution)/shard_map/ppermute | solution.py:24
  24.6 9.7 %collective-permute-start.7 = (bf16[4,16,1536]{2,1,0:T(8,128)(2,1)S(1)}, bf16[4,16,1536]{2,1,0:T(8,128)(2,1)S(1)}, u32[]{:S(2)}, u32[]{:S(2)}) collective-permute-start(bf16[4,16,1536]{2,1,0:T(8,128)(2,1)S(1)} %get-tuple-element.35), channel_id=1, source_target_pairs={{0,4},{4,0},{8,12},{12,8},{1,5},{5,1},{9,13},{13,9},{2,6},{6,2},{1... | collective-permute-start | bytes 589832 | tf_op jit(solution)/shard_map/ppermute | solution.py:24
  25.9 5.2 %copy-start = (bf16[3,1536,384]{2,1,0:T(8,128)(2,1)S(1)}, bf16[3,1536,384]{2,1,0:T(8,128)(2,1)}, u32[]{:S(2)}) copy-start(bf16[3,1536,384]{2,1,0:T(8,128)(2,1)} %refs_2_.12) | copy-start | bytes 10616836
  25.9 8.4 %collective-permute-start.8 = (bf16[4,16,1536]{2,1,0:T(8,128)(2,1)S(1)}, bf16[4,16,1536]{2,1,0:T(8,128)(2,1)S(1)}, u32[]{:S(2)}, u32[]{:S(2)}) collective-permute-start(bf16[4,16,1536]{2,1,0:T(8,128)(2,1)S(1)} %get-tuple-element.38), channel_id=1, source_target_pairs={{0,8},{4,12},{8,0},{12,4},{1,9},{5,13},{9,1},{13,5},{2,10},{6,14},... | collective-permute-start | bytes 589832 | tf_op jit(solution)/shard_map/ppermute | solution.py:24
  26.1 17.6 %collective-permute-start.9 = (bf16[4,16,1536]{2,1,0:T(8,128)(2,1)S(1)}, bf16[4,16,1536]{2,1,0:T(8,128)(2,1)S(1)}, u32[]{:S(2)}, u32[]{:S(2)}) collective-permute-start(bf16[4,16,1536]{2,1,0:T(8,128)(2,1)S(1)} %get-tuple-element.39), channel_id=1, source_target_pairs={{0,12},{4,8},{8,4},{12,0},{1,13},{5,9},{9,5},{13,1},{2,14},{6,10},... | collective-permute-start | bytes 589832 | tf_op jit(solution)/shard_map/ppermute | solution.py:24
  28.5 15.2 %copy-start.6 = (f32[1536]{0:T(1024)S(1)}, f32[1536]{0:T(1024)}, u32[]{:S(2)}) copy-start(f32[1536]{0:T(1024)} %refs_3_.1) | copy-start | bytes 18436
  28.5 15.2 %copy-start.8 = (f32[1536]{0:T(1024)S(1)}, f32[1536]{0:T(1024)}, u32[]{:S(2)}) copy-start(f32[1536]{0:T(1024)} %refs_4_.4) | copy-start | bytes 18436
  28.5 18.9 %copy-start.9 = (s32[1,32,64]{2,1,0:T(8,128)S(1)}, s32[1,32,64]{2,1,0:T(8,128)}, u32[]{:S(2)}) copy-start(s32[1,32,64]{2,1,0:T(8,128)} %param.8) | copy-start | bytes 24580
  28.5 18.4 %collective-permute-start.13 = (bf16[128,1536]{1,0:T(8,128)(2,1)S(1)}, bf16[128,1536]{1,0:T(8,128)(2,1)S(1)}, u32[]{:S(2)}, u32[]{:S(2)}) collective-permute-start(bf16[128,1536]{1,0:T(8,128)(2,1)S(1)} %shard_map.75.refs_0_), channel_id=1, source_target_pairs={{0,2},{1,3},{2,0},{3,1},{4,6},{5,7},{6,4},{7,5},{8,10},{9,11},{10,... | collective-permute-start | bytes 1179656 | tf_op jit(solution)/shard_map/ppermute | solution.py:24
  28.8 21.7 %collective-permute-start.20 = (bf16[192,1536]{1,0:T(8,128)(2,1)S(1)}, bf16[192,1536]{1,0:T(8,128)(2,1)S(1)}, u32[]{:S(2)}, u32[]{:S(2)}) collective-permute-start(bf16[192,1536]{1,0:T(8,128)(2,1)S(1)} %shard_map.85.own_ref), channel_id=1, source_target_pairs={{0,4},{4,0},{8,12},{12,8},{1,5},{5,1},{9,13},{13,9},{2,6},{6,2},{1... | collective-permute-start | bytes 1769480 | tf_op jit(solution)/shard_map/ppermute | solution.py:24
  44.1 12.7 %collective-permute-start.11 = (bf16[192,1536]{1,0:T(8,128)(2,1)S(1)}, bf16[192,1536]{1,0:T(8,128)(2,1)S(1)}, u32[]{:S(2)}, u32[]{:S(2)}) collective-permute-start(bf16[192,1536]{1,0:T(8,128)(2,1)S(1)} %shard_map.77.refs_0_), channel_id=1, source_target_pairs={{0,2},{1,3},{2,0},{3,1},{4,6},{5,7},{6,4},{7,5},{8,10},{9,11},{10,... | collective-permute-start | bytes 1769480 | tf_op jit(solution)/shard_map/ppermute | solution.py:24
  44.4 3.9 %collective-permute-start.12 = (bf16[128,1536]{1,0:T(8,128)(2,1)S(1)}, bf16[128,1536]{1,0:T(8,128)(2,1)S(1)}, u32[]{:S(2)}, u32[]{:S(2)}) collective-permute-start(bf16[128,1536]{1,0:T(8,128)(2,1)S(1)} %shard_map.75.refs_0_), channel_id=1, source_target_pairs={{0,1},{1,0},{2,3},{3,2},{4,5},{5,4},{6,7},{7,6},{8,9},{9,8},{10,11... | collective-permute-start | bytes 1179656 | tf_op jit(solution)/shard_map/ppermute | solution.py:24
  46.9 13.0 %collective-permute-start.14 = (bf16[128,1536]{1,0:T(8,128)(2,1)S(1)}, bf16[128,1536]{1,0:T(8,128)(2,1)S(1)}, u32[]{:S(2)}, u32[]{:S(2)}) collective-permute-start(bf16[128,1536]{1,0:T(8,128)(2,1)S(1)} %collective-permute-done.13.refs_0_), channel_id=1, source_target_pairs={{0,1},{1,0},{2,3},{3,2},{4,5},{5,4},{6,7},{7,6},{8,9},{9,8},{10,11... | collective-permute-start | bytes 1179656 | tf_op jit(solution)/shard_map/ppermute | solution.py:24
  46.9 20.7 %collective-permute-start.10 = (bf16[192,1536]{1,0:T(8,128)(2,1)S(1)}, bf16[192,1536]{1,0:T(8,128)(2,1)S(1)}, u32[]{:S(2)}, u32[]{:S(2)}) collective-permute-start(bf16[192,1536]{1,0:T(8,128)(2,1)S(1)} %shard_map.77.refs_0_), channel_id=1, source_target_pairs={{0,1},{1,0},{2,3},{3,2},{4,5},{5,4},{6,7},{7,6},{8,9},{9,8},{10,11... | collective-permute-start | bytes 1769480 | tf_op jit(solution)/shard_map/ppermute | solution.py:24
  47.4 1.3 %copy-start.4 = (bf16[384,1536]{1,0:T(8,128)(2,1)S(1)}, bf16[384,1536]{1,0:T(8,128)(2,1)}, u32[]{:S(2)}) copy-start(bf16[384,1536]{1,0:T(8,128)(2,1)} %refs_2_.13) | copy-start | bytes 3538948
  48.7 31.6 %collective-permute-start.25 = (bf16[384,1536]{1,0:T(8,128)(2,1)S(1)}, bf16[384,1536]{1,0:T(8,128)(2,1)S(1)}, u32[]{:S(2)}, u32[]{:S(2)}) collective-permute-start(bf16[384,1536]{1,0:T(8,128)(2,1)S(1)} %copy-done.4), channel_id=1, source_target_pairs={{0,1},{1,0},{2,3},{3,2},{4,5},{5,4},{6,7},{7,6},{8,9},{9,8},{10,11... | collective-permute-start | bytes 3538952 | tf_op jit(solution)/shard_map/ppermute | solution.py:24
  50.6 10.5 %copy-start.10 = (f32[4]{0:T(128)S(1)}, f32[4]{0:T(128)}, u32[]{:S(2)}) copy-start(f32[4]{0:T(128)} %refs_5_.9) | copy-start | bytes 52
  50.7 31.8 %collective-permute-start.21 = (bf16[384,1536]{1,0:T(8,128)(2,1)S(1)}, bf16[384,1536]{1,0:T(8,128)(2,1)S(1)}, u32[]{:S(2)}, u32[]{:S(2)}) collective-permute-start(bf16[384,1536]{1,0:T(8,128)(2,1)S(1)} %shard_map.86.refs_6_.refs_2_), channel_id=1, source_target_pairs={{0,1},{1,0},{2,3},{3,2},{4,5},{5,4},{6,7},{7,6},{8,9},{9,8},{10,11... | collective-permute-start | bytes 3538952 | tf_op jit(solution)/shard_map/ppermute | solution.py:24
  56.8 12.9 %collective-permute-start.15 = (bf16[192,1536]{1,0:T(8,128)(2,1)S(1)}, bf16[192,1536]{1,0:T(8,128)(2,1)S(1)}, u32[]{:S(2)}, u32[]{:S(2)}) collective-permute-start(bf16[192,1536]{1,0:T(8,128)(2,1)S(1)} %collective-permute-done.11.refs_0_), channel_id=1, source_target_pairs={{0,1},{1,0},{2,3},{3,2},{4,5},{5,4},{6,7},{7,6},{8,9},{9,8},{10,11... | collective-permute-start | bytes 1769480 | tf_op jit(solution)/shard_map/ppermute | solution.py:24
  67.6 12.8 %collective-permute-start.22 = (bf16[1,256,384]{2,1,0:T(8,128)(2,1)S(1)}, bf16[1,256,384]{2,1,0:T(8,128)(2,1)S(1)}, u32[]{:S(2)}, u32[]{:S(2)}) collective-permute-start(bf16[1,256,384]{2,1,0:T(8,128)(2,1)S(1)} %get-tuple-element.44), channel_id=1, source_target_pairs={{0,1},{1,0},{2,3},{3,2},{4,5},{5,4},{6,7},{7,6},{8,9},{9,8},{10,11... | collective-permute-start | bytes 589832 | tf_op jit(solution)/shard_map/ppermute | solution.py:24
  67.7 13.0 %collective-permute-start.23 = (bf16[1,256,384]{2,1,0:T(8,128)(2,1)S(1)}, bf16[1,256,384]{2,1,0:T(8,128)(2,1)S(1)}, u32[]{:S(2)}, u32[]{:S(2)}) collective-permute-start(bf16[1,256,384]{2,1,0:T(8,128)(2,1)S(1)} %get-tuple-element.45), channel_id=1, source_target_pairs={{0,2},{1,3},{2,0},{3,1},{4,6},{5,7},{6,4},{7,5},{8,10},{9,11},{10,... | collective-permute-start | bytes 589832 | tf_op jit(solution)/shard_map/ppermute | solution.py:24
  69.7 12.8 %collective-permute-start.24 = (bf16[1,256,384]{2,1,0:T(8,128)(2,1)S(1)}, bf16[1,256,384]{2,1,0:T(8,128)(2,1)S(1)}, u32[]{:S(2)}, u32[]{:S(2)}) collective-permute-start(bf16[1,256,384]{2,1,0:T(8,128)(2,1)S(1)} %get-tuple-element.46), channel_id=1, source_target_pairs={{0,3},{1,2},{2,1},{3,0},{4,7},{5,6},{6,5},{7,4},{8,11},{9,10},{10,... | collective-permute-start | bytes 589832 | tf_op jit(solution)/shard_map/ppermute | solution.py:24
  80.3 4.0 %collective-permute-start.26 = (bf16[1,256,384]{2,1,0:T(8,128)(2,1)S(1)}, bf16[1,256,384]{2,1,0:T(8,128)(2,1)S(1)}, u32[]{:S(2)}, u32[]{:S(2)}) collective-permute-start(bf16[1,256,384]{2,1,0:T(8,128)(2,1)S(1)} %get-tuple-element.54), channel_id=1, source_target_pairs={{0,1},{1,0},{2,3},{3,2},{4,5},{5,4},{6,7},{7,6},{8,9},{9,8},{10,11... | collective-permute-start | bytes 589832 | tf_op jit(solution)/shard_map/ppermute | solution.py:24
  80.4 6.1 %collective-permute-start.16 = (bf16[1,256,384]{2,1,0:T(8,128)(2,1)S(1)}, bf16[1,256,384]{2,1,0:T(8,128)(2,1)S(1)}, u32[]{:S(2)}, u32[]{:S(2)}) collective-permute-start(bf16[1,256,384]{2,1,0:T(8,128)(2,1)S(1)} %get-tuple-element.50), channel_id=1, source_target_pairs={{0,2},{1,3},{2,0},{3,1},{4,6},{5,7},{6,4},{7,5},{8,10},{9,11},{10,... | collective-permute-start | bytes 589832 | tf_op jit(solution)/shard_map/ppermute | solution.py:24
  80.7 10.6 %collective-permute-start.17 = (bf16[1,256,384]{2,1,0:T(8,128)(2,1)S(1)}, bf16[1,256,384]{2,1,0:T(8,128)(2,1)S(1)}, u32[]{:S(2)}, u32[]{:S(2)}) collective-permute-start(bf16[1,256,384]{2,1,0:T(8,128)(2,1)S(1)} %get-tuple-element.51), channel_id=1, source_target_pairs={{0,3},{1,2},{2,1},{3,0},{4,7},{5,6},{6,5},{7,4},{8,11},{9,10},{10,... | collective-permute-start | bytes 589832 | tf_op jit(solution)/shard_map/ppermute | solution.py:24

commit v7 on v6

--- a/solution.py
+++ b/solution.py
@@ -521,15 +521,14 @@
     south_pieces = gather_pieces(south_normed)
     spans = [(piece, row, 0, WS) for piece in range(count) for row in range(rows)]
     (local_0_normed,) = norm(local_0_pieces, gain, bias, [spans])
-    local_1_pieces[0] = after(local_1, south_normed)
-    local_0, local_1 = project([[local_0_normed], local_1_pieces], weights)
+    (local_0,) = project([[local_0_normed]], weights)
     spans = [(0, row, 0, near) for row in range(rows)]
     spans += [(which, row, 0, half) for which in (1, 2) for row in range(rows)]
-    (rest_normed,) = norm([after(south_1, local_0), east, corner], gain, bias, [spans])
+    (rest_normed,) = norm([south_1, east, corner], gain, bias, [spans])
     rest_pieces = gather_pieces(rest_normed)
     split = count // 2
     near_lanes, far_lanes, all_lanes = (0, split), (split, count), (0, count)
-    (south_near,) = project([south_pieces[:split]], weights)
+    south_near, local_1 = project([south_pieces[:split], local_1_pieces], weights)
     south_pieces[split] = after(south_pieces[split], south_near)
     (south_far,) = project([south_pieces[split:]], weights)
     (rest_near,) = project([rest_pieces[:split]], weights)

time: 93.8 us -> 95.2 us (1.015)
  the two profiles are of different devices: /device:TPU:19 before, /device:TPU:0 now
where the time goes in v7:
time: 95.2 us; the launch traced here: 93.3 us
  waiting for transfers between devices  31.8 us (33%)
  Pallas kernels  30.1 us (32%)
  starting transfers between devices  28.2 us (30%)
  local copies, waits for them, and re-layouts  2.83 us (3%)
    ppermute x27, waiting for transfers between devices, permute_by(): return lax.ppermute(value, axis, pairs)  31.8 us
    ppermute x27, starting transfers between devices, permute_by(): return lax.ppermute(value, axis, pairs)  28.2 us
    pallas_call x3, Pallas kernels, attend(): pl.pallas_call(functools.partial(attend_kernel, layout, ranges, head_widt...  13.5 us
    pallas_call x5, Pallas kernels, project(): pl.pallas_call(functools.partial(project_kernel, [len(group) for group in...  8.99 us
    unnamed x16, local copies, waits for them, and re-layouts  2.83 us
    pallas_call x4, Pallas kernels, norm(): pl.pallas_call(functools.partial(norm_kernel, groups), out_shape=[jax.Sha...  2.11 us
    pallas_call x1, Pallas kernels, finish_last(): pl.pallas_call(functools.partial(last_kernel, count, chunks, spans), out_...  2.05 us
  transfers between devices with their start and end apart: 27, of which 7 were waited for; matrix products, arithmetic and copies ran while one was open for 0% of the time, Pallas kernels for 30%

profile of v7, /device:TPU:0, one launch (start us, length us, event | category | flops | bytes accessed | tf_op | source)
XLA Modules:
  0.0 93.3 jit_solution(3904552394417064606)
XLA Ops:
  0.0 1.4 %copy-done.1 = bf16[1,8,1,64,1536]{4,3,2,1,0:T(8,128)(2,1)S(1)} copy-done((bf16[1,8,1,64,1536]{4,3,2,1,0:T(8,128)(2,1)S(1)}, bf16[1,8,1,64,1536]{4,3,2,1,0:T(8,128)(2,1)}, u32[]{:S(2)}) %copy-start.1) | copy-done | bytes 1572888
  1.4 0.7 copy-done.4
  2.1 0.7 copy-done.5
  2.8 0.2 shard_map.74.refs_2_
  3.1 3.0 %collective-permute-start.3 = (bf16[64,1536]{1,0:T(8,128)(2,1)S(1)}, bf16[64,1536]{1,0:T(8,128)(2,1)S(1)}, u32[]{:S(2)}, u32[]{:S(2)}) collective-permute-start(bf16[64,1536]{1,0:T(8,128)(2,1)S(1)} %shard_map.74.refs_2_), channel_id=1, source_target_pairs={{0,2},{1,3},{2,0},{3,1},{4,6},{5,7},{6,4},{7,5},{8,10},{9,11},{10,... | collective-permute-start | bytes 589832 | tf_op jit(solution)/shard_map/ppermute | solution.py:24
  6.1 0.1 cut.1
  6.4 2.0 %collective-permute-start.18 = (bf16[96,1536]{1,0:T(8,128)(2,1)S(1)}, bf16[96,1536]{1,0:T(8,128)(2,1)S(1)}, u32[]{:S(2)}, u32[]{:S(2)}) collective-permute-start(bf16[96,1536]{1,0:T(8,128)(2,1)S(1)} %shard_map.84), channel_id=1, source_target_pairs={{0,2},{1,3},{2,0},{3,1},{4,6},{5,7},{6,4},{7,5},{8,10},{9,11},{10,... | collective-permute-start | bytes 884744 | tf_op jit(solution)/shard_map/ppermute | solution.py:24
  8.4 1.6 %collective-permute-start.5 = (bf16[4,16,1536]{2,1,0:T(8,128)(2,1)S(1)}, bf16[4,16,1536]{2,1,0:T(8,128)(2,1)S(1)}, u32[]{:S(2)}, u32[]{:S(2)}) collective-permute-start(bf16[4,16,1536]{2,1,0:T(8,128)(2,1)S(1)} %get-tuple-element.31), channel_id=1, source_target_pairs={{0,4},{4,0},{8,12},{12,8},{1,5},{5,1},{9,13},{13,9},{2,6},{6,2},{1... | collective-permute-start | bytes 589832 | tf_op jit(solution)/shard_map/ppermute | solution.py:24
  10.0 0.4 collective-permute-start
  10.4 1.4 %collective-permute-done.3.refs_4_ = bf16[64,1536]{1,0:T(8,128)(2,1)S(1)} collective-permute-done((bf16[64,1536]{1,0:T(8,128)(2,1)S(1)}, bf16[64,1536]{1,0:T(8,128)(2,1)S(1)}, u32[]{:S(2)}, u32[]{:S(2)}) %collective-permute-start.3) | collective-permute-done | bytes 196640 | tf_op jit(solution)/shard_map/ppermute | solution.py:24
  11.8 3.1 %collective-permute-start.6 = (bf16[4,16,1536]{2,1,0:T(8,128)(2,1)S(1)}, bf16[4,16,1536]{2,1,0:T(8,128)(2,1)S(1)}, u32[]{:S(2)}, u32[]{:S(2)}) collective-permute-start(bf16[4,16,1536]{2,1,0:T(8,128)(2,1)S(1)} %get-tuple-element.32), channel_id=1, source_target_pairs={{0,8},{4,12},{8,0},{12,4},{1,9},{5,13},{9,1},{13,5},{2,10},{6,14},... | collective-permute-start | bytes 589832 | tf_op jit(solution)/shard_map/ppermute | solution.py:24
  15.0 10.8 %collective-permute-done.18.own_ref = bf16[96,1536]{1,0:T(8,128)(2,1)S(1)} collective-permute-done((bf16[96,1536]{1,0:T(8,128)(2,1)S(1)}, bf16[96,1536]{1,0:T(8,128)(2,1)S(1)}, u32[]{:S(2)}, u32[]{:S(2)}) %collective-permute-start.18) | collective-permute-done | bytes 294944 | tf_op jit(solution)/shard_map/ppermute | solution.py:24
  25.7 1.8 %collective-permute-start.19 = (bf16[96,1536]{1,0:T(8,128)(2,1)S(1)}, bf16[96,1536]{1,0:T(8,128)(2,1)S(1)}, u32[]{:S(2)}, u32[]{:S(2)}) collective-permute-start(bf16[96,1536]{1,0:T(8,128)(2,1)S(1)} %collective-permute-done.18.own_ref), channel_id=1, source_target_pairs={{0,16},{16,0},{1,17},{17,1},{2,18},{18,2},{3,19},{19,3},{4,20},{20... | collective-permute-start | bytes 884744 | tf_op jit(solution)/shard_map/ppermute | solution.py:24
  27.5 3.6 %collective-permute-start.7 = (bf16[4,16,1536]{2,1,0:T(8,128)(2,1)S(1)}, bf16[4,16,1536]{2,1,0:T(8,128)(2,1)S(1)}, u32[]{:S(2)}, u32[]{:S(2)}) collective-permute-start(bf16[4,16,1536]{2,1,0:T(8,128)(2,1)S(1)} %get-tuple-element.33), channel_id=1, source_target_pairs={{0,12},{4,8},{8,4},{12,0},{1,13},{5,9},{9,5},{13,1},{2,14},{6,10},... | collective-permute-start | bytes 589832 | tf_op jit(solution)/shard_map/ppermute | solution.py:24
  31.1 0.5 collective-permute-start.12
  31.6 3.4 %collective-permute-done.7.refs_2_.refs_9_ = bf16[4,16,1536]{2,1,0:T(8,128)(2,1)S(1)} collective-permute-done((bf16[4,16,1536]{2,1,0:T(8,128)(2,1)S(1)}, bf16[4,16,1536]{2,1,0:T(8,128)(2,1)S(1)}, u32[]{:S(2)}, u32[]{:S(2)}) %collective-permute-start.7) | collective-permute-done | bytes 196640 | tf_op jit(solution)/shard_map/ppermute | solution.py:24
  35.0 0.5 collective-permute-start.4
  35.5 0.3 shard_map.73.refs_0_
  35.8 1.6 %collective-permute-start.13 = (bf16[128,1536]{1,0:T(8,128)(2,1)S(1)}, bf16[128,1536]{1,0:T(8,128)(2,1)S(1)}, u32[]{:S(2)}, u32[]{:S(2)}) collective-permute-start(bf16[128,1536]{1,0:T(8,128)(2,1)S(1)} %shard_map.73.refs_0_), channel_id=1, source_target_pairs={{0,2},{1,3},{2,0},{3,1},{4,6},{5,7},{6,4},{7,5},{8,10},{9,11},{10,... | collective-permute-start | bytes 1179656 | tf_op jit(solution)/shard_map/ppermute | solution.py:24
  37.4 0.4 shard_map.76.refs_0_
  37.9 0.6 collective-permute-start.9
  38.5 3.8 %collective-permute-start.20 = (bf16[192,1536]{1,0:T(8,128)(2,1)S(1)}, bf16[192,1536]{1,0:T(8,128)(2,1)S(1)}, u32[]{:S(2)}, u32[]{:S(2)}) collective-permute-start(bf16[192,1536]{1,0:T(8,128)(2,1)S(1)} %shard_map.85.own_ref), channel_id=1, source_target_pairs={{0,4},{4,0},{8,12},{12,8},{1,5},{5,1},{9,13},{13,9},{2,6},{6,2},{1... | collective-permute-start | bytes 1769480 | tf_op jit(solution)/shard_map/ppermute | solution.py:24
  42.3 0.5 collective-permute-start.1
  42.8 0.4 tags.1
  43.2 1.1 %shard_map.78.refs_0_ = bf16[512,1536]{1,0:T(8,128)(2,1)S(1)} custom-call(bf16[4,32,1536]{2,1,0:T(8,128)(2,1)S(1)} %get-tuple-element.34.refs_0_, bf16[4,32,1536]{2,1,0:T(8,128)(2,1)S(1)} %collective-permute-done.10.refs_1_, bf16[4,32,1536]{2,1,0:T(8,128)(2,1)S(1)} %collective-permute-done.11.refs_2_, ...), custom_call_target="tpu_custom_call" | custom-call | flops 7864320 | bytes 3145728 | tf_op jit(solution)/shard_map/pallas_call | solution.py:102
  44.3 3.6 %collective-permute-done.13.refs_0_ = bf16[128,1536]{1,0:T(8,128)(2,1)S(1)} collective-permute-done((bf16[128,1536]{1,0:T(8,128)(2,1)S(1)}, bf16[128,1536]{1,0:T(8,128)(2,1)S(1)}, u32[]{:S(2)}, u32[]{:S(2)}) %collective-permute-start.13) | collective-permute-done | bytes 393248 | tf_op jit(solution)/shard_map/ppermute | solution.py:24
  47.9 2.2 %shard_map.79.refs_0_ = bf16[512,1152]{1,0:T(8,128)(2,1)S(1)} custom-call(bf16[512,1536]{1,0:T(8,128)(2,1)S(1)} %shard_map.78.refs_0_, bf16[3,1536,384]{2,1,0:T(8,128)(2,1)S(1)} %copy-done), custom_call_target="tpu_custom_call" | custom-call | flops 1811939328 | bytes 6291456 | tf_op jit(solution)/shard_map/pallas_call | solution.py:197
  50.1 0.6 collective-permute-start.25
  50.7 2.2 %shard_map.75 = (bf16[256,1152]{1,0:T(8,128)(2,1)S(1)}, bf16[256,1152]{1,0:T(8,128)(2,1)S(1)}) custom-call(bf16[128,1536]{1,0:T(8,128)(2,1)S(1)} %shard_map.73.refs_0_, bf16[128,1536]{1,0:T(8,128)(2,1)S(1)} %collective-permute-done.1.refs_1_, bf16[64,1536]{1,0:T(8,128)(2,1)S(1)} %shard_map.74.refs_2_, bf16[64,1536]{1,0:T(8,128)(2,1)S(1)} %collective-permute-done.2.refs_3_, ...), custom_call_target="tpu_custom_call" | custom-call | flops 1811939328 | bytes 6291456 | tf_op jit(solution)/shard_map/pallas_call | solution.py:197
  52.9 6.7 %collective-permute-done.9.refs_0_ = bf16[192,1536]{1,0:T(8,128)(2,1)S(1)} collective-permute-done((bf16[192,1536]{1,0:T(8,128)(2,1)S(1)}, bf16[192,1536]{1,0:T(8,128)(2,1)S(1)}, u32[]{:S(2)}, u32[]{:S(2)}) %collective-permute-start.9) | collective-permute-done | bytes 589856 | tf_op jit(solution)/shard_map/ppermute | solution.py:24
  59.6 0.1 shard_map.86.refs_6_.refs_2_
  59.7 0.6 collective-permute-start.21
  60.3 1.7 %shard_map.77.refs_1_ = bf16[384,1152]{1,0:T(8,128)(2,1)S(1)} custom-call(bf16[192,1536]{1,0:T(8,128)(2,1)S(1)} %shard_map.76.refs_0_, bf16[192,1536]{1,0:T(8,128)(2,1)S(1)} %collective-permute-done.8.refs_1_, bf16[3,1536,384]{2,1,0:T(8,128)(2,1)S(1)} %copy-done), custom_call_target="tpu_custom_call" | custom-call | flops 1358954496 | bytes 5603328 | tf_op jit(solution)/shard_map/pallas_call | solution.py:197
  62.0 1.2 %shard_map.80.refs_2_ = bf16[256,1152]{1,0:T(8,128)(2,1)S(1)} custom-call(bf16[128,1536]{1,0:T(8,128)(2,1)S(1)} %collective-permute-done.13.refs_0_, bf16[128,1536]{1,0:T(8,128)(2,1)S(1)} %collective-permute-done.14.refs_1_, bf16[3,1536,384]{2,1,0:T(8,128)(2,1)S(1)} %copy-done), custom_call_target="tpu_custom_call" | custom-call | flops 905969664 | bytes 4915200 | tf_op jit(solution)/shard_map/pallas_call | solution.py:197
  63.2 6.5 %shard_map.81 = (bf16[1,256,384]{2,1,0:T(8,128)(2,1)S(1)}, bf16[1,256,384]{2,1,0:T(8,128)(2,1)S(1)}, bf16[1,256,384]{2,1,0:T(8,128)(2,1)S(1)}, bf16[1,256,384]{2,1,0:T(8,128)(2,1)S(1)}) custom-call(bf16[512,1152]{1,0:T(8,128)(2,1)S(1)} %shard_map.79.refs_0_, bf16[256,1152]{1,0:T(8,128)(2,1)S(1)} %get-tuple-element.35.refs_1_, ...), custom_call_target="tpu_custom_call" | custom-call | flops 4294967296 | bytes 2359296 | tf_op jit(solution)/shard_map/pallas_call | solution.py:285
  69.7 0.1 collective-permute-start.22
  69.8 1.6 %collective-permute-start.23 = (bf16[1,256,384]{2,1,0:T(8,128)(2,1)S(1)}, bf16[1,256,384]{2,1,0:T(8,128)(2,1)S(1)}, u32[]{:S(2)}, u32[]{:S(2)}) collective-permute-start(bf16[1,256,384]{2,1,0:T(8,128)(2,1)S(1)} %get-tuple-element.41), channel_id=1, source_target_pairs={{0,2},{1,3},{2,0},{3,1},{4,6},{5,7},{6,4},{7,5},{8,10},{9,11},{10,... | collective-permute-start | bytes 589832 | tf_op jit(solution)/shard_map/ppermute | solution.py:24
  71.3 0.3 collective-permute-start.24
  71.6 1.7 %shard_map.82.refs_2_ = bf16[384,1152]{1,0:T(8,128)(2,1)S(1)} custom-call(bf16[192,1536]{1,0:T(8,128)(2,1)S(1)} %collective-permute-done.9.refs_0_, bf16[192,1536]{1,0:T(8,128)(2,1)S(1)} %collective-permute-done.15.refs_1_, bf16[3,1536,384]{2,1,0:T(8,128)(2,1)S(1)} %copy-done), custom_call_target="tpu_custom_call" | custom-call | flops 1358954496 | bytes 5603328 | tf_op jit(solution)/shard_map/pallas_call | solution.py:197
  73.3 3.5 %shard_map.83 = (bf16[1,256,384]{2,1,0:T(8,128)(2,1)S(1)}, bf16[1,256,384]{2,1,0:T(8,128)(2,1)S(1)}) custom-call(bf16[256,1152]{1,0:T(8,128)(2,1)S(1)} %get-tuple-element.48.refs_0_, bf16[384,1152]{1,0:T(8,128)(2,1)S(1)} %shard_map.77.refs_1_, bf16[384,1152]{1,0:T(8,128)(2,1)S(1)} %shard_map.82.refs_2_, bf16[1024,128]{1,0:T(8,128)(2,1)S(1)} %get-tuple-element.44.refs_3_, ...), custom_call_target="tpu_custom_call" | custom-call | flops 2147483648 | bytes 2359296 | tf_op jit(solution)/shard_map/pallas_call | solution.py:285
  76.8 3.5 %shard_map.87 = (bf16[1,256,384]{2,1,0:T(8,128)(2,1)S(1)}, bf16[1,256,384]{2,1,0:T(8,128)(2,1)S(1)}) custom-call(bf16[256,1152]{1,0:T(8,128)(2,1)S(1)} %get-tuple-element.48.refs_0_, bf16[384,1152]{1,0:T(8,128)(2,1)S(1)} %shard_map.77.refs_1_, bf16[384,1152]{1,0:T(8,128)(2,1)S(1)} %shard_map.82.refs_2_, bf16[1024,128]{1,0:T(8,128)(2,1)S(1)} %get-tuple-element.44.refs_3_, ...), custom_call_target="tpu_custom_call" | custom-call | flops 2147483648 | bytes 2359296 | tf_op jit(solution)/shard_map/pallas_call | solution.py:285
  80.3 0.4 collective-permute-start.26
  80.8 1.5 %collective-permute-start.16 = (bf16[1,256,384]{2,1,0:T(8,128)(2,1)S(1)}, bf16[1,256,384]{2,1,0:T(8,128)(2,1)S(1)}, u32[]{:S(2)}, u32[]{:S(2)}) collective-permute-start(bf16[1,256,384]{2,1,0:T(8,128)(2,1)S(1)} %get-tuple-element.46), channel_id=1, source_target_pairs={{0,2},{1,3},{2,0},{3,1},{4,6},{5,7},{6,4},{7,5},{8,10},{9,11},{10,... | collective-permute-start | bytes 589832 | tf_op jit(solution)/shard_map/ppermute | solution.py:24
  82.3 1.8 %shard_map.88.refs_5_ = bf16[8,32,1536]{2,1,0:T(8,128)(2,1)S(1)} custom-call(bf16[256,384]{1,0:T(8,128)(2,1)S(1)} %bitcast.19, bf16[256,384]{1,0:T(8,128)(2,1)S(1)} %bitcast.20, bf16[256,384]{1,0:T(8,128)(2,1)S(1)} %bitcast.21, bf16[256,384]{1,0:T(8,128)(2,1)S(1)} %bitcast.22, bf16[384,1536]{1,0:T(8,128)(2,1)S(1)} %copy-done.3, ...), custom_call_target="tpu_custom_call" | custom-call | flops 1207959552 | bytes 7077888 | tf_op jit(solution)/shard_map/pallas_call | solution.py:342
  84.1 1.0 %shard_map.89.refs_4_ = f32[256,1536]{1,0:T(8,128)S(1)} custom-call(bf16[256,384]{1,0:T(8,128)(2,1)S(1)} %bitcast.17, bf16[256,384]{1,0:T(8,128)(2,1)S(1)} %bitcast.18, bf16[384,1536]{1,0:T(8,128)(2,1)S(1)} %copy-done.3, bf16[384,1536]{1,0:T(8,128)(2,1)S(1)} %collective-permute-done.25.refs_5_.refs_3_), custom_call_target="tpu_custom_call" | custom-call | flops 603979776 | bytes 2752512 | tf_op jit(solution)/shard_map/pallas_call | solution.py:317
  85.1 3.5 %collective-permute-done.16 = bf16[1,256,384]{2,1,0:T(8,128)(2,1)S(1)} collective-permute-done((bf16[1,256,384]{2,1,0:T(8,128)(2,1)S(1)}, bf16[1,256,384]{2,1,0:T(8,128)(2,1)S(1)}, u32[]{:S(2)}, u32[]{:S(2)}) %collective-permute-start.16) | collective-permute-done | bytes 196640 | tf_op jit(solution)/shard_map/ppermute | solution.py:24
  88.5 2.6 %collective-permute-done.17 = bf16[1,256,384]{2,1,0:T(8,128)(2,1)S(1)} collective-permute-done((bf16[1,256,384]{2,1,0:T(8,128)(2,1)S(1)}, bf16[1,256,384]{2,1,0:T(8,128)(2,1)S(1)}, u32[]{:S(2)}, u32[]{:S(2)}) %collective-permute-start.17) | collective-permute-done | bytes 196640 | tf_op jit(solution)/shard_map/ppermute | solution.py:24
  91.1 2.1 %shard_map.90 = bf16[8,64,1536]{2,1,0:T(8,128)(2,1)} custom-call(bf16[256,384]{1,0:T(8,128)(2,1)S(1)} %bitcast.23, bf16[256,384]{1,0:T(8,128)(2,1)S(1)} %bitcast.24, bf16[384,1536]{1,0:T(8,128)(2,1)S(1)} %shard_map.86.refs_6_.refs_2_, bf16[384,1536]{1,0:T(8,128)(2,1)S(1)} %collective-permute-done.21.refs_7_.refs_3_, f32[256,1536]{1,0:T(8,128)S(1)} %shard_map.89.refs_4_, ...), custom_call_target="tpu_custom_call" | custom-call | flops 603979776 | bytes 7077888 | tf_op jit(solution)/shard_map/pallas_call | solution.py:388
  (42 shorter events, 0.3 us)
Async XLA Ops:
  0.0 1.4 %copy-start.1 = (bf16[1,8,1,64,1536]{4,3,2,1,0:T(8,128)(2,1)S(1)}, bf16[1,8,1,64,1536]{4,3,2,1,0:T(8,128)(2,1)}, u32[]{:S(2)}) copy-start(bf16[1,8,1,64,1536]{4,3,2,1,0:T(8,128)(2,1)} %param.7) | copy-start | bytes 4718596
  1.4 0.7 copy-start.4
  2.1 0.7 copy-start.5
  2.8 3.5 %copy-start.3 = (bf16[384,1536]{1,0:T(8,128)(2,1)S(1)}, bf16[384,1536]{1,0:T(8,128)(2,1)}, u32[]{:S(2)}) copy-start(bf16[384,1536]{1,0:T(8,128)(2,1)} %refs_2_.11) | copy-start | bytes 3538948
  3.1 8.8 %collective-permute-start.3 = (bf16[64,1536]{1,0:T(8,128)(2,1)S(1)}, bf16[64,1536]{1,0:T(8,128)(2,1)S(1)}, u32[]{:S(2)}, u32[]{:S(2)}) collective-permute-start(bf16[64,1536]{1,0:T(8,128)(2,1)S(1)} %shard_map.74.refs_2_), channel_id=1, source_target_pairs={{0,2},{1,3},{2,0},{3,1},{4,6},{5,7},{6,4},{7,5},{8,10},{9,11},{10,... | collective-permute-start | bytes 589832 | tf_op jit(solution)/shard_map/ppermute | solution.py:24
  6.2 24.9 %collective-permute-start.11 = (bf16[4,32,1536]{2,1,0:T(8,128)(2,1)S(1)}, bf16[4,32,1536]{2,1,0:T(8,128)(2,1)S(1)}, u32[]{:S(2)}, u32[]{:S(2)}) collective-permute-start(bf16[4,32,1536]{2,1,0:T(8,128)(2,1)S(1)} %get-tuple-element.34.refs_0_), channel_id=1, source_target_pairs={{0,2},{1,3},{2,0},{3,1},{4,6},{5,7},{6,4},{7,5},{8,10},{9,11},{10,... | collective-permute-start | bytes 1179656 | tf_op jit(solution)/shard_map/ppermute | solution.py:24
  6.3 36.6 %copy-start = (bf16[3,1536,384]{2,1,0:T(8,128)(2,1)S(1)}, bf16[3,1536,384]{2,1,0:T(8,128)(2,1)}, u32[]{:S(2)}) copy-start(bf16[3,1536,384]{2,1,0:T(8,128)(2,1)} %refs_2_.10) | copy-start | bytes 10616836
  6.4 19.4 %collective-permute-start.18 = (bf16[96,1536]{1,0:T(8,128)(2,1)S(1)}, bf16[96,1536]{1,0:T(8,128)(2,1)S(1)}, u32[]{:S(2)}, u32[]{:S(2)}) collective-permute-start(bf16[96,1536]{1,0:T(8,128)(2,1)S(1)} %shard_map.84), channel_id=1, source_target_pairs={{0,2},{1,3},{2,0},{3,1},{4,6},{5,7},{6,4},{7,5},{8,10},{9,11},{10,... | collective-permute-start | bytes 884744 | tf_op jit(solution)/shard_map/ppermute | solution.py:24
  8.4 19.1 %collective-permute-start.5 = (bf16[4,16,1536]{2,1,0:T(8,128)(2,1)S(1)}, bf16[4,16,1536]{2,1,0:T(8,128)(2,1)S(1)}, u32[]{:S(2)}, u32[]{:S(2)}) collective-permute-start(bf16[4,16,1536]{2,1,0:T(8,128)(2,1)S(1)} %get-tuple-element.31), channel_id=1, source_target_pairs={{0,4},{4,0},{8,12},{12,8},{1,5},{5,1},{9,13},{13,9},{2,6},{6,2},{1... | collective-permute-start | bytes 589832 | tf_op jit(solution)/shard_map/ppermute | solution.py:24
  10.0 25.0 %collective-permute-start = (bf16[4,32,1536]{2,1,0:T(8,128)(2,1)S(1)}, bf16[4,32,1536]{2,1,0:T(8,128)(2,1)S(1)}, u32[]{:S(2)}, u32[]{:S(2)}) collective-permute-start(bf16[4,32,1536]{2,1,0:T(8,128)(2,1)S(1)} %get-tuple-element.29), channel_id=1, source_target_pairs={{0,4},{4,0},{8,12},{12,8},{1,5},{5,1},{9,13},{13,9},{2,6},{6,2},{1... | collective-permute-start | bytes 1179656 | tf_op jit(solution)/shard_map/ppermute | solution.py:24
  11.8 19.3 %collective-permute-start.6 = (bf16[4,16,1536]{2,1,0:T(8,128)(2,1)S(1)}, bf16[4,16,1536]{2,1,0:T(8,128)(2,1)S(1)}, u32[]{:S(2)}, u32[]{:S(2)}) collective-permute-start(bf16[4,16,1536]{2,1,0:T(8,128)(2,1)S(1)} %get-tuple-element.32), channel_id=1, source_target_pairs={{0,8},{4,12},{8,0},{12,4},{1,9},{5,13},{9,1},{13,5},{2,10},{6,14},... | collective-permute-start | bytes 589832 | tf_op jit(solution)/shard_map/ppermute | solution.py:24
  25.7 10.1 %collective-permute-start.19 = (bf16[96,1536]{1,0:T(8,128)(2,1)S(1)}, bf16[96,1536]{1,0:T(8,128)(2,1)S(1)}, u32[]{:S(2)}, u32[]{:S(2)}) collective-permute-start(bf16[96,1536]{1,0:T(8,128)(2,1)S(1)} %collective-permute-done.18.own_ref), channel_id=1, source_target_pairs={{0,16},{16,0},{1,17},{17,1},{2,18},{18,2},{3,19},{19,3},{4,20},{20... | collective-permute-start | bytes 884744 | tf_op jit(solution)/shard_map/ppermute | solution.py:24
  27.5 15.3 %copy-start.6 = (s32[1,32,64]{2,1,0:T(8,128)S(1)}, s32[1,32,64]{2,1,0:T(8,128)}, u32[]{:S(2)}) copy-start(s32[1,32,64]{2,1,0:T(8,128)} %param.8) | copy-start | bytes 24580
  27.5 7.5 %collective-permute-start.7 = (bf16[4,16,1536]{2,1,0:T(8,128)(2,1)S(1)}, bf16[4,16,1536]{2,1,0:T(8,128)(2,1)S(1)}, u32[]{:S(2)}, u32[]{:S(2)}) collective-permute-start(bf16[4,16,1536]{2,1,0:T(8,128)(2,1)S(1)} %get-tuple-element.33), channel_id=1, source_target_pairs={{0,12},{4,8},{8,4},{12,0},{1,13},{5,9},{9,5},{13,1},{2,14},{6,10},... | collective-permute-start | bytes 589832 | tf_op jit(solution)/shard_map/ppermute | solution.py:24
  31.1 11.2 %collective-permute-start.10 = (bf16[4,32,1536]{2,1,0:T(8,128)(2,1)S(1)}, bf16[4,32,1536]{2,1,0:T(8,128)(2,1)S(1)}, u32[]{:S(2)}, u32[]{:S(2)}) collective-permute-start(bf16[4,32,1536]{2,1,0:T(8,128)(2,1)S(1)} %get-tuple-element.34.refs_0_), channel_id=1, source_target_pairs={{0,1},{1,0},{2,3},{3,2},{4,5},{5,4},{6,7},{7,6},{8,9},{9,8},{10,11... | collective-permute-start | bytes 1179656 | tf_op jit(solution)/shard_map/ppermute | solution.py:24
  31.1 11.2 %collective-permute-start.12 = (bf16[4,32,1536]{2,1,0:T(8,128)(2,1)S(1)}, bf16[4,32,1536]{2,1,0:T(8,128)(2,1)S(1)}, u32[]{:S(2)}, u32[]{:S(2)}) collective-permute-start(bf16[4,32,1536]{2,1,0:T(8,128)(2,1)S(1)} %collective-permute-done.11.refs_2_), channel_id=1, source_target_pairs={{0,1},{1,0},{2,3},{3,2},{4,5},{5,4},{6,7},{7,6},{8,9},{9,8},{10,11... | collective-permute-start | bytes 1179656 | tf_op jit(solution)/shard_map/ppermute | solution.py:24
  35.0 2.9 %collective-permute-start.2 = (bf16[64,1536]{1,0:T(8,128)(2,1)S(1)}, bf16[64,1536]{1,0:T(8,128)(2,1)S(1)}, u32[]{:S(2)}, u32[]{:S(2)}) collective-permute-start(bf16[64,1536]{1,0:T(8,128)(2,1)S(1)} %shard_map.74.refs_2_), channel_id=1, source_target_pairs={{0,1},{1,0},{2,3},{3,2},{4,5},{5,4},{6,7},{7,6},{8,9},{9,8},{10,11... | collective-permute-start | bytes 589832 | tf_op jit(solution)/shard_map/ppermute | solution.py:24
  35.0 3.5 %collective-permute-start.4 = (bf16[64,1536]{1,0:T(8,128)(2,1)S(1)}, bf16[64,1536]{1,0:T(8,128)(2,1)S(1)}, u32[]{:S(2)}, u32[]{:S(2)}) collective-permute-start(bf16[64,1536]{1,0:T(8,128)(2,1)S(1)} %collective-permute-done.3.refs_4_), channel_id=1, source_target_pairs={{0,1},{1,0},{2,3},{3,2},{4,5},{5,4},{6,7},{7,6},{8,9},{9,8},{10,11... | collective-permute-start | bytes 589832 | tf_op jit(solution)/shard_map/ppermute | solution.py:24
  35.8 12.1 %collective-permute-start.13 = (bf16[128,1536]{1,0:T(8,128)(2,1)S(1)}, bf16[128,1536]{1,0:T(8,128)(2,1)S(1)}, u32[]{:S(2)}, u32[]{:S(2)}) collective-permute-start(bf16[128,1536]{1,0:T(8,128)(2,1)S(1)} %shard_map.73.refs_0_), channel_id=1, source_target_pairs={{0,2},{1,3},{2,0},{3,1},{4,6},{5,7},{6,4},{7,5},{8,10},{9,11},{10,... | collective-permute-start | bytes 1179656 | tf_op jit(solution)/shard_map/ppermute | solution.py:24
  37.9 21.7 %collective-permute-start.9 = (bf16[192,1536]{1,0:T(8,128)(2,1)S(1)}, bf16[192,1536]{1,0:T(8,128)(2,1)S(1)}, u32[]{:S(2)}, u32[]{:S(2)}) collective-permute-start(bf16[192,1536]{1,0:T(8,128)(2,1)S(1)} %shard_map.76.refs_0_), channel_id=1, source_target_pairs={{0,2},{1,3},{2,0},{3,1},{4,6},{5,7},{6,4},{7,5},{8,10},{9,11},{10,... | collective-permute-start | bytes 1769480 | tf_op jit(solution)/shard_map/ppermute | solution.py:24
  38.5 21.1 %collective-permute-start.20 = (bf16[192,1536]{1,0:T(8,128)(2,1)S(1)}, bf16[192,1536]{1,0:T(8,128)(2,1)S(1)}, u32[]{:S(2)}, u32[]{:S(2)}) collective-permute-start(bf16[192,1536]{1,0:T(8,128)(2,1)S(1)} %shard_map.85.own_ref), channel_id=1, source_target_pairs={{0,4},{4,0},{8,12},{12,8},{1,5},{5,1},{9,13},{13,9},{2,6},{6,2},{1... | collective-permute-start | bytes 1769480 | tf_op jit(solution)/shard_map/ppermute | solution.py:24
  42.3 17.9 %collective-permute-start.8 = (bf16[192,1536]{1,0:T(8,128)(2,1)S(1)}, bf16[192,1536]{1,0:T(8,128)(2,1)S(1)}, u32[]{:S(2)}, u32[]{:S(2)}) collective-permute-start(bf16[192,1536]{1,0:T(8,128)(2,1)S(1)} %shard_map.76.refs_0_), channel_id=1, source_target_pairs={{0,1},{1,0},{2,3},{3,2},{4,5},{5,4},{6,7},{7,6},{8,9},{9,8},{10,11... | collective-permute-start | bytes 1769480 | tf_op jit(solution)/shard_map/ppermute | solution.py:24
  42.3 7.8 %collective-permute-start.1 = (bf16[128,1536]{1,0:T(8,128)(2,1)S(1)}, bf16[128,1536]{1,0:T(8,128)(2,1)S(1)}, u32[]{:S(2)}, u32[]{:S(2)}) collective-permute-start(bf16[128,1536]{1,0:T(8,128)(2,1)S(1)} %shard_map.73.refs_0_), channel_id=1, source_target_pairs={{0,1},{1,0},{2,3},{3,2},{4,5},{5,4},{6,7},{7,6},{8,9},{9,8},{10,11... | collective-permute-start | bytes 1179656 | tf_op jit(solution)/shard_map/ppermute | solution.py:24
  47.9 14.1 %collective-permute-start.14 = (bf16[128,1536]{1,0:T(8,128)(2,1)S(1)}, bf16[128,1536]{1,0:T(8,128)(2,1)S(1)}, u32[]{:S(2)}, u32[]{:S(2)}) collective-permute-start(bf16[128,1536]{1,0:T(8,128)(2,1)S(1)} %collective-permute-done.13.refs_0_), channel_id=1, source_target_pairs={{0,1},{1,0},{2,3},{3,2},{4,5},{5,4},{6,7},{7,6},{8,9},{9,8},{10,11... | collective-permute-start | bytes 1179656 | tf_op jit(solution)/shard_map/ppermute | solution.py:24
  50.1 30.2 %collective-permute-start.25 = (bf16[384,1536]{1,0:T(8,128)(2,1)S(1)}, bf16[384,1536]{1,0:T(8,128)(2,1)S(1)}, u32[]{:S(2)}, u32[]{:S(2)}) collective-permute-start(bf16[384,1536]{1,0:T(8,128)(2,1)S(1)} %copy-done.3), channel_id=1, source_target_pairs={{0,1},{1,0},{2,3},{3,2},{4,5},{5,4},{6,7},{7,6},{8,9},{9,8},{10,11... | collective-permute-start | bytes 3538952 | tf_op jit(solution)/shard_map/ppermute | solution.py:24
  59.6 11.7 %collective-permute-start.15 = (bf16[192,1536]{1,0:T(8,128)(2,1)S(1)}, bf16[192,1536]{1,0:T(8,128)(2,1)S(1)}, u32[]{:S(2)}, u32[]{:S(2)}) collective-permute-start(bf16[192,1536]{1,0:T(8,128)(2,1)S(1)} %collective-permute-done.9.refs_0_), channel_id=1, source_target_pairs={{0,1},{1,0},{2,3},{3,2},{4,5},{5,4},{6,7},{7,6},{8,9},{9,8},{10,11... | collective-permute-start | bytes 1769480 | tf_op jit(solution)/shard_map/ppermute | solution.py:24
  59.7 22.6 %collective-permute-start.21 = (bf16[384,1536]{1,0:T(8,128)(2,1)S(1)}, bf16[384,1536]{1,0:T(8,128)(2,1)S(1)}, u32[]{:S(2)}, u32[]{:S(2)}) collective-permute-start(bf16[384,1536]{1,0:T(8,128)(2,1)S(1)} %shard_map.86.refs_6_.refs_2_), channel_id=1, source_target_pairs={{0,1},{1,0},{2,3},{3,2},{4,5},{5,4},{6,7},{7,6},{8,9},{9,8},{10,11... | collective-permute-start | bytes 3538952 | tf_op jit(solution)/shard_map/ppermute | solution.py:24
  62.0 1.2 %copy-start.7 = (f32[4]{0:T(128)S(1)}, f32[4]{0:T(128)}, u32[]{:S(2)}) copy-start(f32[4]{0:T(128)} %refs_5_.7) | copy-start | bytes 52
  69.7 11.1 %collective-permute-start.22 = (bf16[1,256,384]{2,1,0:T(8,128)(2,1)S(1)}, bf16[1,256,384]{2,1,0:T(8,128)(2,1)S(1)}, u32[]{:S(2)}, u32[]{:S(2)}) collective-permute-start(bf16[1,256,384]{2,1,0:T(8,128)(2,1)S(1)} %get-tuple-element.40), channel_id=1, source_target_pairs={{0,1},{1,0},{2,3},{3,2},{4,5},{5,4},{6,7},{7,6},{8,9},{9,8},{10,11... | collective-permute-start | bytes 589832 | tf_op jit(solution)/shard_map/ppermute | solution.py:24
  69.8 12.5 %collective-permute-start.23 = (bf16[1,256,384]{2,1,0:T(8,128)(2,1)S(1)}, bf16[1,256,384]{2,1,0:T(8,128)(2,1)S(1)}, u32[]{:S(2)}, u32[]{:S(2)}) collective-permute-start(bf16[1,256,384]{2,1,0:T(8,128)(2,1)S(1)} %get-tuple-element.41), channel_id=1, source_target_pairs={{0,2},{1,3},{2,0},{3,1},{4,6},{5,7},{6,4},{7,5},{8,10},{9,11},{10,... | collective-permute-start | bytes 589832 | tf_op jit(solution)/shard_map/ppermute | solution.py:24
  71.3 11.0 %collective-permute-start.24 = (bf16[1,256,384]{2,1,0:T(8,128)(2,1)S(1)}, bf16[1,256,384]{2,1,0:T(8,128)(2,1)S(1)}, u32[]{:S(2)}, u32[]{:S(2)}) collective-permute-start(bf16[1,256,384]{2,1,0:T(8,128)(2,1)S(1)} %get-tuple-element.42), channel_id=1, source_target_pairs={{0,3},{1,2},{2,1},{3,0},{4,7},{5,6},{6,5},{7,4},{8,11},{9,10},{10,... | collective-permute-start | bytes 589832 | tf_op jit(solution)/shard_map/ppermute | solution.py:24
  76.8 5.5 %copy-start.2 = (bf16[1,8,1,64,1536]{4,3,2,1,0:T(8,128)(2,1)S(1)}, bf16[1,8,1,64,1536]{4,3,2,1,0:T(8,128)(2,1)}, u32[]{:S(2)}) copy-start(bf16[1,8,1,64,1536]{4,3,2,1,0:T(8,128)(2,1)} %param.7) | copy-start | bytes 4718596
  80.3 3.8 %collective-permute-start.26 = (bf16[1,256,384]{2,1,0:T(8,128)(2,1)S(1)}, bf16[1,256,384]{2,1,0:T(8,128)(2,1)S(1)}, u32[]{:S(2)}, u32[]{:S(2)}) collective-permute-start(bf16[1,256,384]{2,1,0:T(8,128)(2,1)S(1)} %get-tuple-element.50), channel_id=1, source_target_pairs={{0,1},{1,0},{2,3},{3,2},{4,5},{5,4},{6,7},{7,6},{8,9},{9,8},{10,11... | collective-permute-start | bytes 589832 | tf_op jit(solution)/shard_map/ppermute | solution.py:24
  80.8 7.8 %collective-permute-start.16 = (bf16[1,256,384]{2,1,0:T(8,128)(2,1)S(1)}, bf16[1,256,384]{2,1,0:T(8,128)(2,1)S(1)}, u32[]{:S(2)}, u32[]{:S(2)}) collective-permute-start(bf16[1,256,384]{2,1,0:T(8,128)(2,1)S(1)} %get-tuple-element.46), channel_id=1, source_target_pairs={{0,2},{1,3},{2,0},{3,1},{4,6},{5,7},{6,4},{7,5},{8,10},{9,11},{10,... | collective-permute-start | bytes 589832 | tf_op jit(solution)/shard_map/ppermute | solution.py:24
  82.3 8.8 %collective-permute-start.17 = (bf16[1,256,384]{2,1,0:T(8,128)(2,1)S(1)}, bf16[1,256,384]{2,1,0:T(8,128)(2,1)S(1)}, u32[]{:S(2)}, u32[]{:S(2)}) collective-permute-start(bf16[1,256,384]{2,1,0:T(8,128)(2,1)S(1)} %get-tuple-element.47), channel_id=1, source_target_pairs={{0,3},{1,2},{2,1},{3,0},{4,7},{5,6},{6,5},{7,4},{8,11},{9,10},{10,... | collective-permute-start | bytes 589832 | tf_op jit(solution)/shard_map/ppermute | solution.py:24

commit v8 on v7

--- a/solution.py
+++ b/solution.py
@@ -503,10 +503,15 @@
     weights = triple_projection_matrix
     scales = logit_scaling_per_part
 
-    boxes = [(rows, half, WS), (0, half, WS), (0, half + WS, near), (rows, 0, half), (0, 0, half)]
-    local_0, south_0, south_1, east, corner = cut(blocked, rows, boxes)
-    spans = [(0, rows + row, half + WS, near) for row in range(rows)]
-    (local_1,) = norm([blocked], gain, bias, [spans])
+    boxes = [
+        (rows, half, WS),
+        (rows, half + WS, near),
+        (0, half, WS),
+        (0, half + WS, near),
+        (rows, 0, half),
+        (0, 0, half),
+    ]
+    local_0, local_1, south_0, south_1, east, corner = cut(blocked, rows, boxes)
     south_0 = exchange(south_0, 1, "win")
     south_1 = exchange(south_1, 1, "win")
     east = permute_by(east, "win", west)
@@ -528,7 +533,9 @@
     rest_pieces = gather_pieces(rest_normed)
     split = count // 2
     near_lanes, far_lanes, all_lanes = (0, split), (split, count), (0, count)
-    south_near, local_1 = project([south_pieces[:split], local_1_pieces], weights)
+    spans = [(piece, row, 0, near) for piece in range(count) for row in range(rows)]
+    (local_1_normed,) = norm(local_1_pieces, gain, bias, [spans])
+    south_near, local_1 = project([south_pieces[:split], [local_1_normed]], weights)
     south_pieces[split] = after(south_pieces[split], south_near)
     (south_far,) = project([south_pieces[split:]], weights)
     (rest_near,) = project([rest_pieces[:split]], weights)

time: 95.2 us -> 84.6 us (0.89); the launches traced: 93.3 us -> 84.3 us
  waiting for transfers between devices: 31.8 us -> 25.1 us
  local copies, waits for them, and re-layouts: 2.83 us -> 1.44 us
  starting transfers between devices: 28.2 us -> 27 us
    ppermute x27, waiting for transfers between devices: 31.8 us -> 25.1 us  [permute_by(): return lax.ppermute(value, axis, pairs)]
    unnamed x16, local copies, waits for them, and re-layouts: 2.83 us -> 1.44 us
    ppermute x27, starting transfers between devices: 28.2 us -> 27 us  [permute_by(): return lax.ppermute(value, axis, pairs)]
  transfers between devices with their start and end apart: 27 -> 27, of which waited for: 7 -> 9; matrix products, arithmetic and copies ran while one was open for 0% -> 0% of each run, Pallas kernels for 30% -> 34%
where the time goes in v8:
time: 84.6 us; the launch traced here: 84.3 us
  Pallas kernels  30.4 us (36%)
  starting transfers between devices  27 us (32%)
  waiting for transfers between devices  25.1 us (30%)
  local copies, waits for them, and re-layouts  1.44 us (2%)
    ppermute x27, starting transfers between devices, permute_by(): return lax.ppermute(value, axis, pairs)  27 us
    ppermute x27, waiting for transfers between devices, permute_by(): return lax.ppermute(value, axis, pairs)  25.1 us
    pallas_call x3, Pallas kernels, attend(): pl.pallas_call(functools.partial(attend_kernel, layout, ranges, head_widt...  13.5 us
    pallas_call x5, Pallas kernels, project(): pl.pallas_call(functools.partial(project_kernel, [len(group) for group in...  9.01 us
    pallas_call x4, Pallas kernels, norm(): pl.pallas_call(functools.partial(norm_kernel, groups), out_shape=[jax.Sha...  2.43 us
    pallas_call x1, Pallas kernels, finish_last(): pl.pallas_call(functools.partial(last_kernel, count, chunks, spans), out_...  2.05 us
    pallas_call x1, Pallas kernels, finish(): pl.pallas_call(functools.partial(finish_kernel, count, spans), out_shape=...  1.79 us
  transfers between devices with their start and end apart: 27, of which 9 were waited for; matrix products, arithmetic and copies ran while one was open for 0% of the time, Pallas kernels for 34%

profile of v8, /device:TPU:0, one launch (start us, length us, event | category | flops | bytes accessed | tf_op | source)
XLA Modules:
  0.0 84.3 jit_solution(1040307059409410650)
XLA Ops:
  0.0 1.4 %copy-done.1 = bf16[1,8,1,64,1536]{4,3,2,1,0:T(8,128)(2,1)S(1)} copy-done((bf16[1,8,1,64,1536]{4,3,2,1,0:T(8,128)(2,1)S(1)}, bf16[1,8,1,64,1536]{4,3,2,1,0:T(8,128)(2,1)}, u32[]{:S(2)}) %copy-start.1) | copy-done | bytes 1572888
  1.4 0.1 cut.1
  1.5 3.1 %collective-permute-start = (bf16[4,32,1536]{2,1,0:T(8,128)(2,1)S(1)}, bf16[4,32,1536]{2,1,0:T(8,128)(2,1)S(1)}, u32[]{:S(2)}, u32[]{:S(2)}) collective-permute-start(bf16[4,32,1536]{2,1,0:T(8,128)(2,1)S(1)} %get-tuple-element.30), channel_id=1, source_target_pairs={{0,4},{4,0},{8,12},{12,8},{1,5},{5,1},{9,13},{13,9},{2,6},{6,2},{1... | collective-permute-start | bytes 1179656 | tf_op jit(solution)/shard_map/ppermute | solution.py:24
  4.6 1.5 %collective-permute-start.3 = (bf16[4,16,1536]{2,1,0:T(8,128)(2,1)S(1)}, bf16[4,16,1536]{2,1,0:T(8,128)(2,1)S(1)}, u32[]{:S(2)}, u32[]{:S(2)}) collective-permute-start(bf16[4,16,1536]{2,1,0:T(8,128)(2,1)S(1)} %get-tuple-element.31.refs_0_), channel_id=1, source_target_pairs={{0,2},{1,3},{2,0},{3,1},{4,6},{5,7},{6,4},{7,5},{8,10},{9,11},{10,... | collective-permute-start | bytes 589832 | tf_op jit(solution)/shard_map/ppermute | solution.py:24
  6.2 0.6 collective-permute-start.18
  6.8 0.6 collective-permute-start.5
  7.4 1.4 %collective-permute-start.11 = (bf16[4,32,1536]{2,1,0:T(8,128)(2,1)S(1)}, bf16[4,32,1536]{2,1,0:T(8,128)(2,1)S(1)}, u32[]{:S(2)}, u32[]{:S(2)}) collective-permute-start(bf16[4,32,1536]{2,1,0:T(8,128)(2,1)S(1)} %get-tuple-element.36.refs_0_), channel_id=1, source_target_pairs={{0,2},{1,3},{2,0},{3,1},{4,6},{5,7},{6,4},{7,5},{8,10},{9,11},{10,... | collective-permute-start | bytes 1179656 | tf_op jit(solution)/shard_map/ppermute | solution.py:24
  8.8 3.7 %collective-permute-done.3.refs_2_ = bf16[4,16,1536]{2,1,0:T(8,128)(2,1)S(1)} collective-permute-done((bf16[4,16,1536]{2,1,0:T(8,128)(2,1)S(1)}, bf16[4,16,1536]{2,1,0:T(8,128)(2,1)S(1)}, u32[]{:S(2)}, u32[]{:S(2)}) %collective-permute-start.3) | collective-permute-done | bytes 196640 | tf_op jit(solution)/shard_map/ppermute | solution.py:24
  12.4 2.6 %collective-permute-start.6 = (bf16[4,16,1536]{2,1,0:T(8,128)(2,1)S(1)}, bf16[4,16,1536]{2,1,0:T(8,128)(2,1)S(1)}, u32[]{:S(2)}, u32[]{:S(2)}) collective-permute-start(bf16[4,16,1536]{2,1,0:T(8,128)(2,1)S(1)} %get-tuple-element.34), channel_id=1, source_target_pairs={{0,8},{4,12},{8,0},{12,4},{1,9},{5,13},{9,1},{13,5},{2,10},{6,14},... | collective-permute-start | bytes 589832 | tf_op jit(solution)/shard_map/ppermute | solution.py:24
  15.0 3.7 %collective-permute-done.18.own_ref = bf16[96,1536]{1,0:T(8,128)(2,1)S(1)} collective-permute-done((bf16[96,1536]{1,0:T(8,128)(2,1)S(1)}, bf16[96,1536]{1,0:T(8,128)(2,1)S(1)}, u32[]{:S(2)}, u32[]{:S(2)}) %collective-permute-start.18) | collective-permute-done | bytes 294944 | tf_op jit(solution)/shard_map/ppermute | solution.py:24
  18.7 1.5 %collective-permute-start.19 = (bf16[96,1536]{1,0:T(8,128)(2,1)S(1)}, bf16[96,1536]{1,0:T(8,128)(2,1)S(1)}, u32[]{:S(2)}, u32[]{:S(2)}) collective-permute-start(bf16[96,1536]{1,0:T(8,128)(2,1)S(1)} %collective-permute-done.18.own_ref), channel_id=1, source_target_pairs={{0,16},{16,0},{1,17},{17,1},{2,18},{18,2},{3,19},{19,3},{4,20},{20... | collective-permute-start | bytes 884744 | tf_op jit(solution)/shard_map/ppermute | solution.py:24
  20.2 1.9 %collective-permute-done.5.refs_0_.refs_7_ = bf16[4,16,1536]{2,1,0:T(8,128)(2,1)S(1)} collective-permute-done((bf16[4,16,1536]{2,1,0:T(8,128)(2,1)S(1)}, bf16[4,16,1536]{2,1,0:T(8,128)(2,1)S(1)}, u32[]{:S(2)}, u32[]{:S(2)}) %collective-permute-start.5) | collective-permute-done | bytes 196640 | tf_op jit(solution)/shard_map/ppermute | solution.py:24
  22.2 3.8 %collective-permute-start.7 = (bf16[4,16,1536]{2,1,0:T(8,128)(2,1)S(1)}, bf16[4,16,1536]{2,1,0:T(8,128)(2,1)S(1)}, u32[]{:S(2)}, u32[]{:S(2)}) collective-permute-start(bf16[4,16,1536]{2,1,0:T(8,128)(2,1)S(1)} %get-tuple-element.35), channel_id=1, source_target_pairs={{0,12},{4,8},{8,4},{12,0},{1,13},{5,9},{9,5},{13,1},{2,14},{6,10},... | collective-permute-start | bytes 589832 | tf_op jit(solution)/shard_map/ppermute | solution.py:24
  26.0 0.3 shard_map.73.refs_0_
  26.3 1.6 %collective-permute-start.13 = (bf16[128,1536]{1,0:T(8,128)(2,1)S(1)}, bf16[128,1536]{1,0:T(8,128)(2,1)S(1)}, u32[]{:S(2)}, u32[]{:S(2)}) collective-permute-start(bf16[128,1536]{1,0:T(8,128)(2,1)S(1)} %shard_map.73.refs_0_), channel_id=1, source_target_pairs={{0,2},{1,3},{2,0},{3,1},{4,6},{5,7},{6,4},{7,5},{8,10},{9,11},{10,... | collective-permute-start | bytes 1179656 | tf_op jit(solution)/shard_map/ppermute | solution.py:24
  27.9 2.3 %collective-permute-done.7.refs_2_.refs_9_ = bf16[4,16,1536]{2,1,0:T(8,128)(2,1)S(1)} collective-permute-done((bf16[4,16,1536]{2,1,0:T(8,128)(2,1)S(1)}, bf16[4,16,1536]{2,1,0:T(8,128)(2,1)S(1)}, u32[]{:S(2)}, u32[]{:S(2)}) %collective-permute-start.7) | collective-permute-done | bytes 196640 | tf_op jit(solution)/shard_map/ppermute | solution.py:24
  30.2 0.5 collective-permute-start.4
  30.7 0.4 shard_map.76.refs_0_
  31.2 0.4 collective-permute-done.2.refs_1_
  31.6 1.4 %collective-permute-start.9 = (bf16[192,1536]{1,0:T(8,128)(2,1)S(1)}, bf16[192,1536]{1,0:T(8,128)(2,1)S(1)}, u32[]{:S(2)}, u32[]{:S(2)}) collective-permute-start(bf16[192,1536]{1,0:T(8,128)(2,1)S(1)} %shard_map.76.refs_0_), channel_id=1, source_target_pairs={{0,2},{1,3},{2,0},{3,1},{4,6},{5,7},{6,4},{7,5},{8,10},{9,11},{10,... | collective-permute-start | bytes 1769480 | tf_op jit(solution)/shard_map/ppermute | solution.py:24
  33.0 3.3 %collective-permute-start.20 = (bf16[192,1536]{1,0:T(8,128)(2,1)S(1)}, bf16[192,1536]{1,0:T(8,128)(2,1)S(1)}, u32[]{:S(2)}, u32[]{:S(2)}) collective-permute-start(bf16[192,1536]{1,0:T(8,128)(2,1)S(1)} %shard_map.85.own_ref), channel_id=1, source_target_pairs={{0,4},{4,0},{8,12},{12,8},{1,5},{5,1},{9,13},{13,9},{2,6},{6,2},{1... | collective-permute-start | bytes 1769480 | tf_op jit(solution)/shard_map/ppermute | solution.py:24
  36.3 2.1 %collective-permute-done.13.refs_0_ = bf16[128,1536]{1,0:T(8,128)(2,1)S(1)} collective-permute-done((bf16[128,1536]{1,0:T(8,128)(2,1)S(1)}, bf16[128,1536]{1,0:T(8,128)(2,1)S(1)}, u32[]{:S(2)}, u32[]{:S(2)}) %collective-permute-start.13) | collective-permute-done | bytes 393248 | tf_op jit(solution)/shard_map/ppermute | solution.py:24
  38.4 0.4 tags.1
  38.7 0.6 shard_map.74.refs_2_
  39.3 0.6 collective-permute-start.14
  39.9 1.1 %shard_map.78.refs_0_ = bf16[512,1536]{1,0:T(8,128)(2,1)S(1)} custom-call(bf16[4,32,1536]{2,1,0:T(8,128)(2,1)S(1)} %get-tuple-element.36.refs_0_, bf16[4,32,1536]{2,1,0:T(8,128)(2,1)S(1)} %collective-permute-done.10.refs_1_, bf16[4,32,1536]{2,1,0:T(8,128)(2,1)S(1)} %collective-permute-done.11.refs_2_, ...), custom_call_target="tpu_custom_call" | custom-call | flops 7864320 | bytes 3145728 | tf_op jit(solution)/shard_map/pallas_call | solution.py:102
  41.0 2.2 %shard_map.79.refs_0_ = bf16[512,1152]{1,0:T(8,128)(2,1)S(1)} custom-call(bf16[512,1536]{1,0:T(8,128)(2,1)S(1)} %shard_map.78.refs_0_, bf16[3,1536,384]{2,1,0:T(8,128)(2,1)S(1)} %copy-done), custom_call_target="tpu_custom_call" | custom-call | flops 1811939328 | bytes 6291456 | tf_op jit(solution)/shard_map/pallas_call | solution.py:197
  43.2 0.1 collective-permute-start.25
  43.3 2.2 %shard_map.75 = (bf16[256,1152]{1,0:T(8,128)(2,1)S(1)}, bf16[256,1152]{1,0:T(8,128)(2,1)S(1)}) custom-call(bf16[128,1536]{1,0:T(8,128)(2,1)S(1)} %shard_map.73.refs_0_, bf16[128,1536]{1,0:T(8,128)(2,1)S(1)} %collective-permute-done.1.refs_1_, bf16[256,1536]{1,0:T(8,128)(2,1)S(1)} %shard_map.74.refs_2_, bf16[3,1536,384]{2,1,0:T(8,128)(2,1)S(1)} %copy-done), custom_call_target="tpu_custom_call" | custom-call | flops 1811939328 | bytes 6291456 | tf_op jit(solution)/shard_map/pallas_call | solution.py:197
  45.5 5.0 %collective-permute-done.9.refs_0_ = bf16[192,1536]{1,0:T(8,128)(2,1)S(1)} collective-permute-done((bf16[192,1536]{1,0:T(8,128)(2,1)S(1)}, bf16[192,1536]{1,0:T(8,128)(2,1)S(1)}, u32[]{:S(2)}, u32[]{:S(2)}) %collective-permute-start.9) | collective-permute-done | bytes 589856 | tf_op jit(solution)/shard_map/ppermute | solution.py:24
  50.5 0.1 shard_map.86.refs_6_.refs_2_
  50.6 0.6 collective-permute-start.21
  51.2 1.7 %shard_map.77.refs_1_ = bf16[384,1152]{1,0:T(8,128)(2,1)S(1)} custom-call(bf16[192,1536]{1,0:T(8,128)(2,1)S(1)} %shard_map.76.refs_0_, bf16[192,1536]{1,0:T(8,128)(2,1)S(1)} %collective-permute-done.8.refs_1_, bf16[3,1536,384]{2,1,0:T(8,128)(2,1)S(1)} %copy-done), custom_call_target="tpu_custom_call" | custom-call | flops 1358954496 | bytes 5603328 | tf_op jit(solution)/shard_map/pallas_call | solution.py:197
  52.9 1.2 %shard_map.80.refs_2_ = bf16[256,1152]{1,0:T(8,128)(2,1)S(1)} custom-call(bf16[128,1536]{1,0:T(8,128)(2,1)S(1)} %collective-permute-done.13.refs_0_, bf16[128,1536]{1,0:T(8,128)(2,1)S(1)} %collective-permute-done.14.refs_1_, bf16[3,1536,384]{2,1,0:T(8,128)(2,1)S(1)} %copy-done), custom_call_target="tpu_custom_call" | custom-call | flops 905969664 | bytes 4915200 | tf_op jit(solution)/shard_map/pallas_call | solution.py:197
  54.2 6.5 %shard_map.81 = (bf16[1,256,384]{2,1,0:T(8,128)(2,1)S(1)}, bf16[1,256,384]{2,1,0:T(8,128)(2,1)S(1)}, bf16[1,256,384]{2,1,0:T(8,128)(2,1)S(1)}, bf16[1,256,384]{2,1,0:T(8,128)(2,1)S(1)}) custom-call(bf16[512,1152]{1,0:T(8,128)(2,1)S(1)} %shard_map.79.refs_0_, bf16[256,1152]{1,0:T(8,128)(2,1)S(1)} %get-tuple-element.37.refs_1_, ...), custom_call_target="tpu_custom_call" | custom-call | flops 4294967296 | bytes 2359296 | tf_op jit(solution)/shard_map/pallas_call | solution.py:285
  60.6 0.1 collective-permute-start.22
  60.7 1.5 %collective-permute-start.23 = (bf16[1,256,384]{2,1,0:T(8,128)(2,1)S(1)}, bf16[1,256,384]{2,1,0:T(8,128)(2,1)S(1)}, u32[]{:S(2)}, u32[]{:S(2)}) collective-permute-start(bf16[1,256,384]{2,1,0:T(8,128)(2,1)S(1)} %get-tuple-element.43), channel_id=1, source_target_pairs={{0,2},{1,3},{2,0},{3,1},{4,6},{5,7},{6,4},{7,5},{8,10},{9,11},{10,... | collective-permute-start | bytes 589832 | tf_op jit(solution)/shard_map/ppermute | solution.py:24
  62.3 0.3 collective-permute-start.24
  62.6 1.7 %shard_map.82.refs_2_ = bf16[384,1152]{1,0:T(8,128)(2,1)S(1)} custom-call(bf16[192,1536]{1,0:T(8,128)(2,1)S(1)} %collective-permute-done.9.refs_0_, bf16[192,1536]{1,0:T(8,128)(2,1)S(1)} %collective-permute-done.15.refs_1_, bf16[3,1536,384]{2,1,0:T(8,128)(2,1)S(1)} %copy-done), custom_call_target="tpu_custom_call" | custom-call | flops 1358954496 | bytes 5603328 | tf_op jit(solution)/shard_map/pallas_call | solution.py:197
  64.3 3.5 %shard_map.83 = (bf16[1,256,384]{2,1,0:T(8,128)(2,1)S(1)}, bf16[1,256,384]{2,1,0:T(8,128)(2,1)S(1)}) custom-call(bf16[256,1152]{1,0:T(8,128)(2,1)S(1)} %get-tuple-element.50.refs_0_, bf16[384,1152]{1,0:T(8,128)(2,1)S(1)} %shard_map.77.refs_1_, bf16[384,1152]{1,0:T(8,128)(2,1)S(1)} %shard_map.82.refs_2_, bf16[1024,128]{1,0:T(8,128)(2,1)S(1)} %get-tuple-element.46.refs_3_, ...), custom_call_target="tpu_custom_call" | custom-call | flops 2147483648 | bytes 2359296 | tf_op jit(solution)/shard_map/pallas_call | solution.py:285
  67.8 3.5 %shard_map.87 = (bf16[1,256,384]{2,1,0:T(8,128)(2,1)S(1)}, bf16[1,256,384]{2,1,0:T(8,128)(2,1)S(1)}) custom-call(bf16[256,1152]{1,0:T(8,128)(2,1)S(1)} %get-tuple-element.50.refs_0_, bf16[384,1152]{1,0:T(8,128)(2,1)S(1)} %shard_map.77.refs_1_, bf16[384,1152]{1,0:T(8,128)(2,1)S(1)} %shard_map.82.refs_2_, bf16[1024,128]{1,0:T(8,128)(2,1)S(1)} %get-tuple-element.46.refs_3_, ...), custom_call_target="tpu_custom_call" | custom-call | flops 2147483648 | bytes 2359296 | tf_op jit(solution)/shard_map/pallas_call | solution.py:285
  71.3 0.4 collective-permute-start.26
  71.7 1.5 %collective-permute-start.16 = (bf16[1,256,384]{2,1,0:T(8,128)(2,1)S(1)}, bf16[1,256,384]{2,1,0:T(8,128)(2,1)S(1)}, u32[]{:S(2)}, u32[]{:S(2)}) collective-permute-start(bf16[1,256,384]{2,1,0:T(8,128)(2,1)S(1)} %get-tuple-element.48), channel_id=1, source_target_pairs={{0,2},{1,3},{2,0},{3,1},{4,6},{5,7},{6,4},{7,5},{8,10},{9,11},{10,... | collective-permute-start | bytes 589832 | tf_op jit(solution)/shard_map/ppermute | solution.py:24
  73.3 1.8 %shard_map.88.refs_5_ = bf16[8,32,1536]{2,1,0:T(8,128)(2,1)S(1)} custom-call(bf16[256,384]{1,0:T(8,128)(2,1)S(1)} %bitcast.18, bf16[256,384]{1,0:T(8,128)(2,1)S(1)} %bitcast.19, bf16[256,384]{1,0:T(8,128)(2,1)S(1)} %bitcast.20, bf16[256,384]{1,0:T(8,128)(2,1)S(1)} %bitcast.21, bf16[384,1536]{1,0:T(8,128)(2,1)S(1)} %copy-done.3, ...), custom_call_target="tpu_custom_call" | custom-call | flops 1207959552 | bytes 7077888 | tf_op jit(solution)/shard_map/pallas_call | solution.py:342
  75.1 1.0 %shard_map.89.refs_4_ = f32[256,1536]{1,0:T(8,128)S(1)} custom-call(bf16[256,384]{1,0:T(8,128)(2,1)S(1)} %bitcast.16, bf16[256,384]{1,0:T(8,128)(2,1)S(1)} %bitcast.17, bf16[384,1536]{1,0:T(8,128)(2,1)S(1)} %copy-done.3, bf16[384,1536]{1,0:T(8,128)(2,1)S(1)} %collective-permute-done.25.refs_5_.refs_3_), custom_call_target="tpu_custom_call" | custom-call | flops 603979776 | bytes 2752512 | tf_op jit(solution)/shard_map/pallas_call | solution.py:317
  76.0 3.5 %collective-permute-done.16 = bf16[1,256,384]{2,1,0:T(8,128)(2,1)S(1)} collective-permute-done((bf16[1,256,384]{2,1,0:T(8,128)(2,1)S(1)}, bf16[1,256,384]{2,1,0:T(8,128)(2,1)S(1)}, u32[]{:S(2)}, u32[]{:S(2)}) %collective-permute-start.16) | collective-permute-done | bytes 196640 | tf_op jit(solution)/shard_map/ppermute | solution.py:24
  79.5 2.6 %collective-permute-done.17 = bf16[1,256,384]{2,1,0:T(8,128)(2,1)S(1)} collective-permute-done((bf16[1,256,384]{2,1,0:T(8,128)(2,1)S(1)}, bf16[1,256,384]{2,1,0:T(8,128)(2,1)S(1)}, u32[]{:S(2)}, u32[]{:S(2)}) %collective-permute-start.17) | collective-permute-done | bytes 196640 | tf_op jit(solution)/shard_map/ppermute | solution.py:24
  82.1 2.1 %shard_map.90 = bf16[8,64,1536]{2,1,0:T(8,128)(2,1)} custom-call(bf16[256,384]{1,0:T(8,128)(2,1)S(1)} %bitcast.22, bf16[256,384]{1,0:T(8,128)(2,1)S(1)} %bitcast.23, bf16[384,1536]{1,0:T(8,128)(2,1)S(1)} %shard_map.86.refs_6_.refs_2_, bf16[384,1536]{1,0:T(8,128)(2,1)S(1)} %collective-permute-done.21.refs_7_.refs_3_, f32[256,1536]{1,0:T(8,128)S(1)} %shard_map.89.refs_4_, ...), custom_call_target="tpu_custom_call" | custom-call | flops 603979776 | bytes 7077888 | tf_op jit(solution)/shard_map/pallas_call | solution.py:388
  (42 shorter events, 0.3 us)
Async XLA Ops:
  0.0 1.4 %copy-start.1 = (bf16[1,8,1,64,1536]{4,3,2,1,0:T(8,128)(2,1)S(1)}, bf16[1,8,1,64,1536]{4,3,2,1,0:T(8,128)(2,1)}, u32[]{:S(2)}) copy-start(bf16[1,8,1,64,1536]{4,3,2,1,0:T(8,128)(2,1)} %param.7) | copy-start | bytes 4718596
  1.4 4.7 %copy-start.3 = (bf16[384,1536]{1,0:T(8,128)(2,1)S(1)}, bf16[384,1536]{1,0:T(8,128)(2,1)}, u32[]{:S(2)}) copy-start(bf16[384,1536]{1,0:T(8,128)(2,1)} %refs_2_.9) | copy-start | bytes 3538948
  1.4 24.5 %copy-start.4 = (f32[1536]{0:T(1024)S(1)}, f32[1536]{0:T(1024)}, u32[]{:S(2)}) copy-start(f32[1536]{0:T(1024)} %refs_4_.6) | copy-start | bytes 18436
  1.4 24.5 %copy-start.5 = (f32[1536]{0:T(1024)S(1)}, f32[1536]{0:T(1024)}, u32[]{:S(2)}) copy-start(f32[1536]{0:T(1024)} %refs_5_.6) | copy-start | bytes 18436
  1.5 24.4 %collective-permute-start = (bf16[4,32,1536]{2,1,0:T(8,128)(2,1)S(1)}, bf16[4,32,1536]{2,1,0:T(8,128)(2,1)S(1)}, u32[]{:S(2)}, u32[]{:S(2)}) collective-permute-start(bf16[4,32,1536]{2,1,0:T(8,128)(2,1)S(1)} %get-tuple-element.30), channel_id=1, source_target_pairs={{0,4},{4,0},{8,12},{12,8},{1,5},{5,1},{9,13},{13,9},{2,6},{6,2},{1... | collective-permute-start | bytes 1179656 | tf_op jit(solution)/shard_map/ppermute | solution.py:24
  4.6 7.8 %collective-permute-start.3 = (bf16[4,16,1536]{2,1,0:T(8,128)(2,1)S(1)}, bf16[4,16,1536]{2,1,0:T(8,128)(2,1)S(1)}, u32[]{:S(2)}, u32[]{:S(2)}) collective-permute-start(bf16[4,16,1536]{2,1,0:T(8,128)(2,1)S(1)} %get-tuple-element.31.refs_0_), channel_id=1, source_target_pairs={{0,2},{1,3},{2,0},{3,1},{4,6},{5,7},{6,4},{7,5},{8,10},{9,11},{10,... | collective-permute-start | bytes 589832 | tf_op jit(solution)/shard_map/ppermute | solution.py:24
  6.1 32.2 %copy-start = (bf16[3,1536,384]{2,1,0:T(8,128)(2,1)S(1)}, bf16[3,1536,384]{2,1,0:T(8,128)(2,1)}, u32[]{:S(2)}) copy-start(bf16[3,1536,384]{2,1,0:T(8,128)(2,1)} %refs_2_.8) | copy-start | bytes 10616836
  6.2 12.5 %collective-permute-start.18 = (bf16[96,1536]{1,0:T(8,128)(2,1)S(1)}, bf16[96,1536]{1,0:T(8,128)(2,1)S(1)}, u32[]{:S(2)}, u32[]{:S(2)}) collective-permute-start(bf16[96,1536]{1,0:T(8,128)(2,1)S(1)} %shard_map.84), channel_id=1, source_target_pairs={{0,2},{1,3},{2,0},{3,1},{4,6},{5,7},{6,4},{7,5},{8,10},{9,11},{10,... | collective-permute-start | bytes 884744 | tf_op jit(solution)/shard_map/ppermute | solution.py:24
  6.8 15.4 %collective-permute-start.5 = (bf16[4,16,1536]{2,1,0:T(8,128)(2,1)S(1)}, bf16[4,16,1536]{2,1,0:T(8,128)(2,1)S(1)}, u32[]{:S(2)}, u32[]{:S(2)}) collective-permute-start(bf16[4,16,1536]{2,1,0:T(8,128)(2,1)S(1)} %get-tuple-element.33), channel_id=1, source_target_pairs={{0,4},{4,0},{8,12},{12,8},{1,5},{5,1},{9,13},{13,9},{2,6},{6,2},{1... | collective-permute-start | bytes 589832 | tf_op jit(solution)/shard_map/ppermute | solution.py:24
  7.4 22.8 %collective-permute-start.11 = (bf16[4,32,1536]{2,1,0:T(8,128)(2,1)S(1)}, bf16[4,32,1536]{2,1,0:T(8,128)(2,1)S(1)}, u32[]{:S(2)}, u32[]{:S(2)}) collective-permute-start(bf16[4,32,1536]{2,1,0:T(8,128)(2,1)S(1)} %get-tuple-element.36.refs_0_), channel_id=1, source_target_pairs={{0,2},{1,3},{2,0},{3,1},{4,6},{5,7},{6,4},{7,5},{8,10},{9,11},{10,... | collective-permute-start | bytes 1179656 | tf_op jit(solution)/shard_map/ppermute | solution.py:24
  12.4 13.9 %collective-permute-start.6 = (bf16[4,16,1536]{2,1,0:T(8,128)(2,1)S(1)}, bf16[4,16,1536]{2,1,0:T(8,128)(2,1)S(1)}, u32[]{:S(2)}, u32[]{:S(2)}) collective-permute-start(bf16[4,16,1536]{2,1,0:T(8,128)(2,1)S(1)} %get-tuple-element.34), channel_id=1, source_target_pairs={{0,8},{4,12},{8,0},{12,4},{1,9},{5,13},{9,1},{13,5},{2,10},{6,14},... | collective-permute-start | bytes 589832 | tf_op jit(solution)/shard_map/ppermute | solution.py:24
  18.7 11.9 %collective-permute-start.19 = (bf16[96,1536]{1,0:T(8,128)(2,1)S(1)}, bf16[96,1536]{1,0:T(8,128)(2,1)S(1)}, u32[]{:S(2)}, u32[]{:S(2)}) collective-permute-start(bf16[96,1536]{1,0:T(8,128)(2,1)S(1)} %collective-permute-done.18.own_ref), channel_id=1, source_target_pairs={{0,16},{16,0},{1,17},{17,1},{2,18},{18,2},{3,19},{19,3},{4,20},{20... | collective-permute-start | bytes 884744 | tf_op jit(solution)/shard_map/ppermute | solution.py:24
  22.2 16.2 %copy-start.6 = (s32[1,32,64]{2,1,0:T(8,128)S(1)}, s32[1,32,64]{2,1,0:T(8,128)}, u32[]{:S(2)}) copy-start(s32[1,32,64]{2,1,0:T(8,128)} %param.8) | copy-start | bytes 24580
  22.2 8.0 %collective-permute-start.7 = (bf16[4,16,1536]{2,1,0:T(8,128)(2,1)S(1)}, bf16[4,16,1536]{2,1,0:T(8,128)(2,1)S(1)}, u32[]{:S(2)}, u32[]{:S(2)}) collective-permute-start(bf16[4,16,1536]{2,1,0:T(8,128)(2,1)S(1)} %get-tuple-element.35), channel_id=1, source_target_pairs={{0,12},{4,8},{8,4},{12,0},{1,13},{5,9},{9,5},{13,1},{2,14},{6,10},... | collective-permute-start | bytes 589832 | tf_op jit(solution)/shard_map/ppermute | solution.py:24
  26.0 10.3 %collective-permute-start.10 = (bf16[4,32,1536]{2,1,0:T(8,128)(2,1)S(1)}, bf16[4,32,1536]{2,1,0:T(8,128)(2,1)S(1)}, u32[]{:S(2)}, u32[]{:S(2)}) collective-permute-start(bf16[4,32,1536]{2,1,0:T(8,128)(2,1)S(1)} %get-tuple-element.36.refs_0_), channel_id=1, source_target_pairs={{0,1},{1,0},{2,3},{3,2},{4,5},{5,4},{6,7},{7,6},{8,9},{9,8},{10,11... | collective-permute-start | bytes 1179656 | tf_op jit(solution)/shard_map/ppermute | solution.py:24
  26.3 12.1 %collective-permute-start.13 = (bf16[128,1536]{1,0:T(8,128)(2,1)S(1)}, bf16[128,1536]{1,0:T(8,128)(2,1)S(1)}, u32[]{:S(2)}, u32[]{:S(2)}) collective-permute-start(bf16[128,1536]{1,0:T(8,128)(2,1)S(1)} %shard_map.73.refs_0_), channel_id=1, source_target_pairs={{0,2},{1,3},{2,0},{3,1},{4,6},{5,7},{6,4},{7,5},{8,10},{9,11},{10,... | collective-permute-start | bytes 1179656 | tf_op jit(solution)/shard_map/ppermute | solution.py:24
  30.1 1.4 %collective-permute-start.2 = (bf16[4,16,1536]{2,1,0:T(8,128)(2,1)S(1)}, bf16[4,16,1536]{2,1,0:T(8,128)(2,1)S(1)}, u32[]{:S(2)}, u32[]{:S(2)}) collective-permute-start(bf16[4,16,1536]{2,1,0:T(8,128)(2,1)S(1)} %get-tuple-element.31.refs_0_), channel_id=1, source_target_pairs={{0,1},{1,0},{2,3},{3,2},{4,5},{5,4},{6,7},{7,6},{8,9},{9,8},{10,11... | collective-permute-start | bytes 589832 | tf_op jit(solution)/shard_map/ppermute | solution.py:24
  30.2 2.9 %collective-permute-start.4 = (bf16[4,16,1536]{2,1,0:T(8,128)(2,1)S(1)}, bf16[4,16,1536]{2,1,0:T(8,128)(2,1)S(1)}, u32[]{:S(2)}, u32[]{:S(2)}) collective-permute-start(bf16[4,16,1536]{2,1,0:T(8,128)(2,1)S(1)} %collective-permute-done.3.refs_2_), channel_id=1, source_target_pairs={{0,1},{1,0},{2,3},{3,2},{4,5},{5,4},{6,7},{7,6},{8,9},{9,8},{10,11... | collective-permute-start | bytes 589832 | tf_op jit(solution)/shard_map/ppermute | solution.py:24
  30.7 8.6 %collective-permute-start.12 = (bf16[4,32,1536]{2,1,0:T(8,128)(2,1)S(1)}, bf16[4,32,1536]{2,1,0:T(8,128)(2,1)S(1)}, u32[]{:S(2)}, u32[]{:S(2)}) collective-permute-start(bf16[4,32,1536]{2,1,0:T(8,128)(2,1)S(1)} %collective-permute-done.11.refs_2_), channel_id=1, source_target_pairs={{0,1},{1,0},{2,3},{3,2},{4,5},{5,4},{6,7},{7,6},{8,9},{9,8},{10,11... | collective-permute-start | bytes 1179656 | tf_op jit(solution)/shard_map/ppermute | solution.py:24
  31.6 18.9 %collective-permute-start.9 = (bf16[192,1536]{1,0:T(8,128)(2,1)S(1)}, bf16[192,1536]{1,0:T(8,128)(2,1)S(1)}, u32[]{:S(2)}, u32[]{:S(2)}) collective-permute-start(bf16[192,1536]{1,0:T(8,128)(2,1)S(1)} %shard_map.76.refs_0_), channel_id=1, source_target_pairs={{0,2},{1,3},{2,0},{3,1},{4,6},{5,7},{6,4},{7,5},{8,10},{9,11},{10,... | collective-permute-start | bytes 1769480 | tf_op jit(solution)/shard_map/ppermute | solution.py:24
  33.0 17.5 %collective-permute-start.20 = (bf16[192,1536]{1,0:T(8,128)(2,1)S(1)}, bf16[192,1536]{1,0:T(8,128)(2,1)S(1)}, u32[]{:S(2)}, u32[]{:S(2)}) collective-permute-start(bf16[192,1536]{1,0:T(8,128)(2,1)S(1)} %shard_map.85.own_ref), channel_id=1, source_target_pairs={{0,4},{4,0},{8,12},{12,8},{1,5},{5,1},{9,13},{13,9},{2,6},{6,2},{1... | collective-permute-start | bytes 1769480 | tf_op jit(solution)/shard_map/ppermute | solution.py:24
  36.3 14.9 %collective-permute-start.8 = (bf16[192,1536]{1,0:T(8,128)(2,1)S(1)}, bf16[192,1536]{1,0:T(8,128)(2,1)S(1)}, u32[]{:S(2)}, u32[]{:S(2)}) collective-permute-start(bf16[192,1536]{1,0:T(8,128)(2,1)S(1)} %shard_map.76.refs_0_), channel_id=1, source_target_pairs={{0,1},{1,0},{2,3},{3,2},{4,5},{5,4},{6,7},{7,6},{8,9},{9,8},{10,11... | collective-permute-start | bytes 1769480 | tf_op jit(solution)/shard_map/ppermute | solution.py:24
  38.4 4.9 %collective-permute-start.1 = (bf16[128,1536]{1,0:T(8,128)(2,1)S(1)}, bf16[128,1536]{1,0:T(8,128)(2,1)S(1)}, u32[]{:S(2)}, u32[]{:S(2)}) collective-permute-start(bf16[128,1536]{1,0:T(8,128)(2,1)S(1)} %shard_map.73.refs_0_), channel_id=1, source_target_pairs={{0,1},{1,0},{2,3},{3,2},{4,5},{5,4},{6,7},{7,6},{8,9},{9,8},{10,11... | collective-permute-start | bytes 1179656 | tf_op jit(solution)/shard_map/ppermute | solution.py:24
  39.3 13.6 %collective-permute-start.14 = (bf16[128,1536]{1,0:T(8,128)(2,1)S(1)}, bf16[128,1536]{1,0:T(8,128)(2,1)S(1)}, u32[]{:S(2)}, u32[]{:S(2)}) collective-permute-start(bf16[128,1536]{1,0:T(8,128)(2,1)S(1)} %collective-permute-done.13.refs_0_), channel_id=1, source_target_pairs={{0,1},{1,0},{2,3},{3,2},{4,5},{5,4},{6,7},{7,6},{8,9},{9,8},{10,11... | collective-permute-start | bytes 1179656 | tf_op jit(solution)/shard_map/ppermute | solution.py:24
  43.2 28.1 %collective-permute-start.25 = (bf16[384,1536]{1,0:T(8,128)(2,1)S(1)}, bf16[384,1536]{1,0:T(8,128)(2,1)S(1)}, u32[]{:S(2)}, u32[]{:S(2)}) collective-permute-start(bf16[384,1536]{1,0:T(8,128)(2,1)S(1)} %copy-done.3), channel_id=1, source_target_pairs={{0,1},{1,0},{2,3},{3,2},{4,5},{5,4},{6,7},{7,6},{8,9},{9,8},{10,11... | collective-permute-start | bytes 3538952 | tf_op jit(solution)/shard_map/ppermute | solution.py:24
  50.5 11.7 %collective-permute-start.15 = (bf16[192,1536]{1,0:T(8,128)(2,1)S(1)}, bf16[192,1536]{1,0:T(8,128)(2,1)S(1)}, u32[]{:S(2)}, u32[]{:S(2)}) collective-permute-start(bf16[192,1536]{1,0:T(8,128)(2,1)S(1)} %collective-permute-done.9.refs_0_), channel_id=1, source_target_pairs={{0,1},{1,0},{2,3},{3,2},{4,5},{5,4},{6,7},{7,6},{8,9},{9,8},{10,11... | collective-permute-start | bytes 1769480 | tf_op jit(solution)/shard_map/ppermute | solution.py:24
  50.6 22.6 %collective-permute-start.21 = (bf16[384,1536]{1,0:T(8,128)(2,1)S(1)}, bf16[384,1536]{1,0:T(8,128)(2,1)S(1)}, u32[]{:S(2)}, u32[]{:S(2)}) collective-permute-start(bf16[384,1536]{1,0:T(8,128)(2,1)S(1)} %shard_map.86.refs_6_.refs_2_), channel_id=1, source_target_pairs={{0,1},{1,0},{2,3},{3,2},{4,5},{5,4},{6,7},{7,6},{8,9},{9,8},{10,11... | collective-permute-start | bytes 3538952 | tf_op jit(solution)/shard_map/ppermute | solution.py:24
  52.9 1.2 %copy-start.7 = (f32[4]{0:T(128)S(1)}, f32[4]{0:T(128)}, u32[]{:S(2)}) copy-start(f32[4]{0:T(128)} %refs_5_.9) | copy-start | bytes 52
  60.6 11.1 %collective-permute-start.22 = (bf16[1,256,384]{2,1,0:T(8,128)(2,1)S(1)}, bf16[1,256,384]{2,1,0:T(8,128)(2,1)S(1)}, u32[]{:S(2)}, u32[]{:S(2)}) collective-permute-start(bf16[1,256,384]{2,1,0:T(8,128)(2,1)S(1)} %get-tuple-element.42), channel_id=1, source_target_pairs={{0,1},{1,0},{2,3},{3,2},{4,5},{5,4},{6,7},{7,6},{8,9},{9,8},{10,11... | collective-permute-start | bytes 589832 | tf_op jit(solution)/shard_map/ppermute | solution.py:24
  60.7 12.5 %collective-permute-start.23 = (bf16[1,256,384]{2,1,0:T(8,128)(2,1)S(1)}, bf16[1,256,384]{2,1,0:T(8,128)(2,1)S(1)}, u32[]{:S(2)}, u32[]{:S(2)}) collective-permute-start(bf16[1,256,384]{2,1,0:T(8,128)(2,1)S(1)} %get-tuple-element.43), channel_id=1, source_target_pairs={{0,2},{1,3},{2,0},{3,1},{4,6},{5,7},{6,4},{7,5},{8,10},{9,11},{10,... | collective-permute-start | bytes 589832 | tf_op jit(solution)/shard_map/ppermute | solution.py:24
  62.3 11.0 %collective-permute-start.24 = (bf16[1,256,384]{2,1,0:T(8,128)(2,1)S(1)}, bf16[1,256,384]{2,1,0:T(8,128)(2,1)S(1)}, u32[]{:S(2)}, u32[]{:S(2)}) collective-permute-start(bf16[1,256,384]{2,1,0:T(8,128)(2,1)S(1)} %get-tuple-element.44), channel_id=1, source_target_pairs={{0,3},{1,2},{2,1},{3,0},{4,7},{5,6},{6,5},{7,4},{8,11},{9,10},{10,... | collective-permute-start | bytes 589832 | tf_op jit(solution)/shard_map/ppermute | solution.py:24
  67.8 5.5 %copy-start.2 = (bf16[1,8,1,64,1536]{4,3,2,1,0:T(8,128)(2,1)S(1)}, bf16[1,8,1,64,1536]{4,3,2,1,0:T(8,128)(2,1)}, u32[]{:S(2)}) copy-start(bf16[1,8,1,64,1536]{4,3,2,1,0:T(8,128)(2,1)} %param.7) | copy-start | bytes 4718596
  71.3 3.8 %collective-permute-start.26 = (bf16[1,256,384]{2,1,0:T(8,128)(2,1)S(1)}, bf16[1,256,384]{2,1,0:T(8,128)(2,1)S(1)}, u32[]{:S(2)}, u32[]{:S(2)}) collective-permute-start(bf16[1,256,384]{2,1,0:T(8,128)(2,1)S(1)} %get-tuple-element.52), channel_id=1, source_target_pairs={{0,1},{1,0},{2,3},{3,2},{4,5},{5,4},{6,7},{7,6},{8,9},{9,8},{10,11... | collective-permute-start | bytes 589832 | tf_op jit(solution)/shard_map/ppermute | solution.py:24
  71.7 7.8 %collective-permute-start.16 = (bf16[1,256,384]{2,1,0:T(8,128)(2,1)S(1)}, bf16[1,256,384]{2,1,0:T(8,128)(2,1)S(1)}, u32[]{:S(2)}, u32[]{:S(2)}) collective-permute-start(bf16[1,256,384]{2,1,0:T(8,128)(2,1)S(1)} %get-tuple-element.48), channel_id=1, source_target_pairs={{0,2},{1,3},{2,0},{3,1},{4,6},{5,7},{6,4},{7,5},{8,10},{9,11},{10,... | collective-permute-start | bytes 589832 | tf_op jit(solution)/shard_map/ppermute | solution.py:24
  73.2 8.9 %collective-permute-start.17 = (bf16[1,256,384]{2,1,0:T(8,128)(2,1)S(1)}, bf16[1,256,384]{2,1,0:T(8,128)(2,1)S(1)}, u32[]{:S(2)}, u32[]{:S(2)}) collective-permute-start(bf16[1,256,384]{2,1,0:T(8,128)(2,1)S(1)} %get-tuple-element.49), channel_id=1, source_target_pairs={{0,3},{1,2},{2,1},{3,0},{4,7},{5,6},{6,5},{7,4},{8,11},{9,10},{10,... | collective-permute-start | bytes 589832 | tf_op jit(solution)/shard_map/ppermute | solution.py:24

commit v9 on v8

--- a/solution.py
+++ b/solution.py
@@ -299,11 +299,9 @@
 
 
 def product(attended, weights, columns=slice(None)):
-    total = None
-    for piece, weight in zip(attended, weights, strict=True):
-        term = jnp.dot(piece[...], weight[:, columns], preferred_element_type=F32)
-        total = term if total is None else total + term
-    return total
+    rows = jnp.concatenate([piece[...] for piece in attended], axis=1)
+    depth = jnp.concatenate([weight[:, columns] for weight in weights], axis=0)
+    return jnp.dot(rows, depth, preferred_element_type=F32)
 
 
 def partial_kernel(count, *refs):
@@ -562,12 +560,12 @@
     shape = (row_count, col_count, width)
     done = finish(first, out_weights, [blocked, south_0], spans, (row_count, WS, width))
     second[0] = after(second[0], done)
-    base = partial(second[:split], out_weights[:split])
+    base = partial(second[:-1], out_weights[:-1])
     spans = [(0, rows + row, half + WS, near, row, WS) for row in range(rows)]
     spans += [(1, row, 0, near, rows + row, WS) for row in range(rows)]
     spans += [(2, row, 0, half, row, WS + near) for row in range(rows)]
     spans += [(3, row, 0, half, rows + row, WS + near) for row in range(rows)]
-    mixed = finish_last(second[split:], out_weights[split:], base, done, [blocked, south_1, east, corner], spans, shape)
+    mixed = finish_last(second[-1:], out_weights[-1:], base, done, [blocked, south_1, east, corner], spans, shape)
     return mixed[None, :, None]
 
 

time: 84.6 us -> 84.2 us (level)
  transfers between devices with their start and end apart: 27 -> 27, of which waited for: 9 -> 9; matrix products, arithmetic and copies ran while one was open for 0% -> 0% of each run, Pallas kernels for 34% -> 33%
where the time goes in v9:
time: 84.2 us; the launch traced here: 83.9 us
  Pallas kernels  29.8 us (35%)
  starting transfers between devices  27 us (32%)
  waiting for transfers between devices  25.3 us (30%)
  local copies, waits for them, and re-layouts  1.44 us (2%)
    ppermute x27, starting transfers between devices, permute_by(): return lax.ppermute(value, axis, pairs)  27 us
    ppermute x27, waiting for transfers between devices, permute_by(): return lax.ppermute(value, axis, pairs)  25.3 us
    pallas_call x3, Pallas kernels, attend(): pl.pallas_call(functools.partial(attend_kernel, layout, ranges, head_widt...  13.5 us
    pallas_call x5, Pallas kernels, project(): pl.pallas_call(functools.partial(project_kernel, [len(group) for group in...  9.01 us
    pallas_call x4, Pallas kernels, norm(): pl.pallas_call(functools.partial(norm_kernel, groups), out_shape=[jax.Sha...  2.42 us
  transfers between devices with their start and end apart: 27, of which 9 were waited for; matrix products, arithmetic and copies ran while one was open for 0% of the time, Pallas kernels for 33%

profile of v9, /device:TPU:0, one launch (start us, length us, event | category | flops | bytes accessed | tf_op | source)
XLA Modules:
  0.0 83.9 jit_solution(18292408445364772651)
XLA Ops:
  0.0 1.4 %copy-done.1 = bf16[1,8,1,64,1536]{4,3,2,1,0:T(8,128)(2,1)S(1)} copy-done((bf16[1,8,1,64,1536]{4,3,2,1,0:T(8,128)(2,1)S(1)}, bf16[1,8,1,64,1536]{4,3,2,1,0:T(8,128)(2,1)}, u32[]{:S(2)}) %copy-start.1) | copy-done | bytes 1572888
  1.4 0.1 cut.1
  1.5 3.1 %collective-permute-start = (bf16[4,32,1536]{2,1,0:T(8,128)(2,1)S(1)}, bf16[4,32,1536]{2,1,0:T(8,128)(2,1)S(1)}, u32[]{:S(2)}, u32[]{:S(2)}) collective-permute-start(bf16[4,32,1536]{2,1,0:T(8,128)(2,1)S(1)} %get-tuple-element.30), channel_id=1, source_target_pairs={{0,4},{4,0},{8,12},{12,8},{1,5},{5,1},{9,13},{13,9},{2,6},{6,2},{1... | collective-permute-start | bytes 1179656 | tf_op jit(solution)/shard_map/ppermute | solution.py:24
  4.6 1.5 %collective-permute-start.3 = (bf16[4,16,1536]{2,1,0:T(8,128)(2,1)S(1)}, bf16[4,16,1536]{2,1,0:T(8,128)(2,1)S(1)}, u32[]{:S(2)}, u32[]{:S(2)}) collective-permute-start(bf16[4,16,1536]{2,1,0:T(8,128)(2,1)S(1)} %get-tuple-element.31.refs_0_), channel_id=1, source_target_pairs={{0,2},{1,3},{2,0},{3,1},{4,6},{5,7},{6,4},{7,5},{8,10},{9,11},{10,... | collective-permute-start | bytes 589832 | tf_op jit(solution)/shard_map/ppermute | solution.py:24
  6.2 0.6 collective-permute-start.17
  6.8 0.6 collective-permute-start.5
  7.4 1.4 %collective-permute-start.11 = (bf16[4,32,1536]{2,1,0:T(8,128)(2,1)S(1)}, bf16[4,32,1536]{2,1,0:T(8,128)(2,1)S(1)}, u32[]{:S(2)}, u32[]{:S(2)}) collective-permute-start(bf16[4,32,1536]{2,1,0:T(8,128)(2,1)S(1)} %get-tuple-element.36.refs_0_), channel_id=1, source_target_pairs={{0,2},{1,3},{2,0},{3,1},{4,6},{5,7},{6,4},{7,5},{8,10},{9,11},{10,... | collective-permute-start | bytes 1179656 | tf_op jit(solution)/shard_map/ppermute | solution.py:24
  8.8 3.7 %collective-permute-done.3.refs_2_ = bf16[4,16,1536]{2,1,0:T(8,128)(2,1)S(1)} collective-permute-done((bf16[4,16,1536]{2,1,0:T(8,128)(2,1)S(1)}, bf16[4,16,1536]{2,1,0:T(8,128)(2,1)S(1)}, u32[]{:S(2)}, u32[]{:S(2)}) %collective-permute-start.3) | collective-permute-done | bytes 196640 | tf_op jit(solution)/shard_map/ppermute | solution.py:24
  12.4 2.6 %collective-permute-start.6 = (bf16[4,16,1536]{2,1,0:T(8,128)(2,1)S(1)}, bf16[4,16,1536]{2,1,0:T(8,128)(2,1)S(1)}, u32[]{:S(2)}, u32[]{:S(2)}) collective-permute-start(bf16[4,16,1536]{2,1,0:T(8,128)(2,1)S(1)} %get-tuple-element.34), channel_id=1, source_target_pairs={{0,8},{4,12},{8,0},{12,4},{1,9},{5,13},{9,1},{13,5},{2,10},{6,14},... | collective-permute-start | bytes 589832 | tf_op jit(solution)/shard_map/ppermute | solution.py:24
  15.0 3.7 %collective-permute-done.17.own_ref = bf16[96,1536]{1,0:T(8,128)(2,1)S(1)} collective-permute-done((bf16[96,1536]{1,0:T(8,128)(2,1)S(1)}, bf16[96,1536]{1,0:T(8,128)(2,1)S(1)}, u32[]{:S(2)}, u32[]{:S(2)}) %collective-permute-start.17) | collective-permute-done | bytes 294944 | tf_op jit(solution)/shard_map/ppermute | solution.py:24
  18.7 1.5 %collective-permute-start.18 = (bf16[96,1536]{1,0:T(8,128)(2,1)S(1)}, bf16[96,1536]{1,0:T(8,128)(2,1)S(1)}, u32[]{:S(2)}, u32[]{:S(2)}) collective-permute-start(bf16[96,1536]{1,0:T(8,128)(2,1)S(1)} %collective-permute-done.17.own_ref), channel_id=1, source_target_pairs={{0,16},{16,0},{1,17},{17,1},{2,18},{18,2},{3,19},{19,3},{4,20},{20... | collective-permute-start | bytes 884744 | tf_op jit(solution)/shard_map/ppermute | solution.py:24
  20.2 1.9 %collective-permute-done.5.refs_0_.refs_5_ = bf16[4,16,1536]{2,1,0:T(8,128)(2,1)S(1)} collective-permute-done((bf16[4,16,1536]{2,1,0:T(8,128)(2,1)S(1)}, bf16[4,16,1536]{2,1,0:T(8,128)(2,1)S(1)}, u32[]{:S(2)}, u32[]{:S(2)}) %collective-permute-start.5) | collective-permute-done | bytes 196640 | tf_op jit(solution)/shard_map/ppermute | solution.py:24
  22.2 3.8 %collective-permute-start.7 = (bf16[4,16,1536]{2,1,0:T(8,128)(2,1)S(1)}, bf16[4,16,1536]{2,1,0:T(8,128)(2,1)S(1)}, u32[]{:S(2)}, u32[]{:S(2)}) collective-permute-start(bf16[4,16,1536]{2,1,0:T(8,128)(2,1)S(1)} %get-tuple-element.35), channel_id=1, source_target_pairs={{0,12},{4,8},{8,4},{12,0},{1,13},{5,9},{9,5},{13,1},{2,14},{6,10},... | collective-permute-start | bytes 589832 | tf_op jit(solution)/shard_map/ppermute | solution.py:24
  26.0 0.3 shard_map.73.refs_0_
  26.3 1.6 %collective-permute-start.13 = (bf16[128,1536]{1,0:T(8,128)(2,1)S(1)}, bf16[128,1536]{1,0:T(8,128)(2,1)S(1)}, u32[]{:S(2)}, u32[]{:S(2)}) collective-permute-start(bf16[128,1536]{1,0:T(8,128)(2,1)S(1)} %shard_map.73.refs_0_), channel_id=1, source_target_pairs={{0,2},{1,3},{2,0},{3,1},{4,6},{5,7},{6,4},{7,5},{8,10},{9,11},{10,... | collective-permute-start | bytes 1179656 | tf_op jit(solution)/shard_map/ppermute | solution.py:24
  27.9 2.3 %collective-permute-done.7.refs_2_.refs_7_ = bf16[4,16,1536]{2,1,0:T(8,128)(2,1)S(1)} collective-permute-done((bf16[4,16,1536]{2,1,0:T(8,128)(2,1)S(1)}, bf16[4,16,1536]{2,1,0:T(8,128)(2,1)S(1)}, u32[]{:S(2)}, u32[]{:S(2)}) %collective-permute-start.7) | collective-permute-done | bytes 196640 | tf_op jit(solution)/shard_map/ppermute | solution.py:24
  30.2 0.5 collective-permute-start.4
  30.7 0.4 shard_map.76.refs_0_
  31.2 0.4 collective-permute-done.2.refs_1_
  31.6 1.4 %collective-permute-start.9 = (bf16[192,1536]{1,0:T(8,128)(2,1)S(1)}, bf16[192,1536]{1,0:T(8,128)(2,1)S(1)}, u32[]{:S(2)}, u32[]{:S(2)}) collective-permute-start(bf16[192,1536]{1,0:T(8,128)(2,1)S(1)} %shard_map.76.refs_0_), channel_id=1, source_target_pairs={{0,2},{1,3},{2,0},{3,1},{4,6},{5,7},{6,4},{7,5},{8,10},{9,11},{10,... | collective-permute-start | bytes 1769480 | tf_op jit(solution)/shard_map/ppermute | solution.py:24
  33.0 3.3 %collective-permute-start.19 = (bf16[192,1536]{1,0:T(8,128)(2,1)S(1)}, bf16[192,1536]{1,0:T(8,128)(2,1)S(1)}, u32[]{:S(2)}, u32[]{:S(2)}) collective-permute-start(bf16[192,1536]{1,0:T(8,128)(2,1)S(1)} %shard_map.85.own_ref), channel_id=1, source_target_pairs={{0,4},{4,0},{8,12},{12,8},{1,5},{5,1},{9,13},{13,9},{2,6},{6,2},{1... | collective-permute-start | bytes 1769480 | tf_op jit(solution)/shard_map/ppermute | solution.py:24
  36.3 2.1 %collective-permute-done.13.refs_0_ = bf16[128,1536]{1,0:T(8,128)(2,1)S(1)} collective-permute-done((bf16[128,1536]{1,0:T(8,128)(2,1)S(1)}, bf16[128,1536]{1,0:T(8,128)(2,1)S(1)}, u32[]{:S(2)}, u32[]{:S(2)}) %collective-permute-start.13) | collective-permute-done | bytes 393248 | tf_op jit(solution)/shard_map/ppermute | solution.py:24
  38.4 0.4 tags.1
  38.7 0.6 shard_map.74.refs_2_
  39.3 0.6 collective-permute-start.14
  39.9 1.1 %shard_map.78.refs_0_ = bf16[512,1536]{1,0:T(8,128)(2,1)S(1)} custom-call(bf16[4,32,1536]{2,1,0:T(8,128)(2,1)S(1)} %get-tuple-element.36.refs_0_, bf16[4,32,1536]{2,1,0:T(8,128)(2,1)S(1)} %collective-permute-done.10.refs_1_, bf16[4,32,1536]{2,1,0:T(8,128)(2,1)S(1)} %collective-permute-done.11.refs_2_, ...), custom_call_target="tpu_custom_call" | custom-call | flops 7864320 | bytes 3145728 | tf_op jit(solution)/shard_map/pallas_call | solution.py:102
  41.0 2.2 %shard_map.79.refs_0_ = bf16[512,1152]{1,0:T(8,128)(2,1)S(1)} custom-call(bf16[512,1536]{1,0:T(8,128)(2,1)S(1)} %shard_map.78.refs_0_, bf16[3,1536,384]{2,1,0:T(8,128)(2,1)S(1)} %copy-done), custom_call_target="tpu_custom_call" | custom-call | flops 1811939328 | bytes 6291456 | tf_op jit(solution)/shard_map/pallas_call | solution.py:197
  43.2 0.1 collective-permute-start.24
  43.3 2.2 %shard_map.75 = (bf16[256,1152]{1,0:T(8,128)(2,1)S(1)}, bf16[256,1152]{1,0:T(8,128)(2,1)S(1)}) custom-call(bf16[128,1536]{1,0:T(8,128)(2,1)S(1)} %shard_map.73.refs_0_, bf16[128,1536]{1,0:T(8,128)(2,1)S(1)} %collective-permute-done.1.refs_1_, bf16[256,1536]{1,0:T(8,128)(2,1)S(1)} %shard_map.74.refs_2_, bf16[3,1536,384]{2,1,0:T(8,128)(2,1)S(1)} %copy-done), custom_call_target="tpu_custom_call" | custom-call | flops 1811939328 | bytes 6291456 | tf_op jit(solution)/shard_map/pallas_call | solution.py:197
  45.5 5.0 %collective-permute-done.9.refs_0_ = bf16[192,1536]{1,0:T(8,128)(2,1)S(1)} collective-permute-done((bf16[192,1536]{1,0:T(8,128)(2,1)S(1)}, bf16[192,1536]{1,0:T(8,128)(2,1)S(1)}, u32[]{:S(2)}, u32[]{:S(2)}) %collective-permute-start.9) | collective-permute-done | bytes 589856 | tf_op jit(solution)/shard_map/ppermute | solution.py:24
  50.5 0.1 shard_map.86.refs_6_.refs_5_
  50.6 0.6 collective-permute-start.20
  51.2 1.7 %shard_map.77.refs_1_ = bf16[384,1152]{1,0:T(8,128)(2,1)S(1)} custom-call(bf16[192,1536]{1,0:T(8,128)(2,1)S(1)} %shard_map.76.refs_0_, bf16[192,1536]{1,0:T(8,128)(2,1)S(1)} %collective-permute-done.8.refs_1_, bf16[3,1536,384]{2,1,0:T(8,128)(2,1)S(1)} %copy-done), custom_call_target="tpu_custom_call" | custom-call | flops 1358954496 | bytes 5603328 | tf_op jit(solution)/shard_map/pallas_call | solution.py:197
  52.9 1.2 %shard_map.80.refs_2_ = bf16[256,1152]{1,0:T(8,128)(2,1)S(1)} custom-call(bf16[128,1536]{1,0:T(8,128)(2,1)S(1)} %collective-permute-done.13.refs_0_, bf16[128,1536]{1,0:T(8,128)(2,1)S(1)} %collective-permute-done.14.refs_1_, bf16[3,1536,384]{2,1,0:T(8,128)(2,1)S(1)} %copy-done), custom_call_target="tpu_custom_call" | custom-call | flops 905969664 | bytes 4915200 | tf_op jit(solution)/shard_map/pallas_call | solution.py:197
  54.2 6.5 %shard_map.81 = (bf16[1,256,384]{2,1,0:T(8,128)(2,1)S(1)}, bf16[1,256,384]{2,1,0:T(8,128)(2,1)S(1)}, bf16[1,256,384]{2,1,0:T(8,128)(2,1)S(1)}, bf16[1,256,384]{2,1,0:T(8,128)(2,1)S(1)}) custom-call(bf16[512,1152]{1,0:T(8,128)(2,1)S(1)} %shard_map.79.refs_0_, bf16[256,1152]{1,0:T(8,128)(2,1)S(1)} %get-tuple-element.37.refs_1_, ...), custom_call_target="tpu_custom_call" | custom-call | flops 4294967296 | bytes 2359296 | tf_op jit(solution)/shard_map/pallas_call | solution.py:285
  60.6 0.1 collective-permute-start.21
  60.7 1.5 %collective-permute-start.22 = (bf16[1,256,384]{2,1,0:T(8,128)(2,1)S(1)}, bf16[1,256,384]{2,1,0:T(8,128)(2,1)S(1)}, u32[]{:S(2)}, u32[]{:S(2)}) collective-permute-start(bf16[1,256,384]{2,1,0:T(8,128)(2,1)S(1)} %get-tuple-element.43), channel_id=1, source_target_pairs={{0,2},{1,3},{2,0},{3,1},{4,6},{5,7},{6,4},{7,5},{8,10},{9,11},{10,... | collective-permute-start | bytes 589832 | tf_op jit(solution)/shard_map/ppermute | solution.py:24
  62.3 0.3 collective-permute-start.23
  62.6 1.7 %shard_map.82.refs_2_ = bf16[384,1152]{1,0:T(8,128)(2,1)S(1)} custom-call(bf16[192,1536]{1,0:T(8,128)(2,1)S(1)} %collective-permute-done.9.refs_0_, bf16[192,1536]{1,0:T(8,128)(2,1)S(1)} %collective-permute-done.15.refs_1_, bf16[3,1536,384]{2,1,0:T(8,128)(2,1)S(1)} %copy-done), custom_call_target="tpu_custom_call" | custom-call | flops 1358954496 | bytes 5603328 | tf_op jit(solution)/shard_map/pallas_call | solution.py:197
  64.3 3.5 %shard_map.83 = (bf16[1,256,384]{2,1,0:T(8,128)(2,1)S(1)}, bf16[1,256,384]{2,1,0:T(8,128)(2,1)S(1)}) custom-call(bf16[256,1152]{1,0:T(8,128)(2,1)S(1)} %get-tuple-element.50.refs_0_, bf16[384,1152]{1,0:T(8,128)(2,1)S(1)} %shard_map.77.refs_1_, bf16[384,1152]{1,0:T(8,128)(2,1)S(1)} %shard_map.82.refs_2_, bf16[1024,128]{1,0:T(8,128)(2,1)S(1)} %get-tuple-element.46.refs_3_, ...), custom_call_target="tpu_custom_call" | custom-call | flops 2147483648 | bytes 2359296 | tf_op jit(solution)/shard_map/pallas_call | solution.py:285
  67.8 3.5 %shard_map.87 = (bf16[1,256,384]{2,1,0:T(8,128)(2,1)S(1)}, bf16[1,256,384]{2,1,0:T(8,128)(2,1)S(1)}) custom-call(bf16[256,1152]{1,0:T(8,128)(2,1)S(1)} %get-tuple-element.50.refs_0_, bf16[384,1152]{1,0:T(8,128)(2,1)S(1)} %shard_map.77.refs_1_, bf16[384,1152]{1,0:T(8,128)(2,1)S(1)} %shard_map.82.refs_2_, bf16[1024,128]{1,0:T(8,128)(2,1)S(1)} %get-tuple-element.46.refs_3_, ...), custom_call_target="tpu_custom_call" | custom-call | flops 2147483648 | bytes 2359296 | tf_op jit(solution)/shard_map/pallas_call | solution.py:285
  71.3 0.4 collective-permute-start.25
  71.7 1.5 %collective-permute-start.26 = (bf16[1,256,384]{2,1,0:T(8,128)(2,1)S(1)}, bf16[1,256,384]{2,1,0:T(8,128)(2,1)S(1)}, u32[]{:S(2)}, u32[]{:S(2)}) collective-permute-start(bf16[1,256,384]{2,1,0:T(8,128)(2,1)S(1)} %get-tuple-element.49), channel_id=1, source_target_pairs={{0,2},{1,3},{2,0},{3,1},{4,6},{5,7},{6,4},{7,5},{8,10},{9,11},{10,... | collective-permute-start | bytes 589832 | tf_op jit(solution)/shard_map/ppermute | solution.py:24
  73.3 1.4 %shard_map.88.refs_3_ = bf16[8,32,1536]{2,1,0:T(8,128)(2,1)S(1)} custom-call(bf16[256,384]{1,0:T(8,128)(2,1)S(1)} %bitcast.19, bf16[256,384]{1,0:T(8,128)(2,1)S(1)} %bitcast.20, bf16[256,384]{1,0:T(8,128)(2,1)S(1)} %bitcast.21, bf16[256,384]{1,0:T(8,128)(2,1)S(1)} %bitcast.22, bf16[384,1536]{1,0:T(8,128)(2,1)S(1)} %copy-done.3, ...), custom_call_target="tpu_custom_call" | custom-call | flops 1207959552 | bytes 7077888 | tf_op jit(solution)/shard_map/pallas_call | solution.py:340
  74.7 4.8 %collective-permute-done.26 = bf16[1,256,384]{2,1,0:T(8,128)(2,1)S(1)} collective-permute-done((bf16[1,256,384]{2,1,0:T(8,128)(2,1)S(1)}, bf16[1,256,384]{2,1,0:T(8,128)(2,1)S(1)}, u32[]{:S(2)}, u32[]{:S(2)}) %collective-permute-start.26) | collective-permute-done | bytes 196640 | tf_op jit(solution)/shard_map/ppermute | solution.py:24
  79.5 1.2 %shard_map.89.refs_2_ = f32[256,1536]{1,0:T(8,128)S(1)} custom-call(bf16[256,384]{1,0:T(8,128)(2,1)S(1)} %bitcast.16, bf16[256,384]{1,0:T(8,128)(2,1)S(1)} %bitcast.17, bf16[256,384]{1,0:T(8,128)(2,1)S(1)} %bitcast.18, bf16[384,1536]{1,0:T(8,128)(2,1)S(1)} %copy-done.3, bf16[384,1536]{1,0:T(8,128)(2,1)S(1)} %collective-permute-done.24.refs_5_.refs_4_, ...), custom_call_target="tpu_custom_call" | custom-call | flops 905969664 | bytes 2752512 | tf_op jit(solution)/shard_map/pallas_call | solution.py:315
  80.7 1.4 %collective-permute-done.16 = bf16[1,256,384]{2,1,0:T(8,128)(2,1)S(1)} collective-permute-done((bf16[1,256,384]{2,1,0:T(8,128)(2,1)S(1)}, bf16[1,256,384]{2,1,0:T(8,128)(2,1)S(1)}, u32[]{:S(2)}, u32[]{:S(2)}) %collective-permute-start.16) | collective-permute-done | bytes 196640 | tf_op jit(solution)/shard_map/ppermute | solution.py:24
  82.1 1.7 %shard_map.90 = bf16[8,64,1536]{2,1,0:T(8,128)(2,1)} custom-call(bf16[256,384]{1,0:T(8,128)(2,1)S(1)} %bitcast.23, bf16[384,1536]{1,0:T(8,128)(2,1)S(1)} %collective-permute-done.20.refs_7_.refs_1_, f32[256,1536]{1,0:T(8,128)S(1)} %shard_map.89.refs_2_, bf16[8,32,1536]{2,1,0:T(8,128)(2,1)S(1)} %shard_map.88.refs_3_, bf16[8,64,1536]{2,1,0:T(8,128)(2,1)S(1)} %bitcast.15, ...), custom_call_target="tpu_custom_call" | custom-call | flops 301989888 | bytes 7077888 | tf_op jit(solution)/shard_map/pallas_call | solution.py:386
  (42 shorter events, 0.3 us)
Async XLA Ops:
  0.0 1.4 %copy-start.1 = (bf16[1,8,1,64,1536]{4,3,2,1,0:T(8,128)(2,1)S(1)}, bf16[1,8,1,64,1536]{4,3,2,1,0:T(8,128)(2,1)}, u32[]{:S(2)}) copy-start(bf16[1,8,1,64,1536]{4,3,2,1,0:T(8,128)(2,1)} %param.7) | copy-start | bytes 4718596
  1.4 4.7 %copy-start.3 = (bf16[384,1536]{1,0:T(8,128)(2,1)S(1)}, bf16[384,1536]{1,0:T(8,128)(2,1)}, u32[]{:S(2)}) copy-start(bf16[384,1536]{1,0:T(8,128)(2,1)} %refs_3_.5) | copy-start | bytes 3538948
  1.4 24.5 %copy-start.4 = (f32[1536]{0:T(1024)S(1)}, f32[1536]{0:T(1024)}, u32[]{:S(2)}) copy-start(f32[1536]{0:T(1024)} %refs_4_.6) | copy-start | bytes 18436
  1.4 24.5 %copy-start.5 = (f32[1536]{0:T(1024)S(1)}, f32[1536]{0:T(1024)}, u32[]{:S(2)}) copy-start(f32[1536]{0:T(1024)} %refs_5_.6) | copy-start | bytes 18436
  1.5 24.4 %collective-permute-start = (bf16[4,32,1536]{2,1,0:T(8,128)(2,1)S(1)}, bf16[4,32,1536]{2,1,0:T(8,128)(2,1)S(1)}, u32[]{:S(2)}, u32[]{:S(2)}) collective-permute-start(bf16[4,32,1536]{2,1,0:T(8,128)(2,1)S(1)} %get-tuple-element.30), channel_id=1, source_target_pairs={{0,4},{4,0},{8,12},{12,8},{1,5},{5,1},{9,13},{13,9},{2,6},{6,2},{1... | collective-permute-start | bytes 1179656 | tf_op jit(solution)/shard_map/ppermute | solution.py:24
  4.6 7.8 %collective-permute-start.3 = (bf16[4,16,1536]{2,1,0:T(8,128)(2,1)S(1)}, bf16[4,16,1536]{2,1,0:T(8,128)(2,1)S(1)}, u32[]{:S(2)}, u32[]{:S(2)}) collective-permute-start(bf16[4,16,1536]{2,1,0:T(8,128)(2,1)S(1)} %get-tuple-element.31.refs_0_), channel_id=1, source_target_pairs={{0,2},{1,3},{2,0},{3,1},{4,6},{5,7},{6,4},{7,5},{8,10},{9,11},{10,... | collective-permute-start | bytes 589832 | tf_op jit(solution)/shard_map/ppermute | solution.py:24
  6.1 32.2 %copy-start = (bf16[3,1536,384]{2,1,0:T(8,128)(2,1)S(1)}, bf16[3,1536,384]{2,1,0:T(8,128)(2,1)}, u32[]{:S(2)}) copy-start(bf16[3,1536,384]{2,1,0:T(8,128)(2,1)} %refs_2_.7) | copy-start | bytes 10616836
  6.2 12.5 %collective-permute-start.17 = (bf16[96,1536]{1,0:T(8,128)(2,1)S(1)}, bf16[96,1536]{1,0:T(8,128)(2,1)S(1)}, u32[]{:S(2)}, u32[]{:S(2)}) collective-permute-start(bf16[96,1536]{1,0:T(8,128)(2,1)S(1)} %shard_map.84), channel_id=1, source_target_pairs={{0,2},{1,3},{2,0},{3,1},{4,6},{5,7},{6,4},{7,5},{8,10},{9,11},{10,... | collective-permute-start | bytes 884744 | tf_op jit(solution)/shard_map/ppermute | solution.py:24
  6.8 15.4 %collective-permute-start.5 = (bf16[4,16,1536]{2,1,0:T(8,128)(2,1)S(1)}, bf16[4,16,1536]{2,1,0:T(8,128)(2,1)S(1)}, u32[]{:S(2)}, u32[]{:S(2)}) collective-permute-start(bf16[4,16,1536]{2,1,0:T(8,128)(2,1)S(1)} %get-tuple-element.33), channel_id=1, source_target_pairs={{0,4},{4,0},{8,12},{12,8},{1,5},{5,1},{9,13},{13,9},{2,6},{6,2},{1... | collective-permute-start | bytes 589832 | tf_op jit(solution)/shard_map/ppermute | solution.py:24
  7.4 22.8 %collective-permute-start.11 = (bf16[4,32,1536]{2,1,0:T(8,128)(2,1)S(1)}, bf16[4,32,1536]{2,1,0:T(8,128)(2,1)S(1)}, u32[]{:S(2)}, u32[]{:S(2)}) collective-permute-start(bf16[4,32,1536]{2,1,0:T(8,128)(2,1)S(1)} %get-tuple-element.36.refs_0_), channel_id=1, source_target_pairs={{0,2},{1,3},{2,0},{3,1},{4,6},{5,7},{6,4},{7,5},{8,10},{9,11},{10,... | collective-permute-start | bytes 1179656 | tf_op jit(solution)/shard_map/ppermute | solution.py:24
  12.4 13.9 %collective-permute-start.6 = (bf16[4,16,1536]{2,1,0:T(8,128)(2,1)S(1)}, bf16[4,16,1536]{2,1,0:T(8,128)(2,1)S(1)}, u32[]{:S(2)}, u32[]{:S(2)}) collective-permute-start(bf16[4,16,1536]{2,1,0:T(8,128)(2,1)S(1)} %get-tuple-element.34), channel_id=1, source_target_pairs={{0,8},{4,12},{8,0},{12,4},{1,9},{5,13},{9,1},{13,5},{2,10},{6,14},... | collective-permute-start | bytes 589832 | tf_op jit(solution)/shard_map/ppermute | solution.py:24
  18.7 11.9 %collective-permute-start.18 = (bf16[96,1536]{1,0:T(8,128)(2,1)S(1)}, bf16[96,1536]{1,0:T(8,128)(2,1)S(1)}, u32[]{:S(2)}, u32[]{:S(2)}) collective-permute-start(bf16[96,1536]{1,0:T(8,128)(2,1)S(1)} %collective-permute-done.17.own_ref), channel_id=1, source_target_pairs={{0,16},{16,0},{1,17},{17,1},{2,18},{18,2},{3,19},{19,3},{4,20},{20... | collective-permute-start | bytes 884744 | tf_op jit(solution)/shard_map/ppermute | solution.py:24
  22.2 16.2 %copy-start.6 = (s32[1,32,64]{2,1,0:T(8,128)S(1)}, s32[1,32,64]{2,1,0:T(8,128)}, u32[]{:S(2)}) copy-start(s32[1,32,64]{2,1,0:T(8,128)} %param.8) | copy-start | bytes 24580
  22.2 8.0 %collective-permute-start.7 = (bf16[4,16,1536]{2,1,0:T(8,128)(2,1)S(1)}, bf16[4,16,1536]{2,1,0:T(8,128)(2,1)S(1)}, u32[]{:S(2)}, u32[]{:S(2)}) collective-permute-start(bf16[4,16,1536]{2,1,0:T(8,128)(2,1)S(1)} %get-tuple-element.35), channel_id=1, source_target_pairs={{0,12},{4,8},{8,4},{12,0},{1,13},{5,9},{9,5},{13,1},{2,14},{6,10},... | collective-permute-start | bytes 589832 | tf_op jit(solution)/shard_map/ppermute | solution.py:24
  26.0 10.3 %collective-permute-start.10 = (bf16[4,32,1536]{2,1,0:T(8,128)(2,1)S(1)}, bf16[4,32,1536]{2,1,0:T(8,128)(2,1)S(1)}, u32[]{:S(2)}, u32[]{:S(2)}) collective-permute-start(bf16[4,32,1536]{2,1,0:T(8,128)(2,1)S(1)} %get-tuple-element.36.refs_0_), channel_id=1, source_target_pairs={{0,1},{1,0},{2,3},{3,2},{4,5},{5,4},{6,7},{7,6},{8,9},{9,8},{10,11... | collective-permute-start | bytes 1179656 | tf_op jit(solution)/shard_map/ppermute | solution.py:24
  26.3 12.1 %collective-permute-start.13 = (bf16[128,1536]{1,0:T(8,128)(2,1)S(1)}, bf16[128,1536]{1,0:T(8,128)(2,1)S(1)}, u32[]{:S(2)}, u32[]{:S(2)}) collective-permute-start(bf16[128,1536]{1,0:T(8,128)(2,1)S(1)} %shard_map.73.refs_0_), channel_id=1, source_target_pairs={{0,2},{1,3},{2,0},{3,1},{4,6},{5,7},{6,4},{7,5},{8,10},{9,11},{10,... | collective-permute-start | bytes 1179656 | tf_op jit(solution)/shard_map/ppermute | solution.py:24
  30.1 1.4 %collective-permute-start.2 = (bf16[4,16,1536]{2,1,0:T(8,128)(2,1)S(1)}, bf16[4,16,1536]{2,1,0:T(8,128)(2,1)S(1)}, u32[]{:S(2)}, u32[]{:S(2)}) collective-permute-start(bf16[4,16,1536]{2,1,0:T(8,128)(2,1)S(1)} %get-tuple-element.31.refs_0_), channel_id=1, source_target_pairs={{0,1},{1,0},{2,3},{3,2},{4,5},{5,4},{6,7},{7,6},{8,9},{9,8},{10,11... | collective-permute-start | bytes 589832 | tf_op jit(solution)/shard_map/ppermute | solution.py:24
  30.2 2.9 %collective-permute-start.4 = (bf16[4,16,1536]{2,1,0:T(8,128)(2,1)S(1)}, bf16[4,16,1536]{2,1,0:T(8,128)(2,1)S(1)}, u32[]{:S(2)}, u32[]{:S(2)}) collective-permute-start(bf16[4,16,1536]{2,1,0:T(8,128)(2,1)S(1)} %collective-permute-done.3.refs_2_), channel_id=1, source_target_pairs={{0,1},{1,0},{2,3},{3,2},{4,5},{5,4},{6,7},{7,6},{8,9},{9,8},{10,11... | collective-permute-start | bytes 589832 | tf_op jit(solution)/shard_map/ppermute | solution.py:24
  30.7 8.6 %collective-permute-start.12 = (bf16[4,32,1536]{2,1,0:T(8,128)(2,1)S(1)}, bf16[4,32,1536]{2,1,0:T(8,128)(2,1)S(1)}, u32[]{:S(2)}, u32[]{:S(2)}) collective-permute-start(bf16[4,32,1536]{2,1,0:T(8,128)(2,1)S(1)} %collective-permute-done.11.refs_2_), channel_id=1, source_target_pairs={{0,1},{1,0},{2,3},{3,2},{4,5},{5,4},{6,7},{7,6},{8,9},{9,8},{10,11... | collective-permute-start | bytes 1179656 | tf_op jit(solution)/shard_map/ppermute | solution.py:24
  31.6 18.9 %collective-permute-start.9 = (bf16[192,1536]{1,0:T(8,128)(2,1)S(1)}, bf16[192,1536]{1,0:T(8,128)(2,1)S(1)}, u32[]{:S(2)}, u32[]{:S(2)}) collective-permute-start(bf16[192,1536]{1,0:T(8,128)(2,1)S(1)} %shard_map.76.refs_0_), channel_id=1, source_target_pairs={{0,2},{1,3},{2,0},{3,1},{4,6},{5,7},{6,4},{7,5},{8,10},{9,11},{10,... | collective-permute-start | bytes 1769480 | tf_op jit(solution)/shard_map/ppermute | solution.py:24
  33.0 17.5 %collective-permute-start.19 = (bf16[192,1536]{1,0:T(8,128)(2,1)S(1)}, bf16[192,1536]{1,0:T(8,128)(2,1)S(1)}, u32[]{:S(2)}, u32[]{:S(2)}) collective-permute-start(bf16[192,1536]{1,0:T(8,128)(2,1)S(1)} %shard_map.85.own_ref), channel_id=1, source_target_pairs={{0,4},{4,0},{8,12},{12,8},{1,5},{5,1},{9,13},{13,9},{2,6},{6,2},{1... | collective-permute-start | bytes 1769480 | tf_op jit(solution)/shard_map/ppermute | solution.py:24
  36.3 14.9 %collective-permute-start.8 = (bf16[192,1536]{1,0:T(8,128)(2,1)S(1)}, bf16[192,1536]{1,0:T(8,128)(2,1)S(1)}, u32[]{:S(2)}, u32[]{:S(2)}) collective-permute-start(bf16[192,1536]{1,0:T(8,128)(2,1)S(1)} %shard_map.76.refs_0_), channel_id=1, source_target_pairs={{0,1},{1,0},{2,3},{3,2},{4,5},{5,4},{6,7},{7,6},{8,9},{9,8},{10,11... | collective-permute-start | bytes 1769480 | tf_op jit(solution)/shard_map/ppermute | solution.py:24
  38.4 4.8 %collective-permute-start.1 = (bf16[128,1536]{1,0:T(8,128)(2,1)S(1)}, bf16[128,1536]{1,0:T(8,128)(2,1)S(1)}, u32[]{:S(2)}, u32[]{:S(2)}) collective-permute-start(bf16[128,1536]{1,0:T(8,128)(2,1)S(1)} %shard_map.73.refs_0_), channel_id=1, source_target_pairs={{0,1},{1,0},{2,3},{3,2},{4,5},{5,4},{6,7},{7,6},{8,9},{9,8},{10,11... | collective-permute-start | bytes 1179656 | tf_op jit(solution)/shard_map/ppermute | solution.py:24
  39.3 13.6 %collective-permute-start.14 = (bf16[128,1536]{1,0:T(8,128)(2,1)S(1)}, bf16[128,1536]{1,0:T(8,128)(2,1)S(1)}, u32[]{:S(2)}, u32[]{:S(2)}) collective-permute-start(bf16[128,1536]{1,0:T(8,128)(2,1)S(1)} %collective-permute-done.13.refs_0_), channel_id=1, source_target_pairs={{0,1},{1,0},{2,3},{3,2},{4,5},{5,4},{6,7},{7,6},{8,9},{9,8},{10,11... | collective-permute-start | bytes 1179656 | tf_op jit(solution)/shard_map/ppermute | solution.py:24
  43.2 28.1 %collective-permute-start.24 = (bf16[384,1536]{1,0:T(8,128)(2,1)S(1)}, bf16[384,1536]{1,0:T(8,128)(2,1)S(1)}, u32[]{:S(2)}, u32[]{:S(2)}) collective-permute-start(bf16[384,1536]{1,0:T(8,128)(2,1)S(1)} %copy-done.3), channel_id=1, source_target_pairs={{0,1},{1,0},{2,3},{3,2},{4,5},{5,4},{6,7},{7,6},{8,9},{9,8},{10,11... | collective-permute-start | bytes 3538952 | tf_op jit(solution)/shard_map/ppermute | solution.py:24
  50.5 11.7 %collective-permute-start.15 = (bf16[192,1536]{1,0:T(8,128)(2,1)S(1)}, bf16[192,1536]{1,0:T(8,128)(2,1)S(1)}, u32[]{:S(2)}, u32[]{:S(2)}) collective-permute-start(bf16[192,1536]{1,0:T(8,128)(2,1)S(1)} %collective-permute-done.9.refs_0_), channel_id=1, source_target_pairs={{0,1},{1,0},{2,3},{3,2},{4,5},{5,4},{6,7},{7,6},{8,9},{9,8},{10,11... | collective-permute-start | bytes 1769480 | tf_op jit(solution)/shard_map/ppermute | solution.py:24
  50.6 22.6 %collective-permute-start.20 = (bf16[384,1536]{1,0:T(8,128)(2,1)S(1)}, bf16[384,1536]{1,0:T(8,128)(2,1)S(1)}, u32[]{:S(2)}, u32[]{:S(2)}) collective-permute-start(bf16[384,1536]{1,0:T(8,128)(2,1)S(1)} %shard_map.86.refs_6_.refs_5_), channel_id=1, source_target_pairs={{0,1},{1,0},{2,3},{3,2},{4,5},{5,4},{6,7},{7,6},{8,9},{9,8},{10,11... | collective-permute-start | bytes 3538952 | tf_op jit(solution)/shard_map/ppermute | solution.py:24
  52.9 1.2 %copy-start.7 = (f32[4]{0:T(128)S(1)}, f32[4]{0:T(128)}, u32[]{:S(2)}) copy-start(f32[4]{0:T(128)} %refs_5_.9) | copy-start | bytes 52
  60.6 11.1 %collective-permute-start.21 = (bf16[1,256,384]{2,1,0:T(8,128)(2,1)S(1)}, bf16[1,256,384]{2,1,0:T(8,128)(2,1)S(1)}, u32[]{:S(2)}, u32[]{:S(2)}) collective-permute-start(bf16[1,256,384]{2,1,0:T(8,128)(2,1)S(1)} %get-tuple-element.42), channel_id=1, source_target_pairs={{0,1},{1,0},{2,3},{3,2},{4,5},{5,4},{6,7},{7,6},{8,9},{9,8},{10,11... | collective-permute-start | bytes 589832 | tf_op jit(solution)/shard_map/ppermute | solution.py:24
  60.7 12.5 %collective-permute-start.22 = (bf16[1,256,384]{2,1,0:T(8,128)(2,1)S(1)}, bf16[1,256,384]{2,1,0:T(8,128)(2,1)S(1)}, u32[]{:S(2)}, u32[]{:S(2)}) collective-permute-start(bf16[1,256,384]{2,1,0:T(8,128)(2,1)S(1)} %get-tuple-element.43), channel_id=1, source_target_pairs={{0,2},{1,3},{2,0},{3,1},{4,6},{5,7},{6,4},{7,5},{8,10},{9,11},{10,... | collective-permute-start | bytes 589832 | tf_op jit(solution)/shard_map/ppermute | solution.py:24
  62.3 11.0 %collective-permute-start.23 = (bf16[1,256,384]{2,1,0:T(8,128)(2,1)S(1)}, bf16[1,256,384]{2,1,0:T(8,128)(2,1)S(1)}, u32[]{:S(2)}, u32[]{:S(2)}) collective-permute-start(bf16[1,256,384]{2,1,0:T(8,128)(2,1)S(1)} %get-tuple-element.44), channel_id=1, source_target_pairs={{0,3},{1,2},{2,1},{3,0},{4,7},{5,6},{6,5},{7,4},{8,11},{9,10},{10,... | collective-permute-start | bytes 589832 | tf_op jit(solution)/shard_map/ppermute | solution.py:24
  67.8 5.5 %copy-start.2 = (bf16[1,8,1,64,1536]{4,3,2,1,0:T(8,128)(2,1)S(1)}, bf16[1,8,1,64,1536]{4,3,2,1,0:T(8,128)(2,1)}, u32[]{:S(2)}) copy-start(bf16[1,8,1,64,1536]{4,3,2,1,0:T(8,128)(2,1)} %param.7) | copy-start | bytes 4718596
  71.3 3.4 %collective-permute-start.25 = (bf16[1,256,384]{2,1,0:T(8,128)(2,1)S(1)}, bf16[1,256,384]{2,1,0:T(8,128)(2,1)S(1)}, u32[]{:S(2)}, u32[]{:S(2)}) collective-permute-start(bf16[1,256,384]{2,1,0:T(8,128)(2,1)S(1)} %get-tuple-element.52), channel_id=1, source_target_pairs={{0,1},{1,0},{2,3},{3,2},{4,5},{5,4},{6,7},{7,6},{8,9},{9,8},{10,11... | collective-permute-start | bytes 589832 | tf_op jit(solution)/shard_map/ppermute | solution.py:24
  71.7 7.8 %collective-permute-start.26 = (bf16[1,256,384]{2,1,0:T(8,128)(2,1)S(1)}, bf16[1,256,384]{2,1,0:T(8,128)(2,1)S(1)}, u32[]{:S(2)}, u32[]{:S(2)}) collective-permute-start(bf16[1,256,384]{2,1,0:T(8,128)(2,1)S(1)} %get-tuple-element.49), channel_id=1, source_target_pairs={{0,2},{1,3},{2,0},{3,1},{4,6},{5,7},{6,4},{7,5},{8,10},{9,11},{10,... | collective-permute-start | bytes 589832 | tf_op jit(solution)/shard_map/ppermute | solution.py:24
  73.2 8.9 %collective-permute-start.16 = (bf16[1,256,384]{2,1,0:T(8,128)(2,1)S(1)}, bf16[1,256,384]{2,1,0:T(8,128)(2,1)S(1)}, u32[]{:S(2)}, u32[]{:S(2)}) collective-permute-start(bf16[1,256,384]{2,1,0:T(8,128)(2,1)S(1)} %get-tuple-element.48), channel_id=1, source_target_pairs={{0,3},{1,2},{2,1},{3,0},{4,7},{5,6},{6,5},{7,4},{8,11},{9,10},{10,... | collective-permute-start | bytes 589832 | tf_op jit(solution)/shard_map/ppermute | solution.py:24

commit v10 on v9

--- a/solution.py
+++ b/solution.py
@@ -304,24 +304,36 @@
     return jnp.dot(rows, depth, preferred_element_type=F32)
 
 
-def partial_kernel(count, *refs):
-    *refs, out_ref = refs
-    out_ref[...] = product(refs[:count], refs[count:])
-
-
-def partial(attended, weights):
+def partial_kernel(count, spans, *refs):
+    attended, weights = refs[:count], refs[count : 2 * count]
+    done_ref, *sources, out_ref, mixed_ref, semaphore = refs[2 * count :]
+    copy = pltpu.make_async_copy(
+        done_ref, mixed_ref.at[:, pl.ds(0, done_ref.shape[1]), :], semaphore.at[0]
+    )
+    copy.start()
+    total = product(attended, weights)
+    at = 0
+    for which, row, start, pixels in spans:
+        held = sources[which][row, start : start + pixels, :].astype(F32)
+        out_ref[at : at + pixels, :] = held + total[at : at + pixels]
+        at += pixels
+    copy.wait()
+
+
+def partial(attended, weights, done, sources, spans, shape):
     pixels, depth = attended[0].shape
     width = weights[0].shape[1]
     return pl.pallas_call(
-        functools.partial(partial_kernel, len(weights)),
-        out_shape=jax.ShapeDtypeStruct((pixels, width), F32),
-        in_specs=[VMEM] * (2 * len(weights)),
-        out_specs=VMEM,
+        functools.partial(partial_kernel, len(weights), spans),
+        out_shape=[jax.ShapeDtypeStruct((pixels, width), F32), jax.ShapeDtypeStruct(shape, BF16)],
+        in_specs=[VMEM] * (2 * len(weights) + 1 + len(sources)),
+        out_specs=[VMEM, HELD],
+        scratch_shapes=[pltpu.SemaphoreType.DMA((1,))],
         compiler_params=pltpu.CompilerParams(vmem_limit_bytes=20 << 20),
         cost_estimate=pl.CostEstimate(
             flops=2 * pixels * width * depth * len(weights), bytes_accessed=2 * width * (depth + 2 * pixels), transcendentals=0
         ),
-    )(*attended, *weights)
+    )(*attended, *weights, done, *sources)
 
 
 def finish_kernel(count, spans, *refs):
@@ -351,22 +363,17 @@
 
 def last_kernel(count, chunks, spans, *refs):
     attended, weights = refs[:count], refs[count : 2 * count]
-    base_ref, done_ref, *sources, out_ref, ready, semaphore = refs[2 * count :]
-    left, size, width = done_ref.shape[1], ready.shape[1], ready.shape[2]
+    base_ref, _, out_ref, ready, semaphore = refs[2 * count :]
+    size, width = ready.shape[1], ready.shape[2]
+    left = out_ref.shape[1] - size
     wide = width // chunks
-    copies = [
-        pltpu.make_async_copy(done_ref, out_ref.at[:, pl.ds(0, left), :], semaphore.at[chunks])
-    ]
-    copies[0].start()
+    copies = []
     for chunk in range(chunks):
         columns = slice(chunk * wide, (chunk + 1) * wide)
-        total = product(attended, weights, columns) + base_ref[:, columns]
+        total = (product(attended, weights, columns) + base_ref[:, columns]).astype(BF16)
         at = 0
-        for which, row, start, pixels, into, column in spans:
-            held = sources[which][row, start : start + pixels, columns].astype(F32)
-            ready[into, column - left : column - left + pixels, columns] = (
-                held + total[at : at + pixels]
-            ).astype(BF16)
+        for pixels, into, column in spans:
+            ready[into, column - left : column - left + pixels, columns] = total[at : at + pixels]
             at += pixels
         place = pl.ds(chunk * wide, wide)
         copy = pltpu.make_async_copy(
@@ -378,25 +385,26 @@
         copy.wait()
 
 
-def finish_last(attended, weights, base, done, sources, spans, shape):
+def finish_last(attended, weights, base, mixed, done_columns, spans):
     count = len(weights)
-    row_count, col_count, width = shape
+    row_count, col_count, width = mixed.shape
     pixels, depth = attended[0].shape
     chunks = 3 if width % (3 * 2 * LANE) == 0 else 1
     return pl.pallas_call(
         functools.partial(last_kernel, count, chunks, spans),
-        out_shape=jax.ShapeDtypeStruct(shape, BF16),
-        in_specs=[VMEM] * (2 * count + 2 + len(sources)),
+        out_shape=jax.ShapeDtypeStruct(mixed.shape, BF16),
+        in_specs=[VMEM] * (2 * count + 1) + [HELD],
         out_specs=HELD,
+        input_output_aliases={2 * count + 1: 0},
         scratch_shapes=[
-            pltpu.VMEM((row_count, col_count - done.shape[1], width), BF16),
-            pltpu.SemaphoreType.DMA((chunks + 1,)),
+            pltpu.VMEM((row_count, col_count - done_columns, width), BF16),
+            pltpu.SemaphoreType.DMA((chunks,)),
         ],
         compiler_params=pltpu.CompilerParams(vmem_limit_bytes=20 << 20),
         cost_estimate=pl.CostEstimate(
             flops=2 * pixels * width * depth * count, bytes_accessed=2 * width * (width + 3 * pixels), transcendentals=0
         ),
-    )(*attended, *weights, base, done, *sources)
+    )(*attended, *weights, base, mixed)
 
 
 def send_heads(outs):
@@ -501,15 +509,15 @@
     weights = triple_projection_matrix
     scales = logit_scaling_per_part
 
+    local_0 = blocked[rows:, half : half + WS]
     boxes = [
-        (rows, half, WS),
         (rows, half + WS, near),
         (0, half, WS),
         (0, half + WS, near),
         (rows, 0, half),
         (0, 0, half),
     ]
-    local_0, local_1, south_0, south_1, east, corner = cut(blocked, rows, boxes)
+    local_1, south_0, south_1, east, corner = cut(blocked, rows, boxes)
     south_0 = exchange(south_0, 1, "win")
     south_1 = exchange(south_1, 1, "win")
     east = permute_by(east, "win", west)
@@ -560,12 +568,14 @@
     shape = (row_count, col_count, width)
     done = finish(first, out_weights, [blocked, south_0], spans, (row_count, WS, width))
     second[0] = after(second[0], done)
-    base = partial(second[:-1], out_weights[:-1])
     spans = [(0, rows + row, half + WS, near, row, WS) for row in range(rows)]
     spans += [(1, row, 0, near, rows + row, WS) for row in range(rows)]
     spans += [(2, row, 0, half, row, WS + near) for row in range(rows)]
     spans += [(3, row, 0, half, rows + row, WS + near) for row in range(rows)]
-    mixed = finish_last(second[-1:], out_weights[-1:], base, done, [blocked, south_1, east, corner], spans, shape)
+    sources = [blocked, south_1, east, corner]
+    base, mixed = partial(second[:-1], out_weights[:-1], done, sources, [span[:4] for span in spans], shape)
+    spans = [span[3:] for span in spans]
+    mixed = finish_last(second[-1:], out_weights[-1:], base, mixed, WS, spans)
     return mixed[None, :, None]
 
 

time: 84.2 us -> 88.5 us (1.051)
  waiting for transfers between devices: 25.3 us -> 33.1 us
  starting transfers between devices: 27 us -> 21.5 us
  local copies, waits for them, and re-layouts: 1.44 us -> 2.73 us
    ppermute x27, waiting for transfers between devices: 25.3 us -> 33.1 us  [permute_by(): return lax.ppermute(value, axis, pairs)]
    ppermute x27, starting transfers between devices: 27 us -> 21.5 us  [permute_by(): return lax.ppermute(value, axis, pairs)]
    unnamed x16 -> x18, local copies, waits for them, and re-layouts: 1.44 us -> 2.71 us
  transfers between devices with their start and end apart: 27 -> 27, of which waited for: 9 -> 7; matrix products, arithmetic and copies ran while one was open for 0% -> 0% of each run, Pallas kernels for 33% -> 33%
where the time goes in v10:
time: 88.5 us; the launch traced here: 88.2 us
  waiting for transfers between devices  33.1 us (37%)
  Pallas kernels  30.4 us (34%)
  starting transfers between devices  21.5 us (24%)
  local copies, waits for them, and re-layouts  2.73 us (3%)
    ppermute x27, waiting for transfers between devices, permute_by(): return lax.ppermute(value, axis, pairs)  33.1 us
    ppermute x27, starting transfers between devices, permute_by(): return lax.ppermute(value, axis, pairs)  21.5 us
    pallas_call x3, Pallas kernels, attend(): pl.pallas_call(functools.partial(attend_kernel, layout, ranges, head_widt...  13.6 us
    pallas_call x5, Pallas kernels, project(): pl.pallas_call(functools.partial(project_kernel, [len(group) for group in...  8.99 us
    unnamed x18, local copies, waits for them, and re-layouts  2.71 us
    pallas_call x4, Pallas kernels, norm(): pl.pallas_call(functools.partial(norm_kernel, groups), out_shape=[jax.Sha...  2.43 us
  transfers between devices with their start and end apart: 27, of which 7 were waited for; matrix products, arithmetic and copies ran while one was open for 0% of the time, Pallas kernels for 33%

profile of v10, /device:TPU:0, one launch (start us, length us, event | category | flops | bytes accessed | tf_op | source)
XLA Modules:
  0.0 88.2 jit_solution(9395518649600910087)
XLA Ops:
  0.0 1.4 %copy-done.1 = bf16[1,8,1,64,1536]{4,3,2,1,0:T(8,128)(2,1)S(1)} copy-done((bf16[1,8,1,64,1536]{4,3,2,1,0:T(8,128)(2,1)S(1)}, bf16[1,8,1,64,1536]{4,3,2,1,0:T(8,128)(2,1)}, u32[]{:S(2)}) %copy-start.1) | copy-done | bytes 1572888
  1.4 0.1 cut.1
  1.5 3.1 %collective-permute-start.5 = (bf16[4,16,1536]{2,1,0:T(8,128)(2,1)S(1)}, bf16[4,16,1536]{2,1,0:T(8,128)(2,1)S(1)}, u32[]{:S(2)}, u32[]{:S(2)}) collective-permute-start(bf16[4,16,1536]{2,1,0:T(8,128)(2,1)S(1)} %get-tuple-element.34), channel_id=1, source_target_pairs={{0,4},{4,0},{8,12},{12,8},{1,5},{5,1},{9,13},{13,9},{2,6},{6,2},{1... | collective-permute-start | bytes 589832 | tf_op jit(solution)/shard_map/ppermute | solution.py:24
  4.6 1.6 %collective-permute-start.11 = (bf16[4,32,1536]{2,1,0:T(8,128)(2,1)S(1)}, bf16[4,32,1536]{2,1,0:T(8,128)(2,1)S(1)}, u32[]{:S(2)}, u32[]{:S(2)}) collective-permute-start(bf16[4,32,1536]{2,1,0:T(8,128)(2,1)S(1)} %slice.4.refs_0_), channel_id=1, source_target_pairs={{0,2},{1,3},{2,0},{3,1},{4,6},{5,7},{6,4},{7,5},{8,10},{9,11},{10,... | collective-permute-start | bytes 1179656 | tf_op jit(solution)/shard_map/ppermute | solution.py:24
  6.2 1.3 %copy-done.3 = bf16[384,1536]{1,0:T(8,128)(2,1)S(1)} copy-done((bf16[384,1536]{1,0:T(8,128)(2,1)S(1)}, bf16[384,1536]{1,0:T(8,128)(2,1)}, u32[]{:S(2)}) %copy-start.3) | copy-done | bytes 1179672
  7.5 0.6 collective-permute-start.17
  8.1 2.6 %collective-permute-start.6 = (bf16[4,16,1536]{2,1,0:T(8,128)(2,1)S(1)}, bf16[4,16,1536]{2,1,0:T(8,128)(2,1)S(1)}, u32[]{:S(2)}, u32[]{:S(2)}) collective-permute-start(bf16[4,16,1536]{2,1,0:T(8,128)(2,1)S(1)} %get-tuple-element.35), channel_id=1, source_target_pairs={{0,8},{4,12},{8,0},{12,4},{1,9},{5,13},{9,1},{13,5},{2,10},{6,14},... | collective-permute-start | bytes 589832 | tf_op jit(solution)/shard_map/ppermute | solution.py:24
  10.7 1.0 %collective-permute-start.7 = (bf16[4,16,1536]{2,1,0:T(8,128)(2,1)S(1)}, bf16[4,16,1536]{2,1,0:T(8,128)(2,1)S(1)}, u32[]{:S(2)}, u32[]{:S(2)}) collective-permute-start(bf16[4,16,1536]{2,1,0:T(8,128)(2,1)S(1)} %get-tuple-element.36), channel_id=1, source_target_pairs={{0,12},{4,8},{8,4},{12,0},{1,13},{5,9},{9,5},{13,1},{2,14},{6,10},... | collective-permute-start | bytes 589832 | tf_op jit(solution)/shard_map/ppermute | solution.py:24
  11.8 0.2 collective-permute-start
  12.0 9.6 %collective-permute-done.17.own_ref = bf16[96,1536]{1,0:T(8,128)(2,1)S(1)} collective-permute-done((bf16[96,1536]{1,0:T(8,128)(2,1)S(1)}, bf16[96,1536]{1,0:T(8,128)(2,1)S(1)}, u32[]{:S(2)}, u32[]{:S(2)}) %collective-permute-start.17) | collective-permute-done | bytes 294944 | tf_op jit(solution)/shard_map/ppermute | solution.py:24
  21.6 1.5 %collective-permute-start.18 = (bf16[96,1536]{1,0:T(8,128)(2,1)S(1)}, bf16[96,1536]{1,0:T(8,128)(2,1)S(1)}, u32[]{:S(2)}, u32[]{:S(2)}) collective-permute-start(bf16[96,1536]{1,0:T(8,128)(2,1)S(1)} %collective-permute-done.17.own_ref), channel_id=1, source_target_pairs={{0,16},{16,0},{1,17},{17,1},{2,18},{18,2},{3,19},{19,3},{4,20},{20... | collective-permute-start | bytes 884744 | tf_op jit(solution)/shard_map/ppermute | solution.py:24
  23.1 1.4 %collective-permute-done.6.refs_1_.refs_9_ = bf16[4,16,1536]{2,1,0:T(8,128)(2,1)S(1)} collective-permute-done((bf16[4,16,1536]{2,1,0:T(8,128)(2,1)S(1)}, bf16[4,16,1536]{2,1,0:T(8,128)(2,1)S(1)}, u32[]{:S(2)}, u32[]{:S(2)}) %collective-permute-start.6) | collective-permute-done | bytes 196640 | tf_op jit(solution)/shard_map/ppermute | solution.py:24
  24.5 1.5 %collective-permute-start.3 = (bf16[4,16,1536]{2,1,0:T(8,128)(2,1)S(1)}, bf16[4,16,1536]{2,1,0:T(8,128)(2,1)S(1)}, u32[]{:S(2)}, u32[]{:S(2)}) collective-permute-start(bf16[4,16,1536]{2,1,0:T(8,128)(2,1)S(1)} %get-tuple-element.32.refs_0_), channel_id=1, source_target_pairs={{0,2},{1,3},{2,0},{3,1},{4,6},{5,7},{6,4},{7,5},{8,10},{9,11},{10,... | collective-permute-start | bytes 589832 | tf_op jit(solution)/shard_map/ppermute | solution.py:24
  26.0 0.5 collective-permute-start.12
  26.5 3.7 %collective-permute-done.3.refs_2_ = bf16[4,16,1536]{2,1,0:T(8,128)(2,1)S(1)} collective-permute-done((bf16[4,16,1536]{2,1,0:T(8,128)(2,1)S(1)}, bf16[4,16,1536]{2,1,0:T(8,128)(2,1)S(1)}, u32[]{:S(2)}, u32[]{:S(2)}) %collective-permute-start.3) | collective-permute-done | bytes 196640 | tf_op jit(solution)/shard_map/ppermute | solution.py:24
  30.2 0.5 collective-permute-start.4
  30.7 0.3 shard_map.73.refs_0_
  31.0 1.6 %collective-permute-start.13 = (bf16[128,1536]{1,0:T(8,128)(2,1)S(1)}, bf16[128,1536]{1,0:T(8,128)(2,1)S(1)}, u32[]{:S(2)}, u32[]{:S(2)}) collective-permute-start(bf16[128,1536]{1,0:T(8,128)(2,1)S(1)} %shard_map.73.refs_0_), channel_id=1, source_target_pairs={{0,2},{1,3},{2,0},{3,1},{4,6},{5,7},{6,4},{7,5},{8,10},{9,11},{10,... | collective-permute-start | bytes 1179656 | tf_op jit(solution)/shard_map/ppermute | solution.py:24
  32.6 0.4 shard_map.76.refs_0_
  33.1 0.6 collective-permute-start.9
  33.7 0.7 collective-permute-start.19
  34.4 0.5 collective-permute-start.1
  34.9 0.4 tags.1
  35.2 0.6 shard_map.74.refs_2_
  35.8 7.3 %collective-permute-done.13.refs_0_ = bf16[128,1536]{1,0:T(8,128)(2,1)S(1)} collective-permute-done((bf16[128,1536]{1,0:T(8,128)(2,1)S(1)}, bf16[128,1536]{1,0:T(8,128)(2,1)S(1)}, u32[]{:S(2)}, u32[]{:S(2)}) %collective-permute-start.13) | collective-permute-done | bytes 393248 | tf_op jit(solution)/shard_map/ppermute | solution.py:24
  43.1 1.1 %shard_map.78.refs_0_ = bf16[512,1536]{1,0:T(8,128)(2,1)S(1)} custom-call(bf16[4,32,1536]{2,1,0:T(8,128)(2,1)S(1)} %slice.4.refs_0_, bf16[4,32,1536]{2,1,0:T(8,128)(2,1)S(1)} %collective-permute-done.10.refs_1_, bf16[4,32,1536]{2,1,0:T(8,128)(2,1)S(1)} %collective-permute-done.11.refs_2_, bf16[4,32,1536]{2,1,0:T(8,128)(2,1)S(1)} %collective-permute-done.12.refs_3_, ...), custom_call_target="tpu_custom_call" | custom-call | flops 7864320 | bytes 3145728 | tf_op jit(solution)/shard_map/pallas_call | solution.py:102
  44.2 2.2 %shard_map.79.refs_0_ = bf16[512,1152]{1,0:T(8,128)(2,1)S(1)} custom-call(bf16[512,1536]{1,0:T(8,128)(2,1)S(1)} %shard_map.78.refs_0_, bf16[3,1536,384]{2,1,0:T(8,128)(2,1)S(1)} %copy-done), custom_call_target="tpu_custom_call" | custom-call | flops 1811939328 | bytes 6291456 | tf_op jit(solution)/shard_map/pallas_call | solution.py:197
  46.4 0.6 collective-permute-start.24
  47.0 2.2 %shard_map.75 = (bf16[256,1152]{1,0:T(8,128)(2,1)S(1)}, bf16[256,1152]{1,0:T(8,128)(2,1)S(1)}) custom-call(bf16[128,1536]{1,0:T(8,128)(2,1)S(1)} %shard_map.73.refs_0_, bf16[128,1536]{1,0:T(8,128)(2,1)S(1)} %collective-permute-done.1.refs_1_, bf16[256,1536]{1,0:T(8,128)(2,1)S(1)} %shard_map.74.refs_2_, bf16[3,1536,384]{2,1,0:T(8,128)(2,1)S(1)} %copy-done), custom_call_target="tpu_custom_call" | custom-call | flops 1811939328 | bytes 6291456 | tf_op jit(solution)/shard_map/pallas_call | solution.py:197
  49.2 5.5 %collective-permute-done.9.refs_0_ = bf16[192,1536]{1,0:T(8,128)(2,1)S(1)} collective-permute-done((bf16[192,1536]{1,0:T(8,128)(2,1)S(1)}, bf16[192,1536]{1,0:T(8,128)(2,1)S(1)}, u32[]{:S(2)}, u32[]{:S(2)}) %collective-permute-start.9) | collective-permute-done | bytes 589856 | tf_op jit(solution)/shard_map/ppermute | solution.py:24
  54.8 0.1 shard_map.86.refs_6_.refs_5_
  54.9 0.6 collective-permute-start.20
  55.4 1.7 %shard_map.77.refs_1_ = bf16[384,1152]{1,0:T(8,128)(2,1)S(1)} custom-call(bf16[192,1536]{1,0:T(8,128)(2,1)S(1)} %shard_map.76.refs_0_, bf16[192,1536]{1,0:T(8,128)(2,1)S(1)} %collective-permute-done.8.refs_1_, bf16[3,1536,384]{2,1,0:T(8,128)(2,1)S(1)} %copy-done), custom_call_target="tpu_custom_call" | custom-call | flops 1358954496 | bytes 5603328 | tf_op jit(solution)/shard_map/pallas_call | solution.py:197
  57.2 1.2 %shard_map.80.refs_2_ = bf16[256,1152]{1,0:T(8,128)(2,1)S(1)} custom-call(bf16[128,1536]{1,0:T(8,128)(2,1)S(1)} %collective-permute-done.13.refs_0_, bf16[128,1536]{1,0:T(8,128)(2,1)S(1)} %collective-permute-done.14.refs_1_, bf16[3,1536,384]{2,1,0:T(8,128)(2,1)S(1)} %copy-done), custom_call_target="tpu_custom_call" | custom-call | flops 905969664 | bytes 4915200 | tf_op jit(solution)/shard_map/pallas_call | solution.py:197
  58.4 6.5 %shard_map.81 = (bf16[1,256,384]{2,1,0:T(8,128)(2,1)S(1)}, bf16[1,256,384]{2,1,0:T(8,128)(2,1)S(1)}, bf16[1,256,384]{2,1,0:T(8,128)(2,1)S(1)}, bf16[1,256,384]{2,1,0:T(8,128)(2,1)S(1)}) custom-call(bf16[512,1152]{1,0:T(8,128)(2,1)S(1)} %shard_map.79.refs_0_, bf16[256,1152]{1,0:T(8,128)(2,1)S(1)} %get-tuple-element.37.refs_1_, ...), custom_call_target="tpu_custom_call" | custom-call | flops 4294967296 | bytes 2359296 | tf_op jit(solution)/shard_map/pallas_call | solution.py:285
  64.9 0.1 collective-permute-start.21
  65.0 1.6 %collective-permute-start.22 = (bf16[1,256,384]{2,1,0:T(8,128)(2,1)S(1)}, bf16[1,256,384]{2,1,0:T(8,128)(2,1)S(1)}, u32[]{:S(2)}, u32[]{:S(2)}) collective-permute-start(bf16[1,256,384]{2,1,0:T(8,128)(2,1)S(1)} %get-tuple-element.43), channel_id=1, source_target_pairs={{0,2},{1,3},{2,0},{3,1},{4,6},{5,7},{6,4},{7,5},{8,10},{9,11},{10,... | collective-permute-start | bytes 589832 | tf_op jit(solution)/shard_map/ppermute | solution.py:24
  66.5 0.3 collective-permute-start.23
  66.8 1.7 %shard_map.82.refs_2_ = bf16[384,1152]{1,0:T(8,128)(2,1)S(1)} custom-call(bf16[192,1536]{1,0:T(8,128)(2,1)S(1)} %collective-permute-done.9.refs_0_, bf16[192,1536]{1,0:T(8,128)(2,1)S(1)} %collective-permute-done.15.refs_1_, bf16[3,1536,384]{2,1,0:T(8,128)(2,1)S(1)} %copy-done), custom_call_target="tpu_custom_call" | custom-call | flops 1358954496 | bytes 5603328 | tf_op jit(solution)/shard_map/pallas_call | solution.py:197
  68.5 3.5 %shard_map.83 = (bf16[1,256,384]{2,1,0:T(8,128)(2,1)S(1)}, bf16[1,256,384]{2,1,0:T(8,128)(2,1)S(1)}) custom-call(bf16[256,1152]{1,0:T(8,128)(2,1)S(1)} %get-tuple-element.50.refs_0_, bf16[384,1152]{1,0:T(8,128)(2,1)S(1)} %shard_map.77.refs_1_, bf16[384,1152]{1,0:T(8,128)(2,1)S(1)} %shard_map.82.refs_2_, bf16[1024,128]{1,0:T(8,128)(2,1)S(1)} %get-tuple-element.46.refs_3_, ...), custom_call_target="tpu_custom_call" | custom-call | flops 2147483648 | bytes 2359296 | tf_op jit(solution)/shard_map/pallas_call | solution.py:285
  72.1 3.5 %shard_map.87 = (bf16[1,256,384]{2,1,0:T(8,128)(2,1)S(1)}, bf16[1,256,384]{2,1,0:T(8,128)(2,1)S(1)}) custom-call(bf16[256,1152]{1,0:T(8,128)(2,1)S(1)} %get-tuple-element.50.refs_0_, bf16[384,1152]{1,0:T(8,128)(2,1)S(1)} %shard_map.77.refs_1_, bf16[384,1152]{1,0:T(8,128)(2,1)S(1)} %shard_map.82.refs_2_, bf16[1024,128]{1,0:T(8,128)(2,1)S(1)} %get-tuple-element.46.refs_3_, ...), custom_call_target="tpu_custom_call" | custom-call | flops 2147483648 | bytes 2359296 | tf_op jit(solution)/shard_map/pallas_call | solution.py:285
  75.6 0.4 collective-permute-start.25
  76.0 1.5 %collective-permute-start.26 = (bf16[1,256,384]{2,1,0:T(8,128)(2,1)S(1)}, bf16[1,256,384]{2,1,0:T(8,128)(2,1)S(1)}, u32[]{:S(2)}, u32[]{:S(2)}) collective-permute-start(bf16[1,256,384]{2,1,0:T(8,128)(2,1)S(1)} %get-tuple-element.49), channel_id=1, source_target_pairs={{0,2},{1,3},{2,0},{3,1},{4,6},{5,7},{6,4},{7,5},{8,10},{9,11},{10,... | collective-permute-start | bytes 589832 | tf_op jit(solution)/shard_map/ppermute | solution.py:24
  77.5 1.4 %shard_map.88.refs_6_ = bf16[8,32,1536]{2,1,0:T(8,128)(2,1)S(1)} custom-call(bf16[256,384]{1,0:T(8,128)(2,1)S(1)} %bitcast.21, bf16[256,384]{1,0:T(8,128)(2,1)S(1)} %bitcast.22, bf16[256,384]{1,0:T(8,128)(2,1)S(1)} %bitcast.23, bf16[256,384]{1,0:T(8,128)(2,1)S(1)} %bitcast.24, bf16[384,1536]{1,0:T(8,128)(2,1)S(1)} %copy-done.4, ...), custom_call_target="tpu_custom_call" | custom-call | flops 1207959552 | bytes 7077888 | tf_op jit(solution)/shard_map/pallas_call | solution.py:352
  79.0 4.9 %collective-permute-done.26 = bf16[1,256,384]{2,1,0:T(8,128)(2,1)S(1)} collective-permute-done((bf16[1,256,384]{2,1,0:T(8,128)(2,1)S(1)}, bf16[1,256,384]{2,1,0:T(8,128)(2,1)S(1)}, u32[]{:S(2)}, u32[]{:S(2)}) %collective-permute-start.26) | collective-permute-done | bytes 196640 | tf_op jit(solution)/shard_map/ppermute | solution.py:24
  83.8 1.8 %shard_map.89 = (f32[256,1536]{1,0:T(8,128)S(1)}, bf16[8,64,1536]{2,1,0:T(8,128)(2,1)}) custom-call(bf16[256,384]{1,0:T(8,128)(2,1)S(1)} %bitcast.17, bf16[256,384]{1,0:T(8,128)(2,1)S(1)} %bitcast.18, bf16[256,384]{1,0:T(8,128)(2,1)S(1)} %bitcast.19, bf16[384,1536]{1,0:T(8,128)(2,1)S(1)} %copy-done.4, ...), custom_call_target="tpu_custom_call" | custom-call | flops 905969664 | bytes 2752512 | tf_op jit(solution)/shard_map/pallas_call | solution.py:326
  85.6 0.8 collective-permute-done.16
  86.4 1.6 %shard_map.90 = bf16[8,64,1536]{2,1,0:T(8,128)(2,1)} custom-call(bf16[256,384]{1,0:T(8,128)(2,1)S(1)} %bitcast.20, bf16[384,1536]{1,0:T(8,128)(2,1)S(1)} %collective-permute-done.20.refs_7_.refs_1_, f32[256,1536]{1,0:T(8,128)S(1)} %get-tuple-element.55.refs_2_, bf16[8,64,1536]{2,1,0:T(8,128)(2,1)} %get-tuple-element.56.refs_3_), custom_call_target="tpu_custom_call", output_to_operand_aliasing={{}: (3, {})} | custom-call | flops 301989888 | bytes 7077888 | tf_op jit(solution)/shard_map/pallas_call | solution.py:393
  (45 shorter events, 0.3 us)
Async XLA Ops:
  0.0 1.4 %copy-start.1 = (bf16[1,8,1,64,1536]{4,3,2,1,0:T(8,128)(2,1)S(1)}, bf16[1,8,1,64,1536]{4,3,2,1,0:T(8,128)(2,1)}, u32[]{:S(2)}) copy-start(bf16[1,8,1,64,1536]{4,3,2,1,0:T(8,128)(2,1)} %param.7) | copy-start | bytes 4718596
  1.4 3.2 %copy-start.2 = (bf16[1,8,1,64,1536]{4,3,2,1,0:T(8,128)(2,1)S(1)}, bf16[1,8,1,64,1536]{4,3,2,1,0:T(8,128)(2,1)}, u32[]{:S(2)}) copy-start(bf16[1,8,1,64,1536]{4,3,2,1,0:T(8,128)(2,1)} %param.7) | copy-start | bytes 4718596
  1.4 29.3 %copy-start.5 = (f32[1536]{0:T(1024)S(1)}, f32[1536]{0:T(1024)}, u32[]{:S(2)}) copy-start(f32[1536]{0:T(1024)} %refs_4_.6) | copy-start | bytes 18436
  1.4 29.3 %copy-start.6 = (f32[1536]{0:T(1024)S(1)}, f32[1536]{0:T(1024)}, u32[]{:S(2)}) copy-start(f32[1536]{0:T(1024)} %refs_5_.6) | copy-start | bytes 18436
  1.5 10.3 %collective-permute-start.5 = (bf16[4,16,1536]{2,1,0:T(8,128)(2,1)S(1)}, bf16[4,16,1536]{2,1,0:T(8,128)(2,1)S(1)}, u32[]{:S(2)}, u32[]{:S(2)}) collective-permute-start(bf16[4,16,1536]{2,1,0:T(8,128)(2,1)S(1)} %get-tuple-element.34), channel_id=1, source_target_pairs={{0,4},{4,0},{8,12},{12,8},{1,5},{5,1},{9,13},{13,9},{2,6},{6,2},{1... | collective-permute-start | bytes 589832 | tf_op jit(solution)/shard_map/ppermute | solution.py:24
  4.6 21.3 %collective-permute-start.11 = (bf16[4,32,1536]{2,1,0:T(8,128)(2,1)S(1)}, bf16[4,32,1536]{2,1,0:T(8,128)(2,1)S(1)}, u32[]{:S(2)}, u32[]{:S(2)}) collective-permute-start(bf16[4,32,1536]{2,1,0:T(8,128)(2,1)S(1)} %slice.4.refs_0_), channel_id=1, source_target_pairs={{0,2},{1,3},{2,0},{3,1},{4,6},{5,7},{6,4},{7,5},{8,10},{9,11},{10,... | collective-permute-start | bytes 1179656 | tf_op jit(solution)/shard_map/ppermute | solution.py:24
  6.2 1.3 %copy-start.3 = (bf16[384,1536]{1,0:T(8,128)(2,1)S(1)}, bf16[384,1536]{1,0:T(8,128)(2,1)}, u32[]{:S(2)}) copy-start(bf16[384,1536]{1,0:T(8,128)(2,1)} %refs_3_.5) | copy-start | bytes 3538948
  7.5 27.4 %copy-start = (bf16[3,1536,384]{2,1,0:T(8,128)(2,1)S(1)}, bf16[3,1536,384]{2,1,0:T(8,128)(2,1)}, u32[]{:S(2)}) copy-start(bf16[3,1536,384]{2,1,0:T(8,128)(2,1)} %refs_2_.7) | copy-start | bytes 10616836
  7.5 14.1 %collective-permute-start.17 = (bf16[96,1536]{1,0:T(8,128)(2,1)S(1)}, bf16[96,1536]{1,0:T(8,128)(2,1)S(1)}, u32[]{:S(2)}, u32[]{:S(2)}) collective-permute-start(bf16[96,1536]{1,0:T(8,128)(2,1)S(1)} %shard_map.84), channel_id=1, source_target_pairs={{0,2},{1,3},{2,0},{3,1},{4,6},{5,7},{6,4},{7,5},{8,10},{9,11},{10,... | collective-permute-start | bytes 884744 | tf_op jit(solution)/shard_map/ppermute | solution.py:24
  8.1 16.3 %collective-permute-start.6 = (bf16[4,16,1536]{2,1,0:T(8,128)(2,1)S(1)}, bf16[4,16,1536]{2,1,0:T(8,128)(2,1)S(1)}, u32[]{:S(2)}, u32[]{:S(2)}) collective-permute-start(bf16[4,16,1536]{2,1,0:T(8,128)(2,1)S(1)} %get-tuple-element.35), channel_id=1, source_target_pairs={{0,8},{4,12},{8,0},{12,4},{1,9},{5,13},{9,1},{13,5},{2,10},{6,14},... | collective-permute-start | bytes 589832 | tf_op jit(solution)/shard_map/ppermute | solution.py:24
  10.7 15.2 %collective-permute-start.7 = (bf16[4,16,1536]{2,1,0:T(8,128)(2,1)S(1)}, bf16[4,16,1536]{2,1,0:T(8,128)(2,1)S(1)}, u32[]{:S(2)}, u32[]{:S(2)}) collective-permute-start(bf16[4,16,1536]{2,1,0:T(8,128)(2,1)S(1)} %get-tuple-element.36), channel_id=1, source_target_pairs={{0,12},{4,8},{8,4},{12,0},{1,13},{5,9},{9,5},{13,1},{2,14},{6,10},... | collective-permute-start | bytes 589832 | tf_op jit(solution)/shard_map/ppermute | solution.py:24
  11.8 18.4 %collective-permute-start = (bf16[4,32,1536]{2,1,0:T(8,128)(2,1)S(1)}, bf16[4,32,1536]{2,1,0:T(8,128)(2,1)S(1)}, u32[]{:S(2)}, u32[]{:S(2)}) collective-permute-start(bf16[4,32,1536]{2,1,0:T(8,128)(2,1)S(1)} %get-tuple-element.31), channel_id=1, source_target_pairs={{0,4},{4,0},{8,12},{12,8},{1,5},{5,1},{9,13},{13,9},{2,6},{6,2},{1... | collective-permute-start | bytes 1179656 | tf_op jit(solution)/shard_map/ppermute | solution.py:24
  21.6 9.4 %collective-permute-start.18 = (bf16[96,1536]{1,0:T(8,128)(2,1)S(1)}, bf16[96,1536]{1,0:T(8,128)(2,1)S(1)}, u32[]{:S(2)}, u32[]{:S(2)}) collective-permute-start(bf16[96,1536]{1,0:T(8,128)(2,1)S(1)} %collective-permute-done.17.own_ref), channel_id=1, source_target_pairs={{0,16},{16,0},{1,17},{17,1},{2,18},{18,2},{3,19},{19,3},{4,20},{20... | collective-permute-start | bytes 884744 | tf_op jit(solution)/shard_map/ppermute | solution.py:24
  24.5 10.4 %copy-start.7 = (s32[1,32,64]{2,1,0:T(8,128)S(1)}, s32[1,32,64]{2,1,0:T(8,128)}, u32[]{:S(2)}) copy-start(s32[1,32,64]{2,1,0:T(8,128)} %param.8) | copy-start | bytes 24580
  24.5 5.7 %collective-permute-start.3 = (bf16[4,16,1536]{2,1,0:T(8,128)(2,1)S(1)}, bf16[4,16,1536]{2,1,0:T(8,128)(2,1)S(1)}, u32[]{:S(2)}, u32[]{:S(2)}) collective-permute-start(bf16[4,16,1536]{2,1,0:T(8,128)(2,1)S(1)} %get-tuple-element.32.refs_0_), channel_id=1, source_target_pairs={{0,2},{1,3},{2,0},{3,1},{4,6},{5,7},{6,4},{7,5},{8,10},{9,11},{10,... | collective-permute-start | bytes 589832 | tf_op jit(solution)/shard_map/ppermute | solution.py:24
  26.0 7.7 %collective-permute-start.10 = (bf16[4,32,1536]{2,1,0:T(8,128)(2,1)S(1)}, bf16[4,32,1536]{2,1,0:T(8,128)(2,1)S(1)}, u32[]{:S(2)}, u32[]{:S(2)}) collective-permute-start(bf16[4,32,1536]{2,1,0:T(8,128)(2,1)S(1)} %slice.4.refs_0_), channel_id=1, source_target_pairs={{0,1},{1,0},{2,3},{3,2},{4,5},{5,4},{6,7},{7,6},{8,9},{9,8},{10,11... | collective-permute-start | bytes 1179656 | tf_op jit(solution)/shard_map/ppermute | solution.py:24
  26.0 8.4 %collective-permute-start.12 = (bf16[4,32,1536]{2,1,0:T(8,128)(2,1)S(1)}, bf16[4,32,1536]{2,1,0:T(8,128)(2,1)S(1)}, u32[]{:S(2)}, u32[]{:S(2)}) collective-permute-start(bf16[4,32,1536]{2,1,0:T(8,128)(2,1)S(1)} %collective-permute-done.11.refs_2_), channel_id=1, source_target_pairs={{0,1},{1,0},{2,3},{3,2},{4,5},{5,4},{6,7},{7,6},{8,9},{9,8},{10,11... | collective-permute-start | bytes 1179656 | tf_op jit(solution)/shard_map/ppermute | solution.py:24
  30.2 2.9 %collective-permute-start.2 = (bf16[4,16,1536]{2,1,0:T(8,128)(2,1)S(1)}, bf16[4,16,1536]{2,1,0:T(8,128)(2,1)S(1)}, u32[]{:S(2)}, u32[]{:S(2)}) collective-permute-start(bf16[4,16,1536]{2,1,0:T(8,128)(2,1)S(1)} %get-tuple-element.32.refs_0_), channel_id=1, source_target_pairs={{0,1},{1,0},{2,3},{3,2},{4,5},{5,4},{6,7},{7,6},{8,9},{9,8},{10,11... | collective-permute-start | bytes 589832 | tf_op jit(solution)/shard_map/ppermute | solution.py:24
  30.2 4.2 %collective-permute-start.4 = (bf16[4,16,1536]{2,1,0:T(8,128)(2,1)S(1)}, bf16[4,16,1536]{2,1,0:T(8,128)(2,1)S(1)}, u32[]{:S(2)}, u32[]{:S(2)}) collective-permute-start(bf16[4,16,1536]{2,1,0:T(8,128)(2,1)S(1)} %collective-permute-done.3.refs_2_), channel_id=1, source_target_pairs={{0,1},{1,0},{2,3},{3,2},{4,5},{5,4},{6,7},{7,6},{8,9},{9,8},{10,11... | collective-permute-start | bytes 589832 | tf_op jit(solution)/shard_map/ppermute | solution.py:24
  31.0 12.1 %collective-permute-start.13 = (bf16[128,1536]{1,0:T(8,128)(2,1)S(1)}, bf16[128,1536]{1,0:T(8,128)(2,1)S(1)}, u32[]{:S(2)}, u32[]{:S(2)}) collective-permute-start(bf16[128,1536]{1,0:T(8,128)(2,1)S(1)} %shard_map.73.refs_0_), channel_id=1, source_target_pairs={{0,2},{1,3},{2,0},{3,1},{4,6},{5,7},{6,4},{7,5},{8,10},{9,11},{10,... | collective-permute-start | bytes 1179656 | tf_op jit(solution)/shard_map/ppermute | solution.py:24
  33.1 21.7 %collective-permute-start.9 = (bf16[192,1536]{1,0:T(8,128)(2,1)S(1)}, bf16[192,1536]{1,0:T(8,128)(2,1)S(1)}, u32[]{:S(2)}, u32[]{:S(2)}) collective-permute-start(bf16[192,1536]{1,0:T(8,128)(2,1)S(1)} %shard_map.76.refs_0_), channel_id=1, source_target_pairs={{0,2},{1,3},{2,0},{3,1},{4,6},{5,7},{6,4},{7,5},{8,10},{9,11},{10,... | collective-permute-start | bytes 1769480 | tf_op jit(solution)/shard_map/ppermute | solution.py:24
  33.7 21.1 %collective-permute-start.19 = (bf16[192,1536]{1,0:T(8,128)(2,1)S(1)}, bf16[192,1536]{1,0:T(8,128)(2,1)S(1)}, u32[]{:S(2)}, u32[]{:S(2)}) collective-permute-start(bf16[192,1536]{1,0:T(8,128)(2,1)S(1)} %shard_map.85.own_ref), channel_id=1, source_target_pairs={{0,4},{4,0},{8,12},{12,8},{1,5},{5,1},{9,13},{13,9},{2,6},{6,2},{1... | collective-permute-start | bytes 1769480 | tf_op jit(solution)/shard_map/ppermute | solution.py:24
  34.3 21.1 %collective-permute-start.8 = (bf16[192,1536]{1,0:T(8,128)(2,1)S(1)}, bf16[192,1536]{1,0:T(8,128)(2,1)S(1)}, u32[]{:S(2)}, u32[]{:S(2)}) collective-permute-start(bf16[192,1536]{1,0:T(8,128)(2,1)S(1)} %shard_map.76.refs_0_), channel_id=1, source_target_pairs={{0,1},{1,0},{2,3},{3,2},{4,5},{5,4},{6,7},{7,6},{8,9},{9,8},{10,11... | collective-permute-start | bytes 1769480 | tf_op jit(solution)/shard_map/ppermute | solution.py:24
  34.4 12.1 %collective-permute-start.1 = (bf16[128,1536]{1,0:T(8,128)(2,1)S(1)}, bf16[128,1536]{1,0:T(8,128)(2,1)S(1)}, u32[]{:S(2)}, u32[]{:S(2)}) collective-permute-start(bf16[128,1536]{1,0:T(8,128)(2,1)S(1)} %shard_map.73.refs_0_), channel_id=1, source_target_pairs={{0,1},{1,0},{2,3},{3,2},{4,5},{5,4},{6,7},{7,6},{8,9},{9,8},{10,11... | collective-permute-start | bytes 1179656 | tf_op jit(solution)/shard_map/ppermute | solution.py:24
  43.1 14.1 %collective-permute-start.14 = (bf16[128,1536]{1,0:T(8,128)(2,1)S(1)}, bf16[128,1536]{1,0:T(8,128)(2,1)S(1)}, u32[]{:S(2)}, u32[]{:S(2)}) collective-permute-start(bf16[128,1536]{1,0:T(8,128)(2,1)S(1)} %collective-permute-done.13.refs_0_), channel_id=1, source_target_pairs={{0,1},{1,0},{2,3},{3,2},{4,5},{5,4},{6,7},{7,6},{8,9},{9,8},{10,11... | collective-permute-start | bytes 1179656 | tf_op jit(solution)/shard_map/ppermute | solution.py:24
  44.2 2.2 %copy-start.4 = (bf16[384,1536]{1,0:T(8,128)(2,1)S(1)}, bf16[384,1536]{1,0:T(8,128)(2,1)}, u32[]{:S(2)}) copy-start(bf16[384,1536]{1,0:T(8,128)(2,1)} %refs_3_.5) | copy-start | bytes 3538948
  46.4 29.2 %collective-permute-start.24 = (bf16[384,1536]{1,0:T(8,128)(2,1)S(1)}, bf16[384,1536]{1,0:T(8,128)(2,1)S(1)}, u32[]{:S(2)}, u32[]{:S(2)}) collective-permute-start(bf16[384,1536]{1,0:T(8,128)(2,1)S(1)} %copy-done.4), channel_id=1, source_target_pairs={{0,1},{1,0},{2,3},{3,2},{4,5},{5,4},{6,7},{7,6},{8,9},{9,8},{10,11... | collective-permute-start | bytes 3538952 | tf_op jit(solution)/shard_map/ppermute | solution.py:24
  54.8 11.8 %collective-permute-start.15 = (bf16[192,1536]{1,0:T(8,128)(2,1)S(1)}, bf16[192,1536]{1,0:T(8,128)(2,1)S(1)}, u32[]{:S(2)}, u32[]{:S(2)}) collective-permute-start(bf16[192,1536]{1,0:T(8,128)(2,1)S(1)} %collective-permute-done.9.refs_0_), channel_id=1, source_target_pairs={{0,1},{1,0},{2,3},{3,2},{4,5},{5,4},{6,7},{7,6},{8,9},{9,8},{10,11... | collective-permute-start | bytes 1769480 | tf_op jit(solution)/shard_map/ppermute | solution.py:24
  54.9 22.7 %collective-permute-start.20 = (bf16[384,1536]{1,0:T(8,128)(2,1)S(1)}, bf16[384,1536]{1,0:T(8,128)(2,1)S(1)}, u32[]{:S(2)}, u32[]{:S(2)}) collective-permute-start(bf16[384,1536]{1,0:T(8,128)(2,1)S(1)} %shard_map.86.refs_6_.refs_5_), channel_id=1, source_target_pairs={{0,1},{1,0},{2,3},{3,2},{4,5},{5,4},{6,7},{7,6},{8,9},{9,8},{10,11... | collective-permute-start | bytes 3538952 | tf_op jit(solution)/shard_map/ppermute | solution.py:24
  57.2 1.2 %copy-start.8 = (f32[4]{0:T(128)S(1)}, f32[4]{0:T(128)}, u32[]{:S(2)}) copy-start(f32[4]{0:T(128)} %refs_5_.9) | copy-start | bytes 52
  64.9 11.1 %collective-permute-start.21 = (bf16[1,256,384]{2,1,0:T(8,128)(2,1)S(1)}, bf16[1,256,384]{2,1,0:T(8,128)(2,1)S(1)}, u32[]{:S(2)}, u32[]{:S(2)}) collective-permute-start(bf16[1,256,384]{2,1,0:T(8,128)(2,1)S(1)} %get-tuple-element.42), channel_id=1, source_target_pairs={{0,1},{1,0},{2,3},{3,2},{4,5},{5,4},{6,7},{7,6},{8,9},{9,8},{10,11... | collective-permute-start | bytes 589832 | tf_op jit(solution)/shard_map/ppermute | solution.py:24
  65.0 12.5 %collective-permute-start.22 = (bf16[1,256,384]{2,1,0:T(8,128)(2,1)S(1)}, bf16[1,256,384]{2,1,0:T(8,128)(2,1)S(1)}, u32[]{:S(2)}, u32[]{:S(2)}) collective-permute-start(bf16[1,256,384]{2,1,0:T(8,128)(2,1)S(1)} %get-tuple-element.43), channel_id=1, source_target_pairs={{0,2},{1,3},{2,0},{3,1},{4,6},{5,7},{6,4},{7,5},{8,10},{9,11},{10,... | collective-permute-start | bytes 589832 | tf_op jit(solution)/shard_map/ppermute | solution.py:24
  66.5 11.0 %collective-permute-start.23 = (bf16[1,256,384]{2,1,0:T(8,128)(2,1)S(1)}, bf16[1,256,384]{2,1,0:T(8,128)(2,1)S(1)}, u32[]{:S(2)}, u32[]{:S(2)}) collective-permute-start(bf16[1,256,384]{2,1,0:T(8,128)(2,1)S(1)} %get-tuple-element.44), channel_id=1, source_target_pairs={{0,3},{1,2},{2,1},{3,0},{4,7},{5,6},{6,5},{7,4},{8,11},{9,10},{10,... | collective-permute-start | bytes 589832 | tf_op jit(solution)/shard_map/ppermute | solution.py:24
  75.6 3.3 %collective-permute-start.25 = (bf16[1,256,384]{2,1,0:T(8,128)(2,1)S(1)}, bf16[1,256,384]{2,1,0:T(8,128)(2,1)S(1)}, u32[]{:S(2)}, u32[]{:S(2)}) collective-permute-start(bf16[1,256,384]{2,1,0:T(8,128)(2,1)S(1)} %get-tuple-element.52), channel_id=1, source_target_pairs={{0,1},{1,0},{2,3},{3,2},{4,5},{5,4},{6,7},{7,6},{8,9},{9,8},{10,11... | collective-permute-start | bytes 589832 | tf_op jit(solution)/shard_map/ppermute | solution.py:24
  76.0 7.8 %collective-permute-start.26 = (bf16[1,256,384]{2,1,0:T(8,128)(2,1)S(1)}, bf16[1,256,384]{2,1,0:T(8,128)(2,1)S(1)}, u32[]{:S(2)}, u32[]{:S(2)}) collective-permute-start(bf16[1,256,384]{2,1,0:T(8,128)(2,1)S(1)} %get-tuple-element.49), channel_id=1, source_target_pairs={{0,2},{1,3},{2,0},{3,1},{4,6},{5,7},{6,4},{7,5},{8,10},{9,11},{10,... | collective-permute-start | bytes 589832 | tf_op jit(solution)/shard_map/ppermute | solution.py:24
  77.5 8.9 %collective-permute-start.16 = (bf16[1,256,384]{2,1,0:T(8,128)(2,1)S(1)}, bf16[1,256,384]{2,1,0:T(8,128)(2,1)S(1)}, u32[]{:S(2)}, u32[]{:S(2)}) collective-permute-start(bf16[1,256,384]{2,1,0:T(8,128)(2,1)S(1)} %get-tuple-element.48), channel_id=1, source_target_pairs={{0,3},{1,2},{2,1},{3,0},{4,7},{5,6},{6,5},{7,4},{8,11},{9,10},{10,... | collective-permute-start | bytes 589832 | tf_op jit(solution)/shard_map/ppermute | solution.py:24

commit v11 on v9

--- a/solution.py
+++ b/solution.py
@@ -304,24 +304,29 @@
     return jnp.dot(rows, depth, preferred_element_type=F32)
 
 
-def partial_kernel(count, *refs):
-    *refs, out_ref = refs
-    out_ref[...] = product(refs[:count], refs[count:])
-
-
-def partial(attended, weights):
+def partial_kernel(count, spans, *refs):
+    attended, weights, sources, out_ref = refs[:count], refs[count : 2 * count], refs[2 * count : -1], refs[-1]
+    total = product(attended, weights)
+    at = 0
+    for which, row, start, pixels in spans:
+        held = sources[which][row, start : start + pixels, :].astype(F32)
+        out_ref[at : at + pixels, :] = held + total[at : at + pixels]
+        at += pixels
+
+
+def partial(attended, weights, sources, spans):
     pixels, depth = attended[0].shape
     width = weights[0].shape[1]
     return pl.pallas_call(
-        functools.partial(partial_kernel, len(weights)),
+        functools.partial(partial_kernel, len(weights), spans),
         out_shape=jax.ShapeDtypeStruct((pixels, width), F32),
-        in_specs=[VMEM] * (2 * len(weights)),
+        in_specs=[VMEM] * (2 * len(weights) + len(sources)),
         out_specs=VMEM,
         compiler_params=pltpu.CompilerParams(vmem_limit_bytes=20 << 20),
         cost_estimate=pl.CostEstimate(
             flops=2 * pixels * width * depth * len(weights), bytes_accessed=2 * width * (depth + 2 * pixels), transcendentals=0
         ),
-    )(*attended, *weights)
+    )(*attended, *weights, *sources)
 
 
 def finish_kernel(count, spans, *refs):
@@ -351,7 +356,7 @@
 
 def last_kernel(count, chunks, spans, *refs):
     attended, weights = refs[:count], refs[count : 2 * count]
-    base_ref, done_ref, *sources, out_ref, ready, semaphore = refs[2 * count :]
+    base_ref, done_ref, out_ref, ready, semaphore = refs[2 * count :]
     left, size, width = done_ref.shape[1], ready.shape[1], ready.shape[2]
     wide = width // chunks
     copies = [
@@ -360,13 +365,10 @@
     copies[0].start()
     for chunk in range(chunks):
         columns = slice(chunk * wide, (chunk + 1) * wide)
-        total = product(attended, weights, columns) + base_ref[:, columns]
+        total = (product(attended, weights, columns) + base_ref[:, columns]).astype(BF16)
         at = 0
-        for which, row, start, pixels, into, column in spans:
-            held = sources[which][row, start : start + pixels, columns].astype(F32)
-            ready[into, column - left : column - left + pixels, columns] = (
-                held + total[at : at + pixels]
-            ).astype(BF16)
+        for pixels, into, column in spans:
+            ready[into, column - left : column - left + pixels, columns] = total[at : at + pixels]
             at += pixels
         place = pl.ds(chunk * wide, wide)
         copy = pltpu.make_async_copy(
@@ -378,15 +380,15 @@
         copy.wait()
 
 
-def finish_last(attended, weights, base, done, sources, spans, shape):
+def finish_last(attended, weights, base, done, spans, shape):
     count = len(weights)
     row_count, col_count, width = shape
     pixels, depth = attended[0].shape
-    chunks = 3 if width % (3 * 2 * LANE) == 0 else 1
+    chunks = 1
     return pl.pallas_call(
         functools.partial(last_kernel, count, chunks, spans),
         out_shape=jax.ShapeDtypeStruct(shape, BF16),
-        in_specs=[VMEM] * (2 * count + 2 + len(sources)),
+        in_specs=[VMEM] * (2 * count + 2),
         out_specs=HELD,
         scratch_shapes=[
             pltpu.VMEM((row_count, col_count - done.shape[1], width), BF16),
@@ -396,7 +398,7 @@
         cost_estimate=pl.CostEstimate(
             flops=2 * pixels * width * depth * count, bytes_accessed=2 * width * (width + 3 * pixels), transcendentals=0
         ),
-    )(*attended, *weights, base, done, *sources)
+    )(*attended, *weights, base, done)
 
 
 def send_heads(outs):
@@ -501,15 +503,15 @@
     weights = triple_projection_matrix
     scales = logit_scaling_per_part
 
+    local_0 = blocked[rows:, half : half + WS]
     boxes = [
-        (rows, half, WS),
         (rows, half + WS, near),
         (0, half, WS),
         (0, half + WS, near),
         (rows, 0, half),
         (0, 0, half),
     ]
-    local_0, local_1, south_0, south_1, east, corner = cut(blocked, rows, boxes)
+    local_1, south_0, south_1, east, corner = cut(blocked, rows, boxes)
     south_0 = exchange(south_0, 1, "win")
     south_1 = exchange(south_1, 1, "win")
     east = permute_by(east, "win", west)
@@ -560,12 +562,14 @@
     shape = (row_count, col_count, width)
     done = finish(first, out_weights, [blocked, south_0], spans, (row_count, WS, width))
     second[0] = after(second[0], done)
-    base = partial(second[:-1], out_weights[:-1])
     spans = [(0, rows + row, half + WS, near, row, WS) for row in range(rows)]
     spans += [(1, row, 0, near, rows + row, WS) for row in range(rows)]
     spans += [(2, row, 0, half, row, WS + near) for row in range(rows)]
     spans += [(3, row, 0, half, rows + row, WS + near) for row in range(rows)]
-    mixed = finish_last(second[-1:], out_weights[-1:], base, done, [blocked, south_1, east, corner], spans, shape)
+    sources = [blocked, south_1, east, corner]
+    base = partial(second[:-1], out_weights[:-1], sources, [span[:4] for span in spans])
+    spans = [span[3:] for span in spans]
+    mixed = finish_last(second[-1:], out_weights[-1:], base, done, spans, shape)
     return mixed[None, :, None]
 
 

time: 84.2 us -> 84 us (level)
  waiting for transfers between devices: 25.3 us -> 23.9 us
  local copies, waits for them, and re-layouts: 1.44 us -> 2.73 us
    ppermute x27, waiting for transfers between devices: 25.3 us -> 23.9 us  [permute_by(): return lax.ppermute(value, axis, pairs)]
    unnamed x16 -> x18, local copies, waits for them, and re-layouts: 1.44 us -> 2.71 us
  transfers between devices with their start and end apart: 27 -> 27, of which waited for: 9 -> 9; matrix products, arithmetic and copies ran while one was open for 0% -> 0% of each run, Pallas kernels for 33% -> 34%
where the time goes in v11:
time: 84 us; the launch traced here: 83.7 us
  Pallas kernels  29.6 us (35%)
  starting transfers between devices  27 us (32%)
  waiting for transfers between devices  23.9 us (28%)
  local copies, waits for them, and re-layouts  2.73 us (3%)
    ppermute x27, starting transfers between devices, permute_by(): return lax.ppermute(value, axis, pairs)  27 us
    ppermute x27, waiting for transfers between devices, permute_by(): return lax.ppermute(value, axis, pairs)  23.9 us
    pallas_call x3, Pallas kernels, attend(): pl.pallas_call(functools.partial(attend_kernel, layout, ranges, head_widt...  13.5 us
    pallas_call x5, Pallas kernels, project(): pl.pallas_call(functools.partial(project_kernel, [len(group) for group in...  8.99 us
    unnamed x18, local copies, waits for them, and re-layouts  2.71 us
    pallas_call x4, Pallas kernels, norm(): pl.pallas_call(functools.partial(norm_kernel, groups), out_shape=[jax.Sha...  2.43 us
  transfers between devices with their start and end apart: 27, of which 9 were waited for; matrix products, arithmetic and copies ran while one was open for 0% of the time, Pallas kernels for 34%

profile of v11, /device:TPU:0, one launch (start us, length us, event | category | flops | bytes accessed | tf_op | source)
XLA Modules:
  0.0 83.7 jit_solution(9450682615093136386)
XLA Ops:
  0.0 1.4 %copy-done.1 = bf16[1,8,1,64,1536]{4,3,2,1,0:T(8,128)(2,1)S(1)} copy-done((bf16[1,8,1,64,1536]{4,3,2,1,0:T(8,128)(2,1)S(1)}, bf16[1,8,1,64,1536]{4,3,2,1,0:T(8,128)(2,1)}, u32[]{:S(2)}) %copy-start.1) | copy-done | bytes 1572888
  1.5 3.1 %collective-permute-start = (bf16[4,32,1536]{2,1,0:T(8,128)(2,1)S(1)}, bf16[4,32,1536]{2,1,0:T(8,128)(2,1)S(1)}, u32[]{:S(2)}, u32[]{:S(2)}) collective-permute-start(bf16[4,32,1536]{2,1,0:T(8,128)(2,1)S(1)} %get-tuple-element.29), channel_id=1, source_target_pairs={{0,4},{4,0},{8,12},{12,8},{1,5},{5,1},{9,13},{13,9},{2,6},{6,2},{1... | collective-permute-start | bytes 1179656 | tf_op jit(solution)/shard_map/ppermute | solution.py:24
  4.6 1.5 %collective-permute-start.3 = (bf16[4,16,1536]{2,1,0:T(8,128)(2,1)S(1)}, bf16[4,16,1536]{2,1,0:T(8,128)(2,1)S(1)}, u32[]{:S(2)}, u32[]{:S(2)}) collective-permute-start(bf16[4,16,1536]{2,1,0:T(8,128)(2,1)S(1)} %get-tuple-element.30.refs_0_), channel_id=1, source_target_pairs={{0,2},{1,3},{2,0},{3,1},{4,6},{5,7},{6,4},{7,5},{8,10},{9,11},{10,... | collective-permute-start | bytes 589832 | tf_op jit(solution)/shard_map/ppermute | solution.py:24
  6.1 1.3 %copy-done.3 = bf16[384,1536]{1,0:T(8,128)(2,1)S(1)} copy-done((bf16[384,1536]{1,0:T(8,128)(2,1)S(1)}, bf16[384,1536]{1,0:T(8,128)(2,1)}, u32[]{:S(2)}) %copy-start.3) | copy-done | bytes 1179672
  7.4 0.6 collective-permute-start.17
  8.0 0.1 collective-permute-start.5
  8.2 1.9 %collective-permute-start.11 = (bf16[4,32,1536]{2,1,0:T(8,128)(2,1)S(1)}, bf16[4,32,1536]{2,1,0:T(8,128)(2,1)S(1)}, u32[]{:S(2)}, u32[]{:S(2)}) collective-permute-start(bf16[4,32,1536]{2,1,0:T(8,128)(2,1)S(1)} %slice.4.refs_0_), channel_id=1, source_target_pairs={{0,2},{1,3},{2,0},{3,1},{4,6},{5,7},{6,4},{7,5},{8,10},{9,11},{10,... | collective-permute-start | bytes 1179656 | tf_op jit(solution)/shard_map/ppermute | solution.py:24
  10.1 2.3 %collective-permute-done.3.refs_2_ = bf16[4,16,1536]{2,1,0:T(8,128)(2,1)S(1)} collective-permute-done((bf16[4,16,1536]{2,1,0:T(8,128)(2,1)S(1)}, bf16[4,16,1536]{2,1,0:T(8,128)(2,1)S(1)}, u32[]{:S(2)}, u32[]{:S(2)}) %collective-permute-start.3) | collective-permute-done | bytes 196640 | tf_op jit(solution)/shard_map/ppermute | solution.py:24
  12.4 2.6 %collective-permute-start.6 = (bf16[4,16,1536]{2,1,0:T(8,128)(2,1)S(1)}, bf16[4,16,1536]{2,1,0:T(8,128)(2,1)S(1)}, u32[]{:S(2)}, u32[]{:S(2)}) collective-permute-start(bf16[4,16,1536]{2,1,0:T(8,128)(2,1)S(1)} %get-tuple-element.33), channel_id=1, source_target_pairs={{0,8},{4,12},{8,0},{12,4},{1,9},{5,13},{9,1},{13,5},{2,10},{6,14},... | collective-permute-start | bytes 589832 | tf_op jit(solution)/shard_map/ppermute | solution.py:24
  15.0 3.7 %collective-permute-done.17.own_ref = bf16[96,1536]{1,0:T(8,128)(2,1)S(1)} collective-permute-done((bf16[96,1536]{1,0:T(8,128)(2,1)S(1)}, bf16[96,1536]{1,0:T(8,128)(2,1)S(1)}, u32[]{:S(2)}, u32[]{:S(2)}) %collective-permute-start.17) | collective-permute-done | bytes 294944 | tf_op jit(solution)/shard_map/ppermute | solution.py:24
  18.7 1.5 %collective-permute-start.18 = (bf16[96,1536]{1,0:T(8,128)(2,1)S(1)}, bf16[96,1536]{1,0:T(8,128)(2,1)S(1)}, u32[]{:S(2)}, u32[]{:S(2)}) collective-permute-start(bf16[96,1536]{1,0:T(8,128)(2,1)S(1)} %collective-permute-done.17.own_ref), channel_id=1, source_target_pairs={{0,16},{16,0},{1,17},{17,1},{2,18},{18,2},{3,19},{19,3},{4,20},{20... | collective-permute-start | bytes 884744 | tf_op jit(solution)/shard_map/ppermute | solution.py:24
  20.2 1.9 %collective-permute-done.5.refs_0_.refs_7_ = bf16[4,16,1536]{2,1,0:T(8,128)(2,1)S(1)} collective-permute-done((bf16[4,16,1536]{2,1,0:T(8,128)(2,1)S(1)}, bf16[4,16,1536]{2,1,0:T(8,128)(2,1)S(1)}, u32[]{:S(2)}, u32[]{:S(2)}) %collective-permute-start.5) | collective-permute-done | bytes 196640 | tf_op jit(solution)/shard_map/ppermute | solution.py:24
  22.2 3.8 %collective-permute-start.7 = (bf16[4,16,1536]{2,1,0:T(8,128)(2,1)S(1)}, bf16[4,16,1536]{2,1,0:T(8,128)(2,1)S(1)}, u32[]{:S(2)}, u32[]{:S(2)}) collective-permute-start(bf16[4,16,1536]{2,1,0:T(8,128)(2,1)S(1)} %get-tuple-element.34), channel_id=1, source_target_pairs={{0,12},{4,8},{8,4},{12,0},{1,13},{5,9},{9,5},{13,1},{2,14},{6,10},... | collective-permute-start | bytes 589832 | tf_op jit(solution)/shard_map/ppermute | solution.py:24
  25.9 0.3 shard_map.73.refs_0_
  26.3 1.6 %collective-permute-start.13 = (bf16[128,1536]{1,0:T(8,128)(2,1)S(1)}, bf16[128,1536]{1,0:T(8,128)(2,1)S(1)}, u32[]{:S(2)}, u32[]{:S(2)}) collective-permute-start(bf16[128,1536]{1,0:T(8,128)(2,1)S(1)} %shard_map.73.refs_0_), channel_id=1, source_target_pairs={{0,2},{1,3},{2,0},{3,1},{4,6},{5,7},{6,4},{7,5},{8,10},{9,11},{10,... | collective-permute-start | bytes 1179656 | tf_op jit(solution)/shard_map/ppermute | solution.py:24
  27.8 2.3 %collective-permute-done.7.refs_2_.refs_9_ = bf16[4,16,1536]{2,1,0:T(8,128)(2,1)S(1)} collective-permute-done((bf16[4,16,1536]{2,1,0:T(8,128)(2,1)S(1)}, bf16[4,16,1536]{2,1,0:T(8,128)(2,1)S(1)}, u32[]{:S(2)}, u32[]{:S(2)}) %collective-permute-start.7) | collective-permute-done | bytes 196640 | tf_op jit(solution)/shard_map/ppermute | solution.py:24
  30.1 0.5 collective-permute-start.4
  30.7 0.4 shard_map.76.refs_0_
  31.2 0.4 collective-permute-done.2.refs_1_
  31.6 1.4 %collective-permute-start.9 = (bf16[192,1536]{1,0:T(8,128)(2,1)S(1)}, bf16[192,1536]{1,0:T(8,128)(2,1)S(1)}, u32[]{:S(2)}, u32[]{:S(2)}) collective-permute-start(bf16[192,1536]{1,0:T(8,128)(2,1)S(1)} %shard_map.76.refs_0_), channel_id=1, source_target_pairs={{0,2},{1,3},{2,0},{3,1},{4,6},{5,7},{6,4},{7,5},{8,10},{9,11},{10,... | collective-permute-start | bytes 1769480 | tf_op jit(solution)/shard_map/ppermute | solution.py:24
  33.0 3.3 %collective-permute-start.19 = (bf16[192,1536]{1,0:T(8,128)(2,1)S(1)}, bf16[192,1536]{1,0:T(8,128)(2,1)S(1)}, u32[]{:S(2)}, u32[]{:S(2)}) collective-permute-start(bf16[192,1536]{1,0:T(8,128)(2,1)S(1)} %shard_map.85.own_ref), channel_id=1, source_target_pairs={{0,4},{4,0},{8,12},{12,8},{1,5},{5,1},{9,13},{13,9},{2,6},{6,2},{1... | collective-permute-start | bytes 1769480 | tf_op jit(solution)/shard_map/ppermute | solution.py:24
  36.3 2.1 %collective-permute-done.13.refs_0_ = bf16[128,1536]{1,0:T(8,128)(2,1)S(1)} collective-permute-done((bf16[128,1536]{1,0:T(8,128)(2,1)S(1)}, bf16[128,1536]{1,0:T(8,128)(2,1)S(1)}, u32[]{:S(2)}, u32[]{:S(2)}) %collective-permute-start.13) | collective-permute-done | bytes 393248 | tf_op jit(solution)/shard_map/ppermute | solution.py:24
  38.3 0.4 tags.1
  38.7 0.6 shard_map.74.refs_2_
  39.3 0.6 collective-permute-start.14
  39.9 1.1 %shard_map.78.refs_0_ = bf16[512,1536]{1,0:T(8,128)(2,1)S(1)} custom-call(bf16[4,32,1536]{2,1,0:T(8,128)(2,1)S(1)} %slice.4.refs_0_, bf16[4,32,1536]{2,1,0:T(8,128)(2,1)S(1)} %collective-permute-done.10.refs_1_, bf16[4,32,1536]{2,1,0:T(8,128)(2,1)S(1)} %collective-permute-done.11.refs_2_, bf16[4,32,1536]{2,1,0:T(8,128)(2,1)S(1)} %collective-permute-done.12.refs_3_, ...), custom_call_target="tpu_custom_call" | custom-call | flops 7864320 | bytes 3145728 | tf_op jit(solution)/shard_map/pallas_call | solution.py:102
  41.0 2.2 %shard_map.79.refs_0_ = bf16[512,1152]{1,0:T(8,128)(2,1)S(1)} custom-call(bf16[512,1536]{1,0:T(8,128)(2,1)S(1)} %shard_map.78.refs_0_, bf16[3,1536,384]{2,1,0:T(8,128)(2,1)S(1)} %copy-done), custom_call_target="tpu_custom_call" | custom-call | flops 1811939328 | bytes 6291456 | tf_op jit(solution)/shard_map/pallas_call | solution.py:197
  43.2 0.1 collective-permute-start.24
  43.3 2.2 %shard_map.75 = (bf16[256,1152]{1,0:T(8,128)(2,1)S(1)}, bf16[256,1152]{1,0:T(8,128)(2,1)S(1)}) custom-call(bf16[128,1536]{1,0:T(8,128)(2,1)S(1)} %shard_map.73.refs_0_, bf16[128,1536]{1,0:T(8,128)(2,1)S(1)} %collective-permute-done.1.refs_1_, bf16[256,1536]{1,0:T(8,128)(2,1)S(1)} %shard_map.74.refs_2_, bf16[3,1536,384]{2,1,0:T(8,128)(2,1)S(1)} %copy-done), custom_call_target="tpu_custom_call" | custom-call | flops 1811939328 | bytes 6291456 | tf_op jit(solution)/shard_map/pallas_call | solution.py:197
  45.5 5.0 %collective-permute-done.9.refs_0_ = bf16[192,1536]{1,0:T(8,128)(2,1)S(1)} collective-permute-done((bf16[192,1536]{1,0:T(8,128)(2,1)S(1)}, bf16[192,1536]{1,0:T(8,128)(2,1)S(1)}, u32[]{:S(2)}, u32[]{:S(2)}) %collective-permute-start.9) | collective-permute-done | bytes 589856 | tf_op jit(solution)/shard_map/ppermute | solution.py:24
  50.5 0.1 shard_map.86.refs_6_.refs_5_
  50.6 0.6 collective-permute-start.20
  51.2 1.7 %shard_map.77.refs_1_ = bf16[384,1152]{1,0:T(8,128)(2,1)S(1)} custom-call(bf16[192,1536]{1,0:T(8,128)(2,1)S(1)} %shard_map.76.refs_0_, bf16[192,1536]{1,0:T(8,128)(2,1)S(1)} %collective-permute-done.8.refs_1_, bf16[3,1536,384]{2,1,0:T(8,128)(2,1)S(1)} %copy-done), custom_call_target="tpu_custom_call" | custom-call | flops 1358954496 | bytes 5603328 | tf_op jit(solution)/shard_map/pallas_call | solution.py:197
  52.9 1.2 %shard_map.80.refs_2_ = bf16[256,1152]{1,0:T(8,128)(2,1)S(1)} custom-call(bf16[128,1536]{1,0:T(8,128)(2,1)S(1)} %collective-permute-done.13.refs_0_, bf16[128,1536]{1,0:T(8,128)(2,1)S(1)} %collective-permute-done.14.refs_1_, bf16[3,1536,384]{2,1,0:T(8,128)(2,1)S(1)} %copy-done), custom_call_target="tpu_custom_call" | custom-call | flops 905969664 | bytes 4915200 | tf_op jit(solution)/shard_map/pallas_call | solution.py:197
  54.1 6.5 %shard_map.81 = (bf16[1,256,384]{2,1,0:T(8,128)(2,1)S(1)}, bf16[1,256,384]{2,1,0:T(8,128)(2,1)S(1)}, bf16[1,256,384]{2,1,0:T(8,128)(2,1)S(1)}, bf16[1,256,384]{2,1,0:T(8,128)(2,1)S(1)}) custom-call(bf16[512,1152]{1,0:T(8,128)(2,1)S(1)} %shard_map.79.refs_0_, bf16[256,1152]{1,0:T(8,128)(2,1)S(1)} %get-tuple-element.35.refs_1_, ...), custom_call_target="tpu_custom_call" | custom-call | flops 4294967296 | bytes 2359296 | tf_op jit(solution)/shard_map/pallas_call | solution.py:285
  60.6 0.1 collective-permute-start.21
  60.7 1.5 %collective-permute-start.22 = (bf16[1,256,384]{2,1,0:T(8,128)(2,1)S(1)}, bf16[1,256,384]{2,1,0:T(8,128)(2,1)S(1)}, u32[]{:S(2)}, u32[]{:S(2)}) collective-permute-start(bf16[1,256,384]{2,1,0:T(8,128)(2,1)S(1)} %get-tuple-element.41), channel_id=1, source_target_pairs={{0,2},{1,3},{2,0},{3,1},{4,6},{5,7},{6,4},{7,5},{8,10},{9,11},{10,... | collective-permute-start | bytes 589832 | tf_op jit(solution)/shard_map/ppermute | solution.py:24
  62.3 0.3 collective-permute-start.23
  62.6 1.7 %shard_map.82.refs_2_ = bf16[384,1152]{1,0:T(8,128)(2,1)S(1)} custom-call(bf16[192,1536]{1,0:T(8,128)(2,1)S(1)} %collective-permute-done.9.refs_0_, bf16[192,1536]{1,0:T(8,128)(2,1)S(1)} %collective-permute-done.15.refs_1_, bf16[3,1536,384]{2,1,0:T(8,128)(2,1)S(1)} %copy-done), custom_call_target="tpu_custom_call" | custom-call | flops 1358954496 | bytes 5603328 | tf_op jit(solution)/shard_map/pallas_call | solution.py:197
  64.2 3.5 %shard_map.83 = (bf16[1,256,384]{2,1,0:T(8,128)(2,1)S(1)}, bf16[1,256,384]{2,1,0:T(8,128)(2,1)S(1)}) custom-call(bf16[256,1152]{1,0:T(8,128)(2,1)S(1)} %get-tuple-element.48.refs_0_, bf16[384,1152]{1,0:T(8,128)(2,1)S(1)} %shard_map.77.refs_1_, bf16[384,1152]{1,0:T(8,128)(2,1)S(1)} %shard_map.82.refs_2_, bf16[1024,128]{1,0:T(8,128)(2,1)S(1)} %get-tuple-element.44.refs_3_, ...), custom_call_target="tpu_custom_call" | custom-call | flops 2147483648 | bytes 2359296 | tf_op jit(solution)/shard_map/pallas_call | solution.py:285
  67.7 3.5 %shard_map.87 = (bf16[1,256,384]{2,1,0:T(8,128)(2,1)S(1)}, bf16[1,256,384]{2,1,0:T(8,128)(2,1)S(1)}) custom-call(bf16[256,1152]{1,0:T(8,128)(2,1)S(1)} %get-tuple-element.48.refs_0_, bf16[384,1152]{1,0:T(8,128)(2,1)S(1)} %shard_map.77.refs_1_, bf16[384,1152]{1,0:T(8,128)(2,1)S(1)} %shard_map.82.refs_2_, bf16[1024,128]{1,0:T(8,128)(2,1)S(1)} %get-tuple-element.44.refs_3_, ...), custom_call_target="tpu_custom_call" | custom-call | flops 2147483648 | bytes 2359296 | tf_op jit(solution)/shard_map/pallas_call | solution.py:285
  71.3 0.4 collective-permute-start.25
  71.7 1.5 %collective-permute-start.26 = (bf16[1,256,384]{2,1,0:T(8,128)(2,1)S(1)}, bf16[1,256,384]{2,1,0:T(8,128)(2,1)S(1)}, u32[]{:S(2)}, u32[]{:S(2)}) collective-permute-start(bf16[1,256,384]{2,1,0:T(8,128)(2,1)S(1)} %get-tuple-element.47), channel_id=1, source_target_pairs={{0,2},{1,3},{2,0},{3,1},{4,6},{5,7},{6,4},{7,5},{8,10},{9,11},{10,... | collective-permute-start | bytes 589832 | tf_op jit(solution)/shard_map/ppermute | solution.py:24
  73.2 1.4 %shard_map.88.refs_3_ = bf16[8,32,1536]{2,1,0:T(8,128)(2,1)S(1)} custom-call(bf16[256,384]{1,0:T(8,128)(2,1)S(1)} %bitcast.17, bf16[256,384]{1,0:T(8,128)(2,1)S(1)} %bitcast.18, bf16[256,384]{1,0:T(8,128)(2,1)S(1)} %bitcast.19, bf16[256,384]{1,0:T(8,128)(2,1)S(1)} %bitcast.21, bf16[384,1536]{1,0:T(8,128)(2,1)S(1)} %copy-done.4, ...), custom_call_target="tpu_custom_call" | custom-call | flops 1207959552 | bytes 7077888 | tf_op jit(solution)/shard_map/pallas_call | solution.py:345
  74.6 4.9 %collective-permute-done.26 = bf16[1,256,384]{2,1,0:T(8,128)(2,1)S(1)} collective-permute-done((bf16[1,256,384]{2,1,0:T(8,128)(2,1)S(1)}, bf16[1,256,384]{2,1,0:T(8,128)(2,1)S(1)}, u32[]{:S(2)}, u32[]{:S(2)}) %collective-permute-start.26) | collective-permute-done | bytes 196640 | tf_op jit(solution)/shard_map/ppermute | solution.py:24
  79.5 1.2 %shard_map.89.refs_2_ = f32[256,1536]{1,0:T(8,128)S(1)} custom-call(bf16[256,384]{1,0:T(8,128)(2,1)S(1)} %bitcast.20, bf16[256,384]{1,0:T(8,128)(2,1)S(1)} %bitcast.22, bf16[256,384]{1,0:T(8,128)(2,1)S(1)} %bitcast.23, bf16[384,1536]{1,0:T(8,128)(2,1)S(1)} %copy-done.4, bf16[384,1536]{1,0:T(8,128)(2,1)S(1)} %collective-permute-done.24.refs_5_.refs_4_, ...), custom_call_target="tpu_custom_call" | custom-call | flops 905969664 | bytes 2752512 | tf_op jit(solution)/shard_map/pallas_call | solution.py:320
  80.7 1.4 %collective-permute-done.16 = bf16[1,256,384]{2,1,0:T(8,128)(2,1)S(1)} collective-permute-done((bf16[1,256,384]{2,1,0:T(8,128)(2,1)S(1)}, bf16[1,256,384]{2,1,0:T(8,128)(2,1)S(1)}, u32[]{:S(2)}, u32[]{:S(2)}) %collective-permute-start.16) | collective-permute-done | bytes 196640 | tf_op jit(solution)/shard_map/ppermute | solution.py:24
  82.0 1.5 %shard_map.90 = bf16[8,64,1536]{2,1,0:T(8,128)(2,1)} custom-call(bf16[256,384]{1,0:T(8,128)(2,1)S(1)} %bitcast.24, bf16[384,1536]{1,0:T(8,128)(2,1)S(1)} %collective-permute-done.20.refs_7_.refs_1_, f32[256,1536]{1,0:T(8,128)S(1)} %shard_map.89.refs_2_, bf16[8,32,1536]{2,1,0:T(8,128)(2,1)S(1)} %shard_map.88.refs_3_), custom_call_target="tpu_custom_call" | custom-call | flops 301989888 | bytes 7077888 | tf_op jit(solution)/shard_map/pallas_call | solution.py:388
  (45 shorter events, 0.4 us)
Async XLA Ops:
  0.0 1.4 %copy-start.1 = (bf16[1,8,1,64,1536]{4,3,2,1,0:T(8,128)(2,1)S(1)}, bf16[1,8,1,64,1536]{4,3,2,1,0:T(8,128)(2,1)}, u32[]{:S(2)}) copy-start(bf16[1,8,1,64,1536]{4,3,2,1,0:T(8,128)(2,1)} %param.7) | copy-start | bytes 4718596
  1.4 6.7 %copy-start.2 = (bf16[1,8,1,64,1536]{4,3,2,1,0:T(8,128)(2,1)S(1)}, bf16[1,8,1,64,1536]{4,3,2,1,0:T(8,128)(2,1)}, u32[]{:S(2)}) copy-start(bf16[1,8,1,64,1536]{4,3,2,1,0:T(8,128)(2,1)} %param.7) | copy-start | bytes 4718596
  1.5 24.4 %collective-permute-start = (bf16[4,32,1536]{2,1,0:T(8,128)(2,1)S(1)}, bf16[4,32,1536]{2,1,0:T(8,128)(2,1)S(1)}, u32[]{:S(2)}, u32[]{:S(2)}) collective-permute-start(bf16[4,32,1536]{2,1,0:T(8,128)(2,1)S(1)} %get-tuple-element.29), channel_id=1, source_target_pairs={{0,4},{4,0},{8,12},{12,8},{1,5},{5,1},{9,13},{13,9},{2,6},{6,2},{1... | collective-permute-start | bytes 1179656 | tf_op jit(solution)/shard_map/ppermute | solution.py:24
  4.6 7.8 %collective-permute-start.3 = (bf16[4,16,1536]{2,1,0:T(8,128)(2,1)S(1)}, bf16[4,16,1536]{2,1,0:T(8,128)(2,1)S(1)}, u32[]{:S(2)}, u32[]{:S(2)}) collective-permute-start(bf16[4,16,1536]{2,1,0:T(8,128)(2,1)S(1)} %get-tuple-element.30.refs_0_), channel_id=1, source_target_pairs={{0,2},{1,3},{2,0},{3,1},{4,6},{5,7},{6,4},{7,5},{8,10},{9,11},{10,... | collective-permute-start | bytes 589832 | tf_op jit(solution)/shard_map/ppermute | solution.py:24
  6.1 1.3 %copy-start.3 = (bf16[384,1536]{1,0:T(8,128)(2,1)S(1)}, bf16[384,1536]{1,0:T(8,128)(2,1)}, u32[]{:S(2)}) copy-start(bf16[384,1536]{1,0:T(8,128)(2,1)} %refs_3_.5) | copy-start | bytes 3538948
  7.4 18.6 %copy-start.5 = (f32[1536]{0:T(1024)S(1)}, f32[1536]{0:T(1024)}, u32[]{:S(2)}) copy-start(f32[1536]{0:T(1024)} %refs_4_.6) | copy-start | bytes 18436
  7.4 18.6 %copy-start.6 = (f32[1536]{0:T(1024)S(1)}, f32[1536]{0:T(1024)}, u32[]{:S(2)}) copy-start(f32[1536]{0:T(1024)} %refs_5_.6) | copy-start | bytes 18436
  7.4 11.3 %collective-permute-start.17 = (bf16[96,1536]{1,0:T(8,128)(2,1)S(1)}, bf16[96,1536]{1,0:T(8,128)(2,1)S(1)}, u32[]{:S(2)}, u32[]{:S(2)}) collective-permute-start(bf16[96,1536]{1,0:T(8,128)(2,1)S(1)} %shard_map.84), channel_id=1, source_target_pairs={{0,2},{1,3},{2,0},{3,1},{4,6},{5,7},{6,4},{7,5},{8,10},{9,11},{10,... | collective-permute-start | bytes 884744 | tf_op jit(solution)/shard_map/ppermute | solution.py:24
  8.0 14.1 %collective-permute-start.5 = (bf16[4,16,1536]{2,1,0:T(8,128)(2,1)S(1)}, bf16[4,16,1536]{2,1,0:T(8,128)(2,1)S(1)}, u32[]{:S(2)}, u32[]{:S(2)}) collective-permute-start(bf16[4,16,1536]{2,1,0:T(8,128)(2,1)S(1)} %get-tuple-element.32), channel_id=1, source_target_pairs={{0,4},{4,0},{8,12},{12,8},{1,5},{5,1},{9,13},{13,9},{2,6},{6,2},{1... | collective-permute-start | bytes 589832 | tf_op jit(solution)/shard_map/ppermute | solution.py:24
  8.1 30.2 %copy-start = (bf16[3,1536,384]{2,1,0:T(8,128)(2,1)S(1)}, bf16[3,1536,384]{2,1,0:T(8,128)(2,1)}, u32[]{:S(2)}) copy-start(bf16[3,1536,384]{2,1,0:T(8,128)(2,1)} %refs_2_.7) | copy-start | bytes 10616836
  8.2 22.0 %collective-permute-start.11 = (bf16[4,32,1536]{2,1,0:T(8,128)(2,1)S(1)}, bf16[4,32,1536]{2,1,0:T(8,128)(2,1)S(1)}, u32[]{:S(2)}, u32[]{:S(2)}) collective-permute-start(bf16[4,32,1536]{2,1,0:T(8,128)(2,1)S(1)} %slice.4.refs_0_), channel_id=1, source_target_pairs={{0,2},{1,3},{2,0},{3,1},{4,6},{5,7},{6,4},{7,5},{8,10},{9,11},{10,... | collective-permute-start | bytes 1179656 | tf_op jit(solution)/shard_map/ppermute | solution.py:24
  12.4 13.9 %collective-permute-start.6 = (bf16[4,16,1536]{2,1,0:T(8,128)(2,1)S(1)}, bf16[4,16,1536]{2,1,0:T(8,128)(2,1)S(1)}, u32[]{:S(2)}, u32[]{:S(2)}) collective-permute-start(bf16[4,16,1536]{2,1,0:T(8,128)(2,1)S(1)} %get-tuple-element.33), channel_id=1, source_target_pairs={{0,8},{4,12},{8,0},{12,4},{1,9},{5,13},{9,1},{13,5},{2,10},{6,14},... | collective-permute-start | bytes 589832 | tf_op jit(solution)/shard_map/ppermute | solution.py:24
  18.7 11.9 %collective-permute-start.18 = (bf16[96,1536]{1,0:T(8,128)(2,1)S(1)}, bf16[96,1536]{1,0:T(8,128)(2,1)S(1)}, u32[]{:S(2)}, u32[]{:S(2)}) collective-permute-start(bf16[96,1536]{1,0:T(8,128)(2,1)S(1)} %collective-permute-done.17.own_ref), channel_id=1, source_target_pairs={{0,16},{16,0},{1,17},{17,1},{2,18},{18,2},{3,19},{19,3},{4,20},{20... | collective-permute-start | bytes 884744 | tf_op jit(solution)/shard_map/ppermute | solution.py:24
  22.1 16.2 %copy-start.7 = (s32[1,32,64]{2,1,0:T(8,128)S(1)}, s32[1,32,64]{2,1,0:T(8,128)}, u32[]{:S(2)}) copy-start(s32[1,32,64]{2,1,0:T(8,128)} %param.8) | copy-start | bytes 24580
  22.2 8.0 %collective-permute-start.7 = (bf16[4,16,1536]{2,1,0:T(8,128)(2,1)S(1)}, bf16[4,16,1536]{2,1,0:T(8,128)(2,1)S(1)}, u32[]{:S(2)}, u32[]{:S(2)}) collective-permute-start(bf16[4,16,1536]{2,1,0:T(8,128)(2,1)S(1)} %get-tuple-element.34), channel_id=1, source_target_pairs={{0,12},{4,8},{8,4},{12,0},{1,13},{5,9},{9,5},{13,1},{2,14},{6,10},... | collective-permute-start | bytes 589832 | tf_op jit(solution)/shard_map/ppermute | solution.py:24
  25.9 10.3 %collective-permute-start.10 = (bf16[4,32,1536]{2,1,0:T(8,128)(2,1)S(1)}, bf16[4,32,1536]{2,1,0:T(8,128)(2,1)S(1)}, u32[]{:S(2)}, u32[]{:S(2)}) collective-permute-start(bf16[4,32,1536]{2,1,0:T(8,128)(2,1)S(1)} %slice.4.refs_0_), channel_id=1, source_target_pairs={{0,1},{1,0},{2,3},{3,2},{4,5},{5,4},{6,7},{7,6},{8,9},{9,8},{10,11... | collective-permute-start | bytes 1179656 | tf_op jit(solution)/shard_map/ppermute | solution.py:24
  26.3 12.1 %collective-permute-start.13 = (bf16[128,1536]{1,0:T(8,128)(2,1)S(1)}, bf16[128,1536]{1,0:T(8,128)(2,1)S(1)}, u32[]{:S(2)}, u32[]{:S(2)}) collective-permute-start(bf16[128,1536]{1,0:T(8,128)(2,1)S(1)} %shard_map.73.refs_0_), channel_id=1, source_target_pairs={{0,2},{1,3},{2,0},{3,1},{4,6},{5,7},{6,4},{7,5},{8,10},{9,11},{10,... | collective-permute-start | bytes 1179656 | tf_op jit(solution)/shard_map/ppermute | solution.py:24
  30.1 1.4 %collective-permute-start.2 = (bf16[4,16,1536]{2,1,0:T(8,128)(2,1)S(1)}, bf16[4,16,1536]{2,1,0:T(8,128)(2,1)S(1)}, u32[]{:S(2)}, u32[]{:S(2)}) collective-permute-start(bf16[4,16,1536]{2,1,0:T(8,128)(2,1)S(1)} %get-tuple-element.30.refs_0_), channel_id=1, source_target_pairs={{0,1},{1,0},{2,3},{3,2},{4,5},{5,4},{6,7},{7,6},{8,9},{9,8},{10,11... | collective-permute-start | bytes 589832 | tf_op jit(solution)/shard_map/ppermute | solution.py:24
  30.1 2.9 %collective-permute-start.4 = (bf16[4,16,1536]{2,1,0:T(8,128)(2,1)S(1)}, bf16[4,16,1536]{2,1,0:T(8,128)(2,1)S(1)}, u32[]{:S(2)}, u32[]{:S(2)}) collective-permute-start(bf16[4,16,1536]{2,1,0:T(8,128)(2,1)S(1)} %collective-permute-done.3.refs_2_), channel_id=1, source_target_pairs={{0,1},{1,0},{2,3},{3,2},{4,5},{5,4},{6,7},{7,6},{8,9},{9,8},{10,11... | collective-permute-start | bytes 589832 | tf_op jit(solution)/shard_map/ppermute | solution.py:24
  30.6 8.7 %collective-permute-start.12 = (bf16[4,32,1536]{2,1,0:T(8,128)(2,1)S(1)}, bf16[4,32,1536]{2,1,0:T(8,128)(2,1)S(1)}, u32[]{:S(2)}, u32[]{:S(2)}) collective-permute-start(bf16[4,32,1536]{2,1,0:T(8,128)(2,1)S(1)} %collective-permute-done.11.refs_2_), channel_id=1, source_target_pairs={{0,1},{1,0},{2,3},{3,2},{4,5},{5,4},{6,7},{7,6},{8,9},{9,8},{10,11... | collective-permute-start | bytes 1179656 | tf_op jit(solution)/shard_map/ppermute | solution.py:24
  31.6 18.9 %collective-permute-start.9 = (bf16[192,1536]{1,0:T(8,128)(2,1)S(1)}, bf16[192,1536]{1,0:T(8,128)(2,1)S(1)}, u32[]{:S(2)}, u32[]{:S(2)}) collective-permute-start(bf16[192,1536]{1,0:T(8,128)(2,1)S(1)} %shard_map.76.refs_0_), channel_id=1, source_target_pairs={{0,2},{1,3},{2,0},{3,1},{4,6},{5,7},{6,4},{7,5},{8,10},{9,11},{10,... | collective-permute-start | bytes 1769480 | tf_op jit(solution)/shard_map/ppermute | solution.py:24
  33.0 17.5 %collective-permute-start.19 = (bf16[192,1536]{1,0:T(8,128)(2,1)S(1)}, bf16[192,1536]{1,0:T(8,128)(2,1)S(1)}, u32[]{:S(2)}, u32[]{:S(2)}) collective-permute-start(bf16[192,1536]{1,0:T(8,128)(2,1)S(1)} %shard_map.85.own_ref), channel_id=1, source_target_pairs={{0,4},{4,0},{8,12},{12,8},{1,5},{5,1},{9,13},{13,9},{2,6},{6,2},{1... | collective-permute-start | bytes 1769480 | tf_op jit(solution)/shard_map/ppermute | solution.py:24
  36.3 14.9 %collective-permute-start.8 = (bf16[192,1536]{1,0:T(8,128)(2,1)S(1)}, bf16[192,1536]{1,0:T(8,128)(2,1)S(1)}, u32[]{:S(2)}, u32[]{:S(2)}) collective-permute-start(bf16[192,1536]{1,0:T(8,128)(2,1)S(1)} %shard_map.76.refs_0_), channel_id=1, source_target_pairs={{0,1},{1,0},{2,3},{3,2},{4,5},{5,4},{6,7},{7,6},{8,9},{9,8},{10,11... | collective-permute-start | bytes 1769480 | tf_op jit(solution)/shard_map/ppermute | solution.py:24
  38.3 4.9 %collective-permute-start.1 = (bf16[128,1536]{1,0:T(8,128)(2,1)S(1)}, bf16[128,1536]{1,0:T(8,128)(2,1)S(1)}, u32[]{:S(2)}, u32[]{:S(2)}) collective-permute-start(bf16[128,1536]{1,0:T(8,128)(2,1)S(1)} %shard_map.73.refs_0_), channel_id=1, source_target_pairs={{0,1},{1,0},{2,3},{3,2},{4,5},{5,4},{6,7},{7,6},{8,9},{9,8},{10,11... | collective-permute-start | bytes 1179656 | tf_op jit(solution)/shard_map/ppermute | solution.py:24
  39.3 13.6 %collective-permute-start.14 = (bf16[128,1536]{1,0:T(8,128)(2,1)S(1)}, bf16[128,1536]{1,0:T(8,128)(2,1)S(1)}, u32[]{:S(2)}, u32[]{:S(2)}) collective-permute-start(bf16[128,1536]{1,0:T(8,128)(2,1)S(1)} %collective-permute-done.13.refs_0_), channel_id=1, source_target_pairs={{0,1},{1,0},{2,3},{3,2},{4,5},{5,4},{6,7},{7,6},{8,9},{9,8},{10,11... | collective-permute-start | bytes 1179656 | tf_op jit(solution)/shard_map/ppermute | solution.py:24
  41.0 2.2 %copy-start.4 = (bf16[384,1536]{1,0:T(8,128)(2,1)S(1)}, bf16[384,1536]{1,0:T(8,128)(2,1)}, u32[]{:S(2)}) copy-start(bf16[384,1536]{1,0:T(8,128)(2,1)} %refs_3_.5) | copy-start | bytes 3538948
  43.2 28.1 %collective-permute-start.24 = (bf16[384,1536]{1,0:T(8,128)(2,1)S(1)}, bf16[384,1536]{1,0:T(8,128)(2,1)S(1)}, u32[]{:S(2)}, u32[]{:S(2)}) collective-permute-start(bf16[384,1536]{1,0:T(8,128)(2,1)S(1)} %copy-done.4), channel_id=1, source_target_pairs={{0,1},{1,0},{2,3},{3,2},{4,5},{5,4},{6,7},{7,6},{8,9},{9,8},{10,11... | collective-permute-start | bytes 3538952 | tf_op jit(solution)/shard_map/ppermute | solution.py:24
  50.5 11.8 %collective-permute-start.15 = (bf16[192,1536]{1,0:T(8,128)(2,1)S(1)}, bf16[192,1536]{1,0:T(8,128)(2,1)S(1)}, u32[]{:S(2)}, u32[]{:S(2)}) collective-permute-start(bf16[192,1536]{1,0:T(8,128)(2,1)S(1)} %collective-permute-done.9.refs_0_), channel_id=1, source_target_pairs={{0,1},{1,0},{2,3},{3,2},{4,5},{5,4},{6,7},{7,6},{8,9},{9,8},{10,11... | collective-permute-start | bytes 1769480 | tf_op jit(solution)/shard_map/ppermute | solution.py:24
  50.6 22.6 %collective-permute-start.20 = (bf16[384,1536]{1,0:T(8,128)(2,1)S(1)}, bf16[384,1536]{1,0:T(8,128)(2,1)S(1)}, u32[]{:S(2)}, u32[]{:S(2)}) collective-permute-start(bf16[384,1536]{1,0:T(8,128)(2,1)S(1)} %shard_map.86.refs_6_.refs_5_), channel_id=1, source_target_pairs={{0,1},{1,0},{2,3},{3,2},{4,5},{5,4},{6,7},{7,6},{8,9},{9,8},{10,11... | collective-permute-start | bytes 3538952 | tf_op jit(solution)/shard_map/ppermute | solution.py:24
  52.9 1.2 %copy-start.8 = (f32[4]{0:T(128)S(1)}, f32[4]{0:T(128)}, u32[]{:S(2)}) copy-start(f32[4]{0:T(128)} %refs_5_.9) | copy-start | bytes 52
  60.6 11.1 %collective-permute-start.21 = (bf16[1,256,384]{2,1,0:T(8,128)(2,1)S(1)}, bf16[1,256,384]{2,1,0:T(8,128)(2,1)S(1)}, u32[]{:S(2)}, u32[]{:S(2)}) collective-permute-start(bf16[1,256,384]{2,1,0:T(8,128)(2,1)S(1)} %get-tuple-element.40), channel_id=1, source_target_pairs={{0,1},{1,0},{2,3},{3,2},{4,5},{5,4},{6,7},{7,6},{8,9},{9,8},{10,11... | collective-permute-start | bytes 589832 | tf_op jit(solution)/shard_map/ppermute | solution.py:24
  60.7 12.5 %collective-permute-start.22 = (bf16[1,256,384]{2,1,0:T(8,128)(2,1)S(1)}, bf16[1,256,384]{2,1,0:T(8,128)(2,1)S(1)}, u32[]{:S(2)}, u32[]{:S(2)}) collective-permute-start(bf16[1,256,384]{2,1,0:T(8,128)(2,1)S(1)} %get-tuple-element.41), channel_id=1, source_target_pairs={{0,2},{1,3},{2,0},{3,1},{4,6},{5,7},{6,4},{7,5},{8,10},{9,11},{10,... | collective-permute-start | bytes 589832 | tf_op jit(solution)/shard_map/ppermute | solution.py:24
  62.3 11.0 %collective-permute-start.23 = (bf16[1,256,384]{2,1,0:T(8,128)(2,1)S(1)}, bf16[1,256,384]{2,1,0:T(8,128)(2,1)S(1)}, u32[]{:S(2)}, u32[]{:S(2)}) collective-permute-start(bf16[1,256,384]{2,1,0:T(8,128)(2,1)S(1)} %get-tuple-element.42), channel_id=1, source_target_pairs={{0,3},{1,2},{2,1},{3,0},{4,7},{5,6},{6,5},{7,4},{8,11},{9,10},{10,... | collective-permute-start | bytes 589832 | tf_op jit(solution)/shard_map/ppermute | solution.py:24
  71.3 3.3 %collective-permute-start.25 = (bf16[1,256,384]{2,1,0:T(8,128)(2,1)S(1)}, bf16[1,256,384]{2,1,0:T(8,128)(2,1)S(1)}, u32[]{:S(2)}, u32[]{:S(2)}) collective-permute-start(bf16[1,256,384]{2,1,0:T(8,128)(2,1)S(1)} %get-tuple-element.50), channel_id=1, source_target_pairs={{0,1},{1,0},{2,3},{3,2},{4,5},{5,4},{6,7},{7,6},{8,9},{9,8},{10,11... | collective-permute-start | bytes 589832 | tf_op jit(solution)/shard_map/ppermute | solution.py:24
  71.7 7.8 %collective-permute-start.26 = (bf16[1,256,384]{2,1,0:T(8,128)(2,1)S(1)}, bf16[1,256,384]{2,1,0:T(8,128)(2,1)S(1)}, u32[]{:S(2)}, u32[]{:S(2)}) collective-permute-start(bf16[1,256,384]{2,1,0:T(8,128)(2,1)S(1)} %get-tuple-element.47), channel_id=1, source_target_pairs={{0,2},{1,3},{2,0},{3,1},{4,6},{5,7},{6,4},{7,5},{8,10},{9,11},{10,... | collective-permute-start | bytes 589832 | tf_op jit(solution)/shard_map/ppermute | solution.py:24
  73.2 8.8 %collective-permute-start.16 = (bf16[1,256,384]{2,1,0:T(8,128)(2,1)S(1)}, bf16[1,256,384]{2,1,0:T(8,128)(2,1)S(1)}, u32[]{:S(2)}, u32[]{:S(2)}) collective-permute-start(bf16[1,256,384]{2,1,0:T(8,128)(2,1)S(1)} %get-tuple-element.46), channel_id=1, source_target_pairs={{0,3},{1,2},{2,1},{3,0},{4,7},{5,6},{6,5},{7,4},{8,11},{9,10},{10,... | collective-permute-start | bytes 589832 | tf_op jit(solution)/shard_map/ppermute | solution.py:24
